TPU v7x, 32 devices: a whole 2x2x4 slice. The times are simulated.
32 devices in a mesh: section: 4 (over x, core), dp: 8 (over z, y).
Axes of the slice: x: 2, y: 2, z: 4, core: 2. Of those that a mesh axis runs over, the one named last changes fastest.
Arguments:
- activations: bfloat16 [4, 4, 2048, 1024], P('section', None, 'dp'), may hold values from -6 to 6
- section_weights: bfloat16 [4, 1024, 1024], P('section'), may hold values from -0.1875 to 0.1875
- cand_table: bfloat16 [128, 2048], replicated, may hold values from -6 to 6
- cand_index: int32 [4, 8, 64], P(None, 'dp'), may hold values from 0 to 127
- cand_count: int32 [4, 8], P(None, 'dp'), may hold values from 1 to 64, as said below
- pooled_cotangent: bfloat16 [4, 8, 1024], P(None, 'dp'), may hold values from -6 to 6
Outputs:
- weight_grads: float32 [4, 1024, 1024], P('section', 'dp')
- table_grads: float32 [128, 2048], P('dp', 'section')
Inputs may be any that keep to these rules, and one draw needn't show every extreme that they name: `cand_count`: the first sample of every micro-batch has all 64 candidates valid.
All inputs are finite; a program needn't handle non-finite values.
Results may differ from a plain program's by a relative error of at most 0.014.
Values may be sent and summed in bfloat16 or wider, within the bound.
No kernel may reach another device: no remote copies, remote signals or barrier semaphores. Data moves between devices by JAX's collectives and lax.ppermute only.
A program may use at most 64 MiB of HBM per device.

v0:
```python
import functools
import math

import jax
import jax.numpy as jnp
from jax import lax
from jax.experimental import pallas as pl
from jax.experimental.pallas import tpu as pltpu
from jax.sharding import PartitionSpec as P

HEAD = 64
PAIR = 2 * HEAD
TILE = 256
MIB = 1024 * 1024
HBM = pl.BlockSpec(memory_space=pltpu.HBM)
VMEM = pl.BlockSpec(memory_space=pltpu.VMEM)
SMEM = pl.BlockSpec(memory_space=pltpu.SMEM)
BF16 = jnp.bfloat16
F32 = jnp.float32
LIGHT = pl.CostEstimate(flops=1024, bytes_accessed=1024, transcendentals=0)

NN = (((1,), (0,)), ((), ()))
NT = (((1,), (1,)), ((), ()))
TN = (((0,), (0,)), ((), ()))


def dot(left, right, dims):
    return lax.dot_general(left, right, dims, preferred_element_type=F32)


def gelu_parts(hidden):
    root = math.sqrt(2.0 / math.pi)
    square = hidden * hidden
    bent = jnp.tanh(root * hidden * (1.0 + 0.044715 * square))
    share = 0.5 + 0.5 * bent
    slope = share + (0.5 * root) * hidden * (1.0 - bent * bent) * (1.0 + (3 * 0.044715) * square)
    return hidden * share, slope


def high_low(values):
    high = values.astype(BF16)
    return high, (values - high.astype(F32)).astype(BF16)


def stay(array):
    return pltpu.with_memory_space_constraint(array, pltpu.HBM)


def first_kernel(
    m, flag_ref, count_ref, acts_hbm, weight, table_hbm, index_hbm, pooled_hbm, after_hbm,
    grad_hbm, aux_hbm, share_hbm, high_hbm, acts, table, index_ref, pooled_ref, grad, aux, share_ref, high_ref, sems,
):
    rows, width = acts.shape
    table_rows = table.shape[0]
    pairs = width // PAIR
    tiles = width // TILE
    tile = [slice(q * TILE, (q + 1) * TILE) for q in range(tiles)]
    pair = [slice(j * PAIR, (j + 1) * PAIR) for j in range(pairs)]
    load = pltpu.make_async_copy(acts_hbm.at[m], acts, sems.at[0])
    load.start()
    store_aux = pltpu.make_async_copy(aux, aux_hbm, sems.at[1])

    @pl.when(flag_ref[0] == 0)
    def _():
        load.wait()
        for cols in tile:
            hidden = dot(acts[...], weight[:, cols], NN)
            aux[:, cols] = gelu_parts(hidden)[1].astype(BF16)
        store_aux.start()
        store_aux.wait()

    @pl.when(flag_ref[0] == 1)
    def _():
        load_index = pltpu.make_async_copy(index_hbm, index_ref, sems.at[6])
        load_pooled = pltpu.make_async_copy(pooled_hbm, pooled_ref, sems.at[7])
        load_table = pltpu.make_async_copy(table_hbm, table, sems.at[2])
        load_index.start()
        load_pooled.start()
        load_table.start()
        load.wait()
        slopes, highs, lows = [], [], []
        for cols in tile:
            hidden = dot(acts[...], weight[:, cols], NN)
            bent, slope = gelu_parts(hidden)
            high, low = high_low(acts[:, cols].astype(F32) + bent)
            high_ref[:, cols] = high
            slopes.append(slope)
            lows.append(low)
        store_high = pltpu.make_async_copy(high_ref, high_hbm, sems.at[3])
        store_high.start()
        load_table.wait()
        load_index.wait()
        load_pooled.wait()
        index = index_ref[m]
        index = jnp.concatenate([index, index], axis=1)
        onehot = (lax.broadcasted_iota(jnp.int32, (table_rows, PAIR), 0) == index).astype(BF16)
        gathered = dot(onehot, table[...], TN)
        own = (
            lax.broadcasted_iota(jnp.int32, (PAIR, width), 0) // HEAD
            == lax.broadcasted_iota(jnp.int32, (PAIR, width), 1) // HEAD % 2
        )
        keys = jnp.where(own, gathered[:, :width] * (1.0 / math.sqrt(HEAD)), 0.0).astype(BF16)
        values = jnp.where(own, gathered[:, width:], 0.0).astype(BF16)
        allowed = lax.broadcasted_iota(jnp.int32, (2, HEAD, rows), 1) < count_ref[0, m]
        given_row = pooled_ref[m : m + 1].astype(F32) * (1.0 / rows)
        given = jnp.broadcast_to(given_row, (rows, width)).astype(BF16)
        scores = []
        for j, here in enumerate(pair):
            part = slice(j * PAIR % TILE, j * PAIR % TILE + PAIR)
            scores.append(
                dot(
                    jnp.concatenate([keys[:, here], keys[:, here]], axis=1),
                    jnp.concatenate([high_ref[:, here], lows[j * PAIR // TILE][:, part]], axis=1),
                    NT,
                )
            )
        slants = []
        for j, here in enumerate(pair):
            share, slant = soften(scores[j], dot(values[:, here], given[:, here], NT), allowed)
            share_ref[here] = share
            slants.append(slant)
        store_share = pltpu.make_async_copy(share_ref, share_hbm, sems.at[4])
        store_share.start()
        totals = []
        for j, here in enumerate(pair):
            part = slice(j * PAIR % TILE, j * PAIR % TILE + PAIR)
            total = given_row[:, here] + dot(slants[j], keys[:, here], TN)
            totals.append(total)
            aux[:, here] = (total * slopes[j * PAIR // TILE][:, part]).astype(BF16)
        store_aux.start()
        for q, cols in enumerate(tile):
            total = jnp.concatenate(totals[q * TILE // PAIR : (q + 1) * TILE // PAIR], axis=1)
            grad[:, cols] = (total + dot(aux[...], weight[cols, :], NT)).astype(BF16)
        store_grad = pltpu.make_async_copy(grad, grad_hbm, sems.at[5])
        store_grad.start()
        store_high.wait()
        store_share.wait()
        store_aux.wait()
        store_grad.wait()


def lean(share, worth):
    worth = worth.reshape(share.shape)
    centre = jnp.sum(share * worth, axis=1, keepdims=True)
    return (share * (worth - centre)).reshape(worth.shape[0] * worth.shape[1], -1).astype(BF16)


def soften(score, worth, allowed):
    score = jnp.where(allowed, score.reshape(allowed.shape), -1e30)
    raised = jnp.exp(score - jnp.max(score, axis=1, keepdims=True))
    share = raised * (1.0 / jnp.sum(raised, axis=1, keepdims=True))
    return share.reshape(worth.shape).astype(BF16), lean(share, worth)


def first_call(m, flag, count, acts, weight, table, index, pooled, after):
    rows, width = acts.shape[1:]
    turned = (width // HEAD * index.shape[2], rows)
    block = pltpu.HBM((rows, width), BF16)
    return pl.pallas_call(
        functools.partial(first_kernel, m),
        out_shape=(block, block, pltpu.HBM(turned, BF16), block),
        in_specs=[SMEM, SMEM, HBM, VMEM, HBM, HBM, HBM, HBM],
        out_specs=(HBM,) * 4,
        scratch_shapes=[
            pltpu.VMEM((rows, width), BF16),
            pltpu.VMEM(table.shape, BF16),
            pltpu.VMEM(index.shape, jnp.int32),
            pltpu.VMEM(pooled.shape, BF16),
            pltpu.VMEM((rows, width), BF16),
            pltpu.VMEM((rows, width), BF16),
            pltpu.VMEM(turned, BF16),
            pltpu.VMEM((rows, width), BF16),
            pltpu.SemaphoreType.DMA((8,)),
        ],
        compiler_params=pltpu.CompilerParams(vmem_limit_bytes=28 * MIB),
        cost_estimate=LIGHT,
        name="first",
    )(flag, count, stay(acts), weight, stay(table), stay(index), stay(pooled), stay(after))


def table_kernel(replicas, flag_ref, parity_ref, index_ref, pooled_ref, table_hbm, *refs):
    count = (len(refs) - 7) // 2
    sources = refs[: 2 * count]
    send_ref, keep_ref, table, share, high, kv, sems = refs[2 * count :]
    width = high.shape[2]
    rows = high.shape[1]
    table_rows = 2 * keep_ref.shape[0]
    cands = index_ref.shape[2]

    @pl.when(flag_ref[0] == 1)
    def _():
        loads = []
        for m in range(count):
            for k, target in enumerate((share, high)):
                loads.append(pltpu.make_async_copy(sources[k * count + m], target.at[m], sems.at[2 * m + k]))
        loads.append(pltpu.make_async_copy(table_hbm, table, sems.at[2 * count]))
        for load in loads:
            load.start()
        steps = replicas.bit_length() - 1
        shift = (table_rows // replicas).bit_length() - 1
        spot = lax.broadcasted_iota(jnp.int32, (table_rows, cands), 0)
        block = spot >> shift
        low_bit = jnp.where(block < replicas // 2, 1 - parity_ref[0], parity_ref[0])
        for k in range(steps - 1):
            low_bit = low_bit + (((block >> (steps - 2 - k)) & 1) << (k + 1))
        row = (low_bit << shift) + (spot & ((1 << shift) - 1))
        left_half = lax.broadcasted_iota(jnp.int32, (HEAD, PAIR), 1) < HEAD
        own = (
            lax.broadcasted_iota(jnp.int32, (PAIR, width), 0) // HEAD
            == lax.broadcasted_iota(jnp.int32, (PAIR, width), 1) // HEAD % 2
        )
        loads[-1].wait()
        onehots = []
        for m in range(count):
            onehots.append((row == index_ref[m]).astype(BF16))
            given = jnp.broadcast_to(pooled_ref[m : m + 1].astype(F32) * (1.0 / rows), (rows, width)).astype(BF16)
            index = jnp.concatenate([index_ref[m], index_ref[m]], axis=1)
            onehot = (lax.broadcasted_iota(jnp.int32, (table_rows, PAIR), 0) == index).astype(BF16)
            values = jnp.where(own, dot(onehot, table[:, width:], TN), 0.0).astype(BF16)
            for k in range(2):
                loads[2 * m + k].wait()
            for j in range(width // PAIR):
                here = slice(j * PAIR, (j + 1) * PAIR)
                slant = lean(
                    share[m, here].astype(F32).reshape(2, HEAD, rows), dot(values[:, here], given[:, here], NT)
                )
                key = dot(slant, high[m, :, here], NN) * (1.0 / math.sqrt(HEAD))
                value = dot(share[m, here], given[:, here], NN)
                lines = slice(m * cands, (m + 1) * cands)
                kv[lines, here] = jnp.where(left_half, key[:HEAD], key[HEAD:])
                kv[lines, width + j * PAIR : width + (j + 1) * PAIR] = jnp.where(
                    left_half, value[:HEAD], value[HEAD:]
                )
        onehot = jnp.concatenate(onehots, axis=1)
        for at in range(0, 2 * width, 2 * TILE):
            cols = slice(at, at + 2 * TILE)
            kv_high, kv_low = high_low(kv[:, cols])
            part = dot(onehot, kv_high, NN) + dot(onehot, kv_low, NN)
            send_ref[:, cols] = part[: table_rows // 2].astype(BF16)
            keep_ref[:, cols] = part[table_rows // 2 :]


def table_call(flag, parity, index, pooled, table, shares, highs, replicas):
    rows, width = highs[0].shape
    count = len(highs)
    half = (table.shape[0] // 2, 2 * width)
    return pl.pallas_call(
        functools.partial(table_kernel, replicas),
        out_shape=(jax.ShapeDtypeStruct(half, BF16), jax.ShapeDtypeStruct(half, F32)),
        in_specs=[SMEM, SMEM, VMEM, VMEM, HBM] + [HBM] * (2 * count),
        out_specs=(VMEM, VMEM),
        scratch_shapes=[
            pltpu.VMEM(table.shape, BF16),
            pltpu.VMEM((count,) + shares[0].shape, BF16),
            pltpu.VMEM((count,) + highs[0].shape, BF16),
            pltpu.VMEM((count * index.shape[2], 2 * width), F32),
            pltpu.SemaphoreType.DMA((2 * count + 1,)),
        ],
        compiler_params=pltpu.CompilerParams(vmem_limit_bytes=28 * MIB),
        cost_estimate=LIGHT,
        name="table",
    )(flag, parity, index, pooled, stay(table), *map(stay, shares), *map(stay, highs))


def hop_kernel(with_grad, flag_ref, came_hbm, aux_hbm, weight, after_hbm, *rest):
    if with_grad:
        grad_hbm, aux_out, came, aux, grad, sems = rest
    else:
        aux_out, came, aux, sems = rest
    rows, width = came.shape

    @pl.when(flag_ref[0] == 1)
    def _():
        first = pltpu.make_async_copy(came_hbm, came, sems.at[0])
        second = pltpu.make_async_copy(aux_hbm, aux, sems.at[1])
        first.start()
        second.start()
        first.wait()
        second.wait()
        aux[...] = (came[...].astype(F32) * aux[...].astype(F32)).astype(BF16)
        stores = [pltpu.make_async_copy(aux, aux_out, sems.at[2])]
        stores[0].start()
        if with_grad:
            for n in range(width // TILE):
                part = slice(n * TILE, (n + 1) * TILE)
                grad[:, part] = (came[:, part].astype(F32) + dot(aux[...], weight[part, :], NT)).astype(BF16)
            stores.append(pltpu.make_async_copy(grad, grad_hbm, sems.at[3]))
            stores[-1].start()
        for store in stores:
            store.wait()


def hop_call(flag, came, aux, weight, after, with_grad):
    rows, width = came.shape
    block = pltpu.HBM((rows, width), BF16)
    scratch = [pltpu.VMEM((rows, width), BF16)] * (3 if with_grad else 2)
    scratch.append(pltpu.SemaphoreType.DMA((4,)))
    outs = (block, block) if with_grad else (block,)
    return pl.pallas_call(
        functools.partial(hop_kernel, with_grad),
        out_shape=outs,
        in_specs=[SMEM, HBM, HBM, VMEM if with_grad else HBM, HBM],
        out_specs=(HBM,) * len(outs),
        scratch_shapes=scratch,
        input_output_aliases={2: len(outs) - 1},
        compiler_params=pltpu.CompilerParams(vmem_limit_bytes=12 * MIB),
        cost_estimate=LIGHT,
        name="hop" if with_grad else "end",
    )(flag, came, stay(aux), weight if with_grad else stay(weight), stay(after))


def bit_orders(replicas):
    bits = list(range(replicas.bit_length() - 1))
    return [bits, bits[1::-1] + bits[2:]]


def block_order(bits):
    rest = bits[1:]
    order = []
    for i in range(1 << len(rest)):
        order.append(sum(((i >> (len(rest) - 1 - k)) & 1) << bit for k, bit in enumerate(rest)))
    return order


def turn_kernel(replicas, number_ref, acts_hbm, after_hbm, *refs):
    outs = refs[:2]
    acts, turned, sems = refs[2:]
    count, rows, width = acts.shape
    size = width // replicas
    loads = [pltpu.make_async_copy(acts_hbm.at[m], acts.at[m], sems.at[m]) for m in range(count)]
    for load in loads:
        load.start()
    for m in range(count):
        loads[m].wait()
        turned[...] = acts[m].T
        for out, bits in zip(outs, bit_orders(replicas)):
            order = block_order(bits)
            mine = (number_ref[0] >> bits[0]) & 1
            for i, block in enumerate(order + order):
                bit = 1 - mine if i < len(order) else mine
                source = pl.ds(pl.multiple_of((block + (bit << bits[0])) * size, size), size)
                out[i * size : (i + 1) * size, m * rows : (m + 1) * rows] = turned[source]


def turn_call(number, acts, after, replicas):
    count, rows, width = acts.shape
    return pl.pallas_call(
        functools.partial(turn_kernel, replicas),
        out_shape=(jax.ShapeDtypeStruct((width, count * rows), BF16),) * 2,
        in_specs=[SMEM, HBM, HBM],
        out_specs=(VMEM, VMEM),
        scratch_shapes=[
            pltpu.VMEM(acts.shape, BF16),
            pltpu.VMEM((width, rows), BF16),
            pltpu.SemaphoreType.DMA((count,)),
        ],
        compiler_params=pltpu.CompilerParams(vmem_limit_bytes=24 * MIB),
        cost_estimate=LIGHT,
        name="turn",
    )(number, stay(acts), after)


def weight_kernel(flag_ref, *refs):
    turned, refs = refs[:2], refs[2:]
    count = len(refs) - 7
    delta_hbm, came, outs = refs[:count], refs[count], refs[count + 1 : count + 5]
    delta, sems = refs[count + 5 :]
    width = delta.shape[1]
    rows = delta.shape[0] // count
    half = width // 2
    copies = [
        pltpu.make_async_copy(delta_hbm[m], delta.at[pl.ds(m * rows, rows)], sems.at[m]) for m in range(count)
    ]
    for copy in copies:
        copy.start()
    for copy in copies:
        copy.wait()

    @pl.when(flag_ref[0] == 1)
    def _():
        tail = pl.ds((count - 1) * rows, rows)
        delta[tail] = (came[...].astype(F32) * delta[tail].astype(F32)).astype(BF16)

    for which in range(2):
        for c in range(2):
            out = outs[2 * c + which]
            for at in range(0, half, TILE):
                cols = slice(c * half + at, c * half + at + TILE)
                product = dot(turned[c][which * half : (which + 1) * half], delta[:, cols], NN)
                out[:, at : at + TILE] = product.astype(out.dtype)


def weight_call(flag, turned, deltas, came):
    rows, width = deltas[0].shape
    count = len(deltas)
    half = (width // 2, width // 2)
    return pl.pallas_call(
        weight_kernel,
        out_shape=(pltpu.HBM(half, BF16), jax.ShapeDtypeStruct(half, F32)) * 2,
        in_specs=[SMEM, VMEM, VMEM] + [HBM] * count + [VMEM],
        out_specs=(VMEM,) * 4,
        scratch_shapes=[
            pltpu.VMEM((count * rows, width), BF16),
            pltpu.SemaphoreType.DMA((count,)),
        ],
        compiler_params=pltpu.CompilerParams(vmem_limit_bytes=28 * MIB),
        cost_estimate=LIGHT,
        name="weight",
    )(flag, *turned, *map(stay, deltas), came)


def own_half(keep, got, bit):
    mine = (lax.axis_index("dp") >> bit) & 1

    def pick(which):
        return lax.dynamic_index_in_dim(keep, which, 0, keepdims=False) + lax.dynamic_index_in_dim(
            got, which, 0, keepdims=False
        ).astype(F32)

    return pick(1 - mine).astype(BF16), pick(mine)


def finish_scatter(send, keep, bits, axes, pairs_of):
    for n, bit in enumerate(bits):
        got = lax.ppermute(send, axes, pairs_of(bit))
        if n + 1 < len(bits):
            lead = (2, keep.shape[0] // 2, keep.shape[1])
            send, keep = own_half(keep.reshape(lead), got.reshape(lead), bits[n + 1])
    return keep + got.astype(F32)


def body(activations, section_weights, cand_table, cand_index, cand_count, pooled_cotangent):
    sections = lax.axis_size("section")
    replicas = lax.axis_size("dp")
    position = lax.axis_index("section")
    replica = lax.axis_index("dp")
    last = sections - 1
    final_flag = position == last
    acts = activations[0]
    weight = section_weights[0]
    micro_count, row_count, model_width = acts.shape

    def flag(truth):
        return truth.astype(jnp.int32).reshape(1)

    number = replica.reshape(1)
    count = cand_count.reshape(1, micro_count)
    pooled = pooled_cotangent.reshape(micro_count, model_width)
    final = flag(final_flag)
    grads, aux, shares, highs = [], [], [], []
    for m in range(micro_count):
        after = aux[m - 1] if m else acts
        out = first_call(m, final, count, acts, weight, cand_table, cand_index, pooled, after)
        for kept, item in zip((grads, aux, shares, highs), out):
            kept.append(item)

    def table_pairs(bit):
        return [(last * replicas + i, last * replicas + (i ^ (1 << bit))) for i in range(replicas)]

    def pairs(bit):
        return [(i, i ^ (1 << bit)) for i in range(replicas)]

    orders = bit_orders(replicas)
    table_send, table_keep = table_call(
        final, number & 1, cand_index, pooled, cand_table, shares, highs, replicas
    )
    own_table = finish_scatter(table_send, table_keep, orders[0], ("section", "dp"), table_pairs)
    for hop in range(last):
        source = last - hop
        received = [lax.ppermute(g, "section", [(source, source - 1)]) for g in grads]
        active = flag(position == source - 1)
        if hop + 1 == last:
            turned = turn_call(number, acts, received[0], replicas)
        for m in range(micro_count):
            after = aux[m - 1] if m else acts
            if hop + 1 == last and m + 2 == micro_count:
                after = own_table
            if hop + 1 < last:
                grads[m], aux[m] = hop_call(active, received[m], aux[m], weight, after, True)
            elif m + 1 < micro_count:
                (aux[m],) = hop_call(active, received[m], aux[m], weight, after, False)

    width = 2 * model_width // sections
    spread = [
        lax.ppermute(own_table[:, s * width : (s + 1) * width].astype(BF16), "section", [(last, s)])
        for s in range(last)
    ]

    pieces = weight_call(active, turned, aux, received[-1])
    sums = [finish_scatter(pieces[2 * c], pieces[2 * c + 1], orders[c], "dp", pairs) for c in range(2)]
    late_flag, sums = lax.optimization_barrier((flag(final_flag), sums))
    table_sum = jnp.where(
        late_flag[0] == 1, own_table[:, last * width :], sum(piece.astype(F32) for piece in spread)
    )
    return jnp.concatenate(sums, axis=1)[None], table_sum


def solution(mesh):
    in_specs = (
        P("section", None, "dp", None),
        P("section", None, None),
        P(),
        P(None, "dp", None),
        P(None, "dp"),
        P(None, "dp", None),
    )
    out_specs = (P("section", "dp", None), P("dp", "section"))
    return jax.shard_map(body, mesh=mesh, in_specs=in_specs, out_specs=out_specs, check_vma=False)
```

profile of v0, /device:TPU:0, one launch (start us, length us, event | category | flops | bytes accessed | tf_op | source)
XLA Modules:
  0.0 106.1 jit_solution(9270920952016137160)
XLA Ops:
  0.7 1.6 %copy-done = bf16[1,1024,1024]{2,1,0:T(8,128)(2,1)S(1)} copy-done((bf16[1,1024,1024]{2,1,0:T(8,128)(2,1)S(1)}, bf16[1,1024,1024]{2,1,0:T(8,128)(2,1)}, u32[]{:S(2)}) %copy-start) | copy-done | bytes 2097176
  2.2 0.7 copy-done.4
  2.9 3.6 %first.4 = (bf16[256,1024]{1,0:T(8,128)(2,1)}, bf16[256,1024]{1,0:T(8,128)(2,1)}, bf16[1024,256]{1,0:T(8,128)(2,1)}, bf16[256,1024]{1,0:T(8,128)(2,1)}) custom-call(s32[1]{0:T(128)} %bitcast.flag_ref, s32[1,4]{1,0:T(1,128)S(1)} %bitcast.66, bf16[4,256,1024]{2,1,0:T(8,128)(2,1)} %bitcast.70, bf16[1024,1024]{1,0:T(8,128)(2,1)S(1)} %bitcast.46, ...), custom_call_target="tpu_custom_call" | custom-call | flops 1024 | bytes 1024 | tf_op jit(solution)/shard_map/first/pallas_call | solution.py:159
  6.5 1.5 %collective-permute-start = (bf16[256,1024]{1,0:T(8,128)(2,1)}, bf16[256,1024]{1,0:T(8,128)(2,1)}, u32[]{:S(2)}, u32[]{:S(2)}) collective-permute-start(bf16[256,1024]{1,0:T(8,128)(2,1)} %get-tuple-element.45), channel_id=1, source_target_pairs={{24,16},{25,17},{26,18},{27,19},{28,20},{29,21},{30,22},{31,23}} | collective-permute-start | bytes 1572872 | tf_op jit(solution)/shard_map/ppermute | solution.py:470
  8.0 3.6 %first.5 = (bf16[256,1024]{1,0:T(8,128)(2,1)}, bf16[256,1024]{1,0:T(8,128)(2,1)}, bf16[1024,256]{1,0:T(8,128)(2,1)}, bf16[256,1024]{1,0:T(8,128)(2,1)}) custom-call(s32[1]{0:T(128)} %bitcast.flag_ref, s32[1,4]{1,0:T(1,128)S(1)} %bitcast.67, bf16[4,256,1024]{2,1,0:T(8,128)(2,1)} %bitcast.72, bf16[1024,1024]{1,0:T(8,128)(2,1)S(1)} %bitcast.47, ...), custom_call_target="tpu_custom_call" | custom-call | flops 1024 | bytes 1024 | tf_op jit(solution)/shard_map/first/pallas_call | solution.py:159
  11.7 0.7 collective-permute-start.3
  12.4 3.6 %first.6 = (bf16[256,1024]{1,0:T(8,128)(2,1)}, bf16[256,1024]{1,0:T(8,128)(2,1)}, bf16[1024,256]{1,0:T(8,128)(2,1)}, bf16[256,1024]{1,0:T(8,128)(2,1)}) custom-call(s32[1]{0:T(128)} %bitcast.flag_ref, s32[1,4]{1,0:T(1,128)S(1)} %bitcast.68, bf16[4,256,1024]{2,1,0:T(8,128)(2,1)} %bitcast.73, bf16[1024,1024]{1,0:T(8,128)(2,1)S(1)} %bitcast.48, ...), custom_call_target="tpu_custom_call" | custom-call | flops 1024 | bytes 1024 | tf_op jit(solution)/shard_map/first/pallas_call | solution.py:159
  16.0 1.5 %collective-permute-start.6 = (bf16[256,1024]{1,0:T(8,128)(2,1)}, bf16[256,1024]{1,0:T(8,128)(2,1)}, u32[]{:S(2)}, u32[]{:S(2)}) collective-permute-start(bf16[256,1024]{1,0:T(8,128)(2,1)} %get-tuple-element.59), channel_id=1, source_target_pairs={{24,16},{25,17},{26,18},{27,19},{28,20},{29,21},{30,22},{31,23}} | collective-permute-start | bytes 1572872 | tf_op jit(solution)/shard_map/ppermute | solution.py:470
  17.5 3.6 %first.7 = (bf16[256,1024]{1,0:T(8,128)(2,1)}, bf16[256,1024]{1,0:T(8,128)(2,1)}, bf16[1024,256]{1,0:T(8,128)(2,1)}, bf16[256,1024]{1,0:T(8,128)(2,1)}) custom-call(s32[1]{0:T(128)} %bitcast.flag_ref, s32[1,4]{1,0:T(1,128)S(1)} %bitcast.69, bf16[4,256,1024]{2,1,0:T(8,128)(2,1)} %bitcast.74, bf16[1024,1024]{1,0:T(8,128)(2,1)S(1)} %bitcast.49, ...), custom_call_target="tpu_custom_call" | custom-call | flops 1024 | bytes 1024 | tf_op jit(solution)/shard_map/first/pallas_call | solution.py:159
  21.1 1.5 %collective-permute-start.12 = (bf16[256,1024]{1,0:T(8,128)(2,1)}, bf16[256,1024]{1,0:T(8,128)(2,1)}, u32[]{:S(2)}, u32[]{:S(2)}) collective-permute-start(bf16[256,1024]{1,0:T(8,128)(2,1)} %get-tuple-element.75), channel_id=1, source_target_pairs={{24,16},{25,17},{26,18},{27,19},{28,20},{29,21},{30,22},{31,23}} | collective-permute-start | bytes 1572872 | tf_op jit(solution)/shard_map/ppermute | solution.py:470
  22.7 1.5 %collective-permute-start.9 = (bf16[64,2048]{1,0:T(8,128)(2,1)S(1)}, bf16[64,2048]{1,0:T(8,128)(2,1)}, u32[]{:S(2)}, u32[]{:S(2)}) collective-permute-start(bf16[64,2048]{1,0:T(8,128)(2,1)S(1)} %get-tuple-element.74), channel_id=1, source_target_pairs={{24,25},{25,24},{26,27},{27,26},{28,29},{29,28},{30,31},{31,30}} | collective-permute-start | bytes 786440 | tf_op jit(solution)/shard_map/ppermute | solution.py:425
  24.3 1.5 %collective-permute-start.1 = (bf16[256,1024]{1,0:T(8,128)(2,1)}, bf16[256,1024]{1,0:T(8,128)(2,1)}, u32[]{:S(2)}, u32[]{:S(2)}) collective-permute-start(bf16[256,1024]{1,0:T(8,128)(2,1)} %get-tuple-element.47), channel_id=1, source_target_pairs={{16,8},{17,9},{18,10},{19,11},{20,12},{21,13},{22,14},{23,15}} | collective-permute-start | bytes 1572872 | tf_op jit(solution)/shard_map/ppermute | solution.py:470
  25.8 0.7 collective-permute-start.4
  26.6 1.5 %collective-permute-start.7 = (bf16[256,1024]{1,0:T(8,128)(2,1)}, bf16[256,1024]{1,0:T(8,128)(2,1)}, u32[]{:S(2)}, u32[]{:S(2)}) collective-permute-start(bf16[256,1024]{1,0:T(8,128)(2,1)} %get-tuple-element.61), channel_id=1, source_target_pairs={{16,8},{17,9},{18,10},{19,11},{20,12},{21,13},{22,14},{23,15}} | collective-permute-start | bytes 1572872 | tf_op jit(solution)/shard_map/ppermute | solution.py:470
  28.1 1.5 %collective-permute-start.13 = (bf16[256,1024]{1,0:T(8,128)(2,1)}, bf16[256,1024]{1,0:T(8,128)(2,1)}, u32[]{:S(2)}, u32[]{:S(2)}) collective-permute-start(bf16[256,1024]{1,0:T(8,128)(2,1)} %get-tuple-element.77), channel_id=1, source_target_pairs={{16,8},{17,9},{18,10},{19,11},{20,12},{21,13},{22,14},{23,15}} | collective-permute-start | bytes 1572872 | tf_op jit(solution)/shard_map/ppermute | solution.py:470
  29.6 1.7 %fusion.2 = (bf16[32,2048]{1,0:T(8,128)(2,1)}, f32[1,32,2048]{2,1,0:T(8,128)S(1)}) fusion(f32[2,32,2048]{2,1,0:T(8,128)S(1)} %bitcast.60, s32[]{:T(128)S(6)} %select_n.54, bf16[2,32,2048]{2,1,0:T(8,128)(2,1)} %bitcast.10, s32[]{:T(128)S(6)} %select_n.52), kind=kLoop, calls=%fused_computation.13 | loop fusion | flops 327680 | bytes 1179656 | tf_op jit(solution)/shard_map/convert_element_type | solution.py:420
  31.3 0.7 collective-permute-start.10
  32.0 0.3 hop.9
  32.2 1.3 %collective-permute-start.2 = (bf16[256,1024]{1,0:T(8,128)(2,1)}, bf16[256,1024]{1,0:T(8,128)(2,1)S(1)}, u32[]{:S(2)}, u32[]{:S(2)}) collective-permute-start(bf16[256,1024]{1,0:T(8,128)(2,1)} %get-tuple-element.49), channel_id=1, source_target_pairs={{8,0},{9,1},{10,2},{11,3},{12,4},{13,5},{14,6},{15,7}} | collective-permute-start | bytes 1572872 | tf_op jit(solution)/shard_map/ppermute | solution.py:470
  33.6 1.3 %collective-permute-start.5 = (bf16[256,1024]{1,0:T(8,128)(2,1)}, bf16[256,1024]{1,0:T(8,128)(2,1)S(1)}, u32[]{:S(2)}, u32[]{:S(2)}) collective-permute-start(bf16[256,1024]{1,0:T(8,128)(2,1)} %get-tuple-element.57), channel_id=1, source_target_pairs={{8,0},{9,1},{10,2},{11,3},{12,4},{13,5},{14,6},{15,7}} | collective-permute-start | bytes 1572872 | tf_op jit(solution)/shard_map/ppermute | solution.py:470
  35.0 1.3 %collective-permute-start.8 = (bf16[256,1024]{1,0:T(8,128)(2,1)}, bf16[256,1024]{1,0:T(8,128)(2,1)}, u32[]{:S(2)}, u32[]{:S(2)}) collective-permute-start(bf16[256,1024]{1,0:T(8,128)(2,1)} %get-tuple-element.63), channel_id=1, source_target_pairs={{8,0},{9,1},{10,2},{11,3},{12,4},{13,5},{14,6},{15,7}} | collective-permute-start | bytes 1572872 | tf_op jit(solution)/shard_map/ppermute | solution.py:470
  36.3 1.3 %collective-permute-start.14 = (bf16[256,1024]{1,0:T(8,128)(2,1)}, bf16[256,1024]{1,0:T(8,128)(2,1)S(1)}, u32[]{:S(2)}, u32[]{:S(2)}) collective-permute-start(bf16[256,1024]{1,0:T(8,128)(2,1)} %get-tuple-element.80), channel_id=1, source_target_pairs={{8,0},{9,1},{10,2},{11,3},{12,4},{13,5},{14,6},{15,7}} | collective-permute-start | bytes 1572872 | tf_op jit(solution)/shard_map/ppermute | solution.py:470
  37.7 0.7 collective-permute-start.11
  38.4 0.7 fusion.6
  39.1 5.3 %collective-permute-done.2.after_hbm.came_hbm = bf16[256,1024]{1,0:T(8,128)(2,1)S(1)} collective-permute-done((bf16[256,1024]{1,0:T(8,128)(2,1)}, bf16[256,1024]{1,0:T(8,128)(2,1)S(1)}, u32[]{:S(2)}, u32[]{:S(2)}) %collective-permute-start.2) | collective-permute-done | bytes 524320 | tf_op jit(solution)/shard_map/ppermute | solution.py:470
  44.3 2.3 %turn.1 = (bf16[1024,1024]{1,0:T(8,128)(2,1)S(1)}, bf16[1024,1024]{1,0:T(8,128)(2,1)S(1)}) custom-call(s32[1]{0:T(128)} %bitcast.2.number_ref, bf16[4,256,1024]{2,1,0:T(8,128)(2,1)} %bitcast.77, bf16[256,1024]{1,0:T(8,128)(2,1)S(1)} %collective-permute-done.2.after_hbm.came_hbm), custom_call_target="tpu_custom_call" | custom-call | flops 1024 | bytes 1024 | tf_op jit(solution)/shard_map/turn/pallas_call | solution.py:347
  46.7 2.0 %end.3.after_hbm.refs_2_ = bf16[256,1024]{1,0:T(8,128)(2,1)} custom-call(s32[1]{0:T(128)} %bitcast.1.flag_ref, bf16[256,1024]{1,0:T(8,128)(2,1)S(1)} %collective-permute-done.2.after_hbm.came_hbm, bf16[256,1024]{1,0:T(8,128)(2,1)} %get-tuple-element.52.aux_hbm.after_hbm, bf16[1024,1024]{1,0:T(8,128)(2,1)} %bitcast.43, ...), custom_call_target="tpu_custom_call", output_to_operand_aliasing={{}: (2, {})} | custom-call | flops 1024 | bytes 1024 | tf_op jit(solution)/shard_map/end/pallas_call | solution.py:299
  48.7 1.0 collective-permute-done.5.came_hbm
  49.8 2.1 %end.4.refs_3_ = bf16[256,1024]{1,0:T(8,128)(2,1)} custom-call(s32[1]{0:T(128)} %bitcast.1.flag_ref, bf16[256,1024]{1,0:T(8,128)(2,1)S(1)} %collective-permute-done.5.came_hbm, bf16[256,1024]{1,0:T(8,128)(2,1)} %get-tuple-element.58.aux_hbm.after_hbm, bf16[1024,1024]{1,0:T(8,128)(2,1)} %bitcast.44, ...), custom_call_target="tpu_custom_call", output_to_operand_aliasing={{}: (2, {})} | custom-call | flops 1024 | bytes 1024 | tf_op jit(solution)/shard_map/end/pallas_call | solution.py:299
  51.8 3.9 %collective-permute-done.8.came_hbm = bf16[256,1024]{1,0:T(8,128)(2,1)} collective-permute-done((bf16[256,1024]{1,0:T(8,128)(2,1)}, bf16[256,1024]{1,0:T(8,128)(2,1)}, u32[]{:S(2)}, u32[]{:S(2)}) %collective-permute-start.8) | collective-permute-done | bytes 524320 | tf_op jit(solution)/shard_map/ppermute | solution.py:470
  55.7 2.2 %end.5.refs_4_ = bf16[256,1024]{1,0:T(8,128)(2,1)} custom-call(s32[1]{0:T(128)} %bitcast.1.flag_ref, bf16[256,1024]{1,0:T(8,128)(2,1)} %collective-permute-done.8.came_hbm, bf16[256,1024]{1,0:T(8,128)(2,1)} %get-tuple-element.64.aux_hbm.after_hbm, bf16[1024,1024]{1,0:T(8,128)(2,1)} %bitcast.45, ...), custom_call_target="tpu_custom_call", output_to_operand_aliasing={{}: (2, {})} | custom-call | flops 1024 | bytes 1024 | tf_op jit(solution)/shard_map/end/pallas_call | solution.py:299
  57.9 3.3 %collective-permute-done.14.refs_6_ = bf16[256,1024]{1,0:T(8,128)(2,1)S(1)} collective-permute-done((bf16[256,1024]{1,0:T(8,128)(2,1)}, bf16[256,1024]{1,0:T(8,128)(2,1)S(1)}, u32[]{:S(2)}, u32[]{:S(2)}) %collective-permute-start.14) | collective-permute-done | bytes 524320 | tf_op jit(solution)/shard_map/ppermute | solution.py:470
  61.2 4.6 %weight.1 = (bf16[512,512]{1,0:T(8,128)(2,1)}, f32[512,512]{1,0:T(8,128)S(1)}, bf16[512,512]{1,0:T(8,128)(2,1)}, f32[512,512]{1,0:T(8,128)S(1)}) custom-call(s32[1]{0:T(128)} %bitcast.1.flag_ref, bf16[1024,1024]{1,0:T(8,128)(2,1)S(1)} %get-tuple-element.50.refs_0_, bf16[1024,1024]{1,0:T(8,128)(2,1)S(1)} %get-tuple-element.51.refs_1_, ...), custom_call_target="tpu_custom_call" | custom-call | flops 1024 | bytes 1024 | tf_op jit(solution)/shard_map/weight/pallas_call | solution.py:397
  65.8 1.6 %collective-permute-start.15 = (bf16[512,512]{1,0:T(8,128)(2,1)}, bf16[512,512]{1,0:T(8,128)(2,1)S(1)}, u32[]{:S(2)}, u32[]{:S(2)}) collective-permute-start(bf16[512,512]{1,0:T(8,128)(2,1)} %get-tuple-element.82), channel_id=1, source_target_pairs={{0,1},{1,0},{2,3},{3,2},{4,5},{5,4},{6,7},{7,6},{8,9},{9,8},{10,11... | collective-permute-start | bytes 1572872 | tf_op jit(solution)/shard_map/ppermute | solution.py:425
  67.4 1.6 %collective-permute-start.18 = (bf16[512,512]{1,0:T(8,128)(2,1)}, bf16[512,512]{1,0:T(8,128)(2,1)S(1)}, u32[]{:S(2)}, u32[]{:S(2)}) collective-permute-start(bf16[512,512]{1,0:T(8,128)(2,1)} %get-tuple-element.84), channel_id=1, source_target_pairs={{0,2},{1,3},{2,0},{3,1},{4,6},{5,7},{6,4},{7,5},{8,10},{9,11},{10,... | collective-permute-start | bytes 1572872 | tf_op jit(solution)/shard_map/ppermute | solution.py:425
  68.9 10.5 %collective-permute-done.15 = bf16[512,512]{1,0:T(8,128)(2,1)S(1)} collective-permute-done((bf16[512,512]{1,0:T(8,128)(2,1)}, bf16[512,512]{1,0:T(8,128)(2,1)S(1)}, u32[]{:S(2)}, u32[]{:S(2)}) %collective-permute-start.15) | collective-permute-done | bytes 524320 | tf_op jit(solution)/shard_map/ppermute | solution.py:425
  79.6 1.6 %collective-permute-start.16 = (bf16[256,512]{1,0:T(8,128)(2,1)S(1)}, bf16[256,512]{1,0:T(8,128)(2,1)S(1)}, u32[]{:S(2)}, u32[]{:S(2)}) collective-permute-start(bf16[256,512]{1,0:T(8,128)(2,1)S(1)} %get-tuple-element.92), channel_id=1, source_target_pairs={{0,2},{1,3},{2,0},{3,1},{4,6},{5,7},{6,4},{7,5},{8,10},{9,11},{10,... | collective-permute-start | bytes 786440 | tf_op jit(solution)/shard_map/ppermute | solution.py:425
  81.5 1.5 %collective-permute-start.19 = (bf16[256,512]{1,0:T(8,128)(2,1)S(1)}, bf16[256,512]{1,0:T(8,128)(2,1)S(1)}, u32[]{:S(2)}, u32[]{:S(2)}) collective-permute-start(bf16[256,512]{1,0:T(8,128)(2,1)S(1)} %get-tuple-element.90), channel_id=1, source_target_pairs={{0,1},{1,0},{2,3},{3,2},{4,5},{5,4},{6,7},{7,6},{8,9},{9,8},{10,11... | collective-permute-start | bytes 786440 | tf_op jit(solution)/shard_map/ppermute | solution.py:425
  83.0 5.4 %collective-permute-done.16 = bf16[256,512]{1,0:T(8,128)(2,1)S(1)} collective-permute-done((bf16[256,512]{1,0:T(8,128)(2,1)S(1)}, bf16[256,512]{1,0:T(8,128)(2,1)S(1)}, u32[]{:S(2)}, u32[]{:S(2)}) %collective-permute-start.16) | collective-permute-done | bytes 262176 | tf_op jit(solution)/shard_map/ppermute | solution.py:425
  88.5 2.7 %collective-permute-start.17 = (bf16[128,512]{1,0:T(8,128)(2,1)S(1)}, bf16[128,512]{1,0:T(8,128)(2,1)S(1)}, u32[]{:S(2)}, u32[]{:S(2)}) collective-permute-start(bf16[128,512]{1,0:T(8,128)(2,1)S(1)} %fusion.3), channel_id=1, source_target_pairs={{0,4},{1,5},{2,6},{3,7},{4,0},{5,1},{6,2},{7,3},{8,12},{9,13},{10,... | collective-permute-start | bytes 393224 | tf_op jit(solution)/shard_map/ppermute | solution.py:425
  91.1 1.3 %collective-permute-start.21 = (bf16[16,512]{1,0:T(8,128)(2,1)S(1)}, bf16[16,512]{1,0:T(8,128)(2,1)S(1)}, u32[]{:S(2)}, u32[]{:S(2)}) collective-permute-start(bf16[16,512]{1,0:T(8,128)(2,1)S(1)} %get-tuple-element.96), channel_id=1, source_target_pairs={{24,0},{25,1},{26,2},{27,3},{28,4},{29,5},{30,6},{31,7}} | collective-permute-start | bytes 49160 | tf_op jit(solution)/shard_map/ppermute | solution.py:485
  92.4 0.7 collective-permute-start.23
  93.1 0.7 collective-permute-start.22
  93.8 0.4 collective-permute-start.20
  94.2 4.3 %collective-permute-done.17 = bf16[128,512]{1,0:T(8,128)(2,1)S(1)} collective-permute-done((bf16[128,512]{1,0:T(8,128)(2,1)S(1)}, bf16[128,512]{1,0:T(8,128)(2,1)S(1)}, u32[]{:S(2)}, u32[]{:S(2)}) %collective-permute-start.17) | collective-permute-done | bytes 131104 | tf_op jit(solution)/shard_map/ppermute | solution.py:425
  98.6 5.3 %collective-permute-done.20 = bf16[128,512]{1,0:T(8,128)(2,1)S(1)} collective-permute-done((bf16[128,512]{1,0:T(8,128)(2,1)S(1)}, bf16[128,512]{1,0:T(8,128)(2,1)S(1)}, u32[]{:S(2)}, u32[]{:S(2)}) %collective-permute-start.20) | collective-permute-done | bytes 131104 | tf_op jit(solution)/shard_map/ppermute | solution.py:425
  103.9 0.8 maximum_bitcast_fusion
  104.7 1.4 %slice_select_fusion = f32[16,512]{1,0:T(8,128)} fusion(f32[16,2048]{1,0:T(8,128)} %get-tuple-element.89.after_hbm, bf16[16,512]{1,0:T(8,128)(2,1)S(1)} %collective-permute-done.23, bf16[16,512]{1,0:T(8,128)(2,1)S(1)} %collective-permute-done.22, bf16[16,512]{1,0:T(8,128)(2,1)S(1)} %collective-permute-done.21, pred[]{:T(512)} %bitcast.31), kind=kLoop, calls=%fused_computation.19 | loop fusion | flops 49152 | bytes 114689 | tf_op jit(solution)/shard_map/jit(_where)/select_n | solution.py:492
  (40 shorter events, 1.0 us)
Async XLA Ops:
  0.6 1.6 %copy-start = (bf16[1,1024,1024]{2,1,0:T(8,128)(2,1)S(1)}, bf16[1,1024,1024]{2,1,0:T(8,128)(2,1)}, u32[]{:S(2)}) copy-start(bf16[1,1024,1024]{2,1,0:T(8,128)(2,1)} %param.7) | copy-start | bytes 6291460
  2.2 0.7 copy-start.4
  6.5 17.7 %collective-permute-start = (bf16[256,1024]{1,0:T(8,128)(2,1)}, bf16[256,1024]{1,0:T(8,128)(2,1)}, u32[]{:S(2)}, u32[]{:S(2)}) collective-permute-start(bf16[256,1024]{1,0:T(8,128)(2,1)} %get-tuple-element.45), channel_id=1, source_target_pairs={{24,16},{25,17},{26,18},{27,19},{28,20},{29,21},{30,22},{31,23}} | collective-permute-start | bytes 1572872 | tf_op jit(solution)/shard_map/ppermute | solution.py:470
  11.7 14.1 %collective-permute-start.3 = (bf16[256,1024]{1,0:T(8,128)(2,1)}, bf16[256,1024]{1,0:T(8,128)(2,1)S(1)}, u32[]{:S(2)}, u32[]{:S(2)}) collective-permute-start(bf16[256,1024]{1,0:T(8,128)(2,1)} %get-tuple-element.53), channel_id=1, source_target_pairs={{24,16},{25,17},{26,18},{27,19},{28,20},{29,21},{30,22},{31,23}} | collective-permute-start | bytes 1572872 | tf_op jit(solution)/shard_map/ppermute | solution.py:470
  16.0 10.5 %collective-permute-start.6 = (bf16[256,1024]{1,0:T(8,128)(2,1)}, bf16[256,1024]{1,0:T(8,128)(2,1)}, u32[]{:S(2)}, u32[]{:S(2)}) collective-permute-start(bf16[256,1024]{1,0:T(8,128)(2,1)} %get-tuple-element.59), channel_id=1, source_target_pairs={{24,16},{25,17},{26,18},{27,19},{28,20},{29,21},{30,22},{31,23}} | collective-permute-start | bytes 1572872 | tf_op jit(solution)/shard_map/ppermute | solution.py:470
  17.5 5.1 %copy-start.2 = (bf16[4,1,1024]{2,0,1:T(4,128)(2,1)S(1)}, bf16[4,1,1024]{2,0,1:T(4,128)(2,1)}, u32[]{:S(2)}) copy-start(bf16[4,1,1024]{2,0,1:T(4,128)(2,1)} %param.11) | copy-start | bytes 24580
  17.5 5.1 %copy-start.3 = (s32[4,1,64]{2,1,0:T(1,128)S(1)}, s32[4,1,64]{2,1,0:T(1,128)}, u32[]{:S(2)}) copy-start(s32[4,1,64]{2,1,0:T(1,128)} %index_ref.1) | copy-start | bytes 3076
  21.1 6.9 %collective-permute-start.12 = (bf16[256,1024]{1,0:T(8,128)(2,1)}, bf16[256,1024]{1,0:T(8,128)(2,1)}, u32[]{:S(2)}, u32[]{:S(2)}) collective-permute-start(bf16[256,1024]{1,0:T(8,128)(2,1)} %get-tuple-element.75), channel_id=1, source_target_pairs={{24,16},{25,17},{26,18},{27,19},{28,20},{29,21},{30,22},{31,23}} | collective-permute-start | bytes 1572872 | tf_op jit(solution)/shard_map/ppermute | solution.py:470
  22.6 1.6 %copy-start.1 = (bf16[1,1024,1024]{2,1,0:T(8,128)(2,1)S(1)}, bf16[1,1024,1024]{2,1,0:T(8,128)(2,1)}, u32[]{:S(2)}) copy-start(bf16[1,1024,1024]{2,1,0:T(8,128)(2,1)} %param.7) | copy-start | bytes 6291460
  22.7 6.9 %collective-permute-start.9 = (bf16[64,2048]{1,0:T(8,128)(2,1)S(1)}, bf16[64,2048]{1,0:T(8,128)(2,1)}, u32[]{:S(2)}, u32[]{:S(2)}) collective-permute-start(bf16[64,2048]{1,0:T(8,128)(2,1)S(1)} %get-tuple-element.74), channel_id=1, source_target_pairs={{24,25},{25,24},{26,27},{27,26},{28,29},{29,28},{30,31},{31,30}} | collective-permute-start | bytes 786440 | tf_op jit(solution)/shard_map/ppermute | solution.py:425
  24.3 7.7 %collective-permute-start.1 = (bf16[256,1024]{1,0:T(8,128)(2,1)}, bf16[256,1024]{1,0:T(8,128)(2,1)}, u32[]{:S(2)}, u32[]{:S(2)}) collective-permute-start(bf16[256,1024]{1,0:T(8,128)(2,1)} %get-tuple-element.47), channel_id=1, source_target_pairs={{16,8},{17,9},{18,10},{19,11},{20,12},{21,13},{22,14},{23,15}} | collective-permute-start | bytes 1572872 | tf_op jit(solution)/shard_map/ppermute | solution.py:470
  25.8 7.7 %collective-permute-start.4 = (bf16[256,1024]{1,0:T(8,128)(2,1)}, bf16[256,1024]{1,0:T(8,128)(2,1)S(1)}, u32[]{:S(2)}, u32[]{:S(2)}) collective-permute-start(bf16[256,1024]{1,0:T(8,128)(2,1)} %get-tuple-element.55), channel_id=1, source_target_pairs={{16,8},{17,9},{18,10},{19,11},{20,12},{21,13},{22,14},{23,15}} | collective-permute-start | bytes 1572872 | tf_op jit(solution)/shard_map/ppermute | solution.py:470
  26.6 8.3 %collective-permute-start.7 = (bf16[256,1024]{1,0:T(8,128)(2,1)}, bf16[256,1024]{1,0:T(8,128)(2,1)}, u32[]{:S(2)}, u32[]{:S(2)}) collective-permute-start(bf16[256,1024]{1,0:T(8,128)(2,1)} %get-tuple-element.61), channel_id=1, source_target_pairs={{16,8},{17,9},{18,10},{19,11},{20,12},{21,13},{22,14},{23,15}} | collective-permute-start | bytes 1572872 | tf_op jit(solution)/shard_map/ppermute | solution.py:470
  28.1 8.2 %collective-permute-start.13 = (bf16[256,1024]{1,0:T(8,128)(2,1)}, bf16[256,1024]{1,0:T(8,128)(2,1)}, u32[]{:S(2)}, u32[]{:S(2)}) collective-permute-start(bf16[256,1024]{1,0:T(8,128)(2,1)} %get-tuple-element.77), channel_id=1, source_target_pairs={{16,8},{17,9},{18,10},{19,11},{20,12},{21,13},{22,14},{23,15}} | collective-permute-start | bytes 1572872 | tf_op jit(solution)/shard_map/ppermute | solution.py:470
  31.3 6.4 %collective-permute-start.10 = (bf16[32,2048]{1,0:T(8,128)(2,1)}, bf16[32,2048]{1,0:T(8,128)(2,1)S(1)}, u32[]{:S(2)}, u32[]{:S(2)}) collective-permute-start(bf16[32,2048]{1,0:T(8,128)(2,1)} %get-tuple-element.94), channel_id=1, source_target_pairs={{24,26},{25,27},{26,24},{27,25},{28,30},{29,31},{30,28},{31,29}} | collective-permute-start | bytes 393224 | tf_op jit(solution)/shard_map/ppermute | solution.py:425
  32.2 12.1 %collective-permute-start.2 = (bf16[256,1024]{1,0:T(8,128)(2,1)}, bf16[256,1024]{1,0:T(8,128)(2,1)S(1)}, u32[]{:S(2)}, u32[]{:S(2)}) collective-permute-start(bf16[256,1024]{1,0:T(8,128)(2,1)} %get-tuple-element.49), channel_id=1, source_target_pairs={{8,0},{9,1},{10,2},{11,3},{12,4},{13,5},{14,6},{15,7}} | collective-permute-start | bytes 1572872 | tf_op jit(solution)/shard_map/ppermute | solution.py:470
  33.6 16.1 %collective-permute-start.5 = (bf16[256,1024]{1,0:T(8,128)(2,1)}, bf16[256,1024]{1,0:T(8,128)(2,1)S(1)}, u32[]{:S(2)}, u32[]{:S(2)}) collective-permute-start(bf16[256,1024]{1,0:T(8,128)(2,1)} %get-tuple-element.57), channel_id=1, source_target_pairs={{8,0},{9,1},{10,2},{11,3},{12,4},{13,5},{14,6},{15,7}} | collective-permute-start | bytes 1572872 | tf_op jit(solution)/shard_map/ppermute | solution.py:470
  35.0 20.7 %collective-permute-start.8 = (bf16[256,1024]{1,0:T(8,128)(2,1)}, bf16[256,1024]{1,0:T(8,128)(2,1)}, u32[]{:S(2)}, u32[]{:S(2)}) collective-permute-start(bf16[256,1024]{1,0:T(8,128)(2,1)} %get-tuple-element.63), channel_id=1, source_target_pairs={{8,0},{9,1},{10,2},{11,3},{12,4},{13,5},{14,6},{15,7}} | collective-permute-start | bytes 1572872 | tf_op jit(solution)/shard_map/ppermute | solution.py:470
  36.3 24.9 %collective-permute-start.14 = (bf16[256,1024]{1,0:T(8,128)(2,1)}, bf16[256,1024]{1,0:T(8,128)(2,1)S(1)}, u32[]{:S(2)}, u32[]{:S(2)}) collective-permute-start(bf16[256,1024]{1,0:T(8,128)(2,1)} %get-tuple-element.80), channel_id=1, source_target_pairs={{8,0},{9,1},{10,2},{11,3},{12,4},{13,5},{14,6},{15,7}} | collective-permute-start | bytes 1572872 | tf_op jit(solution)/shard_map/ppermute | solution.py:470
  37.7 0.7 collective-permute-start.11
  65.8 13.7 %collective-permute-start.15 = (bf16[512,512]{1,0:T(8,128)(2,1)}, bf16[512,512]{1,0:T(8,128)(2,1)S(1)}, u32[]{:S(2)}, u32[]{:S(2)}) collective-permute-start(bf16[512,512]{1,0:T(8,128)(2,1)} %get-tuple-element.82), channel_id=1, source_target_pairs={{0,1},{1,0},{2,3},{3,2},{4,5},{5,4},{6,7},{7,6},{8,9},{9,8},{10,11... | collective-permute-start | bytes 1572872 | tf_op jit(solution)/shard_map/ppermute | solution.py:425
  67.4 13.9 %collective-permute-start.18 = (bf16[512,512]{1,0:T(8,128)(2,1)}, bf16[512,512]{1,0:T(8,128)(2,1)S(1)}, u32[]{:S(2)}, u32[]{:S(2)}) collective-permute-start(bf16[512,512]{1,0:T(8,128)(2,1)} %get-tuple-element.84), channel_id=1, source_target_pairs={{0,2},{1,3},{2,0},{3,1},{4,6},{5,7},{6,4},{7,5},{8,10},{9,11},{10,... | collective-permute-start | bytes 1572872 | tf_op jit(solution)/shard_map/ppermute | solution.py:425
  79.6 8.8 %collective-permute-start.16 = (bf16[256,512]{1,0:T(8,128)(2,1)S(1)}, bf16[256,512]{1,0:T(8,128)(2,1)S(1)}, u32[]{:S(2)}, u32[]{:S(2)}) collective-permute-start(bf16[256,512]{1,0:T(8,128)(2,1)S(1)} %get-tuple-element.92), channel_id=1, source_target_pairs={{0,2},{1,3},{2,0},{3,1},{4,6},{5,7},{6,4},{7,5},{8,10},{9,11},{10,... | collective-permute-start | bytes 786440 | tf_op jit(solution)/shard_map/ppermute | solution.py:425
  81.5 12.3 %collective-permute-start.19 = (bf16[256,512]{1,0:T(8,128)(2,1)S(1)}, bf16[256,512]{1,0:T(8,128)(2,1)S(1)}, u32[]{:S(2)}, u32[]{:S(2)}) collective-permute-start(bf16[256,512]{1,0:T(8,128)(2,1)S(1)} %get-tuple-element.90), channel_id=1, source_target_pairs={{0,1},{1,0},{2,3},{3,2},{4,5},{5,4},{6,7},{7,6},{8,9},{9,8},{10,11... | collective-permute-start | bytes 786440 | tf_op jit(solution)/shard_map/ppermute | solution.py:425
  88.5 10.1 %collective-permute-start.17 = (bf16[128,512]{1,0:T(8,128)(2,1)S(1)}, bf16[128,512]{1,0:T(8,128)(2,1)S(1)}, u32[]{:S(2)}, u32[]{:S(2)}) collective-permute-start(bf16[128,512]{1,0:T(8,128)(2,1)S(1)} %fusion.3), channel_id=1, source_target_pairs={{0,4},{1,5},{2,6},{3,7},{4,0},{5,1},{6,2},{7,3},{8,12},{9,13},{10,... | collective-permute-start | bytes 393224 | tf_op jit(solution)/shard_map/ppermute | solution.py:425
  91.1 13.6 %collective-permute-start.21 = (bf16[16,512]{1,0:T(8,128)(2,1)S(1)}, bf16[16,512]{1,0:T(8,128)(2,1)S(1)}, u32[]{:S(2)}, u32[]{:S(2)}) collective-permute-start(bf16[16,512]{1,0:T(8,128)(2,1)S(1)} %get-tuple-element.96), channel_id=1, source_target_pairs={{24,0},{25,1},{26,2},{27,3},{28,4},{29,5},{30,6},{31,7}} | collective-permute-start | bytes 49160 | tf_op jit(solution)/shard_map/ppermute | solution.py:485
  92.4 12.3 %collective-permute-start.23 = (bf16[16,512]{1,0:T(8,128)(2,1)S(1)}, bf16[16,512]{1,0:T(8,128)(2,1)S(1)}, u32[]{:S(2)}, u32[]{:S(2)}) collective-permute-start(bf16[16,512]{1,0:T(8,128)(2,1)S(1)} %get-tuple-element.97), channel_id=1, source_target_pairs={{24,16},{25,17},{26,18},{27,19},{28,20},{29,21},{30,22},{31,23}} | collective-permute-start | bytes 49160 | tf_op jit(solution)/shard_map/ppermute | solution.py:485
  93.1 11.6 %collective-permute-start.22 = (bf16[16,512]{1,0:T(8,128)(2,1)S(1)}, bf16[16,512]{1,0:T(8,128)(2,1)S(1)}, u32[]{:S(2)}, u32[]{:S(2)}) collective-permute-start(bf16[16,512]{1,0:T(8,128)(2,1)S(1)} %get-tuple-element.98), channel_id=1, source_target_pairs={{24,8},{25,9},{26,10},{27,11},{28,12},{29,13},{30,14},{31,15}} | collective-permute-start | bytes 49160 | tf_op jit(solution)/shard_map/ppermute | solution.py:485
  93.8 10.0 %collective-permute-start.20 = (bf16[128,512]{1,0:T(8,128)(2,1)S(1)}, bf16[128,512]{1,0:T(8,128)(2,1)S(1)}, u32[]{:S(2)}, u32[]{:S(2)}) collective-permute-start(bf16[128,512]{1,0:T(8,128)(2,1)S(1)} %fusion.4), channel_id=1, source_target_pairs={{0,4},{1,5},{2,6},{3,7},{4,0},{5,1},{6,2},{7,3},{8,12},{9,13},{10,... | collective-permute-start | bytes 393224 | tf_op jit(solution)/shard_map/ppermute | solution.py:425
where the time goes:
time: 107 us; the launch traced here: 106 us
  waiting for transfers between devices  39.1 us (37%)
  starting transfers between devices  30.3 us (28%)
  Pallas kernels  28.3 us (26%)
  other arithmetic  5.08 us (5%)
  local copies, waits for them, and re-layouts  2.26 us (2%)
    ppermute x9, waiting for transfers between devices, finish_scatter(): got = lax.ppermute(send, axes, pairs_of(bit))  25.6 us
    ppermute x12, starting transfers between devices, body(): lax.ppermute(g, 'section', [(source, source - 1)])  15.5 us
    pallas_call x4, Pallas kernels, first_call(): pl.pallas_call(functools.partial(first_kernel, m), out_shape=(block, bloc...  14.5 us
    ppermute x12, waiting for transfers between devices, body(): lax.ppermute(g, 'section', [(source, source - 1)])  13.5 us
    ppermute x9, starting transfers between devices, finish_scatter(): got = lax.ppermute(send, axes, pairs_of(bit))  12.3 us
    pallas_call x11, Pallas kernels, hop_call(): pl.pallas_call(functools.partial(hop_kernel, with_grad), out_shape=outs,...  6.82 us
    pallas_call x1, Pallas kernels, weight_call(): pl.pallas_call(weight_kernel, out_shape=(pltpu.HBM(half, BF16), jax.Shape...  4.57 us
    ppermute x3, starting transfers between devices, body(): lax.ppermute(own_table[:, s * width:(s + 1) * width].astype(BF16), 'secti...  2.6 us
  transfers between devices with their start and end apart: 24, of which 8 were waited for; matrix products, arithmetic and copies ran while one was open for 3% of the time, Pallas kernels for 19%

commit v1 on v0

--- a/solution.py
+++ b/solution.py
@@ -46,39 +46,61 @@
     return pltpu.with_memory_space_constraint(array, pltpu.HBM)
 
 
+def own_heads(width):
+    shift = HEAD.bit_length() - 1
+    row = lax.broadcasted_iota(jnp.int32, (PAIR, width), 0) >> shift
+    return row == ((lax.broadcasted_iota(jnp.int32, (PAIR, width), 1) >> shift) & 1)
+
+
 def first_kernel(
-    m, flag_ref, count_ref, acts_hbm, weight, table_hbm, index_hbm, pooled_hbm, after_hbm,
-    grad_hbm, aux_hbm, share_hbm, high_hbm, acts, table, index_ref, pooled_ref, grad, aux, share_ref, high_ref, sems,
+    m, flag_ref, count_hbm, acts_in, weight_in, table_in, index_hbm, pooled_hbm, delta_in,
+    grad_hbm, delta_hbm, share_hbm, high_hbm,
+    count_ref, acts_buf, weight_buf, table_buf, index_ref, pooled_ref, grad, aux, share_ref, high_ref, sems,
 ):
-    rows, width = acts.shape
-    table_rows = table.shape[0]
+    micros, rows, width = acts_in.shape
+    table_rows = table_in.shape[0]
     pairs = width // PAIR
     tiles = width // TILE
     tile = [slice(q * TILE, (q + 1) * TILE) for q in range(tiles)]
     pair = [slice(j * PAIR, (j + 1) * PAIR) for j in range(pairs)]
-    load = pltpu.make_async_copy(acts_hbm.at[m], acts, sems.at[0])
-    load.start()
-    store_aux = pltpu.make_async_copy(aux, aux_hbm, sems.at[1])
-
-    @pl.when(flag_ref[0] == 0)
-    def _():
-        load.wait()
-        for cols in tile:
-            hidden = dot(acts[...], weight[:, cols], NN)
-            aux[:, cols] = gelu_parts(hidden)[1].astype(BF16)
-        store_aux.start()
-        store_aux.wait()
+
+    def copy(source, target, at):
+        started = pltpu.make_async_copy(source, target, sems.at[at])
+        started.start()
+        return started
+
+    if m == 0:
+        acts_ref, weight, table = acts_buf, weight_buf, table_buf
+
+        @pl.when(flag_ref[0] == 0)
+        def _():
+            load_weight = copy(weight_in, weight, 0)
+            loads = [copy(acts_in.at[k], acts_ref.at[k], 1 + k) for k in range(micros)]
+            load_weight.wait()
+            stores = []
+            for k in range(micros):
+                loads[k].wait()
+                for cols in tile:
+                    hidden = dot(acts_ref[k], weight[:, cols], NN)
+                    aux[k, :, cols] = gelu_parts(hidden)[1].astype(BF16)
+                stores.append(copy(aux.at[k], delta_hbm.at[k], 1 + micros + k))
+            for store in stores:
+                store.wait()
+
+    else:
+        acts_ref, weight, table = acts_in, weight_in, table_in
 
     @pl.when(flag_ref[0] == 1)
     def _():
-        load_index = pltpu.make_async_copy(index_hbm, index_ref, sems.at[6])
-        load_pooled = pltpu.make_async_copy(pooled_hbm, pooled_ref, sems.at[7])
-        load_table = pltpu.make_async_copy(table_hbm, table, sems.at[2])
-        load_index.start()
-        load_pooled.start()
-        load_table.start()
-        load.wait()
-        slopes, highs, lows = [], [], []
+        loads = [copy(index_hbm, index_ref, 0), copy(pooled_hbm, pooled_ref, 1), copy(count_hbm, count_ref, 2)]
+        if m == 0:
+            loads.append(copy(table_in, table, 3))
+            load_weight = copy(weight_in, weight, 4)
+            load_acts = copy(acts_in.at[0], acts_ref.at[0], 5)
+            load_acts.wait()
+            load_weight.wait()
+        acts = acts_ref.at[m]
+        slopes, lows = [], []
         for cols in tile:
             hidden = dot(acts[...], weight[:, cols], NN)
             bent, slope = gelu_parts(hidden)
@@ -86,19 +108,14 @@
             high_ref[:, cols] = high
             slopes.append(slope)
             lows.append(low)
-        store_high = pltpu.make_async_copy(high_ref, high_hbm, sems.at[3])
-        store_high.start()
-        load_table.wait()
-        load_index.wait()
-        load_pooled.wait()
+        store_high = copy(high_ref, high_hbm, 6)
+        for load in loads:
+            load.wait()
         index = index_ref[m]
         index = jnp.concatenate([index, index], axis=1)
         onehot = (lax.broadcasted_iota(jnp.int32, (table_rows, PAIR), 0) == index).astype(BF16)
         gathered = dot(onehot, table[...], TN)
-        own = (
-            lax.broadcasted_iota(jnp.int32, (PAIR, width), 0) // HEAD
-            == lax.broadcasted_iota(jnp.int32, (PAIR, width), 1) // HEAD % 2
-        )
+        own = own_heads(width)
         keys = jnp.where(own, gathered[:, :width] * (1.0 / math.sqrt(HEAD)), 0.0).astype(BF16)
         values = jnp.where(own, gathered[:, width:], 0.0).astype(BF16)
         allowed = lax.broadcasted_iota(jnp.int32, (2, HEAD, rows), 1) < count_ref[0, m]
@@ -119,20 +136,18 @@
             share, slant = soften(scores[j], dot(values[:, here], given[:, here], NT), allowed)
             share_ref[here] = share
             slants.append(slant)
-        store_share = pltpu.make_async_copy(share_ref, share_hbm, sems.at[4])
-        store_share.start()
+        store_share = copy(share_ref, share_hbm, 7)
         totals = []
         for j, here in enumerate(pair):
             part = slice(j * PAIR % TILE, j * PAIR % TILE + PAIR)
             total = given_row[:, here] + dot(slants[j], keys[:, here], TN)
             totals.append(total)
-            aux[:, here] = (total * slopes[j * PAIR // TILE][:, part]).astype(BF16)
-        store_aux.start()
+            aux[0, :, here] = (total * slopes[j * PAIR // TILE][:, part]).astype(BF16)
+        store_aux = copy(aux.at[0], delta_hbm.at[m], 8)
         for q, cols in enumerate(tile):
             total = jnp.concatenate(totals[q * TILE // PAIR : (q + 1) * TILE // PAIR], axis=1)
-            grad[:, cols] = (total + dot(aux[...], weight[cols, :], NT)).astype(BF16)
-        store_grad = pltpu.make_async_copy(grad, grad_hbm, sems.at[5])
-        store_grad.start()
+            grad[:, cols] = (total + dot(aux[0], weight[cols, :], NT)).astype(BF16)
+        store_grad = copy(grad, grad_hbm, 9)
         store_high.wait()
         store_share.wait()
         store_aux.wait()
@@ -152,30 +167,42 @@
     return share.reshape(worth.shape).astype(BF16), lean(share, worth)
 
 
-def first_call(m, flag, count, acts, weight, table, index, pooled, after):
-    rows, width = acts.shape[1:]
+def first_call(m, flag, count, acts, weight, table, index, pooled, delta):
+    micros, rows, width = acts.shape
     turned = (width // HEAD * index.shape[2], rows)
     block = pltpu.HBM((rows, width), BF16)
+    big = HBM if m == 0 else VMEM
+    small = pltpu.VMEM((8, 128), BF16)
     return pl.pallas_call(
         functools.partial(first_kernel, m),
-        out_shape=(block, block, pltpu.HBM(turned, BF16), block),
-        in_specs=[SMEM, SMEM, HBM, VMEM, HBM, HBM, HBM, HBM],
+        out_shape=(block, pltpu.HBM(acts.shape, BF16), pltpu.HBM(turned, BF16), block),
+        in_specs=[SMEM, HBM, big, big, big, HBM, HBM, HBM],
         out_specs=(HBM,) * 4,
         scratch_shapes=[
-            pltpu.VMEM((rows, width), BF16),
-            pltpu.VMEM(table.shape, BF16),
+            pltpu.SMEM(count.shape, jnp.int32),
+            pltpu.VMEM(acts.shape, BF16) if m == 0 else small,
+            pltpu.VMEM(weight.shape, BF16) if m == 0 else small,
+            pltpu.VMEM(table.shape, BF16) if m == 0 else small,
             pltpu.VMEM(index.shape, jnp.int32),
             pltpu.VMEM(pooled.shape, BF16),
             pltpu.VMEM((rows, width), BF16),
-            pltpu.VMEM((rows, width), BF16),
+            pltpu.VMEM((micros if m == 0 else 1, rows, width), BF16),
             pltpu.VMEM(turned, BF16),
             pltpu.VMEM((rows, width), BF16),
-            pltpu.SemaphoreType.DMA((8,)),
+            pltpu.SemaphoreType.DMA((max(10, 1 + 2 * micros),)),
         ],
+        input_output_aliases={} if m == 0 else {7: 1},
         compiler_params=pltpu.CompilerParams(vmem_limit_bytes=28 * MIB),
         cost_estimate=LIGHT,
         name="first",
-    )(flag, count, stay(acts), weight, stay(table), stay(index), stay(pooled), stay(after))
+    )(
+        flag,
+        stay(count),
+        *(stay(array) if m == 0 else array for array in (acts, weight, table)),
+        stay(index),
+        stay(pooled),
+        stay(delta),
+    )
 
 
 def table_kernel(replicas, flag_ref, parity_ref, index_ref, pooled_ref, table_hbm, *refs):
@@ -205,10 +232,7 @@
             low_bit = low_bit + (((block >> (steps - 2 - k)) & 1) << (k + 1))
         row = (low_bit << shift) + (spot & ((1 << shift) - 1))
         left_half = lax.broadcasted_iota(jnp.int32, (HEAD, PAIR), 1) < HEAD
-        own = (
-            lax.broadcasted_iota(jnp.int32, (PAIR, width), 0) // HEAD
-            == lax.broadcasted_iota(jnp.int32, (PAIR, width), 1) // HEAD % 2
-        )
+        own = own_heads(width)
         loads[-1].wait()
         onehots = []
         for m in range(count):
@@ -262,23 +286,23 @@
     )(flag, parity, index, pooled, stay(table), *map(stay, shares), *map(stay, highs))
 
 
-def hop_kernel(with_grad, flag_ref, came_hbm, aux_hbm, weight, after_hbm, *rest):
+def hop_kernel(m, with_grad, flag_ref, came_hbm, delta_in, weight, after_hbm, *rest):
     if with_grad:
-        grad_hbm, aux_out, came, aux, grad, sems = rest
+        grad_hbm, delta_hbm, came, aux, grad, sems = rest
     else:
-        aux_out, came, aux, sems = rest
-    rows, width = came.shape
+        delta_hbm, came, aux, sems = rest
+    width = came.shape[1]
 
     @pl.when(flag_ref[0] == 1)
     def _():
         first = pltpu.make_async_copy(came_hbm, came, sems.at[0])
-        second = pltpu.make_async_copy(aux_hbm, aux, sems.at[1])
+        second = pltpu.make_async_copy(delta_in.at[m], aux, sems.at[1])
         first.start()
         second.start()
         first.wait()
         second.wait()
         aux[...] = (came[...].astype(F32) * aux[...].astype(F32)).astype(BF16)
-        stores = [pltpu.make_async_copy(aux, aux_out, sems.at[2])]
+        stores = [pltpu.make_async_copy(aux, delta_hbm.at[m], sems.at[2])]
         stores[0].start()
         if with_grad:
             for n in range(width // TILE):
@@ -290,14 +314,15 @@
             store.wait()
 
 
-def hop_call(flag, came, aux, weight, after, with_grad):
+def hop_call(m, flag, came, delta, weight, after, with_grad):
     rows, width = came.shape
-    block = pltpu.HBM((rows, width), BF16)
     scratch = [pltpu.VMEM((rows, width), BF16)] * (3 if with_grad else 2)
     scratch.append(pltpu.SemaphoreType.DMA((4,)))
-    outs = (block, block) if with_grad else (block,)
+    outs = (pltpu.HBM(delta.shape, BF16),)
+    if with_grad:
+        outs = (pltpu.HBM((rows, width), BF16),) + outs
     return pl.pallas_call(
-        functools.partial(hop_kernel, with_grad),
+        functools.partial(hop_kernel, m, with_grad),
         out_shape=outs,
         in_specs=[SMEM, HBM, HBM, VMEM if with_grad else HBM, HBM],
         out_specs=(HBM,) * len(outs),
@@ -306,7 +331,7 @@
         compiler_params=pltpu.CompilerParams(vmem_limit_bytes=12 * MIB),
         cost_estimate=LIGHT,
         name="hop" if with_grad else "end",
-    )(flag, came, stay(aux), weight if with_grad else stay(weight), stay(after))
+    )(flag, came, stay(delta), weight if with_grad else stay(weight), stay(after))
 
 
 def bit_orders(replicas):
@@ -323,8 +348,9 @@
 
 
 def turn_kernel(replicas, number_ref, acts_hbm, after_hbm, *refs):
-    outs = refs[:2]
-    acts, turned, sems = refs[2:]
+    outs, token_ref = refs[:2], refs[2]
+    acts, turned, sems = refs[3:]
+    token_ref[...] = jnp.zeros_like(token_ref)
     count, rows, width = acts.shape
     size = width // replicas
     loads = [pltpu.make_async_copy(acts_hbm.at[m], acts.at[m], sems.at[m]) for m in range(count)]
@@ -346,9 +372,9 @@
     count, rows, width = acts.shape
     return pl.pallas_call(
         functools.partial(turn_kernel, replicas),
-        out_shape=(jax.ShapeDtypeStruct((width, count * rows), BF16),) * 2,
+        out_shape=(jax.ShapeDtypeStruct((width, count * rows), BF16),) * 2 + (pltpu.HBM((16, 128), BF16),),
         in_specs=[SMEM, HBM, HBM],
-        out_specs=(VMEM, VMEM),
+        out_specs=(VMEM,) * 3,
         scratch_shapes=[
             pltpu.VMEM(acts.shape, BF16),
             pltpu.VMEM((width, rows), BF16),
@@ -360,53 +386,80 @@
     )(number, stay(acts), after)
 
 
-def weight_kernel(flag_ref, *refs):
-    turned, refs = refs[:2], refs[2:]
-    count = len(refs) - 7
-    delta_hbm, came, outs = refs[:count], refs[count], refs[count + 1 : count + 5]
-    delta, sems = refs[count + 5 :]
-    width = delta.shape[1]
-    rows = delta.shape[0] // count
+def early_kernel(turned_first, turned_second, delta_hbm, *refs):
+    outs, (delta, sems) = refs[:4], refs[4:]
+    micros, rows, width = delta.shape
     half = width // 2
-    copies = [
-        pltpu.make_async_copy(delta_hbm[m], delta.at[pl.ds(m * rows, rows)], sems.at[m]) for m in range(count)
-    ]
-    for copy in copies:
-        copy.start()
-    for copy in copies:
-        copy.wait()
-
-    @pl.when(flag_ref[0] == 1)
-    def _():
-        tail = pl.ds((count - 1) * rows, rows)
-        delta[tail] = (came[...].astype(F32) * delta[tail].astype(F32)).astype(BF16)
-
-    for which in range(2):
-        for c in range(2):
-            out = outs[2 * c + which]
+    loads = [pltpu.make_async_copy(delta_hbm.at[m], delta.at[m], sems.at[m]) for m in range(micros)]
+    for load in loads:
+        load.start()
+    for load in loads:
+        load.wait()
+    flat = delta.reshape(micros * rows, width)
+    for c, turned in enumerate((turned_first, turned_second)):
+        for which in range(2):
             for at in range(0, half, TILE):
-                cols = slice(c * half + at, c * half + at + TILE)
-                product = dot(turned[c][which * half : (which + 1) * half], delta[:, cols], NN)
-                out[:, at : at + TILE] = product.astype(out.dtype)
-
-
-def weight_call(flag, turned, deltas, came):
-    rows, width = deltas[0].shape
-    count = len(deltas)
-    half = (width // 2, width // 2)
+                outs[2 * c + which][:, at : at + TILE] = dot(
+                    turned[which * half : (which + 1) * half, : micros * rows],
+                    flat[:, c * half + at : c * half + at + TILE],
+                    NN,
+                )
+
+
+def early_call(turned, delta):
+    micros, rows, width = delta.shape
+    half = jax.ShapeDtypeStruct((width // 2, width // 2), F32)
     return pl.pallas_call(
-        weight_kernel,
-        out_shape=(pltpu.HBM(half, BF16), jax.ShapeDtypeStruct(half, F32)) * 2,
-        in_specs=[SMEM, VMEM, VMEM] + [HBM] * count + [VMEM],
+        early_kernel,
+        out_shape=(half,) * 4,
+        in_specs=[VMEM, VMEM, HBM],
         out_specs=(VMEM,) * 4,
         scratch_shapes=[
-            pltpu.VMEM((count * rows, width), BF16),
-            pltpu.SemaphoreType.DMA((count,)),
+            pltpu.VMEM((micros - 1, rows, width), BF16),
+            pltpu.SemaphoreType.DMA((micros - 1,)),
         ],
         compiler_params=pltpu.CompilerParams(vmem_limit_bytes=28 * MIB),
         cost_estimate=LIGHT,
+        name="early",
+    )(*turned, stay(delta))
+
+
+def weight_kernel(which, flag_ref, turned_first, turned_second, delta_hbm, came, early_first, early_second, *refs):
+    outs, (delta, sem) = refs[:2], refs[2:]
+    rows, width = delta.shape
+    half = width // 2
+    last = delta_hbm.shape[0] - 1
+    load = pltpu.make_async_copy(delta_hbm.at[last], delta, sem.at[0])
+    load.start()
+    load.wait()
+
+    @pl.when(flag_ref[0] == 1)
+    def _():
+        delta[...] = (came[...].astype(F32) * delta[...].astype(F32)).astype(BF16)
+
+    for c, (turned, early) in enumerate(((turned_first, early_first), (turned_second, early_second))):
+        for at in range(0, half, TILE):
+            product = dot(
+                turned[which * half : (which + 1) * half, last * rows :],
+                delta[:, c * half + at : c * half + at + TILE],
+                NN,
+            )
+            outs[c][:, at : at + TILE] = (early[:, at : at + TILE] + product).astype(outs[c].dtype)
+
+
+def weight_call(which, flag, turned, delta, came, early):
+    micros, rows, width = delta.shape
+    half = (width // 2, width // 2)
+    return pl.pallas_call(
+        functools.partial(weight_kernel, which),
+        out_shape=(jax.ShapeDtypeStruct(half, F32) if which else pltpu.HBM(half, BF16),) * 2,
+        in_specs=[SMEM, VMEM, VMEM, HBM, VMEM, VMEM, VMEM],
+        out_specs=(VMEM,) * 2,
+        scratch_shapes=[pltpu.VMEM((rows, width), BF16), pltpu.SemaphoreType.DMA((1,))],
+        compiler_params=pltpu.CompilerParams(vmem_limit_bytes=20 * MIB),
+        cost_estimate=LIGHT,
         name="weight",
-    )(flag, *turned, *map(stay, deltas), came)
+    )(flag, *turned, stay(delta), came, *early)
 
 
 def own_half(keep, got, bit):
@@ -447,12 +500,15 @@
     count = cand_count.reshape(1, micro_count)
     pooled = pooled_cotangent.reshape(micro_count, model_width)
     final = flag(final_flag)
-    grads, aux, shares, highs = [], [], [], []
+    grads, shares, highs = [], [], []
+    delta = acts
     for m in range(micro_count):
-        after = aux[m - 1] if m else acts
-        out = first_call(m, final, count, acts, weight, cand_table, cand_index, pooled, after)
-        for kept, item in zip((grads, aux, shares, highs), out):
-            kept.append(item)
+        grad, delta, share, high = first_call(
+            m, final, count, acts, weight, cand_table, cand_index, pooled, delta
+        )
+        grads.append(grad)
+        shares.append(share)
+        highs.append(high)
 
     def table_pairs(bit):
         return [(last * replicas + i, last * replicas + (i ^ (1 << bit))) for i in range(replicas)]
@@ -469,16 +525,15 @@
         source = last - hop
         received = [lax.ppermute(g, "section", [(source, source - 1)]) for g in grads]
         active = flag(position == source - 1)
-        if hop + 1 == last:
-            turned = turn_call(number, acts, received[0], replicas)
         for m in range(micro_count):
-            after = aux[m - 1] if m else acts
-            if hop + 1 == last and m + 2 == micro_count:
-                after = own_table
             if hop + 1 < last:
-                grads[m], aux[m] = hop_call(active, received[m], aux[m], weight, after, True)
+                after = token if hop == 0 and m == 1 else acts
+                grads[m], delta = hop_call(m, active, received[m], delta, weight, after, True)
+                if hop == 0 and m == 0:
+                    *turned, token = turn_call(number, acts, grads[0], replicas)
             elif m + 1 < micro_count:
-                (aux[m],) = hop_call(active, received[m], aux[m], weight, after, False)
+                after = own_table if m + 2 == micro_count else acts
+                (delta,) = hop_call(m, active, received[m], delta, weight, after, False)
 
     width = 2 * model_width // sections
     spread = [
@@ -486,8 +541,10 @@
         for s in range(last)
     ]
 
-    pieces = weight_call(active, turned, aux, received[-1])
-    sums = [finish_scatter(pieces[2 * c], pieces[2 * c + 1], orders[c], "dp", pairs) for c in range(2)]
+    early = early_call(turned, delta)
+    sends = weight_call(0, active, turned, delta, received[-1], early[::2])
+    keeps = weight_call(1, active, turned, delta, received[-1], early[1::2])
+    sums = [finish_scatter(sends[c], keeps[c], orders[c], "dp", pairs) for c in range(2)]
     late_flag, sums = lax.optimization_barrier((flag(final_flag), sums))
     table_sum = jnp.where(
         late_flag[0] == 1, own_table[:, last * width :], sum(piece.astype(F32) for piece in spread)

time: 107 us -> 110 us (1.028)
  the two profiles are of different devices: /device:TPU:0 before, /device:TPU:3 now
where the time goes in v1:
time: 110 us; the launch traced here: 109 us
  starting transfers between devices  39.1 us (36%)
  Pallas kernels  39 us (35%)
  waiting for transfers between devices  15 us (14%)
  local copies, waits for them, and re-layouts  9.21 us (8%)
  other arithmetic  5.44 us (5%)
  between operations  1.16 us (1%)
    ppermute x12, starting transfers between devices, body(): lax.ppermute(g, 'section', [(source, source - 1)])  20.1 us
    pallas_call x4, Pallas kernels, first_call(): pl.pallas_call(functools.partial(first_kernel, m), out_shape=(block, pltp...  18.7 us
    ppermute x9, starting transfers between devices, finish_scatter(): got = lax.ppermute(send, axes, pairs_of(bit))  15.2 us
    ppermute x9, waiting for transfers between devices, finish_scatter(): got = lax.ppermute(send, axes, pairs_of(bit))  15 us
    pallas_call x1, Pallas kernels, table_call(): pl.pallas_call(functools.partial(table_kernel, replicas), out_shape=(jax....  9.75 us
    unnamed x32, local copies, waits for them, and re-layouts  9.21 us
    pallas_call x2, Pallas kernels, weight_call(): pl.pallas_call(functools.partial(weight_kernel, which), out_shape=(jax.Sh...  4.22 us
    ppermute x3, starting transfers between devices, body(): lax.ppermute(own_table[:, s * width:(s + 1) * width].astype(BF16), 'secti...  3.86 us
  transfers between devices with their start and end apart: 24, of which 4 were waited for; matrix products, arithmetic and copies ran while one was open for 4% of the time, Pallas kernels for 28%

profile of v1, /device:TPU:3, one launch (start us, length us, event | category | flops | bytes accessed | tf_op | source)
XLA Modules:
  0.0 108.9 jit_solution(11708656279407137882)
XLA Ops:
  0.7 6.2 %first.4 = (bf16[256,1024]{1,0:T(8,128)(2,1)}, bf16[4,256,1024]{2,1,0:T(8,128)(2,1)}, bf16[1024,256]{1,0:T(8,128)(2,1)}, bf16[256,1024]{1,0:T(8,128)(2,1)}) custom-call(s32[1]{0:T(128)} %bitcast.flag_ref, s32[1,4]{1,0:T(1,128)} %bitcast.94, bf16[4,256,1024]{2,1,0:T(8,128)(2,1)} %bitcast.43, bf16[1024,1024]{1,0:T(8,128)(2,1)} %bitcast.58, ...), custom_call_target="tpu_custom_call" | custom-call | flops 1024 | bytes 1024 | tf_op jit(solution)/shard_map/first/pallas_call | solution.py:176
  6.9 4.0 %collective-permute-start = (bf16[256,1024]{1,0:T(8,128)(2,1)}, bf16[256,1024]{1,0:T(8,128)(2,1)S(1)}, u32[]{:S(2)}, u32[]{:S(2)}) collective-permute-start(bf16[256,1024]{1,0:T(8,128)(2,1)} %get-tuple-element.50), channel_id=1, source_target_pairs={{24,16},{25,17},{26,18},{27,19},{28,20},{29,21},{30,22},{31,23}} | collective-permute-start | bytes 1572872 | tf_op jit(solution)/shard_map/ppermute | solution.py:526
  11.0 4.2 %first.5 = (bf16[256,1024]{1,0:T(8,128)(2,1)}, bf16[4,256,1024]{2,1,0:T(8,128)(2,1)}, bf16[1024,256]{1,0:T(8,128)(2,1)}, bf16[256,1024]{1,0:T(8,128)(2,1)}) custom-call(s32[1]{0:T(128)} %bitcast.flag_ref, s32[1,4]{1,0:T(1,128)} %bitcast.95, bf16[4,256,1024]{2,1,0:T(8,128)(2,1)S(1)} %bitcast.55, ...), custom_call_target="tpu_custom_call", output_to_operand_aliasing={{1}: (7, {})} | custom-call | flops 1024 | bytes 1024 | tf_op jit(solution)/shard_map/first/pallas_call | solution.py:176
  15.2 2.1 %collective-permute-start.2 = (bf16[256,1024]{1,0:T(8,128)(2,1)}, bf16[256,1024]{1,0:T(8,128)(2,1)}, u32[]{:S(2)}, u32[]{:S(2)}) collective-permute-start(bf16[256,1024]{1,0:T(8,128)(2,1)} %get-tuple-element.59), channel_id=1, source_target_pairs={{24,16},{25,17},{26,18},{27,19},{28,20},{29,21},{30,22},{31,23}} | collective-permute-start | bytes 1572872 | tf_op jit(solution)/shard_map/ppermute | solution.py:526
  17.3 4.2 %first.6 = (bf16[256,1024]{1,0:T(8,128)(2,1)}, bf16[4,256,1024]{2,1,0:T(8,128)(2,1)}, bf16[1024,256]{1,0:T(8,128)(2,1)}, bf16[256,1024]{1,0:T(8,128)(2,1)}) custom-call(s32[1]{0:T(128)} %bitcast.flag_ref, s32[1,4]{1,0:T(1,128)} %bitcast.96, bf16[4,256,1024]{2,1,0:T(8,128)(2,1)S(1)} %bitcast.56, ...), custom_call_target="tpu_custom_call", output_to_operand_aliasing={{1}: (7, {})} | custom-call | flops 1024 | bytes 1024 | tf_op jit(solution)/shard_map/first/pallas_call | solution.py:176
  21.5 2.1 %collective-permute-start.1 = (bf16[256,1024]{1,0:T(8,128)(2,1)}, bf16[256,1024]{1,0:T(8,128)(2,1)}, u32[]{:S(2)}, u32[]{:S(2)}) collective-permute-start(bf16[256,1024]{1,0:T(8,128)(2,1)} %get-tuple-element.58), channel_id=1, source_target_pairs={{24,16},{25,17},{26,18},{27,19},{28,20},{29,21},{30,22},{31,23}} | collective-permute-start | bytes 1572872 | tf_op jit(solution)/shard_map/ppermute | solution.py:526
  23.6 4.2 %first.7 = (bf16[256,1024]{1,0:T(8,128)(2,1)}, bf16[4,256,1024]{2,1,0:T(8,128)(2,1)}, bf16[1024,256]{1,0:T(8,128)(2,1)}, bf16[256,1024]{1,0:T(8,128)(2,1)}) custom-call(s32[1]{0:T(128)} %bitcast.flag_ref, s32[1,4]{1,0:T(1,128)} %bitcast.97, bf16[4,256,1024]{2,1,0:T(8,128)(2,1)S(1)} %bitcast.57, ...), custom_call_target="tpu_custom_call", output_to_operand_aliasing={{1}: (7, {})} | custom-call | flops 1024 | bytes 1024 | tf_op jit(solution)/shard_map/first/pallas_call | solution.py:176
  27.7 2.2 %collective-permute-start.6 = (bf16[256,1024]{1,0:T(8,128)(2,1)}, bf16[256,1024]{1,0:T(8,128)(2,1)}, u32[]{:S(2)}, u32[]{:S(2)}) collective-permute-start(bf16[256,1024]{1,0:T(8,128)(2,1)} %get-tuple-element.65), channel_id=1, source_target_pairs={{24,16},{25,17},{26,18},{27,19},{28,20},{29,21},{30,22},{31,23}} | collective-permute-start | bytes 1572872 | tf_op jit(solution)/shard_map/ppermute | solution.py:526
  29.9 9.8 %table.1 = (bf16[64,2048]{1,0:T(8,128)(2,1)S(1)}, f32[64,2048]{1,0:T(8,128)S(1)}) custom-call(s32[1]{0:T(128)} %bitcast.flag_ref, s32[1]{0:T(128)S(6)} %and.17.parity_ref, s32[4,1,64]{2,1,0:T(1,128)S(1)} %copy-done.15, bf16[4,1024]{1,0:T(4,128)(2,1)S(1)} %bitcast.80, bf16[128,2048]{1,0:T(8,128)(2,1)} %table_hbm.1, ...), custom_call_target="tpu_custom_call" | custom-call | flops 1024 | bytes 1024 | tf_op jit(solution)/shard_map/table/pallas_call | solution.py:271
  39.7 3.1 %collective-permute-start.11 = (bf16[64,2048]{1,0:T(8,128)(2,1)S(1)}, bf16[64,2048]{1,0:T(8,128)(2,1)}, u32[]{:S(2)}, u32[]{:S(2)}) collective-permute-start(bf16[64,2048]{1,0:T(8,128)(2,1)S(1)} %get-tuple-element.85), channel_id=1, source_target_pairs={{24,25},{25,24},{26,27},{27,26},{28,29},{29,28},{30,31},{31,30}} | collective-permute-start | bytes 786440 | tf_op jit(solution)/shard_map/ppermute | solution.py:478
  42.9 0.9 collective-permute-start.5
  43.8 1.0 copy-done.13
  44.9 2.6 %turn.1 = (bf16[1024,1024]{1,0:T(8,128)(2,1)S(1)}, bf16[1024,1024]{1,0:T(8,128)(2,1)S(1)}, bf16[16,128]{1,0:T(8,128)(2,1)}) custom-call(s32[1]{0:T(128)} %bitcast.2.number_ref, bf16[4,256,1024]{2,1,0:T(8,128)(2,1)} %bitcast.46, bf16[256,1024]{1,0:T(8,128)(2,1)S(1)} %copy-done.13), custom_call_target="tpu_custom_call" | custom-call | flops 1024 | bytes 1024 | tf_op jit(solution)/shard_map/turn/pallas_call | solution.py:373
  47.6 1.3 %copy-done.3 = bf16[1024,1024]{1,0:T(8,128)(2,1)} copy-done((bf16[1024,1024]{1,0:T(8,128)(2,1)}, bf16[1024,1024]{1,0:T(8,128)(2,1)S(1)}, u32[]{:S(2)}) %copy-start.3) | copy-done | bytes 2097176
  48.9 0.7 copy-done.5
  49.5 1.5 %collective-permute-start.4 = (bf16[256,1024]{1,0:T(8,128)(2,1)}, bf16[256,1024]{1,0:T(8,128)(2,1)}, u32[]{:S(2)}, u32[]{:S(2)}) collective-permute-start(bf16[256,1024]{1,0:T(8,128)(2,1)} %get-tuple-element.64), channel_id=1, source_target_pairs={{16,8},{17,9},{18,10},{19,11},{20,12},{21,13},{22,14},{23,15}} | collective-permute-start | bytes 1572872 | tf_op jit(solution)/shard_map/ppermute | solution.py:526
  51.0 1.5 %collective-permute-start.3 = (bf16[256,1024]{1,0:T(8,128)(2,1)}, bf16[256,1024]{1,0:T(8,128)(2,1)}, u32[]{:S(2)}, u32[]{:S(2)}) collective-permute-start(bf16[256,1024]{1,0:T(8,128)(2,1)} %get-tuple-element.63), channel_id=1, source_target_pairs={{16,8},{17,9},{18,10},{19,11},{20,12},{21,13},{22,14},{23,15}} | collective-permute-start | bytes 1572872 | tf_op jit(solution)/shard_map/ppermute | solution.py:526
  52.6 1.5 %collective-permute-start.10 = (bf16[256,1024]{1,0:T(8,128)(2,1)}, bf16[256,1024]{1,0:T(8,128)(2,1)}, u32[]{:S(2)}, u32[]{:S(2)}) collective-permute-start(bf16[256,1024]{1,0:T(8,128)(2,1)} %get-tuple-element.73), channel_id=1, source_target_pairs={{16,8},{17,9},{18,10},{19,11},{20,12},{21,13},{22,14},{23,15}} | collective-permute-start | bytes 1572872 | tf_op jit(solution)/shard_map/ppermute | solution.py:526
  54.1 1.0 fusion.2
  55.1 3.2 %collective-permute-start.12 = (bf16[32,2048]{1,0:T(8,128)(2,1)S(1)}, bf16[32,2048]{1,0:T(8,128)(2,1)S(1)}, u32[]{:S(2)}, u32[]{:S(2)}) collective-permute-start(bf16[32,2048]{1,0:T(8,128)(2,1)S(1)} %get-tuple-element.104), channel_id=1, source_target_pairs={{24,26},{25,27},{26,24},{27,25},{28,30},{29,31},{30,28},{31,29}} | collective-permute-start | bytes 393224 | tf_op jit(solution)/shard_map/ppermute | solution.py:478
  58.4 0.7 collective-permute-start.9
  59.1 1.5 %collective-permute-start.8 = (bf16[256,1024]{1,0:T(8,128)(2,1)}, bf16[256,1024]{1,0:T(8,128)(2,1)}, u32[]{:S(2)}, u32[]{:S(2)}) collective-permute-start(bf16[256,1024]{1,0:T(8,128)(2,1)} %get-tuple-element.71), channel_id=1, source_target_pairs={{8,0},{9,1},{10,2},{11,3},{12,4},{13,5},{14,6},{15,7}} | collective-permute-start | bytes 1572872 | tf_op jit(solution)/shard_map/ppermute | solution.py:526
  60.7 1.5 %collective-permute-start.7 = (bf16[256,1024]{1,0:T(8,128)(2,1)}, bf16[256,1024]{1,0:T(8,128)(2,1)}, u32[]{:S(2)}, u32[]{:S(2)}) collective-permute-start(bf16[256,1024]{1,0:T(8,128)(2,1)} %get-tuple-element.70), channel_id=1, source_target_pairs={{8,0},{9,1},{10,2},{11,3},{12,4},{13,5},{14,6},{15,7}} | collective-permute-start | bytes 1572872 | tf_op jit(solution)/shard_map/ppermute | solution.py:526
  62.2 0.7 collective-permute-start.14
  62.9 4.2 %collective-permute-start.13 = (bf16[16,2048]{1,0:T(8,128)(2,1)S(1)}, bf16[16,2048]{1,0:T(8,128)(2,1)S(1)}, u32[]{:S(2)}, u32[]{:S(2)}) collective-permute-start(bf16[16,2048]{1,0:T(8,128)(2,1)S(1)} %fusion.5), channel_id=1, source_target_pairs={{24,28},{25,29},{26,30},{27,31},{28,24},{29,25},{30,26},{31,27}} | collective-permute-start | bytes 196616 | tf_op jit(solution)/shard_map/ppermute | solution.py:478
  67.1 2.4 %collective-permute-done.13 = bf16[16,2048]{1,0:T(8,128)(2,1)S(1)} collective-permute-done((bf16[16,2048]{1,0:T(8,128)(2,1)S(1)}, bf16[16,2048]{1,0:T(8,128)(2,1)S(1)}, u32[]{:S(2)}, u32[]{:S(2)}) %collective-permute-start.13) | collective-permute-done | bytes 65568 | tf_op jit(solution)/shard_map/ppermute | solution.py:478
  69.5 0.7 fusion.6
  70.4 1.5 %copy-done.4 = bf16[1024,1024]{1,0:T(8,128)(2,1)S(1)} copy-done((bf16[1024,1024]{1,0:T(8,128)(2,1)S(1)}, bf16[1024,1024]{1,0:T(8,128)(2,1)}, u32[]{:S(2)}) %copy-start.4) | copy-done | bytes 2097176
  71.9 0.6 copy-done.6
  72.5 3.2 %early.1 = (f32[512,512]{1,0:T(8,128)S(1)}, f32[512,512]{1,0:T(8,128)S(1)}, f32[512,512]{1,0:T(8,128)S(1)}, f32[512,512]{1,0:T(8,128)S(1)}) custom-call(bf16[1024,1024]{1,0:T(8,128)(2,1)S(1)} %copy-done.4, bf16[1024,1024]{1,0:T(8,128)(2,1)S(1)} %copy-done.6, bf16[4,256,1024]{2,1,0:T(8,128)(2,1)} %end.5.delta_hbm), custom_call_target="tpu_custom_call" | custom-call | flops 1024 | bytes 1024 | tf_op jit(solution)/shard_map/early/pallas_call | solution.py:412
  75.8 2.7 %weight.3 = (bf16[512,512]{1,0:T(8,128)(2,1)}, bf16[512,512]{1,0:T(8,128)(2,1)}) custom-call(s32[1]{0:T(128)} %bitcast.1.flag_ref, bf16[1024,1024]{1,0:T(8,128)(2,1)S(1)} %copy-done.4, bf16[1024,1024]{1,0:T(8,128)(2,1)S(1)} %copy-done.6, bf16[4,256,1024]{2,1,0:T(8,128)(2,1)} %end.5.delta_hbm, bf16[256,1024]{1,0:T(8,128)(2,1)S(1)} %collective-permute-done.14.came, ...), custom_call_target="tpu_custom_call" | custom-call | flops 1024 | bytes 1024 | tf_op jit(solution)/shard_map/weight/pallas_call | solution.py:453
  78.5 0.3 collective-permute-start.18
  79.1 1.6 %copy-done.7 = bf16[1024,1024]{1,0:T(8,128)(2,1)S(1)} copy-done((bf16[1024,1024]{1,0:T(8,128)(2,1)S(1)}, bf16[1024,1024]{1,0:T(8,128)(2,1)}, u32[]{:S(2)}) %copy-start.7) | copy-done | bytes 2097176
  80.7 1.2 %copy-done.10 = f32[512,512]{1,0:T(8,128)S(1)} copy-done((f32[512,512]{1,0:T(8,128)S(1)}, f32[512,512]{1,0:T(8,128)}, u32[]{:S(2)}) %copy-start.10) | copy-done | bytes 1048600
  81.9 1.2 %copy-done.12 = f32[512,512]{1,0:T(8,128)S(1)} copy-done((f32[512,512]{1,0:T(8,128)S(1)}, f32[512,512]{1,0:T(8,128)}, u32[]{:S(2)}) %copy-start.12) | copy-done | bytes 1048600
  83.1 1.5 %weight.2 = (f32[512,512]{1,0:T(8,128)S(1)}, f32[512,512]{1,0:T(8,128)S(1)}) custom-call(s32[1]{0:T(128)} %bitcast.1.flag_ref, bf16[1024,1024]{1,0:T(8,128)(2,1)S(1)} %copy-done.4, bf16[1024,1024]{1,0:T(8,128)(2,1)S(1)} %copy-done.7, bf16[4,256,1024]{2,1,0:T(8,128)(2,1)} %end.5.delta_hbm, bf16[256,1024]{1,0:T(8,128)(2,1)S(1)} %collective-permute-done.14.came, ...), custom_call_target="tpu_custom_call" | custom-call | flops 1024 | bytes 1024 | tf_op jit(solution)/shard_map/weight/pallas_call | solution.py:453
  84.6 4.4 %collective-permute-done.18 = bf16[512,512]{1,0:T(8,128)(2,1)} collective-permute-done((bf16[512,512]{1,0:T(8,128)(2,1)}, bf16[512,512]{1,0:T(8,128)(2,1)}, u32[]{:S(2)}, u32[]{:S(2)}) %collective-permute-start.18) | collective-permute-done | bytes 524320 | tf_op jit(solution)/shard_map/ppermute | solution.py:478
  89.0 1.2 %fusion.1 = (bf16[256,512]{1,0:T(8,128)(2,1)S(1)}, f32[1,256,512]{2,1,0:T(8,128)S(1)}) fusion(f32[2,256,512]{2,1,0:T(8,128)S(1)} %bitcast.74, s32[]{:T(128)S(6)} %select_n.57, bf16[2,256,512]{2,1,0:T(8,128)(2,1)} %bitcast.24, s32[]{:T(128)S(6)} %select_n.56), kind=kLoop, calls=%fused_computation.6 | loop fusion | flops 655360 | bytes 2359304 | tf_op jit(solution)/shard_map/convert_element_type | solution.py:473
  90.6 1.3 %collective-permute-start.16 = (bf16[256,512]{1,0:T(8,128)(2,1)S(1)}, bf16[256,512]{1,0:T(8,128)(2,1)S(1)}, u32[]{:S(2)}, u32[]{:S(2)}) collective-permute-start(bf16[256,512]{1,0:T(8,128)(2,1)S(1)} %get-tuple-element.102), channel_id=1, source_target_pairs={{0,2},{1,3},{2,0},{3,1},{4,6},{5,7},{6,4},{7,5},{8,10},{9,11},{10,... | collective-permute-start | bytes 786440 | tf_op jit(solution)/shard_map/ppermute | solution.py:478
  91.9 3.6 %collective-permute-done.19 = bf16[256,512]{1,0:T(8,128)(2,1)S(1)} collective-permute-done((bf16[256,512]{1,0:T(8,128)(2,1)S(1)}, bf16[256,512]{1,0:T(8,128)(2,1)S(1)}, u32[]{:S(2)}, u32[]{:S(2)}) %collective-permute-start.19) | collective-permute-done | bytes 262176 | tf_op jit(solution)/shard_map/ppermute | solution.py:478
  95.5 1.0 collective-permute-start.20
  96.5 1.3 %collective-permute-start.21 = (bf16[16,512]{1,0:T(8,128)(2,1)S(1)}, bf16[16,512]{1,0:T(8,128)(2,1)S(1)}, u32[]{:S(2)}, u32[]{:S(2)}) collective-permute-start(bf16[16,512]{1,0:T(8,128)(2,1)S(1)} %get-tuple-element.106), channel_id=1, source_target_pairs={{24,0},{25,1},{26,2},{27,3},{28,4},{29,5},{30,6},{31,7}} | collective-permute-start | bytes 49160 | tf_op jit(solution)/shard_map/ppermute | solution.py:540
  97.8 1.3 %collective-permute-start.22 = (bf16[16,512]{1,0:T(8,128)(2,1)S(1)}, bf16[16,512]{1,0:T(8,128)(2,1)S(1)}, u32[]{:S(2)}, u32[]{:S(2)}) collective-permute-start(bf16[16,512]{1,0:T(8,128)(2,1)S(1)} %get-tuple-element.108), channel_id=1, source_target_pairs={{24,8},{25,9},{26,10},{27,11},{28,12},{29,13},{30,14},{31,15}} | collective-permute-start | bytes 49160 | tf_op jit(solution)/shard_map/ppermute | solution.py:540
  99.1 1.3 %collective-permute-start.23 = (bf16[16,512]{1,0:T(8,128)(2,1)S(1)}, bf16[16,512]{1,0:T(8,128)(2,1)S(1)}, u32[]{:S(2)}, u32[]{:S(2)}) collective-permute-start(bf16[16,512]{1,0:T(8,128)(2,1)S(1)} %get-tuple-element.107), channel_id=1, source_target_pairs={{24,16},{25,17},{26,18},{27,19},{28,20},{29,21},{30,22},{31,23}} | collective-permute-start | bytes 49160 | tf_op jit(solution)/shard_map/ppermute | solution.py:540
  100.5 1.5 %collective-permute-start.17 = (bf16[128,512]{1,0:T(8,128)(2,1)S(1)}, bf16[128,512]{1,0:T(8,128)(2,1)S(1)}, u32[]{:S(2)}, u32[]{:S(2)}) collective-permute-start(bf16[128,512]{1,0:T(8,128)(2,1)S(1)} %fusion.3), channel_id=1, source_target_pairs={{0,4},{1,5},{2,6},{3,7},{4,0},{5,1},{6,2},{7,3},{8,12},{9,13},{10,... | collective-permute-start | bytes 393224 | tf_op jit(solution)/shard_map/ppermute | solution.py:478
  102.0 4.7 %collective-permute-done.17 = bf16[128,512]{1,0:T(8,128)(2,1)S(1)} collective-permute-done((bf16[128,512]{1,0:T(8,128)(2,1)S(1)}, bf16[128,512]{1,0:T(8,128)(2,1)S(1)}, u32[]{:S(2)}, u32[]{:S(2)}) %collective-permute-start.17) | collective-permute-done | bytes 131104 | tf_op jit(solution)/shard_map/ppermute | solution.py:478
  106.7 0.8 maximum_bitcast_fusion
  107.6 1.4 %slice_select_fusion = f32[16,512]{1,0:T(8,128)} fusion(f32[16,2048]{1,0:T(8,128)} %get-tuple-element.99.after_hbm, bf16[16,512]{1,0:T(8,128)(2,1)S(1)} %collective-permute-done.23, bf16[16,512]{1,0:T(8,128)(2,1)S(1)} %collective-permute-done.22, bf16[16,512]{1,0:T(8,128)(2,1)S(1)} %collective-permute-done.21, pred[]{:T(512)} %bitcast.31), kind=kLoop, calls=%fused_computation.19 | loop fusion | flops 49152 | bytes 114689 | tf_op jit(solution)/shard_map/jit(_where)/select_n | solution.py:549
  (64 shorter events, 1.4 us)
Async XLA Ops:
  0.6 10.3 %copy-start = (bf16[1,4,256,1024]{3,2,1,0:T(8,128)(2,1)S(1)}, bf16[1,4,256,1024]{3,2,1,0:T(8,128)(2,1)}, u32[]{:S(2)}) copy-start(bf16[1,4,256,1024]{3,2,1,0:T(8,128)(2,1)} %param.6) | copy-start | bytes 6291460
  0.6 10.3 %copy-start.1 = (bf16[1,1024,1024]{2,1,0:T(8,128)(2,1)S(1)}, bf16[1,1024,1024]{2,1,0:T(8,128)(2,1)}, u32[]{:S(2)}) copy-start(bf16[1,1024,1024]{2,1,0:T(8,128)(2,1)} %param.7) | copy-start | bytes 6291460
  0.7 10.3 %copy-start.8 = (bf16[128,2048]{1,0:T(8,128)(2,1)S(1)}, bf16[128,2048]{1,0:T(8,128)(2,1)}, u32[]{:S(2)}) copy-start(bf16[128,2048]{1,0:T(8,128)(2,1)} %table_hbm.1) | copy-start | bytes 1572868
  6.9 36.0 %collective-permute-start = (bf16[256,1024]{1,0:T(8,128)(2,1)}, bf16[256,1024]{1,0:T(8,128)(2,1)S(1)}, u32[]{:S(2)}, u32[]{:S(2)}) collective-permute-start(bf16[256,1024]{1,0:T(8,128)(2,1)} %get-tuple-element.50), channel_id=1, source_target_pairs={{24,16},{25,17},{26,18},{27,19},{28,20},{29,21},{30,22},{31,23}} | collective-permute-start | bytes 1572872 | tf_op jit(solution)/shard_map/ppermute | solution.py:526
  15.2 32.3 %collective-permute-start.2 = (bf16[256,1024]{1,0:T(8,128)(2,1)}, bf16[256,1024]{1,0:T(8,128)(2,1)}, u32[]{:S(2)}, u32[]{:S(2)}) collective-permute-start(bf16[256,1024]{1,0:T(8,128)(2,1)} %get-tuple-element.59), channel_id=1, source_target_pairs={{24,16},{25,17},{26,18},{27,19},{28,20},{29,21},{30,22},{31,23}} | collective-permute-start | bytes 1572872 | tf_op jit(solution)/shard_map/ppermute | solution.py:526
  21.5 29.5 %collective-permute-start.1 = (bf16[256,1024]{1,0:T(8,128)(2,1)}, bf16[256,1024]{1,0:T(8,128)(2,1)}, u32[]{:S(2)}, u32[]{:S(2)}) collective-permute-start(bf16[256,1024]{1,0:T(8,128)(2,1)} %get-tuple-element.58), channel_id=1, source_target_pairs={{24,16},{25,17},{26,18},{27,19},{28,20},{29,21},{30,22},{31,23}} | collective-permute-start | bytes 1572872 | tf_op jit(solution)/shard_map/ppermute | solution.py:526
  23.6 6.3 %copy-start.14 = (bf16[4,1,1024]{2,0,1:T(4,128)(2,1)S(1)}, bf16[4,1,1024]{2,0,1:T(4,128)(2,1)}, u32[]{:S(2)}) copy-start(bf16[4,1,1024]{2,0,1:T(4,128)(2,1)} %param.11) | copy-start | bytes 24580
  23.6 6.3 %copy-start.15 = (s32[4,1,64]{2,1,0:T(1,128)S(1)}, s32[4,1,64]{2,1,0:T(1,128)}, u32[]{:S(2)}) copy-start(s32[4,1,64]{2,1,0:T(1,128)} %index_ref.1) | copy-start | bytes 3076
  27.7 24.8 %collective-permute-start.6 = (bf16[256,1024]{1,0:T(8,128)(2,1)}, bf16[256,1024]{1,0:T(8,128)(2,1)}, u32[]{:S(2)}, u32[]{:S(2)}) collective-permute-start(bf16[256,1024]{1,0:T(8,128)(2,1)} %get-tuple-element.65), channel_id=1, source_target_pairs={{24,16},{25,17},{26,18},{27,19},{28,20},{29,21},{30,22},{31,23}} | collective-permute-start | bytes 1572872 | tf_op jit(solution)/shard_map/ppermute | solution.py:526
  29.9 12.9 %copy-start.2 = (bf16[1,1024,1024]{2,1,0:T(8,128)(2,1)S(1)}, bf16[1,1024,1024]{2,1,0:T(8,128)(2,1)}, u32[]{:S(2)}) copy-start(bf16[1,1024,1024]{2,1,0:T(8,128)(2,1)} %param.7) | copy-start | bytes 6291460
  39.7 14.4 %collective-permute-start.11 = (bf16[64,2048]{1,0:T(8,128)(2,1)S(1)}, bf16[64,2048]{1,0:T(8,128)(2,1)}, u32[]{:S(2)}, u32[]{:S(2)}) collective-permute-start(bf16[64,2048]{1,0:T(8,128)(2,1)S(1)} %get-tuple-element.85), channel_id=1, source_target_pairs={{24,25},{25,24},{26,27},{27,26},{28,29},{29,28},{30,31},{31,30}} | collective-permute-start | bytes 786440 | tf_op jit(solution)/shard_map/ppermute | solution.py:478
  42.9 15.4 %collective-permute-start.5 = (bf16[256,1024]{1,0:T(8,128)(2,1)}, bf16[256,1024]{1,0:T(8,128)(2,1)S(1)}, u32[]{:S(2)}, u32[]{:S(2)}) collective-permute-start(bf16[256,1024]{1,0:T(8,128)(2,1)} %get-tuple-element.55.after_hbm), channel_id=1, source_target_pairs={{16,8},{17,9},{18,10},{19,11},{20,12},{21,13},{22,14},{23,15}} | collective-permute-start | bytes 1572872 | tf_op jit(solution)/shard_map/ppermute | solution.py:526
  43.8 1.0 copy-start.13
  47.5 1.4 %copy-start.3 = (bf16[1024,1024]{1,0:T(8,128)(2,1)}, bf16[1024,1024]{1,0:T(8,128)(2,1)S(1)}, u32[]{:S(2)}) copy-start(bf16[1024,1024]{1,0:T(8,128)(2,1)S(1)} %get-tuple-element.56.turned_first) | copy-start | bytes 6291460
  47.5 2.0 %copy-start.5 = (bf16[1024,1024]{1,0:T(8,128)(2,1)}, bf16[1024,1024]{1,0:T(8,128)(2,1)S(1)}, u32[]{:S(2)}) copy-start(bf16[1024,1024]{1,0:T(8,128)(2,1)S(1)} %get-tuple-element.57.turned_second) | copy-start | bytes 6291460
  49.5 9.6 %collective-permute-start.4 = (bf16[256,1024]{1,0:T(8,128)(2,1)}, bf16[256,1024]{1,0:T(8,128)(2,1)}, u32[]{:S(2)}, u32[]{:S(2)}) collective-permute-start(bf16[256,1024]{1,0:T(8,128)(2,1)} %get-tuple-element.64), channel_id=1, source_target_pairs={{16,8},{17,9},{18,10},{19,11},{20,12},{21,13},{22,14},{23,15}} | collective-permute-start | bytes 1572872 | tf_op jit(solution)/shard_map/ppermute | solution.py:526
  51.0 9.6 %collective-permute-start.3 = (bf16[256,1024]{1,0:T(8,128)(2,1)}, bf16[256,1024]{1,0:T(8,128)(2,1)}, u32[]{:S(2)}, u32[]{:S(2)}) collective-permute-start(bf16[256,1024]{1,0:T(8,128)(2,1)} %get-tuple-element.63), channel_id=1, source_target_pairs={{16,8},{17,9},{18,10},{19,11},{20,12},{21,13},{22,14},{23,15}} | collective-permute-start | bytes 1572872 | tf_op jit(solution)/shard_map/ppermute | solution.py:526
  52.6 9.6 %collective-permute-start.10 = (bf16[256,1024]{1,0:T(8,128)(2,1)}, bf16[256,1024]{1,0:T(8,128)(2,1)}, u32[]{:S(2)}, u32[]{:S(2)}) collective-permute-start(bf16[256,1024]{1,0:T(8,128)(2,1)} %get-tuple-element.73), channel_id=1, source_target_pairs={{16,8},{17,9},{18,10},{19,11},{20,12},{21,13},{22,14},{23,15}} | collective-permute-start | bytes 1572872 | tf_op jit(solution)/shard_map/ppermute | solution.py:526
  55.1 7.8 %collective-permute-start.12 = (bf16[32,2048]{1,0:T(8,128)(2,1)S(1)}, bf16[32,2048]{1,0:T(8,128)(2,1)S(1)}, u32[]{:S(2)}, u32[]{:S(2)}) collective-permute-start(bf16[32,2048]{1,0:T(8,128)(2,1)S(1)} %get-tuple-element.104), channel_id=1, source_target_pairs={{24,26},{25,27},{26,24},{27,25},{28,30},{29,31},{30,28},{31,29}} | collective-permute-start | bytes 393224 | tf_op jit(solution)/shard_map/ppermute | solution.py:478
  58.4 11.8 %collective-permute-start.9 = (bf16[256,1024]{1,0:T(8,128)(2,1)}, bf16[256,1024]{1,0:T(8,128)(2,1)S(1)}, u32[]{:S(2)}, u32[]{:S(2)}) collective-permute-start(bf16[256,1024]{1,0:T(8,128)(2,1)} %get-tuple-element.72), channel_id=1, source_target_pairs={{8,0},{9,1},{10,2},{11,3},{12,4},{13,5},{14,6},{15,7}} | collective-permute-start | bytes 1572872 | tf_op jit(solution)/shard_map/ppermute | solution.py:526
  59.1 11.1 %collective-permute-start.8 = (bf16[256,1024]{1,0:T(8,128)(2,1)}, bf16[256,1024]{1,0:T(8,128)(2,1)}, u32[]{:S(2)}, u32[]{:S(2)}) collective-permute-start(bf16[256,1024]{1,0:T(8,128)(2,1)} %get-tuple-element.71), channel_id=1, source_target_pairs={{8,0},{9,1},{10,2},{11,3},{12,4},{13,5},{14,6},{15,7}} | collective-permute-start | bytes 1572872 | tf_op jit(solution)/shard_map/ppermute | solution.py:526
  60.7 9.7 %collective-permute-start.7 = (bf16[256,1024]{1,0:T(8,128)(2,1)}, bf16[256,1024]{1,0:T(8,128)(2,1)}, u32[]{:S(2)}, u32[]{:S(2)}) collective-permute-start(bf16[256,1024]{1,0:T(8,128)(2,1)} %get-tuple-element.70), channel_id=1, source_target_pairs={{8,0},{9,1},{10,2},{11,3},{12,4},{13,5},{14,6},{15,7}} | collective-permute-start | bytes 1572872 | tf_op jit(solution)/shard_map/ppermute | solution.py:526
  62.2 13.6 %collective-permute-start.14 = (bf16[256,1024]{1,0:T(8,128)(2,1)}, bf16[256,1024]{1,0:T(8,128)(2,1)S(1)}, u32[]{:S(2)}, u32[]{:S(2)}) collective-permute-start(bf16[256,1024]{1,0:T(8,128)(2,1)} %get-tuple-element.86), channel_id=1, source_target_pairs={{8,0},{9,1},{10,2},{11,3},{12,4},{13,5},{14,6},{15,7}} | collective-permute-start | bytes 1572872 | tf_op jit(solution)/shard_map/ppermute | solution.py:526
  62.9 6.6 %collective-permute-start.13 = (bf16[16,2048]{1,0:T(8,128)(2,1)S(1)}, bf16[16,2048]{1,0:T(8,128)(2,1)S(1)}, u32[]{:S(2)}, u32[]{:S(2)}) collective-permute-start(bf16[16,2048]{1,0:T(8,128)(2,1)S(1)} %fusion.5), channel_id=1, source_target_pairs={{24,28},{25,29},{26,30},{27,31},{28,24},{29,25},{30,26},{31,27}} | collective-permute-start | bytes 196616 | tf_op jit(solution)/shard_map/ppermute | solution.py:478
  70.3 1.6 %copy-start.4 = (bf16[1024,1024]{1,0:T(8,128)(2,1)S(1)}, bf16[1024,1024]{1,0:T(8,128)(2,1)}, u32[]{:S(2)}) copy-start(bf16[1024,1024]{1,0:T(8,128)(2,1)} %copy-done.3) | copy-start | bytes 6291460
  70.3 2.2 %copy-start.6 = (bf16[1024,1024]{1,0:T(8,128)(2,1)S(1)}, bf16[1024,1024]{1,0:T(8,128)(2,1)}, u32[]{:S(2)}) copy-start(bf16[1024,1024]{1,0:T(8,128)(2,1)} %copy-done.5) | copy-start | bytes 6291460
  75.7 2.8 %copy-start.9 = (f32[512,512]{1,0:T(8,128)}, f32[512,512]{1,0:T(8,128)S(1)}, u32[]{:S(2)}) copy-start(f32[512,512]{1,0:T(8,128)S(1)} %get-tuple-element.87.early_first) | copy-start | bytes 3145732
  75.7 2.8 %copy-start.11 = (f32[512,512]{1,0:T(8,128)}, f32[512,512]{1,0:T(8,128)S(1)}, u32[]{:S(2)}) copy-start(f32[512,512]{1,0:T(8,128)S(1)} %get-tuple-element.88.early_second) | copy-start | bytes 3145732
  78.5 10.5 %collective-permute-start.18 = (bf16[512,512]{1,0:T(8,128)(2,1)}, bf16[512,512]{1,0:T(8,128)(2,1)}, u32[]{:S(2)}, u32[]{:S(2)}) collective-permute-start(bf16[512,512]{1,0:T(8,128)(2,1)} %get-tuple-element.94), channel_id=1, source_target_pairs={{0,2},{1,3},{2,0},{3,1},{4,6},{5,7},{6,4},{7,5},{8,10},{9,11},{10,... | collective-permute-start | bytes 1572872 | tf_op jit(solution)/shard_map/ppermute | solution.py:478
  78.8 11.6 %collective-permute-start.15 = (bf16[512,512]{1,0:T(8,128)(2,1)}, bf16[512,512]{1,0:T(8,128)(2,1)S(1)}, u32[]{:S(2)}, u32[]{:S(2)}) collective-permute-start(bf16[512,512]{1,0:T(8,128)(2,1)} %get-tuple-element.92), channel_id=1, source_target_pairs={{0,1},{1,0},{2,3},{3,2},{4,5},{5,4},{6,7},{7,6},{8,9},{9,8},{10,11... | collective-permute-start | bytes 1572872 | tf_op jit(solution)/shard_map/ppermute | solution.py:478
  79.1 1.6 %copy-start.7 = (bf16[1024,1024]{1,0:T(8,128)(2,1)S(1)}, bf16[1024,1024]{1,0:T(8,128)(2,1)}, u32[]{:S(2)}) copy-start(bf16[1024,1024]{1,0:T(8,128)(2,1)} %copy-done.5) | copy-start | bytes 6291460
  80.7 1.2 %copy-start.10 = (f32[512,512]{1,0:T(8,128)S(1)}, f32[512,512]{1,0:T(8,128)}, u32[]{:S(2)}) copy-start(f32[512,512]{1,0:T(8,128)} %copy-done.9) | copy-start | bytes 3145732
  81.9 1.2 %copy-start.12 = (f32[512,512]{1,0:T(8,128)S(1)}, f32[512,512]{1,0:T(8,128)}, u32[]{:S(2)}) copy-start(f32[512,512]{1,0:T(8,128)} %copy-done.11) | copy-start | bytes 3145732
  90.2 5.3 %collective-permute-start.19 = (bf16[256,512]{1,0:T(8,128)(2,1)S(1)}, bf16[256,512]{1,0:T(8,128)(2,1)S(1)}, u32[]{:S(2)}, u32[]{:S(2)}) collective-permute-start(bf16[256,512]{1,0:T(8,128)(2,1)S(1)} %get-tuple-element.100), channel_id=1, source_target_pairs={{0,1},{1,0},{2,3},{3,2},{4,5},{5,4},{6,7},{7,6},{8,9},{9,8},{10,11... | collective-permute-start | bytes 786440 | tf_op jit(solution)/shard_map/ppermute | solution.py:478
  90.6 9.8 %collective-permute-start.16 = (bf16[256,512]{1,0:T(8,128)(2,1)S(1)}, bf16[256,512]{1,0:T(8,128)(2,1)S(1)}, u32[]{:S(2)}, u32[]{:S(2)}) collective-permute-start(bf16[256,512]{1,0:T(8,128)(2,1)S(1)} %get-tuple-element.102), channel_id=1, source_target_pairs={{0,2},{1,3},{2,0},{3,1},{4,6},{5,7},{6,4},{7,5},{8,10},{9,11},{10,... | collective-permute-start | bytes 786440 | tf_op jit(solution)/shard_map/ppermute | solution.py:478
  95.5 6.4 %collective-permute-start.20 = (bf16[128,512]{1,0:T(8,128)(2,1)S(1)}, bf16[128,512]{1,0:T(8,128)(2,1)S(1)}, u32[]{:S(2)}, u32[]{:S(2)}) collective-permute-start(bf16[128,512]{1,0:T(8,128)(2,1)S(1)} %fusion.4), channel_id=1, source_target_pairs={{0,4},{1,5},{2,6},{3,7},{4,0},{5,1},{6,2},{7,3},{8,12},{9,13},{10,... | collective-permute-start | bytes 393224 | tf_op jit(solution)/shard_map/ppermute | solution.py:478
  96.5 11.0 %collective-permute-start.21 = (bf16[16,512]{1,0:T(8,128)(2,1)S(1)}, bf16[16,512]{1,0:T(8,128)(2,1)S(1)}, u32[]{:S(2)}, u32[]{:S(2)}) collective-permute-start(bf16[16,512]{1,0:T(8,128)(2,1)S(1)} %get-tuple-element.106), channel_id=1, source_target_pairs={{24,0},{25,1},{26,2},{27,3},{28,4},{29,5},{30,6},{31,7}} | collective-permute-start | bytes 49160 | tf_op jit(solution)/shard_map/ppermute | solution.py:540
  97.8 9.7 %collective-permute-start.22 = (bf16[16,512]{1,0:T(8,128)(2,1)S(1)}, bf16[16,512]{1,0:T(8,128)(2,1)S(1)}, u32[]{:S(2)}, u32[]{:S(2)}) collective-permute-start(bf16[16,512]{1,0:T(8,128)(2,1)S(1)} %get-tuple-element.108), channel_id=1, source_target_pairs={{24,8},{25,9},{26,10},{27,11},{28,12},{29,13},{30,14},{31,15}} | collective-permute-start | bytes 49160 | tf_op jit(solution)/shard_map/ppermute | solution.py:540
  99.1 8.4 %collective-permute-start.23 = (bf16[16,512]{1,0:T(8,128)(2,1)S(1)}, bf16[16,512]{1,0:T(8,128)(2,1)S(1)}, u32[]{:S(2)}, u32[]{:S(2)}) collective-permute-start(bf16[16,512]{1,0:T(8,128)(2,1)S(1)} %get-tuple-element.107), channel_id=1, source_target_pairs={{24,16},{25,17},{26,18},{27,19},{28,20},{29,21},{30,22},{31,23}} | collective-permute-start | bytes 49160 | tf_op jit(solution)/shard_map/ppermute | solution.py:540
  100.5 6.2 %collective-permute-start.17 = (bf16[128,512]{1,0:T(8,128)(2,1)S(1)}, bf16[128,512]{1,0:T(8,128)(2,1)S(1)}, u32[]{:S(2)}, u32[]{:S(2)}) collective-permute-start(bf16[128,512]{1,0:T(8,128)(2,1)S(1)} %fusion.3), channel_id=1, source_target_pairs={{0,4},{1,5},{2,6},{3,7},{4,0},{5,1},{6,2},{7,3},{8,12},{9,13},{10,... | collective-permute-start | bytes 393224 | tf_op jit(solution)/shard_map/ppermute | solution.py:478

commit v2 on v1

--- a/solution.py
+++ b/solution.py
@@ -205,13 +205,14 @@
     )
 
 
-def table_kernel(replicas, flag_ref, parity_ref, index_ref, pooled_ref, table_hbm, *refs):
-    count = (len(refs) - 7) // 2
-    sources = refs[: 2 * count]
-    send_ref, keep_ref, table, share, high, kv, sems = refs[2 * count :]
+def table_kernel(replicas, flag_ref, number_ref, index_ref, pooled_ref, table_hbm, after_hbm, *refs):
+    table, share, high, kv, sems = refs[-5:]
+    count = share.shape[0]
+    sources, outs = refs[: 2 * count], refs[2 * count : -5]
     width = high.shape[2]
     rows = high.shape[1]
-    table_rows = 2 * keep_ref.shape[0]
+    table_rows = table.shape[0]
+    span = 2 * width // len(outs)
     cands = index_ref.shape[2]
 
     @pl.when(flag_ref[0] == 1)
@@ -223,14 +224,15 @@
         loads.append(pltpu.make_async_copy(table_hbm, table, sems.at[2 * count]))
         for load in loads:
             load.start()
-        steps = replicas.bit_length() - 1
+        bits = bit_orders(replicas)[1]
         shift = (table_rows // replicas).bit_length() - 1
         spot = lax.broadcasted_iota(jnp.int32, (table_rows, cands), 0)
         block = spot >> shift
-        low_bit = jnp.where(block < replicas // 2, 1 - parity_ref[0], parity_ref[0])
-        for k in range(steps - 1):
-            low_bit = low_bit + (((block >> (steps - 2 - k)) & 1) << (k + 1))
-        row = (low_bit << shift) + (spot & ((1 << shift) - 1))
+        mine = (number_ref[0] >> bits[0]) & 1
+        row = jnp.where(block < replicas // 2, 1 - mine, mine) << bits[0]
+        for k, bit in enumerate(bits[1:]):
+            row = row + (((block >> (len(bits) - 2 - k)) & 1) << bit)
+        row = (row << shift) + (spot & ((1 << shift) - 1))
         left_half = lax.broadcasted_iota(jnp.int32, (HEAD, PAIR), 1) < HEAD
         own = own_heads(width)
         loads[-1].wait()
@@ -256,23 +258,19 @@
                     left_half, value[:HEAD], value[HEAD:]
                 )
         onehot = jnp.concatenate(onehots, axis=1)
-        for at in range(0, 2 * width, 2 * TILE):
-            cols = slice(at, at + 2 * TILE)
-            kv_high, kv_low = high_low(kv[:, cols])
-            part = dot(onehot, kv_high, NN) + dot(onehot, kv_low, NN)
-            send_ref[:, cols] = part[: table_rows // 2].astype(BF16)
-            keep_ref[:, cols] = part[table_rows // 2 :]
-
-
-def table_call(flag, parity, index, pooled, table, shares, highs, replicas):
+        for k, out in enumerate(outs):
+            kv_high, kv_low = high_low(kv[:, k * span : (k + 1) * span])
+            out[...] = (dot(onehot, kv_high, NN) + dot(onehot, kv_low, NN)).astype(BF16)
+
+
+def table_call(flag, number, index, pooled, table, after, shares, highs, sections, replicas):
     rows, width = highs[0].shape
     count = len(highs)
-    half = (table.shape[0] // 2, 2 * width)
     return pl.pallas_call(
         functools.partial(table_kernel, replicas),
-        out_shape=(jax.ShapeDtypeStruct(half, BF16), jax.ShapeDtypeStruct(half, F32)),
-        in_specs=[SMEM, SMEM, VMEM, VMEM, HBM] + [HBM] * (2 * count),
-        out_specs=(VMEM, VMEM),
+        out_shape=(pltpu.HBM((table.shape[0], 2 * width // sections), BF16),) * sections,
+        in_specs=[SMEM, SMEM, VMEM, VMEM, HBM, HBM] + [HBM] * (2 * count),
+        out_specs=(VMEM,) * sections,
         scratch_shapes=[
             pltpu.VMEM(table.shape, BF16),
             pltpu.VMEM((count,) + shares[0].shape, BF16),
@@ -283,32 +281,29 @@
         compiler_params=pltpu.CompilerParams(vmem_limit_bytes=28 * MIB),
         cost_estimate=LIGHT,
         name="table",
-    )(flag, parity, index, pooled, stay(table), *map(stay, shares), *map(stay, highs))
-
-
-def hop_kernel(m, with_grad, flag_ref, came_hbm, delta_in, weight, after_hbm, *rest):
+    )(flag, number, index, pooled, stay(table), stay(after), *map(stay, shares), *map(stay, highs))
+
+
+def hop_kernel(m, with_grad, flag_ref, came, delta_in, weight, after_hbm, *rest):
     if with_grad:
-        grad_hbm, delta_hbm, came, aux, grad, sems = rest
+        grad_hbm, delta_hbm, aux, grad, sems = rest
     else:
-        delta_hbm, came, aux, sems = rest
+        delta_hbm, aux, sems = rest
     width = came.shape[1]
 
     @pl.when(flag_ref[0] == 1)
     def _():
-        first = pltpu.make_async_copy(came_hbm, came, sems.at[0])
-        second = pltpu.make_async_copy(delta_in.at[m], aux, sems.at[1])
-        first.start()
-        second.start()
-        first.wait()
-        second.wait()
+        load = pltpu.make_async_copy(delta_in.at[m], aux, sems.at[0])
+        load.start()
+        load.wait()
         aux[...] = (came[...].astype(F32) * aux[...].astype(F32)).astype(BF16)
-        stores = [pltpu.make_async_copy(aux, delta_hbm.at[m], sems.at[2])]
+        stores = [pltpu.make_async_copy(aux, delta_hbm.at[m], sems.at[1])]
         stores[0].start()
         if with_grad:
             for n in range(width // TILE):
                 part = slice(n * TILE, (n + 1) * TILE)
                 grad[:, part] = (came[:, part].astype(F32) + dot(aux[...], weight[part, :], NT)).astype(BF16)
-            stores.append(pltpu.make_async_copy(grad, grad_hbm, sems.at[3]))
+            stores.append(pltpu.make_async_copy(grad, grad_hbm, sems.at[2]))
             stores[-1].start()
         for store in stores:
             store.wait()
@@ -316,15 +311,15 @@
 
 def hop_call(m, flag, came, delta, weight, after, with_grad):
     rows, width = came.shape
-    scratch = [pltpu.VMEM((rows, width), BF16)] * (3 if with_grad else 2)
-    scratch.append(pltpu.SemaphoreType.DMA((4,)))
+    scratch = [pltpu.VMEM((rows, width), BF16)] * (2 if with_grad else 1)
+    scratch.append(pltpu.SemaphoreType.DMA((3,)))
     outs = (pltpu.HBM(delta.shape, BF16),)
     if with_grad:
         outs = (pltpu.HBM((rows, width), BF16),) + outs
     return pl.pallas_call(
         functools.partial(hop_kernel, m, with_grad),
         out_shape=outs,
-        in_specs=[SMEM, HBM, HBM, VMEM if with_grad else HBM, HBM],
+        in_specs=[SMEM, VMEM, HBM, VMEM if with_grad else HBM, HBM],
         out_specs=(HBM,) * len(outs),
         scratch_shapes=scratch,
         input_output_aliases={2: len(outs) - 1},
@@ -372,7 +367,7 @@
     count, rows, width = acts.shape
     return pl.pallas_call(
         functools.partial(turn_kernel, replicas),
-        out_shape=(jax.ShapeDtypeStruct((width, count * rows), BF16),) * 2 + (pltpu.HBM((16, 128), BF16),),
+        out_shape=(pltpu.HBM((width, count * rows), BF16),) * 2 + (pltpu.HBM((16, 128), BF16),),
         in_specs=[SMEM, HBM, HBM],
         out_specs=(VMEM,) * 3,
         scratch_shapes=[
@@ -424,13 +419,24 @@
     )(*turned, stay(delta))
 
 
-def weight_kernel(which, flag_ref, turned_first, turned_second, delta_hbm, came, early_first, early_second, *refs):
+def weight_kernel(
+    replicas, which, flag_ref, turned_first, turned_second, delta_hbm, came, early_first, early_second, table_ref, *refs
+):
     outs, (delta, sem) = refs[:2], refs[2:]
     rows, width = delta.shape
     half = width // 2
+    size = width // replicas
+    lines = table_ref.shape[0] // replicas
+    pitch = outs[1].shape[0] // (replicas // 2)
     last = delta_hbm.shape[0] - 1
     load = pltpu.make_async_copy(delta_hbm.at[last], delta, sem.at[0])
     load.start()
+    table = table_ref[which * table_ref.shape[0] // 2 : (which + 1) * table_ref.shape[0] // 2].astype(F32)
+    for i in range(replicas // 2):
+        extra = table[i * lines : (i + 1) * lines]
+        if extra.shape != (pitch - size, half):
+            extra = jnp.pad(extra, ((0, pitch - size - lines), (0, half - extra.shape[1])))
+        outs[1][i * pitch + size : (i + 1) * pitch] = extra.astype(outs[1].dtype)
     load.wait()
 
     @pl.when(flag_ref[0] == 1)
@@ -439,27 +445,35 @@
 
     for c, (turned, early) in enumerate(((turned_first, early_first), (turned_second, early_second))):
         for at in range(0, half, TILE):
-            product = dot(
+            cols = slice(at, at + TILE)
+            product = early[:, cols] + dot(
                 turned[which * half : (which + 1) * half, last * rows :],
                 delta[:, c * half + at : c * half + at + TILE],
                 NN,
             )
-            outs[c][:, at : at + TILE] = (early[:, at : at + TILE] + product).astype(outs[c].dtype)
-
-
-def weight_call(which, flag, turned, delta, came, early):
+            product = product.astype(outs[c].dtype)
+            if c == 0:
+                outs[c][:, cols] = product
+            else:
+                for i in range(replicas // 2):
+                    outs[c][i * pitch : i * pitch + size, cols] = product[i * size : (i + 1) * size]
+
+
+def weight_call(which, flag, turned, delta, came, early, table, replicas):
     micros, rows, width = delta.shape
-    half = (width // 2, width // 2)
+    half = width // 2
+    extra = max(16, table.shape[0] // replicas) * (replicas // 2)
+    array = functools.partial(jax.ShapeDtypeStruct, dtype=F32) if which else functools.partial(pltpu.HBM, dtype=BF16)
     return pl.pallas_call(
-        functools.partial(weight_kernel, which),
-        out_shape=(jax.ShapeDtypeStruct(half, F32) if which else pltpu.HBM(half, BF16),) * 2,
-        in_specs=[SMEM, VMEM, VMEM, HBM, VMEM, VMEM, VMEM],
+        functools.partial(weight_kernel, replicas, which),
+        out_shape=(array((half, half)), array((half + extra, half))),
+        in_specs=[SMEM, VMEM, VMEM, HBM] + [VMEM] * 4,
         out_specs=(VMEM,) * 2,
         scratch_shapes=[pltpu.VMEM((rows, width), BF16), pltpu.SemaphoreType.DMA((1,))],
         compiler_params=pltpu.CompilerParams(vmem_limit_bytes=20 * MIB),
         cost_estimate=LIGHT,
         name="weight",
-    )(flag, *turned, stay(delta), came, *early)
+    )(flag, *turned, stay(delta), came, *early, table)
 
 
 def own_half(keep, got, bit):
@@ -510,46 +524,37 @@
         shares.append(share)
         highs.append(high)
 
-    def table_pairs(bit):
-        return [(last * replicas + i, last * replicas + (i ^ (1 << bit))) for i in range(replicas)]
-
     def pairs(bit):
         return [(i, i ^ (1 << bit)) for i in range(replicas)]
 
-    orders = bit_orders(replicas)
-    table_send, table_keep = table_call(
-        final, number & 1, cand_index, pooled, cand_table, shares, highs, replicas
-    )
-    own_table = finish_scatter(table_send, table_keep, orders[0], ("section", "dp"), table_pairs)
     for hop in range(last):
         source = last - hop
         received = [lax.ppermute(g, "section", [(source, source - 1)]) for g in grads]
         active = flag(position == source - 1)
         for m in range(micro_count):
             if hop + 1 < last:
-                after = token if hop == 0 and m == 1 else acts
+                after = token if hop == 1 and m == 0 else acts
                 grads[m], delta = hop_call(m, active, received[m], delta, weight, after, True)
-                if hop == 0 and m == 0:
-                    *turned, token = turn_call(number, acts, grads[0], replicas)
             elif m + 1 < micro_count:
-                after = own_table if m + 2 == micro_count else acts
-                (delta,) = hop_call(m, active, received[m], delta, weight, after, False)
-
-    width = 2 * model_width // sections
-    spread = [
-        lax.ppermute(own_table[:, s * width : (s + 1) * width].astype(BF16), "section", [(last, s)])
-        for s in range(last)
-    ]
-
+                (delta,) = hop_call(m, active, received[m], delta, weight, acts, False)
+        if hop == 0:
+            parts = table_call(
+                final, number, cand_index, pooled, cand_table, grads[-1], shares, highs, sections, replicas
+            )
+            *turned, token = turn_call(number, acts, grads[-1], replicas)
+
+    spread = [lax.ppermute(parts[s], "section", [(last, s)]) for s in range(last)]
+    table_part = jnp.where(final_flag, parts[last], sum(spread))
+
+    orders = bit_orders(replicas)
     early = early_call(turned, delta)
-    sends = weight_call(0, active, turned, delta, received[-1], early[::2])
-    keeps = weight_call(1, active, turned, delta, received[-1], early[1::2])
+    sends = weight_call(0, active, turned, delta, received[-1], early[::2], table_part, replicas)
+    keeps = weight_call(1, active, turned, delta, received[-1], early[1::2], table_part, replicas)
     sums = [finish_scatter(sends[c], keeps[c], orders[c], "dp", pairs) for c in range(2)]
-    late_flag, sums = lax.optimization_barrier((flag(final_flag), sums))
-    table_sum = jnp.where(
-        late_flag[0] == 1, own_table[:, last * width :], sum(piece.astype(F32) for piece in spread)
-    )
-    return jnp.concatenate(sums, axis=1)[None], table_sum
+    size = model_width // replicas
+    lines = cand_table.shape[0] // replicas
+    table_sum = sums[1][size : size + lines, : 2 * model_width // sections]
+    return jnp.concatenate([sums[0], sums[1][:size]], axis=1)[None], table_sum
 
 
 def solution(mesh):

time: 110 us -> 117 us (1.064)
  the two profiles are of different devices: /device:TPU:3 before, /device:TPU:6 now
where the time goes in v2:
time: 117 us; the launch traced here: 116 us
  Pallas kernels  39.3 us (34%)
  waiting for transfers between devices  36.5 us (31%)
  starting transfers between devices  29 us (25%)
  local copies, waits for them, and re-layouts  7.44 us (6%)
  other arithmetic  2.39 us (2%)
  between operations  1.18 us (1%)
    ppermute x6, waiting for transfers between devices, finish_scatter(): got = lax.ppermute(send, axes, pairs_of(bit))  20.9 us
    pallas_call x11, Pallas kernels, hop_call(): pl.pallas_call(functools.partial(hop_kernel, m, with_grad), out_shape=out...  18.3 us
    ppermute x12, starting transfers between devices, body(): lax.ppermute(g, 'section', [(source, source - 1)])  17.1 us
    ppermute x3, waiting for transfers between devices, body(): lax.ppermute(parts[s], 'section', [(last, s)])  15.6 us
    ppermute x6, starting transfers between devices, finish_scatter(): got = lax.ppermute(send, axes, pairs_of(bit))  9.16 us
    pallas_call x4, Pallas kernels, first_call(): pl.pallas_call(functools.partial(first_kernel, m), out_shape=(block, pltp...  8.11 us
    unnamed x36, local copies, waits for them, and re-layouts  6.81 us
    pallas_call x1, Pallas kernels, turn_call(): pl.pallas_call(functools.partial(turn_kernel, replicas), out_shape=(pltpu...  4.38 us
  transfers between devices with their start and end apart: 21, of which 5 were waited for; matrix products, arithmetic and copies ran while one was open for 1% of the time, Pallas kernels for 25%

profile of v2, /device:TPU:6, one launch (start us, length us, event | category | flops | bytes accessed | tf_op | source)
XLA Modules:
  0.0 115.9 jit_solution(1215430610378365951)
XLA Ops:
  0.7 7.6 %first.4 = (bf16[256,1024]{1,0:T(8,128)(2,1)}, bf16[4,256,1024]{2,1,0:T(8,128)(2,1)}, bf16[1024,256]{1,0:T(8,128)(2,1)}, bf16[256,1024]{1,0:T(8,128)(2,1)}) custom-call(s32[1]{0:T(128)} %bitcast.4.flag_ref, s32[1,4]{1,0:T(1,128)} %bitcast.78, bf16[4,256,1024]{2,1,0:T(8,128)(2,1)} %bitcast.31, bf16[1024,1024]{1,0:T(8,128)(2,1)} %bitcast.47, ...), custom_call_target="tpu_custom_call" | custom-call | flops 1024 | bytes 1024 | tf_op jit(solution)/shard_map/first/pallas_call | solution.py:176
  8.3 1.3 %collective-permute-start.3 = (bf16[256,1024]{1,0:T(8,128)(2,1)}, bf16[256,1024]{1,0:T(8,128)(2,1)S(1)}, u32[]{:S(2)}, u32[]{:S(2)}) collective-permute-start(bf16[256,1024]{1,0:T(8,128)(2,1)} %get-tuple-element.55), channel_id=1, source_target_pairs={{24,16},{25,17},{26,18},{27,19},{28,20},{29,21},{30,22},{31,23}} | collective-permute-start | bytes 1572872 | tf_op jit(solution)/shard_map/ppermute | solution.py:532
  9.8 1.3 %collective-permute-start.2 = (bf16[256,1024]{1,0:T(8,128)(2,1)}, bf16[256,1024]{1,0:T(8,128)(2,1)}, u32[]{:S(2)}, u32[]{:S(2)}) collective-permute-start(bf16[256,1024]{1,0:T(8,128)(2,1)} %get-tuple-element.54), channel_id=1, source_target_pairs={{24,16},{25,17},{26,18},{27,19},{28,20},{29,21},{30,22},{31,23}} | collective-permute-start | bytes 1572872 | tf_op jit(solution)/shard_map/ppermute | solution.py:532
  11.3 1.3 %collective-permute-start.1 = (bf16[256,1024]{1,0:T(8,128)(2,1)}, bf16[256,1024]{1,0:T(8,128)(2,1)}, u32[]{:S(2)}, u32[]{:S(2)}) collective-permute-start(bf16[256,1024]{1,0:T(8,128)(2,1)} %get-tuple-element.53), channel_id=1, source_target_pairs={{24,16},{25,17},{26,18},{27,19},{28,20},{29,21},{30,22},{31,23}} | collective-permute-start | bytes 1572872 | tf_op jit(solution)/shard_map/ppermute | solution.py:532
  12.8 1.3 %collective-permute-start = (bf16[256,1024]{1,0:T(8,128)(2,1)}, bf16[256,1024]{1,0:T(8,128)(2,1)S(1)}, u32[]{:S(2)}, u32[]{:S(2)}) collective-permute-start(bf16[256,1024]{1,0:T(8,128)(2,1)} %get-tuple-element.52), channel_id=1, source_target_pairs={{24,16},{25,17},{26,18},{27,19},{28,20},{29,21},{30,22},{31,23}} | collective-permute-start | bytes 1572872 | tf_op jit(solution)/shard_map/ppermute | solution.py:532
  14.1 1.6 %copy-done.2 = bf16[1,1024,1024]{2,1,0:T(8,128)(2,1)S(1)} copy-done((bf16[1,1024,1024]{2,1,0:T(8,128)(2,1)S(1)}, bf16[1,1024,1024]{2,1,0:T(8,128)(2,1)}, u32[]{:S(2)}) %copy-start.2) | copy-done | bytes 2097176
  15.7 2.6 %hop.8 = (bf16[256,1024]{1,0:T(8,128)(2,1)}, bf16[4,256,1024]{2,1,0:T(8,128)(2,1)}) custom-call(s32[1]{0:T(128)} %bitcast.3.flag_ref, bf16[256,1024]{1,0:T(8,128)(2,1)S(1)} %collective-permute-done.3.came, bf16[4,256,1024]{2,1,0:T(8,128)(2,1)} %get-tuple-element.56.delta_in, bf16[1024,1024]{1,0:T(8,128)(2,1)S(1)} %bitcast.54, ...), custom_call_target="tpu_custom_call", output_to_operand_aliasing={{1}: (2, {})} | custom-call | flops 1024 | bytes 1024 | tf_op jit(solution)/shard_map/hop/pallas_call | solution.py:319
  18.3 1.3 %collective-permute-start.6 = (bf16[256,1024]{1,0:T(8,128)(2,1)}, bf16[256,1024]{1,0:T(8,128)(2,1)S(1)}, u32[]{:S(2)}, u32[]{:S(2)}) collective-permute-start(bf16[256,1024]{1,0:T(8,128)(2,1)} %get-tuple-element.65), channel_id=1, source_target_pairs={{16,8},{17,9},{18,10},{19,11},{20,12},{21,13},{22,14},{23,15}} | collective-permute-start | bytes 1572872 | tf_op jit(solution)/shard_map/ppermute | solution.py:532
  19.6 3.6 %hop.9 = (bf16[256,1024]{1,0:T(8,128)(2,1)}, bf16[4,256,1024]{2,1,0:T(8,128)(2,1)}) custom-call(s32[1]{0:T(128)} %bitcast.3.flag_ref, bf16[256,1024]{1,0:T(8,128)(2,1)} %collective-permute-done.2.came, bf16[4,256,1024]{2,1,0:T(8,128)(2,1)} %get-tuple-element.57.delta_in, bf16[1024,1024]{1,0:T(8,128)(2,1)S(1)} %bitcast.55, ...), custom_call_target="tpu_custom_call", output_to_operand_aliasing={{1}: (2, {})} | custom-call | flops 1024 | bytes 1024 | tf_op jit(solution)/shard_map/hop/pallas_call | solution.py:319
  23.3 2.1 %collective-permute-start.5 = (bf16[256,1024]{1,0:T(8,128)(2,1)}, bf16[256,1024]{1,0:T(8,128)(2,1)}, u32[]{:S(2)}, u32[]{:S(2)}) collective-permute-start(bf16[256,1024]{1,0:T(8,128)(2,1)} %get-tuple-element.64), channel_id=1, source_target_pairs={{16,8},{17,9},{18,10},{19,11},{20,12},{21,13},{22,14},{23,15}} | collective-permute-start | bytes 1572872 | tf_op jit(solution)/shard_map/ppermute | solution.py:532
  25.4 3.7 %hop.10 = (bf16[256,1024]{1,0:T(8,128)(2,1)}, bf16[4,256,1024]{2,1,0:T(8,128)(2,1)}) custom-call(s32[1]{0:T(128)} %bitcast.3.flag_ref, bf16[256,1024]{1,0:T(8,128)(2,1)} %collective-permute-done.1.came, bf16[4,256,1024]{2,1,0:T(8,128)(2,1)} %get-tuple-element.58.delta_in, bf16[1024,1024]{1,0:T(8,128)(2,1)S(1)} %bitcast.56, ...), custom_call_target="tpu_custom_call", output_to_operand_aliasing={{1}: (2, {})} | custom-call | flops 1024 | bytes 1024 | tf_op jit(solution)/shard_map/hop/pallas_call | solution.py:319
  29.1 2.1 %collective-permute-start.4 = (bf16[256,1024]{1,0:T(8,128)(2,1)}, bf16[256,1024]{1,0:T(8,128)(2,1)}, u32[]{:S(2)}, u32[]{:S(2)}) collective-permute-start(bf16[256,1024]{1,0:T(8,128)(2,1)} %get-tuple-element.63), channel_id=1, source_target_pairs={{16,8},{17,9},{18,10},{19,11},{20,12},{21,13},{22,14},{23,15}} | collective-permute-start | bytes 1572872 | tf_op jit(solution)/shard_map/ppermute | solution.py:532
  31.2 2.7 %hop.11 = (bf16[256,1024]{1,0:T(8,128)(2,1)}, bf16[4,256,1024]{2,1,0:T(8,128)(2,1)}) custom-call(s32[1]{0:T(128)} %bitcast.3.flag_ref, bf16[256,1024]{1,0:T(8,128)(2,1)S(1)} %collective-permute-done.came, bf16[4,256,1024]{2,1,0:T(8,128)(2,1)} %get-tuple-element.59.delta_in, bf16[1024,1024]{1,0:T(8,128)(2,1)S(1)} %bitcast.57, ...), custom_call_target="tpu_custom_call", output_to_operand_aliasing={{1}: (2, {})} | custom-call | flops 1024 | bytes 1024 | tf_op jit(solution)/shard_map/hop/pallas_call | solution.py:319
  33.9 2.1 %collective-permute-start.10 = (bf16[256,1024]{1,0:T(8,128)(2,1)}, bf16[256,1024]{1,0:T(8,128)(2,1)}, u32[]{:S(2)}, u32[]{:S(2)}) collective-permute-start(bf16[256,1024]{1,0:T(8,128)(2,1)} %get-tuple-element.60.after_hbm), channel_id=1, source_target_pairs={{16,8},{17,9},{18,10},{19,11},{20,12},{21,13},{22,14},{23,15}} | collective-permute-start | bytes 1572872 | tf_op jit(solution)/shard_map/ppermute | solution.py:532
  36.0 1.1 table.1
  37.2 0.8 collective-permute-start.12
  38.0 4.4 %turn.1 = (bf16[1024,1024]{1,0:T(8,128)(2,1)}, bf16[1024,1024]{1,0:T(8,128)(2,1)}, bf16[16,128]{1,0:T(8,128)(2,1)}) custom-call(s32[1]{0:T(128)} %bitcast.1.number_ref, bf16[4,256,1024]{2,1,0:T(8,128)(2,1)} %bitcast.37, bf16[256,1024]{1,0:T(8,128)(2,1)S(1)} %copy-done.8), custom_call_target="tpu_custom_call" | custom-call | flops 1024 | bytes 1024 | tf_op jit(solution)/shard_map/turn/pallas_call | solution.py:368
  42.4 0.7 collective-permute-start.9
  43.1 1.1 hop.13
  44.2 1.5 %collective-permute-start.8 = (bf16[256,1024]{1,0:T(8,128)(2,1)}, bf16[256,1024]{1,0:T(8,128)(2,1)}, u32[]{:S(2)}, u32[]{:S(2)}) collective-permute-start(bf16[256,1024]{1,0:T(8,128)(2,1)} %get-tuple-element.71), channel_id=1, source_target_pairs={{8,0},{9,1},{10,2},{11,3},{12,4},{13,5},{14,6},{15,7}} | collective-permute-start | bytes 1572872 | tf_op jit(solution)/shard_map/ppermute | solution.py:532
  45.7 1.1 hop.14
  46.8 1.5 %collective-permute-start.7 = (bf16[256,1024]{1,0:T(8,128)(2,1)}, bf16[256,1024]{1,0:T(8,128)(2,1)}, u32[]{:S(2)}, u32[]{:S(2)}) collective-permute-start(bf16[256,1024]{1,0:T(8,128)(2,1)} %get-tuple-element.70), channel_id=1, source_target_pairs={{8,0},{9,1},{10,2},{11,3},{12,4},{13,5},{14,6},{15,7}} | collective-permute-start | bytes 1572872 | tf_op jit(solution)/shard_map/ppermute | solution.py:532
  48.3 1.1 hop.15
  49.4 0.7 collective-permute-start.11
  50.1 0.7 collective-permute-start.13
  50.8 1.3 %collective-permute-start.14 = (bf16[128,512]{1,0:T(8,128)(2,1)S(1)}, bf16[128,512]{1,0:T(8,128)(2,1)S(1)}, u32[]{:S(2)}, u32[]{:S(2)}) collective-permute-start(bf16[128,512]{1,0:T(8,128)(2,1)S(1)} %copy-done.16), channel_id=1, source_target_pairs={{24,16},{25,17},{26,18},{27,19},{28,20},{29,21},{30,22},{31,23}} | collective-permute-start | bytes 393224 | tf_op jit(solution)/shard_map/ppermute | solution.py:546
  52.1 15.6 %collective-permute-done.14 = bf16[128,512]{1,0:T(8,128)(2,1)S(1)} collective-permute-done((bf16[128,512]{1,0:T(8,128)(2,1)S(1)}, bf16[128,512]{1,0:T(8,128)(2,1)S(1)}, u32[]{:S(2)}, u32[]{:S(2)}) %collective-permute-start.14) | collective-permute-done | bytes 131104 | tf_op jit(solution)/shard_map/ppermute | solution.py:546
  67.8 1.1 end.4.delta_in
  68.9 1.2 %end.5.delta_hbm = bf16[4,256,1024]{2,1,0:T(8,128)(2,1)} custom-call(s32[1]{0:T(128)} %bitcast.flag_ref, bf16[256,1024]{1,0:T(8,128)(2,1)} %collective-permute-done.7.came, bf16[4,256,1024]{2,1,0:T(8,128)(2,1)} %end.4.delta_in, bf16[1024,1024]{1,0:T(8,128)(2,1)} %bitcast.50, bf16[4,256,1024]{2,1,0:T(8,128)(2,1)} %bitcast.43), custom_call_target="tpu_custom_call", output_to_operand_aliasing={{}: (2, {})} | custom-call | flops 1024 | bytes 1024 | tf_op jit(solution)/shard_map/end/pallas_call | solution.py:319
  70.6 0.6 copy-done.5
  71.3 3.2 %early.1 = (f32[512,512]{1,0:T(8,128)S(1)}, f32[512,512]{1,0:T(8,128)S(1)}, f32[512,512]{1,0:T(8,128)S(1)}, f32[512,512]{1,0:T(8,128)S(1)}) custom-call(bf16[1024,1024]{1,0:T(8,128)(2,1)S(1)} %copy-done.4, bf16[1024,1024]{1,0:T(8,128)(2,1)S(1)} %copy-done.5, bf16[4,256,1024]{2,1,0:T(8,128)(2,1)} %end.5.delta_hbm), custom_call_target="tpu_custom_call" | custom-call | flops 1024 | bytes 1024 | tf_op jit(solution)/shard_map/early/pallas_call | solution.py:407
  74.5 2.7 %weight.3 = (bf16[512,512]{1,0:T(8,128)(2,1)}, bf16[576,512]{1,0:T(8,128)(2,1)}) custom-call(s32[1]{0:T(128)} %bitcast.flag_ref, bf16[1024,1024]{1,0:T(8,128)(2,1)S(1)} %copy-done.4, bf16[1024,1024]{1,0:T(8,128)(2,1)S(1)} %copy-done.5, bf16[4,256,1024]{2,1,0:T(8,128)(2,1)} %end.5.delta_hbm, bf16[256,1024]{1,0:T(8,128)(2,1)S(1)} %collective-permute-done.11.came, ...), custom_call_target="tpu_custom_call" | custom-call | flops 1024 | bytes 1024 | tf_op jit(solution)/shard_map/weight/pallas_call | solution.py:467
  77.3 0.6 collective-permute-start.15
  77.8 1.6 %collective-permute-start.18 = (bf16[576,512]{1,0:T(8,128)(2,1)}, bf16[576,512]{1,0:T(8,128)(2,1)S(1)}, u32[]{:S(2)}, u32[]{:S(2)}) collective-permute-start(bf16[576,512]{1,0:T(8,128)(2,1)} %get-tuple-element.95), channel_id=1, source_target_pairs={{0,2},{1,3},{2,0},{3,1},{4,6},{5,7},{6,4},{7,5},{8,10},{9,11},{10,... | collective-permute-start | bytes 1769480 | tf_op jit(solution)/shard_map/ppermute | solution.py:492
  79.4 1.6 %copy-done.6 = bf16[1024,1024]{1,0:T(8,128)(2,1)S(1)} copy-done((bf16[1024,1024]{1,0:T(8,128)(2,1)S(1)}, bf16[1024,1024]{1,0:T(8,128)(2,1)}, u32[]{:S(2)}) %copy-start.6) | copy-done | bytes 2097176
  81.0 1.2 %copy-done.10 = f32[512,512]{1,0:T(8,128)S(1)} copy-done((f32[512,512]{1,0:T(8,128)S(1)}, f32[512,512]{1,0:T(8,128)}, u32[]{:S(2)}) %copy-start.10) | copy-done | bytes 1048600
  82.2 1.2 %copy-done.12 = f32[512,512]{1,0:T(8,128)S(1)} copy-done((f32[512,512]{1,0:T(8,128)S(1)}, f32[512,512]{1,0:T(8,128)}, u32[]{:S(2)}) %copy-start.12) | copy-done | bytes 1048600
  83.4 1.5 %weight.2 = (f32[512,512]{1,0:T(8,128)S(1)}, f32[576,512]{1,0:T(8,128)S(1)}) custom-call(s32[1]{0:T(128)} %bitcast.flag_ref, bf16[1024,1024]{1,0:T(8,128)(2,1)S(1)} %copy-done.4, bf16[1024,1024]{1,0:T(8,128)(2,1)S(1)} %copy-done.6, bf16[4,256,1024]{2,1,0:T(8,128)(2,1)} %end.5.delta_hbm, bf16[256,1024]{1,0:T(8,128)(2,1)S(1)} %collective-permute-done.11.came, ...), custom_call_target="tpu_custom_call" | custom-call | flops 1024 | bytes 1024 | tf_op jit(solution)/shard_map/weight/pallas_call | solution.py:467
  84.9 6.7 %collective-permute-done.15 = bf16[512,512]{1,0:T(8,128)(2,1)} collective-permute-done((bf16[512,512]{1,0:T(8,128)(2,1)}, bf16[512,512]{1,0:T(8,128)(2,1)}, u32[]{:S(2)}, u32[]{:S(2)}) %collective-permute-start.15) | collective-permute-done | bytes 524320 | tf_op jit(solution)/shard_map/ppermute | solution.py:492
  91.6 1.2 %fusion.1 = (bf16[256,512]{1,0:T(8,128)(2,1)S(1)}, f32[1,256,512]{2,1,0:T(8,128)S(1)}) fusion(f32[2,256,512]{2,1,0:T(8,128)S(1)} %bitcast.63, s32[]{:T(128)S(6)} %select_n.48, bf16[2,256,512]{2,1,0:T(8,128)(2,1)} %bitcast.10, s32[]{:T(128)S(6)} %select_n.46), kind=kLoop, calls=%fused_computation.8 | loop fusion | flops 655360 | bytes 2359304 | tf_op jit(solution)/shard_map/convert_element_type | solution.py:487
  92.8 1.6 %collective-permute-start.16 = (bf16[256,512]{1,0:T(8,128)(2,1)S(1)}, bf16[256,512]{1,0:T(8,128)(2,1)S(1)}, u32[]{:S(2)}, u32[]{:S(2)}) collective-permute-start(bf16[256,512]{1,0:T(8,128)(2,1)S(1)} %get-tuple-element.98), channel_id=1, source_target_pairs={{0,2},{1,3},{2,0},{3,1},{4,6},{5,7},{6,4},{7,5},{8,10},{9,11},{10,... | collective-permute-start | bytes 786440 | tf_op jit(solution)/shard_map/ppermute | solution.py:492
  95.2 5.2 %collective-permute-done.16 = bf16[256,512]{1,0:T(8,128)(2,1)S(1)} collective-permute-done((bf16[256,512]{1,0:T(8,128)(2,1)S(1)}, bf16[256,512]{1,0:T(8,128)(2,1)S(1)}, u32[]{:S(2)}, u32[]{:S(2)}) %collective-permute-start.16) | collective-permute-done | bytes 262176 | tf_op jit(solution)/shard_map/ppermute | solution.py:492
  100.5 2.7 %collective-permute-start.17 = (bf16[128,512]{1,0:T(8,128)(2,1)S(1)}, bf16[128,512]{1,0:T(8,128)(2,1)S(1)}, u32[]{:S(2)}, u32[]{:S(2)}) collective-permute-start(bf16[128,512]{1,0:T(8,128)(2,1)S(1)} %fusion.3), channel_id=1, source_target_pairs={{0,4},{1,5},{2,6},{3,7},{4,0},{5,1},{6,2},{7,3},{8,12},{9,13},{10,... | collective-permute-start | bytes 393224 | tf_op jit(solution)/shard_map/ppermute | solution.py:492
  103.2 2.2 %collective-permute-start.20 = (bf16[144,512]{1,0:T(8,128)(2,1)S(1)}, bf16[144,512]{1,0:T(8,128)(2,1)S(1)}, u32[]{:S(2)}, u32[]{:S(2)}) collective-permute-start(bf16[144,512]{1,0:T(8,128)(2,1)S(1)} %fusion.2), channel_id=1, source_target_pairs={{0,4},{1,5},{2,6},{3,7},{4,0},{5,1},{6,2},{7,3},{8,12},{9,13},{10,... | collective-permute-start | bytes 442376 | tf_op jit(solution)/shard_map/ppermute | solution.py:492
  105.3 7.1 %collective-permute-done.17 = bf16[128,512]{1,0:T(8,128)(2,1)S(1)} collective-permute-done((bf16[128,512]{1,0:T(8,128)(2,1)S(1)}, bf16[128,512]{1,0:T(8,128)(2,1)S(1)}, u32[]{:S(2)}, u32[]{:S(2)}) %collective-permute-start.17) | collective-permute-done | bytes 131104 | tf_op jit(solution)/shard_map/ppermute | solution.py:492
  112.5 1.9 %collective-permute-done.20 = bf16[144,512]{1,0:T(8,128)(2,1)S(1)} collective-permute-done((bf16[144,512]{1,0:T(8,128)(2,1)S(1)}, bf16[144,512]{1,0:T(8,128)(2,1)S(1)}, u32[]{:S(2)}, u32[]{:S(2)}) %collective-permute-start.20) | collective-permute-done | bytes 147488 | tf_op jit(solution)/shard_map/ppermute | solution.py:492
  114.4 0.6 slice.9
  115.1 0.8 maximum_bitcast_fusion
  (60 shorter events, 2.1 us)
Async XLA Ops:
  0.6 9.0 %copy-start = (bf16[1,4,256,1024]{3,2,1,0:T(8,128)(2,1)S(1)}, bf16[1,4,256,1024]{3,2,1,0:T(8,128)(2,1)}, u32[]{:S(2)}) copy-start(bf16[1,4,256,1024]{3,2,1,0:T(8,128)(2,1)} %param.6) | copy-start | bytes 6291460
  0.7 9.0 %copy-start.1 = (bf16[1,1024,1024]{2,1,0:T(8,128)(2,1)S(1)}, bf16[1,1024,1024]{2,1,0:T(8,128)(2,1)}, u32[]{:S(2)}) copy-start(bf16[1,1024,1024]{2,1,0:T(8,128)(2,1)} %param.7) | copy-start | bytes 6291460
  0.7 9.0 %copy-start.7 = (bf16[128,2048]{1,0:T(8,128)(2,1)S(1)}, bf16[128,2048]{1,0:T(8,128)(2,1)}, u32[]{:S(2)}) copy-start(bf16[128,2048]{1,0:T(8,128)(2,1)} %table_hbm.1) | copy-start | bytes 1572868
  8.3 5.7 %collective-permute-start.3 = (bf16[256,1024]{1,0:T(8,128)(2,1)}, bf16[256,1024]{1,0:T(8,128)(2,1)S(1)}, u32[]{:S(2)}, u32[]{:S(2)}) collective-permute-start(bf16[256,1024]{1,0:T(8,128)(2,1)} %get-tuple-element.55), channel_id=1, source_target_pairs={{24,16},{25,17},{26,18},{27,19},{28,20},{29,21},{30,22},{31,23}} | collective-permute-start | bytes 1572872 | tf_op jit(solution)/shard_map/ppermute | solution.py:532
  9.8 9.9 %collective-permute-start.2 = (bf16[256,1024]{1,0:T(8,128)(2,1)}, bf16[256,1024]{1,0:T(8,128)(2,1)}, u32[]{:S(2)}, u32[]{:S(2)}) collective-permute-start(bf16[256,1024]{1,0:T(8,128)(2,1)} %get-tuple-element.54), channel_id=1, source_target_pairs={{24,16},{25,17},{26,18},{27,19},{28,20},{29,21},{30,22},{31,23}} | collective-permute-start | bytes 1572872 | tf_op jit(solution)/shard_map/ppermute | solution.py:532
  11.3 14.0 %collective-permute-start.1 = (bf16[256,1024]{1,0:T(8,128)(2,1)}, bf16[256,1024]{1,0:T(8,128)(2,1)}, u32[]{:S(2)}, u32[]{:S(2)}) collective-permute-start(bf16[256,1024]{1,0:T(8,128)(2,1)} %get-tuple-element.53), channel_id=1, source_target_pairs={{24,16},{25,17},{26,18},{27,19},{28,20},{29,21},{30,22},{31,23}} | collective-permute-start | bytes 1572872 | tf_op jit(solution)/shard_map/ppermute | solution.py:532
  12.8 18.4 %collective-permute-start = (bf16[256,1024]{1,0:T(8,128)(2,1)}, bf16[256,1024]{1,0:T(8,128)(2,1)S(1)}, u32[]{:S(2)}, u32[]{:S(2)}) collective-permute-start(bf16[256,1024]{1,0:T(8,128)(2,1)} %get-tuple-element.52), channel_id=1, source_target_pairs={{24,16},{25,17},{26,18},{27,19},{28,20},{29,21},{30,22},{31,23}} | collective-permute-start | bytes 1572872 | tf_op jit(solution)/shard_map/ppermute | solution.py:532
  14.1 1.6 %copy-start.2 = (bf16[1,1024,1024]{2,1,0:T(8,128)(2,1)S(1)}, bf16[1,1024,1024]{2,1,0:T(8,128)(2,1)}, u32[]{:S(2)}) copy-start(bf16[1,1024,1024]{2,1,0:T(8,128)(2,1)} %param.7) | copy-start | bytes 6291460
  18.3 24.1 %collective-permute-start.6 = (bf16[256,1024]{1,0:T(8,128)(2,1)}, bf16[256,1024]{1,0:T(8,128)(2,1)S(1)}, u32[]{:S(2)}, u32[]{:S(2)}) collective-permute-start(bf16[256,1024]{1,0:T(8,128)(2,1)} %get-tuple-element.65), channel_id=1, source_target_pairs={{16,8},{17,9},{18,10},{19,11},{20,12},{21,13},{22,14},{23,15}} | collective-permute-start | bytes 1572872 | tf_op jit(solution)/shard_map/ppermute | solution.py:532
  23.3 19.9 %collective-permute-start.5 = (bf16[256,1024]{1,0:T(8,128)(2,1)}, bf16[256,1024]{1,0:T(8,128)(2,1)}, u32[]{:S(2)}, u32[]{:S(2)}) collective-permute-start(bf16[256,1024]{1,0:T(8,128)(2,1)} %get-tuple-element.64), channel_id=1, source_target_pairs={{16,8},{17,9},{18,10},{19,11},{20,12},{21,13},{22,14},{23,15}} | collective-permute-start | bytes 1572872 | tf_op jit(solution)/shard_map/ppermute | solution.py:532
  29.1 16.6 %collective-permute-start.4 = (bf16[256,1024]{1,0:T(8,128)(2,1)}, bf16[256,1024]{1,0:T(8,128)(2,1)}, u32[]{:S(2)}, u32[]{:S(2)}) collective-permute-start(bf16[256,1024]{1,0:T(8,128)(2,1)} %get-tuple-element.63), channel_id=1, source_target_pairs={{16,8},{17,9},{18,10},{19,11},{20,12},{21,13},{22,14},{23,15}} | collective-permute-start | bytes 1572872 | tf_op jit(solution)/shard_map/ppermute | solution.py:532
  31.2 4.8 %copy-start.13 = (bf16[4,1,1024]{2,0,1:T(4,128)(2,1)S(1)}, bf16[4,1,1024]{2,0,1:T(4,128)(2,1)}, u32[]{:S(2)}) copy-start(bf16[4,1,1024]{2,0,1:T(4,128)(2,1)} %param.11) | copy-start | bytes 24580
  31.2 4.8 %copy-start.14 = (s32[4,1,64]{2,1,0:T(1,128)S(1)}, s32[4,1,64]{2,1,0:T(1,128)}, u32[]{:S(2)}) copy-start(s32[4,1,64]{2,1,0:T(1,128)} %index_ref.1) | copy-start | bytes 3076
  33.9 14.3 %collective-permute-start.10 = (bf16[256,1024]{1,0:T(8,128)(2,1)}, bf16[256,1024]{1,0:T(8,128)(2,1)}, u32[]{:S(2)}, u32[]{:S(2)}) collective-permute-start(bf16[256,1024]{1,0:T(8,128)(2,1)} %get-tuple-element.60.after_hbm), channel_id=1, source_target_pairs={{16,8},{17,9},{18,10},{19,11},{20,12},{21,13},{22,14},{23,15}} | collective-permute-start | bytes 1572872 | tf_op jit(solution)/shard_map/ppermute | solution.py:532
  36.0 2.0 %copy-start.8 = (bf16[256,1024]{1,0:T(8,128)(2,1)S(1)}, bf16[256,1024]{1,0:T(8,128)(2,1)}, u32[]{:S(2)}) copy-start(bf16[256,1024]{1,0:T(8,128)(2,1)} %get-tuple-element.60.after_hbm) | copy-start | bytes 1572868
  37.1 5.2 %copy-start.3 = (bf16[1,1024,1024]{2,1,0:T(8,128)(2,1)S(1)}, bf16[1,1024,1024]{2,1,0:T(8,128)(2,1)}, u32[]{:S(2)}) copy-start(bf16[1,1024,1024]{2,1,0:T(8,128)(2,1)} %param.7) | copy-start | bytes 6291460
  37.2 12.9 %collective-permute-start.12 = (bf16[128,512]{1,0:T(8,128)(2,1)}, bf16[128,512]{1,0:T(8,128)(2,1)S(1)}, u32[]{:S(2)}, u32[]{:S(2)}) collective-permute-start(bf16[128,512]{1,0:T(8,128)(2,1)} %get-tuple-element.87), channel_id=1, source_target_pairs={{24,0},{25,1},{26,2},{27,3},{28,4},{29,5},{30,6},{31,7}} | collective-permute-start | bytes 393224 | tf_op jit(solution)/shard_map/ppermute | solution.py:546
  42.4 25.3 %collective-permute-start.9 = (bf16[256,1024]{1,0:T(8,128)(2,1)}, bf16[256,1024]{1,0:T(8,128)(2,1)S(1)}, u32[]{:S(2)}, u32[]{:S(2)}) collective-permute-start(bf16[256,1024]{1,0:T(8,128)(2,1)} %get-tuple-element.72), channel_id=1, source_target_pairs={{8,0},{9,1},{10,2},{11,3},{12,4},{13,5},{14,6},{15,7}} | collective-permute-start | bytes 1572872 | tf_op jit(solution)/shard_map/ppermute | solution.py:532
  44.2 23.6 %collective-permute-start.8 = (bf16[256,1024]{1,0:T(8,128)(2,1)}, bf16[256,1024]{1,0:T(8,128)(2,1)}, u32[]{:S(2)}, u32[]{:S(2)}) collective-permute-start(bf16[256,1024]{1,0:T(8,128)(2,1)} %get-tuple-element.71), channel_id=1, source_target_pairs={{8,0},{9,1},{10,2},{11,3},{12,4},{13,5},{14,6},{15,7}} | collective-permute-start | bytes 1572872 | tf_op jit(solution)/shard_map/ppermute | solution.py:532
  46.8 22.1 %collective-permute-start.7 = (bf16[256,1024]{1,0:T(8,128)(2,1)}, bf16[256,1024]{1,0:T(8,128)(2,1)}, u32[]{:S(2)}, u32[]{:S(2)}) collective-permute-start(bf16[256,1024]{1,0:T(8,128)(2,1)} %get-tuple-element.70), channel_id=1, source_target_pairs={{8,0},{9,1},{10,2},{11,3},{12,4},{13,5},{14,6},{15,7}} | collective-permute-start | bytes 1572872 | tf_op jit(solution)/shard_map/ppermute | solution.py:532
  48.2 1.9 %copy-start.17 = (bf16[128,512]{1,0:T(8,128)(2,1)S(1)}, bf16[128,512]{1,0:T(8,128)(2,1)}, u32[]{:S(2)}) copy-start(bf16[128,512]{1,0:T(8,128)(2,1)} %get-tuple-element.88) | copy-start | bytes 393220
  48.2 2.5 %copy-start.16 = (bf16[128,512]{1,0:T(8,128)(2,1)S(1)}, bf16[128,512]{1,0:T(8,128)(2,1)}, u32[]{:S(2)}) copy-start(bf16[128,512]{1,0:T(8,128)(2,1)} %get-tuple-element.89) | copy-start | bytes 393220
  48.2 19.5 %copy-start.15 = (bf16[128,512]{1,0:T(8,128)(2,1)S(1)}, bf16[128,512]{1,0:T(8,128)(2,1)}, u32[]{:S(2)}) copy-start(bf16[128,512]{1,0:T(8,128)(2,1)} %get-tuple-element.86) | copy-start | bytes 393220
  49.4 25.1 %collective-permute-start.11 = (bf16[256,1024]{1,0:T(8,128)(2,1)}, bf16[256,1024]{1,0:T(8,128)(2,1)S(1)}, u32[]{:S(2)}, u32[]{:S(2)}) collective-permute-start(bf16[256,1024]{1,0:T(8,128)(2,1)} %get-tuple-element.75), channel_id=1, source_target_pairs={{8,0},{9,1},{10,2},{11,3},{12,4},{13,5},{14,6},{15,7}} | collective-permute-start | bytes 1572872 | tf_op jit(solution)/shard_map/ppermute | solution.py:532
  50.1 0.7 collective-permute-start.13
  50.8 16.9 %collective-permute-start.14 = (bf16[128,512]{1,0:T(8,128)(2,1)S(1)}, bf16[128,512]{1,0:T(8,128)(2,1)S(1)}, u32[]{:S(2)}, u32[]{:S(2)}) collective-permute-start(bf16[128,512]{1,0:T(8,128)(2,1)S(1)} %copy-done.16), channel_id=1, source_target_pairs={{24,16},{25,17},{26,18},{27,19},{28,20},{29,21},{30,22},{31,23}} | collective-permute-start | bytes 393224 | tf_op jit(solution)/shard_map/ppermute | solution.py:546
  68.9 1.7 %copy-start.4 = (bf16[1024,1024]{1,0:T(8,128)(2,1)S(1)}, bf16[1024,1024]{1,0:T(8,128)(2,1)}, u32[]{:S(2)}) copy-start(bf16[1024,1024]{1,0:T(8,128)(2,1)} %get-tuple-element.61.turned_first) | copy-start | bytes 6291460
  68.9 2.4 %copy-start.5 = (bf16[1024,1024]{1,0:T(8,128)(2,1)S(1)}, bf16[1024,1024]{1,0:T(8,128)(2,1)}, u32[]{:S(2)}) copy-start(bf16[1024,1024]{1,0:T(8,128)(2,1)} %get-tuple-element.62.turned_second) | copy-start | bytes 6291460
  74.5 2.8 %copy-start.9 = (f32[512,512]{1,0:T(8,128)}, f32[512,512]{1,0:T(8,128)S(1)}, u32[]{:S(2)}) copy-start(f32[512,512]{1,0:T(8,128)S(1)} %get-tuple-element.76.early_first) | copy-start | bytes 3145732
  74.5 2.8 %copy-start.11 = (f32[512,512]{1,0:T(8,128)}, f32[512,512]{1,0:T(8,128)S(1)}, u32[]{:S(2)}) copy-start(f32[512,512]{1,0:T(8,128)S(1)} %get-tuple-element.77.early_second) | copy-start | bytes 3145732
  77.3 14.4 %collective-permute-start.15 = (bf16[512,512]{1,0:T(8,128)(2,1)}, bf16[512,512]{1,0:T(8,128)(2,1)}, u32[]{:S(2)}, u32[]{:S(2)}) collective-permute-start(bf16[512,512]{1,0:T(8,128)(2,1)} %get-tuple-element.93), channel_id=1, source_target_pairs={{0,1},{1,0},{2,3},{3,2},{4,5},{5,4},{6,7},{7,6},{8,9},{9,8},{10,11... | collective-permute-start | bytes 1572872 | tf_op jit(solution)/shard_map/ppermute | solution.py:492
  77.8 16.7 %collective-permute-start.18 = (bf16[576,512]{1,0:T(8,128)(2,1)}, bf16[576,512]{1,0:T(8,128)(2,1)S(1)}, u32[]{:S(2)}, u32[]{:S(2)}) collective-permute-start(bf16[576,512]{1,0:T(8,128)(2,1)} %get-tuple-element.95), channel_id=1, source_target_pairs={{0,2},{1,3},{2,0},{3,1},{4,6},{5,7},{6,4},{7,5},{8,10},{9,11},{10,... | collective-permute-start | bytes 1769480 | tf_op jit(solution)/shard_map/ppermute | solution.py:492
  79.4 1.6 %copy-start.6 = (bf16[1024,1024]{1,0:T(8,128)(2,1)S(1)}, bf16[1024,1024]{1,0:T(8,128)(2,1)}, u32[]{:S(2)}) copy-start(bf16[1024,1024]{1,0:T(8,128)(2,1)} %get-tuple-element.62.turned_second) | copy-start | bytes 6291460
  81.0 1.2 %copy-start.10 = (f32[512,512]{1,0:T(8,128)S(1)}, f32[512,512]{1,0:T(8,128)}, u32[]{:S(2)}) copy-start(f32[512,512]{1,0:T(8,128)} %copy-done.9) | copy-start | bytes 3145732
  82.2 1.2 %copy-start.12 = (f32[512,512]{1,0:T(8,128)S(1)}, f32[512,512]{1,0:T(8,128)}, u32[]{:S(2)}) copy-start(f32[512,512]{1,0:T(8,128)} %copy-done.11) | copy-start | bytes 3145732
  92.8 7.6 %collective-permute-start.16 = (bf16[256,512]{1,0:T(8,128)(2,1)S(1)}, bf16[256,512]{1,0:T(8,128)(2,1)S(1)}, u32[]{:S(2)}, u32[]{:S(2)}) collective-permute-start(bf16[256,512]{1,0:T(8,128)(2,1)S(1)} %get-tuple-element.98), channel_id=1, source_target_pairs={{0,2},{1,3},{2,0},{3,1},{4,6},{5,7},{6,4},{7,5},{8,10},{9,11},{10,... | collective-permute-start | bytes 786440 | tf_op jit(solution)/shard_map/ppermute | solution.py:492
  94.6 8.5 %collective-permute-start.19 = (bf16[288,512]{1,0:T(8,128)(2,1)S(1)}, bf16[288,512]{1,0:T(8,128)(2,1)S(1)}, u32[]{:S(2)}, u32[]{:S(2)}) collective-permute-start(bf16[288,512]{1,0:T(8,128)(2,1)S(1)} %get-tuple-element.96), channel_id=1, source_target_pairs={{0,1},{1,0},{2,3},{3,2},{4,5},{5,4},{6,7},{7,6},{8,9},{9,8},{10,11... | collective-permute-start | bytes 884744 | tf_op jit(solution)/shard_map/ppermute | solution.py:492
  100.5 12.0 %collective-permute-start.17 = (bf16[128,512]{1,0:T(8,128)(2,1)S(1)}, bf16[128,512]{1,0:T(8,128)(2,1)S(1)}, u32[]{:S(2)}, u32[]{:S(2)}) collective-permute-start(bf16[128,512]{1,0:T(8,128)(2,1)S(1)} %fusion.3), channel_id=1, source_target_pairs={{0,4},{1,5},{2,6},{3,7},{4,0},{5,1},{6,2},{7,3},{8,12},{9,13},{10,... | collective-permute-start | bytes 393224 | tf_op jit(solution)/shard_map/ppermute | solution.py:492
  103.2 11.2 %collective-permute-start.20 = (bf16[144,512]{1,0:T(8,128)(2,1)S(1)}, bf16[144,512]{1,0:T(8,128)(2,1)S(1)}, u32[]{:S(2)}, u32[]{:S(2)}) collective-permute-start(bf16[144,512]{1,0:T(8,128)(2,1)S(1)} %fusion.2), channel_id=1, source_target_pairs={{0,4},{1,5},{2,6},{3,7},{4,0},{5,1},{6,2},{7,3},{8,12},{9,13},{10,... | collective-permute-start | bytes 442376 | tf_op jit(solution)/shard_map/ppermute | solution.py:492

commit v3 on v2

--- a/solution.py
+++ b/solution.py
@@ -46,6 +46,10 @@
     return pltpu.with_memory_space_constraint(array, pltpu.HBM)
 
 
+def near(array):
+    return pltpu.with_memory_space_constraint(array, pltpu.VMEM)
+
+
 def own_heads(width):
     shift = HEAD.bit_length() - 1
     row = lax.broadcasted_iota(jnp.int32, (PAIR, width), 0) >> shift
@@ -54,8 +58,8 @@
 
 def first_kernel(
     m, flag_ref, count_hbm, acts_in, weight_in, table_in, index_hbm, pooled_hbm, delta_in,
-    grad_hbm, delta_hbm, share_hbm, high_hbm,
-    count_ref, acts_buf, weight_buf, table_buf, index_ref, pooled_ref, grad, aux, share_ref, high_ref, sems,
+    grad_hbm, delta_hbm, share_hbm, slant_hbm, high_hbm,
+    count_ref, acts_buf, weight_buf, table_buf, index_ref, pooled_ref, grad, aux, share_ref, slant_ref, high_ref, sems,
 ):
     micros, rows, width = acts_in.shape
     table_rows = table_in.shape[0]
@@ -135,8 +139,10 @@
         for j, here in enumerate(pair):
             share, slant = soften(scores[j], dot(values[:, here], given[:, here], NT), allowed)
             share_ref[here] = share
+            slant_ref[here] = slant
             slants.append(slant)
         store_share = copy(share_ref, share_hbm, 7)
+        store_slant = copy(slant_ref, slant_hbm, 10)
         totals = []
         for j, here in enumerate(pair):
             part = slice(j * PAIR % TILE, j * PAIR % TILE + PAIR)
@@ -150,6 +156,7 @@
         store_grad = copy(grad, grad_hbm, 9)
         store_high.wait()
         store_share.wait()
+        store_slant.wait()
         store_aux.wait()
         store_grad.wait()
 
@@ -175,9 +182,9 @@
     small = pltpu.VMEM((8, 128), BF16)
     return pl.pallas_call(
         functools.partial(first_kernel, m),
-        out_shape=(block, pltpu.HBM(acts.shape, BF16), pltpu.HBM(turned, BF16), block),
+        out_shape=(block, pltpu.HBM(acts.shape, BF16), pltpu.HBM(turned, BF16), pltpu.HBM(turned, BF16), block),
         in_specs=[SMEM, HBM, big, big, big, HBM, HBM, HBM],
-        out_specs=(HBM,) * 4,
+        out_specs=(HBM,) * 5,
         scratch_shapes=[
             pltpu.SMEM(count.shape, jnp.int32),
             pltpu.VMEM(acts.shape, BF16) if m == 0 else small,
@@ -188,8 +195,9 @@
             pltpu.VMEM((rows, width), BF16),
             pltpu.VMEM((micros if m == 0 else 1, rows, width), BF16),
             pltpu.VMEM(turned, BF16),
+            pltpu.VMEM(turned, BF16),
             pltpu.VMEM((rows, width), BF16),
-            pltpu.SemaphoreType.DMA((max(10, 1 + 2 * micros),)),
+            pltpu.SemaphoreType.DMA((max(11, 1 + 2 * micros),)),
         ],
         input_output_aliases={} if m == 0 else {7: 1},
         compiler_params=pltpu.CompilerParams(vmem_limit_bytes=28 * MIB),
@@ -205,23 +213,19 @@
     )
 
 
-def table_kernel(replicas, flag_ref, number_ref, index_ref, pooled_ref, table_hbm, after_hbm, *refs):
-    table, share, high, kv, sems = refs[-5:]
-    count = share.shape[0]
-    sources, outs = refs[: 2 * count], refs[2 * count : -5]
-    width = high.shape[2]
-    rows = high.shape[1]
-    table_rows = table.shape[0]
-    span = 2 * width // len(outs)
+def table_kernel(replicas, flag_ref, number_ref, index_ref, pooled_ref, after_hbm, *refs):
+    share, slant, high, kv, sems = refs[-5:]
+    count, rows, width = high.shape
+    sources, outs = refs[: 3 * count], refs[3 * count : -5]
+    span, table_rows = outs[0].shape[1], outs[0].shape[0]
     cands = index_ref.shape[2]
 
     @pl.when(flag_ref[0] == 1)
     def _():
         loads = []
         for m in range(count):
-            for k, target in enumerate((share, high)):
-                loads.append(pltpu.make_async_copy(sources[k * count + m], target.at[m], sems.at[2 * m + k]))
-        loads.append(pltpu.make_async_copy(table_hbm, table, sems.at[2 * count]))
+            for k, target in enumerate((share, slant, high)):
+                loads.append(pltpu.make_async_copy(sources[k * count + m], target.at[m], sems.at[3 * m + k]))
         for load in loads:
             load.start()
         bits = bit_orders(replicas)[1]
@@ -233,55 +237,54 @@
         for k, bit in enumerate(bits[1:]):
             row = row + (((block >> (len(bits) - 2 - k)) & 1) << bit)
         row = (row << shift) + (spot & ((1 << shift) - 1))
-        left_half = lax.broadcasted_iota(jnp.int32, (HEAD, PAIR), 1) < HEAD
-        own = own_heads(width)
-        loads[-1].wait()
-        onehots = []
+        head = lax.broadcasted_iota(jnp.int32, (cands, TILE), 1) >> (HEAD.bit_length() - 1)
+        ones = jnp.ones((rows, PAIR), BF16)
+        onehot = jnp.concatenate([(row == index_ref[m]).astype(BF16) for m in range(count)], axis=1)
+
+        def by_head(blocks):
+            chosen = blocks[0]
+            for k in range(1, len(blocks)):
+                chosen = jnp.where(head == k, blocks[k], chosen)
+            return chosen
+
         for m in range(count):
-            onehots.append((row == index_ref[m]).astype(BF16))
-            given = jnp.broadcast_to(pooled_ref[m : m + 1].astype(F32) * (1.0 / rows), (rows, width)).astype(BF16)
-            index = jnp.concatenate([index_ref[m], index_ref[m]], axis=1)
-            onehot = (lax.broadcasted_iota(jnp.int32, (table_rows, PAIR), 0) == index).astype(BF16)
-            values = jnp.where(own, dot(onehot, table[:, width:], TN), 0.0).astype(BF16)
-            for k in range(2):
-                loads[2 * m + k].wait()
-            for j in range(width // PAIR):
-                here = slice(j * PAIR, (j + 1) * PAIR)
-                slant = lean(
-                    share[m, here].astype(F32).reshape(2, HEAD, rows), dot(values[:, here], given[:, here], NT)
-                )
-                key = dot(slant, high[m, :, here], NN) * (1.0 / math.sqrt(HEAD))
-                value = dot(share[m, here], given[:, here], NN)
-                lines = slice(m * cands, (m + 1) * cands)
-                kv[lines, here] = jnp.where(left_half, key[:HEAD], key[HEAD:])
-                kv[lines, width + j * PAIR : width + (j + 1) * PAIR] = jnp.where(
-                    left_half, value[:HEAD], value[HEAD:]
-                )
-        onehot = jnp.concatenate(onehots, axis=1)
+            given = pooled_ref[m : m + 1].astype(F32) * (1.0 / rows)
+            lines = slice(m * cands, (m + 1) * cands)
+            for k in range(3):
+                loads[3 * m + k].wait()
+            column = dot(share[m], ones, NN)
+            column = jnp.concatenate([column, column], axis=1)
+            for q in range(width // TILE):
+                cols = slice(q * TILE, (q + 1) * TILE)
+                key = dot(slant[m, cols], high[m, :, cols], NN) * (1.0 / math.sqrt(HEAD))
+                starts = range(0, TILE, cands)
+                kv[lines, cols] = by_head([key[at : at + cands] for at in starts])
+                value = by_head([column[q * TILE + at : q * TILE + at + cands] for at in starts])
+                kv[lines, width + q * TILE : width + (q + 1) * TILE] = value * given[:, cols]
         for k, out in enumerate(outs):
             kv_high, kv_low = high_low(kv[:, k * span : (k + 1) * span])
             out[...] = (dot(onehot, kv_high, NN) + dot(onehot, kv_low, NN)).astype(BF16)
 
 
-def table_call(flag, number, index, pooled, table, after, shares, highs, sections, replicas):
+def table_call(flag, number, index, pooled, table_rows, after, shares, slants, highs, sections, replicas):
     rows, width = highs[0].shape
     count = len(highs)
     return pl.pallas_call(
         functools.partial(table_kernel, replicas),
-        out_shape=(pltpu.HBM((table.shape[0], 2 * width // sections), BF16),) * sections,
-        in_specs=[SMEM, SMEM, VMEM, VMEM, HBM, HBM] + [HBM] * (2 * count),
+        out_shape=(pltpu.HBM((table_rows, 2 * width // sections), BF16),) * sections,
+        in_specs=[SMEM, SMEM, VMEM, VMEM, HBM] + [HBM] * (3 * count),
         out_specs=(VMEM,) * sections,
         scratch_shapes=[
-            pltpu.VMEM(table.shape, BF16),
             pltpu.VMEM((count,) + shares[0].shape, BF16),
+            pltpu.VMEM((count,) + slants[0].shape, BF16),
             pltpu.VMEM((count,) + highs[0].shape, BF16),
             pltpu.VMEM((count * index.shape[2], 2 * width), F32),
-            pltpu.SemaphoreType.DMA((2 * count + 1,)),
+            pltpu.SemaphoreType.DMA((3 * count,)),
         ],
         compiler_params=pltpu.CompilerParams(vmem_limit_bytes=28 * MIB),
         cost_estimate=LIGHT,
         name="table",
-    )(flag, number, index, pooled, stay(table), stay(after), *map(stay, shares), *map(stay, highs))
+    )(flag, number, index, pooled, stay(after), *map(stay, shares), *map(stay, slants), *map(stay, highs))
 
 
 def hop_kernel(m, with_grad, flag_ref, came, delta_in, weight, after_hbm, *rest):
@@ -326,7 +329,7 @@
         compiler_params=pltpu.CompilerParams(vmem_limit_bytes=12 * MIB),
         cost_estimate=LIGHT,
         name="hop" if with_grad else "end",
-    )(flag, came, stay(delta), weight if with_grad else stay(weight), stay(after))
+    )(flag, near(came), stay(delta), weight if with_grad else stay(weight), stay(after))
 
 
 def bit_orders(replicas):
@@ -342,46 +345,41 @@
     return order
 
 
-def turn_kernel(replicas, number_ref, acts_hbm, after_hbm, *refs):
-    outs, token_ref = refs[:2], refs[2]
-    acts, turned, sems = refs[3:]
+def turn_kernel(acts_hbm, after_hbm, out, token_ref, acts, sems):
+    count, rows, width = acts.shape
     token_ref[...] = jnp.zeros_like(token_ref)
-    count, rows, width = acts.shape
-    size = width // replicas
     loads = [pltpu.make_async_copy(acts_hbm.at[m], acts.at[m], sems.at[m]) for m in range(count)]
     for load in loads:
         load.start()
     for m in range(count):
         loads[m].wait()
-        turned[...] = acts[m].T
-        for out, bits in zip(outs, bit_orders(replicas)):
-            order = block_order(bits)
-            mine = (number_ref[0] >> bits[0]) & 1
-            for i, block in enumerate(order + order):
-                bit = 1 - mine if i < len(order) else mine
-                source = pl.ds(pl.multiple_of((block + (bit << bits[0])) * size, size), size)
-                out[i * size : (i + 1) * size, m * rows : (m + 1) * rows] = turned[source]
-
-
-def turn_call(number, acts, after, replicas):
+        out[:, m * rows : (m + 1) * rows] = acts[m].T
+
+
+def turn_call(acts, after):
     count, rows, width = acts.shape
     return pl.pallas_call(
-        functools.partial(turn_kernel, replicas),
-        out_shape=(pltpu.HBM((width, count * rows), BF16),) * 2 + (pltpu.HBM((16, 128), BF16),),
-        in_specs=[SMEM, HBM, HBM],
-        out_specs=(VMEM,) * 3,
-        scratch_shapes=[
-            pltpu.VMEM(acts.shape, BF16),
-            pltpu.VMEM((width, rows), BF16),
-            pltpu.SemaphoreType.DMA((count,)),
-        ],
-        compiler_params=pltpu.CompilerParams(vmem_limit_bytes=24 * MIB),
+        turn_kernel,
+        out_shape=(jax.ShapeDtypeStruct((width, count * rows), BF16), pltpu.HBM((16, 128), BF16)),
+        in_specs=[HBM, HBM],
+        out_specs=(VMEM,) * 2,
+        scratch_shapes=[pltpu.VMEM(acts.shape, BF16), pltpu.SemaphoreType.DMA((count,))],
+        compiler_params=pltpu.CompilerParams(vmem_limit_bytes=20 * MIB),
         cost_estimate=LIGHT,
         name="turn",
-    )(number, stay(acts), after)
-
-
-def early_kernel(turned_first, turned_second, delta_hbm, *refs):
+    )(stay(acts), stay(after))
+
+
+def picked_rows(turned, number, bits, which, size, columns):
+    mine = (number >> bits[0]) & 1
+    base = (mine if which else 1 - mine) << bits[0]
+    return jnp.concatenate(
+        [turned[pl.ds(pl.multiple_of((base + block) * size, size), size), columns] for block in block_order(bits)],
+        axis=0,
+    )
+
+
+def early_kernel(replicas, number_ref, turned, delta_hbm, *refs):
     outs, (delta, sems) = refs[:4], refs[4:]
     micros, rows, width = delta.shape
     half = width // 2
@@ -391,23 +389,22 @@
     for load in loads:
         load.wait()
     flat = delta.reshape(micros * rows, width)
-    for c, turned in enumerate((turned_first, turned_second)):
+    for c, bits in enumerate(bit_orders(replicas)):
         for which in range(2):
+            left = picked_rows(turned, number_ref[0], bits, which, width // replicas, slice(0, micros * rows))
             for at in range(0, half, TILE):
                 outs[2 * c + which][:, at : at + TILE] = dot(
-                    turned[which * half : (which + 1) * half, : micros * rows],
-                    flat[:, c * half + at : c * half + at + TILE],
-                    NN,
+                    left, flat[:, c * half + at : c * half + at + TILE], NN
                 )
 
 
-def early_call(turned, delta):
+def early_call(number, turned, delta, replicas):
     micros, rows, width = delta.shape
     half = jax.ShapeDtypeStruct((width // 2, width // 2), F32)
     return pl.pallas_call(
-        early_kernel,
+        functools.partial(early_kernel, replicas),
         out_shape=(half,) * 4,
-        in_specs=[VMEM, VMEM, HBM],
+        in_specs=[SMEM, VMEM, HBM],
         out_specs=(VMEM,) * 4,
         scratch_shapes=[
             pltpu.VMEM((micros - 1, rows, width), BF16),
@@ -416,11 +413,11 @@
         compiler_params=pltpu.CompilerParams(vmem_limit_bytes=28 * MIB),
         cost_estimate=LIGHT,
         name="early",
-    )(*turned, stay(delta))
+    )(number, turned, stay(delta))
 
 
 def weight_kernel(
-    replicas, which, flag_ref, turned_first, turned_second, delta_hbm, came, early_first, early_second, table_ref, *refs
+    replicas, which, flag_ref, number_ref, turned, delta_hbm, came, early_first, early_second, table_ref, *refs
 ):
     outs, (delta, sem) = refs[:2], refs[2:]
     rows, width = delta.shape
@@ -443,11 +440,12 @@
     def _():
         delta[...] = (came[...].astype(F32) * delta[...].astype(F32)).astype(BF16)
 
-    for c, (turned, early) in enumerate(((turned_first, early_first), (turned_second, early_second))):
+    for c, (bits, early) in enumerate(zip(bit_orders(replicas), (early_first, early_second))):
+        left = picked_rows(turned, number_ref[0], bits, which, size, slice(last * rows, (last + 1) * rows))
         for at in range(0, half, TILE):
             cols = slice(at, at + TILE)
             product = early[:, cols] + dot(
-                turned[which * half : (which + 1) * half, last * rows :],
+                left,
                 delta[:, c * half + at : c * half + at + TILE],
                 NN,
             )
@@ -459,7 +457,7 @@
                     outs[c][i * pitch : i * pitch + size, cols] = product[i * size : (i + 1) * size]
 
 
-def weight_call(which, flag, turned, delta, came, early, table, replicas):
+def weight_call(which, flag, number, turned, delta, came, early, table, replicas):
     micros, rows, width = delta.shape
     half = width // 2
     extra = max(16, table.shape[0] // replicas) * (replicas // 2)
@@ -467,13 +465,13 @@
     return pl.pallas_call(
         functools.partial(weight_kernel, replicas, which),
         out_shape=(array((half, half)), array((half + extra, half))),
-        in_specs=[SMEM, VMEM, VMEM, HBM] + [VMEM] * 4,
+        in_specs=[SMEM, SMEM, VMEM, HBM] + [VMEM] * 4,
         out_specs=(VMEM,) * 2,
         scratch_shapes=[pltpu.VMEM((rows, width), BF16), pltpu.SemaphoreType.DMA((1,))],
         compiler_params=pltpu.CompilerParams(vmem_limit_bytes=20 * MIB),
         cost_estimate=LIGHT,
         name="weight",
-    )(flag, *turned, stay(delta), came, *early, table)
+    )(flag, number, turned, stay(delta), near(came), *early, table)
 
 
 def own_half(keep, got, bit):
@@ -514,14 +512,15 @@
     count = cand_count.reshape(1, micro_count)
     pooled = pooled_cotangent.reshape(micro_count, model_width)
     final = flag(final_flag)
-    grads, shares, highs = [], [], []
+    grads, shares, slants, highs = [], [], [], []
     delta = acts
     for m in range(micro_count):
-        grad, delta, share, high = first_call(
+        grad, delta, share, slant, high = first_call(
             m, final, count, acts, weight, cand_table, cand_index, pooled, delta
         )
         grads.append(grad)
         shares.append(share)
+        slants.append(slant)
         highs.append(high)
 
     def pairs(bit):
@@ -539,17 +538,18 @@
                 (delta,) = hop_call(m, active, received[m], delta, weight, acts, False)
         if hop == 0:
             parts = table_call(
-                final, number, cand_index, pooled, cand_table, grads[-1], shares, highs, sections, replicas
+                final, number, cand_index, pooled, cand_table.shape[0], grads[-1], shares, slants, highs, sections,
+                replicas,
             )
-            *turned, token = turn_call(number, acts, grads[-1], replicas)
+            turned, token = turn_call(acts, grads[-1])
 
     spread = [lax.ppermute(parts[s], "section", [(last, s)]) for s in range(last)]
     table_part = jnp.where(final_flag, parts[last], sum(spread))
 
     orders = bit_orders(replicas)
-    early = early_call(turned, delta)
-    sends = weight_call(0, active, turned, delta, received[-1], early[::2], table_part, replicas)
-    keeps = weight_call(1, active, turned, delta, received[-1], early[1::2], table_part, replicas)
+    early = early_call(number, turned, delta, replicas)
+    sends = weight_call(0, active, number, turned, delta, received[-1], early[::2], table_part, replicas)
+    keeps = weight_call(1, active, number, turned, delta, received[-1], early[1::2], table_part, replicas)
     sums = [finish_scatter(sends[c], keeps[c], orders[c], "dp", pairs) for c in range(2)]
     size = model_width // replicas
     lines = cand_table.shape[0] // replicas

time: 117 us -> 107 us (0.915)
  the two profiles are of different devices: /device:TPU:6 before, /device:TPU:2 now
where the time goes in v3:
time: 107 us; the launch traced here: 106 us
  Pallas kernels  34.9 us (33%)
  starting transfers between devices  30.6 us (29%)
  waiting for transfers between devices  30.6 us (29%)
  local copies, waits for them, and re-layouts  6.49 us (6%)
  other arithmetic  2.35 us (2%)
  between operations  1.18 us (1%)
    ppermute x6, waiting for transfers between devices, finish_scatter(): got = lax.ppermute(send, axes, pairs_of(bit))  20.4 us
    ppermute x12, starting transfers between devices, body(): lax.ppermute(g, 'section', [(source, source - 1)])  16.6 us
    pallas_call x11, Pallas kernels, hop_call(): pl.pallas_call(functools.partial(hop_kernel, m, with_grad), out_shape=out...  16.2 us
    ppermute x6, starting transfers between devices, finish_scatter(): got = lax.ppermute(send, axes, pairs_of(bit))  11.3 us
    ppermute x3, waiting for transfers between devices, body(): lax.ppermute(parts[s], 'section', [(last, s)])  8.37 us
    pallas_call x4, Pallas kernels, first_call(): pl.pallas_call(functools.partial(first_kernel, m), out_shape=(block, pltp...  8.15 us
    unnamed x32, local copies, waits for them, and re-layouts  5.86 us
    pallas_call x2, Pallas kernels, weight_call(): pl.pallas_call(functools.partial(weight_kernel, replicas, which), out_sha...  4.25 us
  transfers between devices with their start and end apart: 21, of which 7 were waited for; matrix products, arithmetic and copies ran while one was open for 1% of the time, Pallas kernels for 23%

profile of v3, /device:TPU:2, one launch (start us, length us, event | category | flops | bytes accessed | tf_op | source)
XLA Modules:
  0.0 106.1 jit_solution(6699122118560083741)
XLA Ops:
  0.7 7.6 %first.4 = (bf16[256,1024]{1,0:T(8,128)(2,1)}, bf16[4,256,1024]{2,1,0:T(8,128)(2,1)}, bf16[1024,256]{1,0:T(8,128)(2,1)}, bf16[1024,256]{1,0:T(8,128)(2,1)}, bf16[256,1024]{1,0:T(8,128)(2,1)}) custom-call(s32[1]{0:T(128)} %bitcast.4.flag_ref, s32[1,4]{1,0:T(1,128)} %bitcast.78, bf16[4,256,1024]{2,1,0:T(8,128)(2,1)} %bitcast.31, bf16[1024,1024]{1,0:T(8,128)(2,1)} %bitcast.47, ...), custom_call_target="tpu_custom_call" | custom-call | flops 1024 | bytes 1024 | tf_op jit(solution)/shard_map/first/pallas_call | solution.py:183
  8.3 1.3 %collective-permute-start.3 = (bf16[256,1024]{1,0:T(8,128)(2,1)}, bf16[256,1024]{1,0:T(8,128)(2,1)S(1)}, u32[]{:S(2)}, u32[]{:S(2)}) collective-permute-start(bf16[256,1024]{1,0:T(8,128)(2,1)} %get-tuple-element.58), channel_id=1, source_target_pairs={{24,16},{25,17},{26,18},{27,19},{28,20},{29,21},{30,22},{31,23}} | collective-permute-start | bytes 1572872 | tf_op jit(solution)/shard_map/ppermute | solution.py:531
  9.8 1.3 %collective-permute-start.2 = (bf16[256,1024]{1,0:T(8,128)(2,1)}, bf16[256,1024]{1,0:T(8,128)(2,1)S(1)}, u32[]{:S(2)}, u32[]{:S(2)}) collective-permute-start(bf16[256,1024]{1,0:T(8,128)(2,1)} %get-tuple-element.57), channel_id=1, source_target_pairs={{24,16},{25,17},{26,18},{27,19},{28,20},{29,21},{30,22},{31,23}} | collective-permute-start | bytes 1572872 | tf_op jit(solution)/shard_map/ppermute | solution.py:531
  11.4 1.3 %collective-permute-start.1 = (bf16[256,1024]{1,0:T(8,128)(2,1)}, bf16[256,1024]{1,0:T(8,128)(2,1)}, u32[]{:S(2)}, u32[]{:S(2)}) collective-permute-start(bf16[256,1024]{1,0:T(8,128)(2,1)} %get-tuple-element.56), channel_id=1, source_target_pairs={{24,16},{25,17},{26,18},{27,19},{28,20},{29,21},{30,22},{31,23}} | collective-permute-start | bytes 1572872 | tf_op jit(solution)/shard_map/ppermute | solution.py:531
  12.8 1.3 %collective-permute-start = (bf16[256,1024]{1,0:T(8,128)(2,1)}, bf16[256,1024]{1,0:T(8,128)(2,1)S(1)}, u32[]{:S(2)}, u32[]{:S(2)}) collective-permute-start(bf16[256,1024]{1,0:T(8,128)(2,1)} %get-tuple-element.55), channel_id=1, source_target_pairs={{24,16},{25,17},{26,18},{27,19},{28,20},{29,21},{30,22},{31,23}} | collective-permute-start | bytes 1572872 | tf_op jit(solution)/shard_map/ppermute | solution.py:531
  14.1 1.6 %copy-done.2 = bf16[1,1024,1024]{2,1,0:T(8,128)(2,1)S(1)} copy-done((bf16[1,1024,1024]{2,1,0:T(8,128)(2,1)S(1)}, bf16[1,1024,1024]{2,1,0:T(8,128)(2,1)}, u32[]{:S(2)}) %copy-start.2) | copy-done | bytes 2097176
  15.7 2.6 %hop.8 = (bf16[256,1024]{1,0:T(8,128)(2,1)}, bf16[4,256,1024]{2,1,0:T(8,128)(2,1)}) custom-call(s32[1]{0:T(128)} %bitcast.3.flag_ref, bf16[256,1024]{1,0:T(8,128)(2,1)S(1)} %collective-permute-done.3.came, bf16[4,256,1024]{2,1,0:T(8,128)(2,1)} %get-tuple-element.59.delta_in, bf16[1024,1024]{1,0:T(8,128)(2,1)S(1)} %bitcast.54, ...), custom_call_target="tpu_custom_call", output_to_operand_aliasing={{1}: (2, {})} | custom-call | flops 1024 | bytes 1024 | tf_op jit(solution)/shard_map/hop/pallas_call | solution.py:322
  18.3 1.3 %collective-permute-start.6 = (bf16[256,1024]{1,0:T(8,128)(2,1)}, bf16[256,1024]{1,0:T(8,128)(2,1)S(1)}, u32[]{:S(2)}, u32[]{:S(2)}) collective-permute-start(bf16[256,1024]{1,0:T(8,128)(2,1)} %get-tuple-element.67), channel_id=1, source_target_pairs={{16,8},{17,9},{18,10},{19,11},{20,12},{21,13},{22,14},{23,15}} | collective-permute-start | bytes 1572872 | tf_op jit(solution)/shard_map/ppermute | solution.py:531
  19.7 2.6 %hop.9 = (bf16[256,1024]{1,0:T(8,128)(2,1)}, bf16[4,256,1024]{2,1,0:T(8,128)(2,1)}) custom-call(s32[1]{0:T(128)} %bitcast.3.flag_ref, bf16[256,1024]{1,0:T(8,128)(2,1)S(1)} %collective-permute-done.2.came, bf16[4,256,1024]{2,1,0:T(8,128)(2,1)} %get-tuple-element.60.delta_in, bf16[1024,1024]{1,0:T(8,128)(2,1)S(1)} %bitcast.55, ...), custom_call_target="tpu_custom_call", output_to_operand_aliasing={{1}: (2, {})} | custom-call | flops 1024 | bytes 1024 | tf_op jit(solution)/shard_map/hop/pallas_call | solution.py:322
  22.3 1.3 %collective-permute-start.5 = (bf16[256,1024]{1,0:T(8,128)(2,1)}, bf16[256,1024]{1,0:T(8,128)(2,1)S(1)}, u32[]{:S(2)}, u32[]{:S(2)}) collective-permute-start(bf16[256,1024]{1,0:T(8,128)(2,1)} %get-tuple-element.66), channel_id=1, source_target_pairs={{16,8},{17,9},{18,10},{19,11},{20,12},{21,13},{22,14},{23,15}} | collective-permute-start | bytes 1572872 | tf_op jit(solution)/shard_map/ppermute | solution.py:531
  23.6 0.9 collective-permute-done.1.came
  24.5 3.7 %hop.10 = (bf16[256,1024]{1,0:T(8,128)(2,1)}, bf16[4,256,1024]{2,1,0:T(8,128)(2,1)}) custom-call(s32[1]{0:T(128)} %bitcast.3.flag_ref, bf16[256,1024]{1,0:T(8,128)(2,1)} %collective-permute-done.1.came, bf16[4,256,1024]{2,1,0:T(8,128)(2,1)} %get-tuple-element.61.delta_in, bf16[1024,1024]{1,0:T(8,128)(2,1)S(1)} %bitcast.56, ...), custom_call_target="tpu_custom_call", output_to_operand_aliasing={{1}: (2, {})} | custom-call | flops 1024 | bytes 1024 | tf_op jit(solution)/shard_map/hop/pallas_call | solution.py:322
  28.2 2.1 %collective-permute-start.4 = (bf16[256,1024]{1,0:T(8,128)(2,1)}, bf16[256,1024]{1,0:T(8,128)(2,1)}, u32[]{:S(2)}, u32[]{:S(2)}) collective-permute-start(bf16[256,1024]{1,0:T(8,128)(2,1)} %get-tuple-element.65), channel_id=1, source_target_pairs={{16,8},{17,9},{18,10},{19,11},{20,12},{21,13},{22,14},{23,15}} | collective-permute-start | bytes 1572872 | tf_op jit(solution)/shard_map/ppermute | solution.py:531
  30.3 0.9 collective-permute-done.came
  31.2 2.7 %hop.11 = (bf16[256,1024]{1,0:T(8,128)(2,1)}, bf16[4,256,1024]{2,1,0:T(8,128)(2,1)}) custom-call(s32[1]{0:T(128)} %bitcast.3.flag_ref, bf16[256,1024]{1,0:T(8,128)(2,1)S(1)} %collective-permute-done.came, bf16[4,256,1024]{2,1,0:T(8,128)(2,1)} %get-tuple-element.62.delta_in, bf16[1024,1024]{1,0:T(8,128)(2,1)S(1)} %bitcast.57, ...), custom_call_target="tpu_custom_call", output_to_operand_aliasing={{1}: (2, {})} | custom-call | flops 1024 | bytes 1024 | tf_op jit(solution)/shard_map/hop/pallas_call | solution.py:322
  33.9 2.1 %collective-permute-start.10 = (bf16[256,1024]{1,0:T(8,128)(2,1)}, bf16[256,1024]{1,0:T(8,128)(2,1)}, u32[]{:S(2)}, u32[]{:S(2)}) collective-permute-start(bf16[256,1024]{1,0:T(8,128)(2,1)} %get-tuple-element.63.after_hbm), channel_id=1, source_target_pairs={{16,8},{17,9},{18,10},{19,11},{20,12},{21,13},{22,14},{23,15}} | collective-permute-start | bytes 1572872 | tf_op jit(solution)/shard_map/ppermute | solution.py:531
  36.0 0.9 table.1
  36.9 0.8 collective-permute-start.12
  37.7 2.3 %turn.1 = (bf16[1024,1024]{1,0:T(8,128)(2,1)S(1)}, bf16[16,128]{1,0:T(8,128)(2,1)}) custom-call(bf16[4,256,1024]{2,1,0:T(8,128)(2,1)} %bitcast.37, bf16[256,1024]{1,0:T(8,128)(2,1)} %get-tuple-element.63.after_hbm), custom_call_target="tpu_custom_call" | custom-call | flops 1024 | bytes 1024 | tf_op jit(solution)/shard_map/turn/pallas_call | solution.py:361
  40.1 1.3 %copy-done.4 = bf16[1024,1024]{1,0:T(8,128)(2,1)} copy-done((bf16[1024,1024]{1,0:T(8,128)(2,1)}, bf16[1024,1024]{1,0:T(8,128)(2,1)S(1)}, u32[]{:S(2)}) %copy-start.4) | copy-done | bytes 2097176
  41.3 0.9 collective-permute-start.9
  42.3 1.5 %collective-permute-start.8 = (bf16[256,1024]{1,0:T(8,128)(2,1)}, bf16[256,1024]{1,0:T(8,128)(2,1)}, u32[]{:S(2)}, u32[]{:S(2)}) collective-permute-start(bf16[256,1024]{1,0:T(8,128)(2,1)} %get-tuple-element.73), channel_id=1, source_target_pairs={{8,0},{9,1},{10,2},{11,3},{12,4},{13,5},{14,6},{15,7}} | collective-permute-start | bytes 1572872 | tf_op jit(solution)/shard_map/ppermute | solution.py:531
  43.8 1.1 %hop.14 = (bf16[256,1024]{1,0:T(8,128)(2,1)}, bf16[4,256,1024]{2,1,0:T(8,128)(2,1)}) custom-call(s32[1]{0:T(128)} %bitcast.8.flag_ref, bf16[256,1024]{1,0:T(8,128)(2,1)} %collective-permute-done.4.came, bf16[4,256,1024]{2,1,0:T(8,128)(2,1)} %get-tuple-element.71.delta_in, bf16[1024,1024]{1,0:T(8,128)(2,1)S(1)} %bitcast.60, ...), custom_call_target="tpu_custom_call", output_to_operand_aliasing={{1}: (2, {})} | custom-call | flops 1024 | bytes 1024 | tf_op jit(solution)/shard_map/hop/pallas_call | solution.py:322
  44.9 1.5 %collective-permute-start.7 = (bf16[256,1024]{1,0:T(8,128)(2,1)}, bf16[256,1024]{1,0:T(8,128)(2,1)}, u32[]{:S(2)}, u32[]{:S(2)}) collective-permute-start(bf16[256,1024]{1,0:T(8,128)(2,1)} %get-tuple-element.72), channel_id=1, source_target_pairs={{8,0},{9,1},{10,2},{11,3},{12,4},{13,5},{14,6},{15,7}} | collective-permute-start | bytes 1572872 | tf_op jit(solution)/shard_map/ppermute | solution.py:531
  46.4 1.1 %hop.15 = (bf16[256,1024]{1,0:T(8,128)(2,1)}, bf16[4,256,1024]{2,1,0:T(8,128)(2,1)}) custom-call(s32[1]{0:T(128)} %bitcast.8.flag_ref, bf16[256,1024]{1,0:T(8,128)(2,1)} %collective-permute-done.10.came, bf16[4,256,1024]{2,1,0:T(8,128)(2,1)} %get-tuple-element.75.delta_in, bf16[1024,1024]{1,0:T(8,128)(2,1)S(1)} %bitcast.61, ...), custom_call_target="tpu_custom_call", output_to_operand_aliasing={{1}: (2, {})} | custom-call | flops 1024 | bytes 1024 | tf_op jit(solution)/shard_map/hop/pallas_call | solution.py:322
  47.5 0.7 collective-permute-start.11
  48.2 0.7 collective-permute-start.13
  48.9 1.3 %collective-permute-start.14 = (bf16[128,512]{1,0:T(8,128)(2,1)S(1)}, bf16[128,512]{1,0:T(8,128)(2,1)S(1)}, u32[]{:S(2)}, u32[]{:S(2)}) collective-permute-start(bf16[128,512]{1,0:T(8,128)(2,1)S(1)} %copy-done.14), channel_id=1, source_target_pairs={{24,16},{25,17},{26,18},{27,19},{28,20},{29,21},{30,22},{31,23}} | collective-permute-start | bytes 393224 | tf_op jit(solution)/shard_map/ppermute | solution.py:546
  50.2 8.4 %collective-permute-done.14 = bf16[128,512]{1,0:T(8,128)(2,1)S(1)} collective-permute-done((bf16[128,512]{1,0:T(8,128)(2,1)S(1)}, bf16[128,512]{1,0:T(8,128)(2,1)S(1)}, u32[]{:S(2)}, u32[]{:S(2)}) %collective-permute-start.14) | collective-permute-done | bytes 131104 | tf_op jit(solution)/shard_map/ppermute | solution.py:546
  58.7 1.1 %end.4.delta_in = bf16[4,256,1024]{2,1,0:T(8,128)(2,1)} custom-call(s32[1]{0:T(128)} %bitcast.flag_ref, bf16[256,1024]{1,0:T(8,128)(2,1)} %collective-permute-done.8.came, bf16[4,256,1024]{2,1,0:T(8,128)(2,1)} %end.3.delta_in, bf16[1024,1024]{1,0:T(8,128)(2,1)} %bitcast.49, bf16[4,256,1024]{2,1,0:T(8,128)(2,1)} %bitcast.42), custom_call_target="tpu_custom_call", output_to_operand_aliasing={{}: (2, {})} | custom-call | flops 1024 | bytes 1024 | tf_op jit(solution)/shard_map/end/pallas_call | solution.py:322
  59.8 1.2 %end.5.delta_hbm = bf16[4,256,1024]{2,1,0:T(8,128)(2,1)} custom-call(s32[1]{0:T(128)} %bitcast.flag_ref, bf16[256,1024]{1,0:T(8,128)(2,1)} %collective-permute-done.7.came, bf16[4,256,1024]{2,1,0:T(8,128)(2,1)} %end.4.delta_in, bf16[1024,1024]{1,0:T(8,128)(2,1)} %bitcast.50, bf16[4,256,1024]{2,1,0:T(8,128)(2,1)} %bitcast.43), custom_call_target="tpu_custom_call", output_to_operand_aliasing={{}: (2, {})} | custom-call | flops 1024 | bytes 1024 | tf_op jit(solution)/shard_map/end/pallas_call | solution.py:322
  61.5 3.2 %early.1 = (f32[512,512]{1,0:T(8,128)S(1)}, f32[512,512]{1,0:T(8,128)S(1)}, f32[512,512]{1,0:T(8,128)S(1)}, f32[512,512]{1,0:T(8,128)S(1)}) custom-call(s32[1]{0:T(128)} %bitcast.1.number_ref, bf16[1024,1024]{1,0:T(8,128)(2,1)S(1)} %copy-done.5, bf16[4,256,1024]{2,1,0:T(8,128)(2,1)} %end.5.delta_hbm), custom_call_target="tpu_custom_call" | custom-call | flops 1024 | bytes 1024 | tf_op jit(solution)/shard_map/early/pallas_call | solution.py:404
  64.7 2.7 %weight.3 = (bf16[512,512]{1,0:T(8,128)(2,1)}, bf16[576,512]{1,0:T(8,128)(2,1)}) custom-call(s32[1]{0:T(128)} %bitcast.flag_ref, s32[1]{0:T(128)} %bitcast.1.number_ref, bf16[1024,1024]{1,0:T(8,128)(2,1)S(1)} %copy-done.5, bf16[4,256,1024]{2,1,0:T(8,128)(2,1)} %end.5.delta_hbm, bf16[256,1024]{1,0:T(8,128)(2,1)S(1)} %collective-permute-done.11.came, ...), custom_call_target="tpu_custom_call" | custom-call | flops 1024 | bytes 1024 | tf_op jit(solution)/shard_map/weight/pallas_call | solution.py:465
  67.5 1.6 %collective-permute-start.15 = (bf16[512,512]{1,0:T(8,128)(2,1)}, bf16[512,512]{1,0:T(8,128)(2,1)}, u32[]{:S(2)}, u32[]{:S(2)}) collective-permute-start(bf16[512,512]{1,0:T(8,128)(2,1)} %get-tuple-element.99), channel_id=1, source_target_pairs={{0,1},{1,0},{2,3},{3,2},{4,5},{5,4},{6,7},{7,6},{8,9},{9,8},{10,11... | collective-permute-start | bytes 1572872 | tf_op jit(solution)/shard_map/ppermute | solution.py:490
  69.1 1.6 %collective-permute-start.18 = (bf16[576,512]{1,0:T(8,128)(2,1)}, bf16[576,512]{1,0:T(8,128)(2,1)S(1)}, u32[]{:S(2)}, u32[]{:S(2)}) collective-permute-start(bf16[576,512]{1,0:T(8,128)(2,1)} %get-tuple-element.101), channel_id=1, source_target_pairs={{0,2},{1,3},{2,0},{3,1},{4,6},{5,7},{6,4},{7,5},{8,10},{9,11},{10,... | collective-permute-start | bytes 1769480 | tf_op jit(solution)/shard_map/ppermute | solution.py:490
  70.7 1.2 %copy-done.8 = f32[512,512]{1,0:T(8,128)S(1)} copy-done((f32[512,512]{1,0:T(8,128)S(1)}, f32[512,512]{1,0:T(8,128)}, u32[]{:S(2)}) %copy-start.8) | copy-done | bytes 1048600
  71.9 1.2 %copy-done.10 = f32[512,512]{1,0:T(8,128)S(1)} copy-done((f32[512,512]{1,0:T(8,128)S(1)}, f32[512,512]{1,0:T(8,128)}, u32[]{:S(2)}) %copy-start.10) | copy-done | bytes 1048600
  73.1 1.5 %weight.2 = (f32[512,512]{1,0:T(8,128)S(1)}, f32[576,512]{1,0:T(8,128)S(1)}) custom-call(s32[1]{0:T(128)} %bitcast.flag_ref, s32[1]{0:T(128)} %bitcast.1.number_ref, bf16[1024,1024]{1,0:T(8,128)(2,1)S(1)} %copy-done.5, bf16[4,256,1024]{2,1,0:T(8,128)(2,1)} %end.5.delta_hbm, bf16[256,1024]{1,0:T(8,128)(2,1)S(1)} %collective-permute-done.11.came, ...), custom_call_target="tpu_custom_call" | custom-call | flops 1024 | bytes 1024 | tf_op jit(solution)/shard_map/weight/pallas_call | solution.py:465
  74.6 7.2 %collective-permute-done.15 = bf16[512,512]{1,0:T(8,128)(2,1)} collective-permute-done((bf16[512,512]{1,0:T(8,128)(2,1)}, bf16[512,512]{1,0:T(8,128)(2,1)}, u32[]{:S(2)}, u32[]{:S(2)}) %collective-permute-start.15) | collective-permute-done | bytes 524320 | tf_op jit(solution)/shard_map/ppermute | solution.py:490
  81.9 1.2 %fusion.1 = (bf16[256,512]{1,0:T(8,128)(2,1)S(1)}, f32[1,256,512]{2,1,0:T(8,128)S(1)}) fusion(f32[2,256,512]{2,1,0:T(8,128)S(1)} %bitcast.63, s32[]{:T(128)S(6)} %select_n.48, bf16[2,256,512]{2,1,0:T(8,128)(2,1)} %bitcast.10, s32[]{:T(128)S(6)} %select_n.46), kind=kLoop, calls=%fused_computation.8 | loop fusion | flops 655360 | bytes 2359304 | tf_op jit(solution)/shard_map/convert_element_type | solution.py:485
  83.1 1.6 %collective-permute-start.16 = (bf16[256,512]{1,0:T(8,128)(2,1)S(1)}, bf16[256,512]{1,0:T(8,128)(2,1)S(1)}, u32[]{:S(2)}, u32[]{:S(2)}) collective-permute-start(bf16[256,512]{1,0:T(8,128)(2,1)S(1)} %get-tuple-element.104), channel_id=1, source_target_pairs={{0,2},{1,3},{2,0},{3,1},{4,6},{5,7},{6,4},{7,5},{8,10},{9,11},{10,... | collective-permute-start | bytes 786440 | tf_op jit(solution)/shard_map/ppermute | solution.py:490
  84.9 1.6 %collective-permute-start.19 = (bf16[288,512]{1,0:T(8,128)(2,1)S(1)}, bf16[288,512]{1,0:T(8,128)(2,1)S(1)}, u32[]{:S(2)}, u32[]{:S(2)}) collective-permute-start(bf16[288,512]{1,0:T(8,128)(2,1)S(1)} %get-tuple-element.102), channel_id=1, source_target_pairs={{0,1},{1,0},{2,3},{3,2},{4,5},{5,4},{6,7},{7,6},{8,9},{9,8},{10,11... | collective-permute-start | bytes 884744 | tf_op jit(solution)/shard_map/ppermute | solution.py:490
  86.5 4.2 %collective-permute-done.16 = bf16[256,512]{1,0:T(8,128)(2,1)S(1)} collective-permute-done((bf16[256,512]{1,0:T(8,128)(2,1)S(1)}, bf16[256,512]{1,0:T(8,128)(2,1)S(1)}, u32[]{:S(2)}, u32[]{:S(2)}) %collective-permute-start.16) | collective-permute-done | bytes 262176 | tf_op jit(solution)/shard_map/ppermute | solution.py:490
  90.7 2.7 %collective-permute-start.17 = (bf16[128,512]{1,0:T(8,128)(2,1)S(1)}, bf16[128,512]{1,0:T(8,128)(2,1)S(1)}, u32[]{:S(2)}, u32[]{:S(2)}) collective-permute-start(bf16[128,512]{1,0:T(8,128)(2,1)S(1)} %fusion.3), channel_id=1, source_target_pairs={{0,4},{1,5},{2,6},{3,7},{4,0},{5,1},{6,2},{7,3},{8,12},{9,13},{10,... | collective-permute-start | bytes 393224 | tf_op jit(solution)/shard_map/ppermute | solution.py:490
  93.4 2.2 %collective-permute-start.20 = (bf16[144,512]{1,0:T(8,128)(2,1)S(1)}, bf16[144,512]{1,0:T(8,128)(2,1)S(1)}, u32[]{:S(2)}, u32[]{:S(2)}) collective-permute-start(bf16[144,512]{1,0:T(8,128)(2,1)S(1)} %fusion.2), channel_id=1, source_target_pairs={{0,4},{1,5},{2,6},{3,7},{4,0},{5,1},{6,2},{7,3},{8,12},{9,13},{10,... | collective-permute-start | bytes 442376 | tf_op jit(solution)/shard_map/ppermute | solution.py:490
  95.6 7.1 %collective-permute-done.17 = bf16[128,512]{1,0:T(8,128)(2,1)S(1)} collective-permute-done((bf16[128,512]{1,0:T(8,128)(2,1)S(1)}, bf16[128,512]{1,0:T(8,128)(2,1)S(1)}, u32[]{:S(2)}, u32[]{:S(2)}) %collective-permute-start.17) | collective-permute-done | bytes 131104 | tf_op jit(solution)/shard_map/ppermute | solution.py:490
  102.7 1.9 %collective-permute-done.20 = bf16[144,512]{1,0:T(8,128)(2,1)S(1)} collective-permute-done((bf16[144,512]{1,0:T(8,128)(2,1)S(1)}, bf16[144,512]{1,0:T(8,128)(2,1)S(1)}, u32[]{:S(2)}, u32[]{:S(2)}) %collective-permute-start.20) | collective-permute-done | bytes 147488 | tf_op jit(solution)/shard_map/ppermute | solution.py:490
  105.3 0.8 maximum_bitcast_fusion
  (56 shorter events, 2.2 us)
Async XLA Ops:
  0.6 9.0 %copy-start = (bf16[1,4,256,1024]{3,2,1,0:T(8,128)(2,1)S(1)}, bf16[1,4,256,1024]{3,2,1,0:T(8,128)(2,1)}, u32[]{:S(2)}) copy-start(bf16[1,4,256,1024]{3,2,1,0:T(8,128)(2,1)} %param.6) | copy-start | bytes 6291460
  0.7 9.0 %copy-start.1 = (bf16[1,1024,1024]{2,1,0:T(8,128)(2,1)S(1)}, bf16[1,1024,1024]{2,1,0:T(8,128)(2,1)}, u32[]{:S(2)}) copy-start(bf16[1,1024,1024]{2,1,0:T(8,128)(2,1)} %param.7) | copy-start | bytes 6291460
  0.7 9.0 %copy-start.6 = (bf16[128,2048]{1,0:T(8,128)(2,1)S(1)}, bf16[128,2048]{1,0:T(8,128)(2,1)}, u32[]{:S(2)}) copy-start(bf16[128,2048]{1,0:T(8,128)(2,1)} %table_in.7) | copy-start | bytes 1572868
  8.3 5.8 %collective-permute-start.3 = (bf16[256,1024]{1,0:T(8,128)(2,1)}, bf16[256,1024]{1,0:T(8,128)(2,1)S(1)}, u32[]{:S(2)}, u32[]{:S(2)}) collective-permute-start(bf16[256,1024]{1,0:T(8,128)(2,1)} %get-tuple-element.58), channel_id=1, source_target_pairs={{24,16},{25,17},{26,18},{27,19},{28,20},{29,21},{30,22},{31,23}} | collective-permute-start | bytes 1572872 | tf_op jit(solution)/shard_map/ppermute | solution.py:531
  9.8 9.9 %collective-permute-start.2 = (bf16[256,1024]{1,0:T(8,128)(2,1)}, bf16[256,1024]{1,0:T(8,128)(2,1)S(1)}, u32[]{:S(2)}, u32[]{:S(2)}) collective-permute-start(bf16[256,1024]{1,0:T(8,128)(2,1)} %get-tuple-element.57), channel_id=1, source_target_pairs={{24,16},{25,17},{26,18},{27,19},{28,20},{29,21},{30,22},{31,23}} | collective-permute-start | bytes 1572872 | tf_op jit(solution)/shard_map/ppermute | solution.py:531
  11.4 13.1 %collective-permute-start.1 = (bf16[256,1024]{1,0:T(8,128)(2,1)}, bf16[256,1024]{1,0:T(8,128)(2,1)}, u32[]{:S(2)}, u32[]{:S(2)}) collective-permute-start(bf16[256,1024]{1,0:T(8,128)(2,1)} %get-tuple-element.56), channel_id=1, source_target_pairs={{24,16},{25,17},{26,18},{27,19},{28,20},{29,21},{30,22},{31,23}} | collective-permute-start | bytes 1572872 | tf_op jit(solution)/shard_map/ppermute | solution.py:531
  12.8 18.4 %collective-permute-start = (bf16[256,1024]{1,0:T(8,128)(2,1)}, bf16[256,1024]{1,0:T(8,128)(2,1)S(1)}, u32[]{:S(2)}, u32[]{:S(2)}) collective-permute-start(bf16[256,1024]{1,0:T(8,128)(2,1)} %get-tuple-element.55), channel_id=1, source_target_pairs={{24,16},{25,17},{26,18},{27,19},{28,20},{29,21},{30,22},{31,23}} | collective-permute-start | bytes 1572872 | tf_op jit(solution)/shard_map/ppermute | solution.py:531
  14.1 1.6 %copy-start.2 = (bf16[1,1024,1024]{2,1,0:T(8,128)(2,1)S(1)}, bf16[1,1024,1024]{2,1,0:T(8,128)(2,1)}, u32[]{:S(2)}) copy-start(bf16[1,1024,1024]{2,1,0:T(8,128)(2,1)} %param.7) | copy-start | bytes 6291460
  18.3 21.7 %collective-permute-start.6 = (bf16[256,1024]{1,0:T(8,128)(2,1)}, bf16[256,1024]{1,0:T(8,128)(2,1)S(1)}, u32[]{:S(2)}, u32[]{:S(2)}) collective-permute-start(bf16[256,1024]{1,0:T(8,128)(2,1)} %get-tuple-element.67), channel_id=1, source_target_pairs={{16,8},{17,9},{18,10},{19,11},{20,12},{21,13},{22,14},{23,15}} | collective-permute-start | bytes 1572872 | tf_op jit(solution)/shard_map/ppermute | solution.py:531
  22.3 20.0 %collective-permute-start.5 = (bf16[256,1024]{1,0:T(8,128)(2,1)}, bf16[256,1024]{1,0:T(8,128)(2,1)S(1)}, u32[]{:S(2)}, u32[]{:S(2)}) collective-permute-start(bf16[256,1024]{1,0:T(8,128)(2,1)} %get-tuple-element.66), channel_id=1, source_target_pairs={{16,8},{17,9},{18,10},{19,11},{20,12},{21,13},{22,14},{23,15}} | collective-permute-start | bytes 1572872 | tf_op jit(solution)/shard_map/ppermute | solution.py:531
  28.2 15.7 %collective-permute-start.4 = (bf16[256,1024]{1,0:T(8,128)(2,1)}, bf16[256,1024]{1,0:T(8,128)(2,1)}, u32[]{:S(2)}, u32[]{:S(2)}) collective-permute-start(bf16[256,1024]{1,0:T(8,128)(2,1)} %get-tuple-element.65), channel_id=1, source_target_pairs={{16,8},{17,9},{18,10},{19,11},{20,12},{21,13},{22,14},{23,15}} | collective-permute-start | bytes 1572872 | tf_op jit(solution)/shard_map/ppermute | solution.py:531
  31.2 4.8 %copy-start.11 = (bf16[4,1,1024]{2,0,1:T(4,128)(2,1)S(1)}, bf16[4,1,1024]{2,0,1:T(4,128)(2,1)}, u32[]{:S(2)}) copy-start(bf16[4,1,1024]{2,0,1:T(4,128)(2,1)} %param.11) | copy-start | bytes 24580
  31.2 4.8 %copy-start.12 = (s32[4,1,64]{2,1,0:T(1,128)S(1)}, s32[4,1,64]{2,1,0:T(1,128)}, u32[]{:S(2)}) copy-start(s32[4,1,64]{2,1,0:T(1,128)} %index_ref.1) | copy-start | bytes 3076
  33.9 12.5 %collective-permute-start.10 = (bf16[256,1024]{1,0:T(8,128)(2,1)}, bf16[256,1024]{1,0:T(8,128)(2,1)}, u32[]{:S(2)}, u32[]{:S(2)}) collective-permute-start(bf16[256,1024]{1,0:T(8,128)(2,1)} %get-tuple-element.63.after_hbm), channel_id=1, source_target_pairs={{16,8},{17,9},{18,10},{19,11},{20,12},{21,13},{22,14},{23,15}} | collective-permute-start | bytes 1572872 | tf_op jit(solution)/shard_map/ppermute | solution.py:531
  36.9 3.1 %copy-start.3 = (bf16[1,1024,1024]{2,1,0:T(8,128)(2,1)S(1)}, bf16[1,1024,1024]{2,1,0:T(8,128)(2,1)}, u32[]{:S(2)}) copy-start(bf16[1,1024,1024]{2,1,0:T(8,128)(2,1)} %param.7) | copy-start | bytes 6291460
  36.9 11.3 %collective-permute-start.12 = (bf16[128,512]{1,0:T(8,128)(2,1)}, bf16[128,512]{1,0:T(8,128)(2,1)S(1)}, u32[]{:S(2)}, u32[]{:S(2)}) collective-permute-start(bf16[128,512]{1,0:T(8,128)(2,1)} %get-tuple-element.93), channel_id=1, source_target_pairs={{24,0},{25,1},{26,2},{27,3},{28,4},{29,5},{30,6},{31,7}} | collective-permute-start | bytes 393224 | tf_op jit(solution)/shard_map/ppermute | solution.py:546
  40.0 1.3 %copy-start.4 = (bf16[1024,1024]{1,0:T(8,128)(2,1)}, bf16[1024,1024]{1,0:T(8,128)(2,1)S(1)}, u32[]{:S(2)}) copy-start(bf16[1024,1024]{1,0:T(8,128)(2,1)S(1)} %get-tuple-element.64.turned) | copy-start | bytes 6291460
  41.3 17.3 %collective-permute-start.9 = (bf16[256,1024]{1,0:T(8,128)(2,1)}, bf16[256,1024]{1,0:T(8,128)(2,1)S(1)}, u32[]{:S(2)}, u32[]{:S(2)}) collective-permute-start(bf16[256,1024]{1,0:T(8,128)(2,1)} %get-tuple-element.74), channel_id=1, source_target_pairs={{8,0},{9,1},{10,2},{11,3},{12,4},{13,5},{14,6},{15,7}} | collective-permute-start | bytes 1572872 | tf_op jit(solution)/shard_map/ppermute | solution.py:531
  42.3 16.4 %collective-permute-start.8 = (bf16[256,1024]{1,0:T(8,128)(2,1)}, bf16[256,1024]{1,0:T(8,128)(2,1)}, u32[]{:S(2)}, u32[]{:S(2)}) collective-permute-start(bf16[256,1024]{1,0:T(8,128)(2,1)} %get-tuple-element.73), channel_id=1, source_target_pairs={{8,0},{9,1},{10,2},{11,3},{12,4},{13,5},{14,6},{15,7}} | collective-permute-start | bytes 1572872 | tf_op jit(solution)/shard_map/ppermute | solution.py:531
  44.9 14.9 %collective-permute-start.7 = (bf16[256,1024]{1,0:T(8,128)(2,1)}, bf16[256,1024]{1,0:T(8,128)(2,1)}, u32[]{:S(2)}, u32[]{:S(2)}) collective-permute-start(bf16[256,1024]{1,0:T(8,128)(2,1)} %get-tuple-element.72), channel_id=1, source_target_pairs={{8,0},{9,1},{10,2},{11,3},{12,4},{13,5},{14,6},{15,7}} | collective-permute-start | bytes 1572872 | tf_op jit(solution)/shard_map/ppermute | solution.py:531
  46.4 1.9 %copy-start.15 = (bf16[128,512]{1,0:T(8,128)(2,1)S(1)}, bf16[128,512]{1,0:T(8,128)(2,1)}, u32[]{:S(2)}) copy-start(bf16[128,512]{1,0:T(8,128)(2,1)} %get-tuple-element.94) | copy-start | bytes 393220
  46.4 2.5 %copy-start.14 = (bf16[128,512]{1,0:T(8,128)(2,1)S(1)}, bf16[128,512]{1,0:T(8,128)(2,1)}, u32[]{:S(2)}) copy-start(bf16[128,512]{1,0:T(8,128)(2,1)} %get-tuple-element.95) | copy-start | bytes 393220
  46.4 12.2 %copy-start.13 = (bf16[128,512]{1,0:T(8,128)(2,1)S(1)}, bf16[128,512]{1,0:T(8,128)(2,1)}, u32[]{:S(2)}) copy-start(bf16[128,512]{1,0:T(8,128)(2,1)} %get-tuple-element.92) | copy-start | bytes 393220
  47.5 17.2 %collective-permute-start.11 = (bf16[256,1024]{1,0:T(8,128)(2,1)}, bf16[256,1024]{1,0:T(8,128)(2,1)S(1)}, u32[]{:S(2)}, u32[]{:S(2)}) collective-permute-start(bf16[256,1024]{1,0:T(8,128)(2,1)} %get-tuple-element.77), channel_id=1, source_target_pairs={{8,0},{9,1},{10,2},{11,3},{12,4},{13,5},{14,6},{15,7}} | collective-permute-start | bytes 1572872 | tf_op jit(solution)/shard_map/ppermute | solution.py:531
  48.2 0.7 collective-permute-start.13
  48.9 9.7 %collective-permute-start.14 = (bf16[128,512]{1,0:T(8,128)(2,1)S(1)}, bf16[128,512]{1,0:T(8,128)(2,1)S(1)}, u32[]{:S(2)}, u32[]{:S(2)}) collective-permute-start(bf16[128,512]{1,0:T(8,128)(2,1)S(1)} %copy-done.14), channel_id=1, source_target_pairs={{24,16},{25,17},{26,18},{27,19},{28,20},{29,21},{30,22},{31,23}} | collective-permute-start | bytes 393224 | tf_op jit(solution)/shard_map/ppermute | solution.py:546
  59.8 1.7 %copy-start.5 = (bf16[1024,1024]{1,0:T(8,128)(2,1)S(1)}, bf16[1024,1024]{1,0:T(8,128)(2,1)}, u32[]{:S(2)}) copy-start(bf16[1024,1024]{1,0:T(8,128)(2,1)} %copy-done.4) | copy-start | bytes 6291460
  64.7 2.8 %copy-start.7 = (f32[512,512]{1,0:T(8,128)}, f32[512,512]{1,0:T(8,128)S(1)}, u32[]{:S(2)}) copy-start(f32[512,512]{1,0:T(8,128)S(1)} %get-tuple-element.78.early_first) | copy-start | bytes 3145732
  64.7 2.8 %copy-start.9 = (f32[512,512]{1,0:T(8,128)}, f32[512,512]{1,0:T(8,128)S(1)}, u32[]{:S(2)}) copy-start(f32[512,512]{1,0:T(8,128)S(1)} %get-tuple-element.79.early_second) | copy-start | bytes 3145732
  67.5 14.4 %collective-permute-start.15 = (bf16[512,512]{1,0:T(8,128)(2,1)}, bf16[512,512]{1,0:T(8,128)(2,1)}, u32[]{:S(2)}, u32[]{:S(2)}) collective-permute-start(bf16[512,512]{1,0:T(8,128)(2,1)} %get-tuple-element.99), channel_id=1, source_target_pairs={{0,1},{1,0},{2,3},{3,2},{4,5},{5,4},{6,7},{7,6},{8,9},{9,8},{10,11... | collective-permute-start | bytes 1572872 | tf_op jit(solution)/shard_map/ppermute | solution.py:490
  69.1 15.6 %collective-permute-start.18 = (bf16[576,512]{1,0:T(8,128)(2,1)}, bf16[576,512]{1,0:T(8,128)(2,1)S(1)}, u32[]{:S(2)}, u32[]{:S(2)}) collective-permute-start(bf16[576,512]{1,0:T(8,128)(2,1)} %get-tuple-element.101), channel_id=1, source_target_pairs={{0,2},{1,3},{2,0},{3,1},{4,6},{5,7},{6,4},{7,5},{8,10},{9,11},{10,... | collective-permute-start | bytes 1769480 | tf_op jit(solution)/shard_map/ppermute | solution.py:490
  70.7 1.2 %copy-start.8 = (f32[512,512]{1,0:T(8,128)S(1)}, f32[512,512]{1,0:T(8,128)}, u32[]{:S(2)}) copy-start(f32[512,512]{1,0:T(8,128)} %copy-done.7) | copy-start | bytes 3145732
  71.9 1.2 %copy-start.10 = (f32[512,512]{1,0:T(8,128)S(1)}, f32[512,512]{1,0:T(8,128)}, u32[]{:S(2)}) copy-start(f32[512,512]{1,0:T(8,128)} %copy-done.9) | copy-start | bytes 3145732
  83.1 7.6 %collective-permute-start.16 = (bf16[256,512]{1,0:T(8,128)(2,1)S(1)}, bf16[256,512]{1,0:T(8,128)(2,1)S(1)}, u32[]{:S(2)}, u32[]{:S(2)}) collective-permute-start(bf16[256,512]{1,0:T(8,128)(2,1)S(1)} %get-tuple-element.104), channel_id=1, source_target_pairs={{0,2},{1,3},{2,0},{3,1},{4,6},{5,7},{6,4},{7,5},{8,10},{9,11},{10,... | collective-permute-start | bytes 786440 | tf_op jit(solution)/shard_map/ppermute | solution.py:490
  84.9 8.5 %collective-permute-start.19 = (bf16[288,512]{1,0:T(8,128)(2,1)S(1)}, bf16[288,512]{1,0:T(8,128)(2,1)S(1)}, u32[]{:S(2)}, u32[]{:S(2)}) collective-permute-start(bf16[288,512]{1,0:T(8,128)(2,1)S(1)} %get-tuple-element.102), channel_id=1, source_target_pairs={{0,1},{1,0},{2,3},{3,2},{4,5},{5,4},{6,7},{7,6},{8,9},{9,8},{10,11... | collective-permute-start | bytes 884744 | tf_op jit(solution)/shard_map/ppermute | solution.py:490
  90.7 12.0 %collective-permute-start.17 = (bf16[128,512]{1,0:T(8,128)(2,1)S(1)}, bf16[128,512]{1,0:T(8,128)(2,1)S(1)}, u32[]{:S(2)}, u32[]{:S(2)}) collective-permute-start(bf16[128,512]{1,0:T(8,128)(2,1)S(1)} %fusion.3), channel_id=1, source_target_pairs={{0,4},{1,5},{2,6},{3,7},{4,0},{5,1},{6,2},{7,3},{8,12},{9,13},{10,... | collective-permute-start | bytes 393224 | tf_op jit(solution)/shard_map/ppermute | solution.py:490
  93.4 11.2 %collective-permute-start.20 = (bf16[144,512]{1,0:T(8,128)(2,1)S(1)}, bf16[144,512]{1,0:T(8,128)(2,1)S(1)}, u32[]{:S(2)}, u32[]{:S(2)}) collective-permute-start(bf16[144,512]{1,0:T(8,128)(2,1)S(1)} %fusion.2), channel_id=1, source_target_pairs={{0,4},{1,5},{2,6},{3,7},{4,0},{5,1},{6,2},{7,3},{8,12},{9,13},{10,... | collective-permute-start | bytes 442376 | tf_op jit(solution)/shard_map/ppermute | solution.py:490

commit v4 on v3

--- a/solution.py
+++ b/solution.py
@@ -44,10 +44,6 @@
 
 def stay(array):
     return pltpu.with_memory_space_constraint(array, pltpu.HBM)
-
-
-def near(array):
-    return pltpu.with_memory_space_constraint(array, pltpu.VMEM)
 
 
 def own_heads(width):
@@ -200,7 +196,7 @@
             pltpu.SemaphoreType.DMA((max(11, 1 + 2 * micros),)),
         ],
         input_output_aliases={} if m == 0 else {7: 1},
-        compiler_params=pltpu.CompilerParams(vmem_limit_bytes=28 * MIB),
+        compiler_params=pltpu.CompilerParams(vmem_limit_bytes=18 * MIB),
         cost_estimate=LIGHT,
         name="first",
     )(
@@ -213,11 +209,12 @@
     )
 
 
-def table_kernel(replicas, flag_ref, number_ref, index_ref, pooled_ref, after_hbm, *refs):
+def table_kernel(flag_ref, index_ref, pooled_ref, after_hbm, *refs):
     share, slant, high, kv, sems = refs[-5:]
     count, rows, width = high.shape
-    sources, outs = refs[: 3 * count], refs[3 * count : -5]
-    span, table_rows = outs[0].shape[1], outs[0].shape[0]
+    sections = (len(refs) - 5 - 3 * count) // 2
+    sources, outs, parts = refs[: 3 * count], refs[3 * count : -5 - sections], refs[-5 - sections : -5]
+    table_rows, span = parts[0].shape
     cands = index_ref.shape[2]
 
     @pl.when(flag_ref[0] == 1)
@@ -228,15 +225,7 @@
                 loads.append(pltpu.make_async_copy(sources[k * count + m], target.at[m], sems.at[3 * m + k]))
         for load in loads:
             load.start()
-        bits = bit_orders(replicas)[1]
-        shift = (table_rows // replicas).bit_length() - 1
-        spot = lax.broadcasted_iota(jnp.int32, (table_rows, cands), 0)
-        block = spot >> shift
-        mine = (number_ref[0] >> bits[0]) & 1
-        row = jnp.where(block < replicas // 2, 1 - mine, mine) << bits[0]
-        for k, bit in enumerate(bits[1:]):
-            row = row + (((block >> (len(bits) - 2 - k)) & 1) << bit)
-        row = (row << shift) + (spot & ((1 << shift) - 1))
+        row = lax.broadcasted_iota(jnp.int32, (table_rows, cands), 0)
         head = lax.broadcasted_iota(jnp.int32, (cands, TILE), 1) >> (HEAD.bit_length() - 1)
         ones = jnp.ones((rows, PAIR), BF16)
         onehot = jnp.concatenate([(row == index_ref[m]).astype(BF16) for m in range(count)], axis=1)
@@ -261,52 +250,62 @@
                 kv[lines, cols] = by_head([key[at : at + cands] for at in starts])
                 value = by_head([column[q * TILE + at : q * TILE + at + cands] for at in starts])
                 kv[lines, width + q * TILE : width + (q + 1) * TILE] = value * given[:, cols]
-        for k, out in enumerate(outs):
+        stores = []
+        for k, part in enumerate(parts):
             kv_high, kv_low = high_low(kv[:, k * span : (k + 1) * span])
-            out[...] = (dot(onehot, kv_high, NN) + dot(onehot, kv_low, NN)).astype(BF16)
-
-
-def table_call(flag, number, index, pooled, table_rows, after, shares, slants, highs, sections, replicas):
+            part[...] = (dot(onehot, kv_high, NN) + dot(onehot, kv_low, NN)).astype(BF16)
+            stores.append(pltpu.make_async_copy(part, outs[k], sems.at[3 * count + k]))
+            stores[k].start()
+        for store in stores:
+            store.wait()
+
+
+def table_call(flag, index, pooled, table_rows, after, shares, slants, highs, sections):
     rows, width = highs[0].shape
     count = len(highs)
+    part = (table_rows, 2 * width // sections)
     return pl.pallas_call(
-        functools.partial(table_kernel, replicas),
-        out_shape=(pltpu.HBM((table_rows, 2 * width // sections), BF16),) * sections,
-        in_specs=[SMEM, SMEM, VMEM, VMEM, HBM] + [HBM] * (3 * count),
-        out_specs=(VMEM,) * sections,
-        scratch_shapes=[
+        table_kernel,
+        out_shape=(pltpu.HBM(part, BF16),) * sections,
+        in_specs=[SMEM, VMEM, VMEM, HBM] + [HBM] * (3 * count),
+        out_specs=(HBM,) * sections,
+        scratch_shapes=[pltpu.VMEM(part, BF16)] * sections
+        + [
             pltpu.VMEM((count,) + shares[0].shape, BF16),
             pltpu.VMEM((count,) + slants[0].shape, BF16),
             pltpu.VMEM((count,) + highs[0].shape, BF16),
             pltpu.VMEM((count * index.shape[2], 2 * width), F32),
-            pltpu.SemaphoreType.DMA((3 * count,)),
+            pltpu.SemaphoreType.DMA((3 * count + sections,)),
         ],
-        compiler_params=pltpu.CompilerParams(vmem_limit_bytes=28 * MIB),
+        compiler_params=pltpu.CompilerParams(vmem_limit_bytes=18 * MIB),
         cost_estimate=LIGHT,
         name="table",
-    )(flag, number, index, pooled, stay(after), *map(stay, shares), *map(stay, slants), *map(stay, highs))
-
-
-def hop_kernel(m, with_grad, flag_ref, came, delta_in, weight, after_hbm, *rest):
+    )(flag, index, pooled, stay(after), *map(stay, shares), *map(stay, slants), *map(stay, highs))
+
+
+def hop_kernel(m, with_grad, flag_ref, came_hbm, delta_in, weight, after_hbm, *rest):
     if with_grad:
-        grad_hbm, delta_hbm, aux, grad, sems = rest
+        grad_hbm, delta_hbm, came, aux, grad, sems = rest
     else:
-        delta_hbm, aux, sems = rest
+        delta_hbm, came, aux, sems = rest
     width = came.shape[1]
 
     @pl.when(flag_ref[0] == 1)
     def _():
-        load = pltpu.make_async_copy(delta_in.at[m], aux, sems.at[0])
-        load.start()
-        load.wait()
+        first = pltpu.make_async_copy(came_hbm, came, sems.at[0])
+        second = pltpu.make_async_copy(delta_in.at[m], aux, sems.at[1])
+        first.start()
+        second.start()
+        first.wait()
+        second.wait()
         aux[...] = (came[...].astype(F32) * aux[...].astype(F32)).astype(BF16)
-        stores = [pltpu.make_async_copy(aux, delta_hbm.at[m], sems.at[1])]
+        stores = [pltpu.make_async_copy(aux, delta_hbm.at[m], sems.at[2])]
         stores[0].start()
         if with_grad:
             for n in range(width // TILE):
                 part = slice(n * TILE, (n + 1) * TILE)
                 grad[:, part] = (came[:, part].astype(F32) + dot(aux[...], weight[part, :], NT)).astype(BF16)
-            stores.append(pltpu.make_async_copy(grad, grad_hbm, sems.at[2]))
+            stores.append(pltpu.make_async_copy(grad, grad_hbm, sems.at[3]))
             stores[-1].start()
         for store in stores:
             store.wait()
@@ -314,22 +313,22 @@
 
 def hop_call(m, flag, came, delta, weight, after, with_grad):
     rows, width = came.shape
-    scratch = [pltpu.VMEM((rows, width), BF16)] * (2 if with_grad else 1)
-    scratch.append(pltpu.SemaphoreType.DMA((3,)))
+    scratch = [pltpu.VMEM((rows, width), BF16)] * (3 if with_grad else 2)
+    scratch.append(pltpu.SemaphoreType.DMA((4,)))
     outs = (pltpu.HBM(delta.shape, BF16),)
     if with_grad:
         outs = (pltpu.HBM((rows, width), BF16),) + outs
     return pl.pallas_call(
         functools.partial(hop_kernel, m, with_grad),
         out_shape=outs,
-        in_specs=[SMEM, VMEM, HBM, VMEM if with_grad else HBM, HBM],
+        in_specs=[SMEM, HBM, HBM, VMEM if with_grad else HBM, HBM],
         out_specs=(HBM,) * len(outs),
         scratch_shapes=scratch,
         input_output_aliases={2: len(outs) - 1},
         compiler_params=pltpu.CompilerParams(vmem_limit_bytes=12 * MIB),
         cost_estimate=LIGHT,
         name="hop" if with_grad else "end",
-    )(flag, near(came), stay(delta), weight if with_grad else stay(weight), stay(after))
+    )(flag, came, stay(delta), weight if with_grad else stay(weight), stay(after))
 
 
 def bit_orders(replicas):
@@ -364,7 +363,7 @@
         in_specs=[HBM, HBM],
         out_specs=(VMEM,) * 2,
         scratch_shapes=[pltpu.VMEM(acts.shape, BF16), pltpu.SemaphoreType.DMA((count,))],
-        compiler_params=pltpu.CompilerParams(vmem_limit_bytes=20 * MIB),
+        compiler_params=pltpu.CompilerParams(vmem_limit_bytes=14 * MIB),
         cost_estimate=LIGHT,
         name="turn",
     )(stay(acts), stay(after))
@@ -410,30 +409,21 @@
             pltpu.VMEM((micros - 1, rows, width), BF16),
             pltpu.SemaphoreType.DMA((micros - 1,)),
         ],
-        compiler_params=pltpu.CompilerParams(vmem_limit_bytes=28 * MIB),
+        compiler_params=pltpu.CompilerParams(vmem_limit_bytes=18 * MIB),
         cost_estimate=LIGHT,
         name="early",
     )(number, turned, stay(delta))
 
 
 def weight_kernel(
-    replicas, which, flag_ref, number_ref, turned, delta_hbm, came, early_first, early_second, table_ref, *refs
+    replicas, which, flag_ref, number_ref, turned, delta_hbm, came, early_first, early_second, *refs
 ):
     outs, (delta, sem) = refs[:2], refs[2:]
     rows, width = delta.shape
     half = width // 2
-    size = width // replicas
-    lines = table_ref.shape[0] // replicas
-    pitch = outs[1].shape[0] // (replicas // 2)
     last = delta_hbm.shape[0] - 1
     load = pltpu.make_async_copy(delta_hbm.at[last], delta, sem.at[0])
     load.start()
-    table = table_ref[which * table_ref.shape[0] // 2 : (which + 1) * table_ref.shape[0] // 2].astype(F32)
-    for i in range(replicas // 2):
-        extra = table[i * lines : (i + 1) * lines]
-        if extra.shape != (pitch - size, half):
-            extra = jnp.pad(extra, ((0, pitch - size - lines), (0, half - extra.shape[1])))
-        outs[1][i * pitch + size : (i + 1) * pitch] = extra.astype(outs[1].dtype)
     load.wait()
 
     @pl.when(flag_ref[0] == 1)
@@ -441,37 +431,26 @@
         delta[...] = (came[...].astype(F32) * delta[...].astype(F32)).astype(BF16)
 
     for c, (bits, early) in enumerate(zip(bit_orders(replicas), (early_first, early_second))):
-        left = picked_rows(turned, number_ref[0], bits, which, size, slice(last * rows, (last + 1) * rows))
+        columns = slice(last * rows, (last + 1) * rows)
+        left = picked_rows(turned, number_ref[0], bits, which, width // replicas, columns)
         for at in range(0, half, TILE):
-            cols = slice(at, at + TILE)
-            product = early[:, cols] + dot(
-                left,
-                delta[:, c * half + at : c * half + at + TILE],
-                NN,
-            )
-            product = product.astype(outs[c].dtype)
-            if c == 0:
-                outs[c][:, cols] = product
-            else:
-                for i in range(replicas // 2):
-                    outs[c][i * pitch : i * pitch + size, cols] = product[i * size : (i + 1) * size]
-
-
-def weight_call(which, flag, number, turned, delta, came, early, table, replicas):
+            product = dot(left, delta[:, c * half + at : c * half + at + TILE], NN)
+            outs[c][:, at : at + TILE] = (early[:, at : at + TILE] + product).astype(outs[c].dtype)
+
+
+def weight_call(which, flag, number, turned, delta, came, early, replicas):
     micros, rows, width = delta.shape
-    half = width // 2
-    extra = max(16, table.shape[0] // replicas) * (replicas // 2)
-    array = functools.partial(jax.ShapeDtypeStruct, dtype=F32) if which else functools.partial(pltpu.HBM, dtype=BF16)
+    half = (width // 2, width // 2)
     return pl.pallas_call(
         functools.partial(weight_kernel, replicas, which),
-        out_shape=(array((half, half)), array((half + extra, half))),
-        in_specs=[SMEM, SMEM, VMEM, HBM] + [VMEM] * 4,
+        out_shape=(jax.ShapeDtypeStruct(half, F32) if which else pltpu.HBM(half, BF16),) * 2,
+        in_specs=[SMEM, SMEM, VMEM, HBM, VMEM, VMEM, VMEM],
         out_specs=(VMEM,) * 2,
         scratch_shapes=[pltpu.VMEM((rows, width), BF16), pltpu.SemaphoreType.DMA((1,))],
-        compiler_params=pltpu.CompilerParams(vmem_limit_bytes=20 * MIB),
+        compiler_params=pltpu.CompilerParams(vmem_limit_bytes=14 * MIB),
         cost_estimate=LIGHT,
         name="weight",
-    )(flag, number, turned, stay(delta), near(came), *early, table)
+    )(flag, number, turned, stay(delta), came, *early)
 
 
 def own_half(keep, got, bit):
@@ -538,23 +517,20 @@
                 (delta,) = hop_call(m, active, received[m], delta, weight, acts, False)
         if hop == 0:
             parts = table_call(
-                final, number, cand_index, pooled, cand_table.shape[0], grads[-1], shares, slants, highs, sections,
-                replicas,
+                final, cand_index, pooled, cand_table.shape[0], grads[-1], shares, slants, highs, sections
             )
             turned, token = turn_call(acts, grads[-1])
 
     spread = [lax.ppermute(parts[s], "section", [(last, s)]) for s in range(last)]
     table_part = jnp.where(final_flag, parts[last], sum(spread))
+    table_sum = lax.psum_scatter(table_part, "dp", scatter_dimension=0, tiled=True).astype(F32)
 
     orders = bit_orders(replicas)
     early = early_call(number, turned, delta, replicas)
-    sends = weight_call(0, active, number, turned, delta, received[-1], early[::2], table_part, replicas)
-    keeps = weight_call(1, active, number, turned, delta, received[-1], early[1::2], table_part, replicas)
+    sends = weight_call(0, active, number, turned, delta, received[-1], early[::2], replicas)
+    keeps = weight_call(1, active, number, turned, delta, received[-1], early[1::2], replicas)
     sums = [finish_scatter(sends[c], keeps[c], orders[c], "dp", pairs) for c in range(2)]
-    size = model_width // replicas
-    lines = cand_table.shape[0] // replicas
-    table_sum = sums[1][size : size + lines, : 2 * model_width // sections]
-    return jnp.concatenate([sums[0], sums[1][:size]], axis=1)[None], table_sum
+    return jnp.concatenate(sums, axis=1)[None], table_sum
 
 
 def solution(mesh):

time: 107 us -> 161 us (1.50)
  the two profiles are of different devices: /device:TPU:2 before, /device:TPU:0 now
where the time goes in v4:
time: 161 us; the launch traced here: 160 us
  waiting for transfers between devices  79.8 us (50%)
  starting transfers between devices  27.7 us (17%)
  Pallas kernels  25.1 us (16%)
  between operations  14.5 us (9%)
  local copies, waits for them, and re-layouts  7.42 us (5%)
  other arithmetic  5.38 us (3%)
    reduce_scatter x1, waiting for transfers between devices, body(): lax.psum_scatter(table_part, 'dp', scatter_dimension=0, tiled=True)  56.1 us
    ppermute x12, waiting for transfers between devices, body(): lax.ppermute(g, 'section', [(source, source - 1)])  14.6 us
    ppermute x12, starting transfers between devices, body(): lax.ppermute(g, 'section', [(source, source - 1)])  13.2 us
    ppermute x6, starting transfers between devices, finish_scatter(): got = lax.ppermute(send, axes, pairs_of(bit))  10.5 us
    ppermute x6, waiting for transfers between devices, finish_scatter(): got = lax.ppermute(send, axes, pairs_of(bit))  9 us
    pallas_call x4, Pallas kernels, first_call(): pl.pallas_call(functools.partial(first_kernel, m), out_shape=(block, pltp...  8.14 us
    unnamed x32, local copies, waits for them, and re-layouts  7.42 us
    pallas_call x11, Pallas kernels, hop_call(): pl.pallas_call(functools.partial(hop_kernel, m, with_grad), out_shape=out...  6.88 us
  transfers between devices with their start and end apart: 22, of which 7 were waited for; matrix products, arithmetic and copies ran while one was open for 3% of the time, Pallas kernels for 9%

profile of v4, /device:TPU:0, one launch (start us, length us, event | category | flops | bytes accessed | tf_op | source)
XLA Modules:
  0.0 159.9 jit_solution(3848528052474268220)
XLA Ops:
  7.3 7.6 %first.4 = (bf16[256,1024]{1,0:T(8,128)(2,1)}, bf16[4,256,1024]{2,1,0:T(8,128)(2,1)}, bf16[1024,256]{1,0:T(8,128)(2,1)}, bf16[1024,256]{1,0:T(8,128)(2,1)}, bf16[256,1024]{1,0:T(8,128)(2,1)}) custom-call(s32[1]{0:T(128)} %bitcast.4.flag_ref, s32[1,4]{1,0:T(1,128)} %bitcast.78, bf16[4,256,1024]{2,1,0:T(8,128)(2,1)} %bitcast.31, bf16[1024,1024]{1,0:T(8,128)(2,1)} %bitcast.47, ...), custom_call_target="tpu_custom_call" | custom-call | flops 1024 | bytes 1024 | tf_op jit(solution)/shard_map/first/pallas_call | solution.py:179
  14.9 0.7 collective-permute-start.3
  15.8 0.7 collective-permute-start.2
  16.5 0.3 first.6
  16.8 1.5 collective-permute-start.1
  18.3 0.7 collective-permute-start
  19.1 1.6 copy-done.2
  20.7 0.7 collective-permute-start.6
  21.5 0.7 collective-permute-start.5
  22.2 1.5 collective-permute-start.4
  23.8 1.6 %collective-permute-start.10 = (bf16[256,1024]{1,0:T(8,128)(2,1)}, bf16[256,1024]{1,0:T(8,128)(2,1)}, u32[]{:S(2)}, u32[]{:S(2)}) collective-permute-start(bf16[256,1024]{1,0:T(8,128)(2,1)} %get-tuple-element.63.after_hbm), channel_id=1, source_target_pairs={{16,8},{17,9},{18,10},{19,11},{20,12},{21,13},{22,14},{23,15}} | collective-permute-start | bytes 1572872 | tf_op jit(solution)/shard_map/ppermute | solution.py:510
  25.4 2.3 %turn.1 = (bf16[1024,1024]{1,0:T(8,128)(2,1)S(1)}, bf16[16,128]{1,0:T(8,128)(2,1)}) custom-call(bf16[4,256,1024]{2,1,0:T(8,128)(2,1)} %bitcast.37, bf16[256,1024]{1,0:T(8,128)(2,1)} %get-tuple-element.63.after_hbm), custom_call_target="tpu_custom_call" | custom-call | flops 1024 | bytes 1024 | tf_op jit(solution)/shard_map/turn/pallas_call | solution.py:360
  27.7 1.3 copy-done.4
  29.1 1.3 collective-permute-start.9
  30.5 1.3 collective-permute-start.8
  31.8 1.3 collective-permute-start.7
  33.1 0.3 hop.15
  33.4 1.3 collective-permute-start.11
  34.7 7.2 %collective-permute-done.9.came_hbm = bf16[256,1024]{1,0:T(8,128)(2,1)S(1)} collective-permute-done((bf16[256,1024]{1,0:T(8,128)(2,1)}, bf16[256,1024]{1,0:T(8,128)(2,1)S(1)}, u32[]{:S(2)}, u32[]{:S(2)}) %collective-permute-start.9) | collective-permute-done | bytes 524320 | tf_op jit(solution)/shard_map/ppermute | solution.py:510
  41.9 2.0 %end.3.delta_in = bf16[4,256,1024]{2,1,0:T(8,128)(2,1)} custom-call(s32[1]{0:T(128)} %bitcast.flag_ref, bf16[256,1024]{1,0:T(8,128)(2,1)S(1)} %collective-permute-done.9.came_hbm, bf16[4,256,1024]{2,1,0:T(8,128)(2,1)} %get-tuple-element.76.delta_in, bf16[1024,1024]{1,0:T(8,128)(2,1)} %bitcast.48, ...), custom_call_target="tpu_custom_call", output_to_operand_aliasing={{}: (2, {})} | custom-call | flops 1024 | bytes 1024 | tf_op jit(solution)/shard_map/end/pallas_call | solution.py:321
  43.9 3.7 %collective-permute-done.8.came_hbm = bf16[256,1024]{1,0:T(8,128)(2,1)} collective-permute-done((bf16[256,1024]{1,0:T(8,128)(2,1)}, bf16[256,1024]{1,0:T(8,128)(2,1)}, u32[]{:S(2)}, u32[]{:S(2)}) %collective-permute-start.8) | collective-permute-done | bytes 524320 | tf_op jit(solution)/shard_map/ppermute | solution.py:510
  47.6 2.2 %end.4.delta_in = bf16[4,256,1024]{2,1,0:T(8,128)(2,1)} custom-call(s32[1]{0:T(128)} %bitcast.flag_ref, bf16[256,1024]{1,0:T(8,128)(2,1)} %collective-permute-done.8.came_hbm, bf16[4,256,1024]{2,1,0:T(8,128)(2,1)} %end.3.delta_in, bf16[1024,1024]{1,0:T(8,128)(2,1)} %bitcast.49, bf16[4,256,1024]{2,1,0:T(8,128)(2,1)} %bitcast.42), custom_call_target="tpu_custom_call", output_to_operand_aliasing={{}: (2, {})} | custom-call | flops 1024 | bytes 1024 | tf_op jit(solution)/shard_map/end/pallas_call | solution.py:321
  49.8 3.7 %collective-permute-done.7.came_hbm = bf16[256,1024]{1,0:T(8,128)(2,1)} collective-permute-done((bf16[256,1024]{1,0:T(8,128)(2,1)}, bf16[256,1024]{1,0:T(8,128)(2,1)}, u32[]{:S(2)}, u32[]{:S(2)}) %collective-permute-start.7) | collective-permute-done | bytes 524320 | tf_op jit(solution)/shard_map/ppermute | solution.py:510
  53.5 2.1 %end.5.delta_hbm = bf16[4,256,1024]{2,1,0:T(8,128)(2,1)} custom-call(s32[1]{0:T(128)} %bitcast.flag_ref, bf16[256,1024]{1,0:T(8,128)(2,1)} %collective-permute-done.7.came_hbm, bf16[4,256,1024]{2,1,0:T(8,128)(2,1)} %end.4.delta_in, bf16[1024,1024]{1,0:T(8,128)(2,1)} %bitcast.50, bf16[4,256,1024]{2,1,0:T(8,128)(2,1)} %bitcast.43), custom_call_target="tpu_custom_call", output_to_operand_aliasing={{}: (2, {})} | custom-call | flops 1024 | bytes 1024 | tf_op jit(solution)/shard_map/end/pallas_call | solution.py:321
  55.7 3.2 %early.1 = (f32[512,512]{1,0:T(8,128)S(1)}, f32[512,512]{1,0:T(8,128)S(1)}, f32[512,512]{1,0:T(8,128)S(1)}, f32[512,512]{1,0:T(8,128)S(1)}) custom-call(s32[1]{0:T(128)} %bitcast.1.number_ref, bf16[1024,1024]{1,0:T(8,128)(2,1)S(1)} %copy-done.5, bf16[4,256,1024]{2,1,0:T(8,128)(2,1)} %end.5.delta_hbm), custom_call_target="tpu_custom_call" | custom-call | flops 1024 | bytes 1024 | tf_op jit(solution)/shard_map/early/pallas_call | solution.py:403
  58.9 1.0 copy-done.11
  59.9 2.8 %weight.3 = (bf16[512,512]{1,0:T(8,128)(2,1)}, bf16[512,512]{1,0:T(8,128)(2,1)}) custom-call(s32[1]{0:T(128)} %bitcast.flag_ref, s32[1]{0:T(128)} %bitcast.1.number_ref, bf16[1024,1024]{1,0:T(8,128)(2,1)S(1)} %copy-done.5, bf16[4,256,1024]{2,1,0:T(8,128)(2,1)} %end.5.delta_hbm, bf16[256,1024]{1,0:T(8,128)(2,1)S(1)} %collective-permute-done.11.came, ...), custom_call_target="tpu_custom_call" | custom-call | flops 1024 | bytes 1024 | tf_op jit(solution)/shard_map/weight/pallas_call | solution.py:444
  62.8 1.6 collective-permute-start.12
  64.3 1.6 collective-permute-start.15
  66.1 1.3 collective-permute-start.18
  67.4 1.3 collective-permute-start.19
  68.7 1.3 collective-permute-start.20
  70.0 1.2 copy-done.10
  71.2 1.2 copy-done.12
  72.5 1.6 %weight.2 = (f32[512,512]{1,0:T(8,128)S(1)}, f32[512,512]{1,0:T(8,128)S(1)}) custom-call(s32[1]{0:T(128)} %bitcast.flag_ref, s32[1]{0:T(128)} %bitcast.1.number_ref, bf16[1024,1024]{1,0:T(8,128)(2,1)S(1)} %copy-done.5, bf16[4,256,1024]{2,1,0:T(8,128)(2,1)} %end.5.delta_hbm, bf16[256,1024]{1,0:T(8,128)(2,1)S(1)} %collective-permute-done.11.came, ...), custom_call_target="tpu_custom_call" | custom-call | flops 1024 | bytes 1024 | tf_op jit(solution)/shard_map/weight/pallas_call | solution.py:444
  74.1 1.0 copy-done.7
  75.1 0.4 collective-permute-done.12
  75.5 1.3 fusion
  76.8 1.6 %collective-permute-start.13 = (bf16[256,512]{1,0:T(8,128)(2,1)S(1)}, bf16[256,512]{1,0:T(8,128)(2,1)S(1)}, u32[]{:S(2)}, u32[]{:S(2)}) collective-permute-start(bf16[256,512]{1,0:T(8,128)(2,1)S(1)} %get-tuple-element.102), channel_id=1, source_target_pairs={{0,2},{1,3},{2,0},{3,1},{4,6},{5,7},{6,4},{7,5},{8,10},{9,11},{10,... | collective-permute-start | bytes 786440 | tf_op jit(solution)/shard_map/ppermute | solution.py:469
  78.4 1.7 %add_select_fusion = bf16[128,512]{1,0:T(8,128)(2,1)} fusion(bf16[128,512]{1,0:T(8,128)(2,1)S(1)} %copy-done.15, bf16[128,512]{1,0:T(8,128)(2,1)} %collective-permute-done.20, bf16[128,512]{1,0:T(8,128)(2,1)S(1)} %collective-permute-done.18, bf16[128,512]{1,0:T(8,128)(2,1)} %collective-permute-done.19, pred[]{:T(512)S(6)} %eq.14), kind=kLoop, calls=%fused_computation.13 | loop fusion | flops 196608 | bytes 655361 | tf_op jit(solution)/shard_map/jit(_where)/select_n | solution.py:525
  80.3 1.6 collective-permute-start.16
  81.9 2.8 %collective-permute-done.13 = bf16[256,512]{1,0:T(8,128)(2,1)S(1)} collective-permute-done((bf16[256,512]{1,0:T(8,128)(2,1)S(1)}, bf16[256,512]{1,0:T(8,128)(2,1)S(1)}, u32[]{:S(2)}, u32[]{:S(2)}) %collective-permute-start.13) | collective-permute-done | bytes 262176 | tf_op jit(solution)/shard_map/ppermute | solution.py:469
  84.7 2.7 %collective-permute-start.14 = (bf16[128,512]{1,0:T(8,128)(2,1)S(1)}, bf16[128,512]{1,0:T(8,128)(2,1)S(1)}, u32[]{:S(2)}, u32[]{:S(2)}) collective-permute-start(bf16[128,512]{1,0:T(8,128)(2,1)S(1)} %fusion.2), channel_id=1, source_target_pairs={{0,4},{1,5},{2,6},{3,7},{4,0},{5,1},{6,2},{7,3},{8,12},{9,13},{10,... | collective-permute-start | bytes 393224 | tf_op jit(solution)/shard_map/ppermute | solution.py:469
  87.4 56.1 %reduce-scatter.2.cloned.1.call-done = bf16[16,512]{1,0:T(8,128)(2,1)} async-done(((bf16[128,512]{1,0:T(8,128)(2,1)}), bf16[16,512]{1,0:T(8,128)(2,1)}) %reduce-scatter.2.cloned.1.call-update) | async-done | bytes 16400 | tf_op jit(solution)/shard_map/reduce_scatter | solution.py:526
  143.5 1.3 convert_element_type.89
  144.9 1.5 collective-permute-start.17
  146.4 5.8 %collective-permute-done.17 = bf16[128,512]{1,0:T(8,128)(2,1)S(1)} collective-permute-done((bf16[128,512]{1,0:T(8,128)(2,1)S(1)}, bf16[128,512]{1,0:T(8,128)(2,1)S(1)}, u32[]{:S(2)}, u32[]{:S(2)}) %collective-permute-start.17) | collective-permute-done | bytes 131104 | tf_op jit(solution)/shard_map/ppermute | solution.py:469
  152.2 0.8 maximum_bitcast_fusion
  (58 shorter events, 1.1 us)
Async XLA Ops:
  7.2 136.3 %reduce-scatter.2.cloned.1.call-start = ((), (), s32[]{:S(2)}) async-start(), calls=%async_computation.1 | async-start | bytes 147456 | tf_op jit(solution)/shard_map/reduce_scatter | solution.py:526
  7.2 8.4 %copy-start = (bf16[1,4,256,1024]{3,2,1,0:T(8,128)(2,1)S(1)}, bf16[1,4,256,1024]{3,2,1,0:T(8,128)(2,1)}, u32[]{:S(2)}) copy-start(bf16[1,4,256,1024]{3,2,1,0:T(8,128)(2,1)} %param.6) | copy-start | bytes 6291460
  7.2 8.4 %copy-start.1 = (bf16[1,1024,1024]{2,1,0:T(8,128)(2,1)S(1)}, bf16[1,1024,1024]{2,1,0:T(8,128)(2,1)}, u32[]{:S(2)}) copy-start(bf16[1,1024,1024]{2,1,0:T(8,128)(2,1)} %param.7) | copy-start | bytes 6291460
  7.2 8.4 %copy-start.6 = (bf16[128,2048]{1,0:T(8,128)(2,1)S(1)}, bf16[128,2048]{1,0:T(8,128)(2,1)}, u32[]{:S(2)}) copy-start(bf16[128,2048]{1,0:T(8,128)(2,1)} %table_in.7) | copy-start | bytes 1572868
  14.9 4.1 %collective-permute-start.3 = (bf16[256,1024]{1,0:T(8,128)(2,1)}, bf16[256,1024]{1,0:T(8,128)(2,1)S(1)}, u32[]{:S(2)}, u32[]{:S(2)}) collective-permute-start(bf16[256,1024]{1,0:T(8,128)(2,1)} %get-tuple-element.58), channel_id=1, source_target_pairs={{24,16},{25,17},{26,18},{27,19},{28,20},{29,21},{30,22},{31,23}} | collective-permute-start | bytes 1572872 | tf_op jit(solution)/shard_map/ppermute | solution.py:510
  15.8 5.6 %collective-permute-start.2 = (bf16[256,1024]{1,0:T(8,128)(2,1)}, bf16[256,1024]{1,0:T(8,128)(2,1)S(1)}, u32[]{:S(2)}, u32[]{:S(2)}) collective-permute-start(bf16[256,1024]{1,0:T(8,128)(2,1)} %get-tuple-element.57), channel_id=1, source_target_pairs={{24,16},{25,17},{26,18},{27,19},{28,20},{29,21},{30,22},{31,23}} | collective-permute-start | bytes 1572872 | tf_op jit(solution)/shard_map/ppermute | solution.py:510
  16.8 5.4 %collective-permute-start.1 = (bf16[256,1024]{1,0:T(8,128)(2,1)}, bf16[256,1024]{1,0:T(8,128)(2,1)}, u32[]{:S(2)}, u32[]{:S(2)}) collective-permute-start(bf16[256,1024]{1,0:T(8,128)(2,1)} %get-tuple-element.56), channel_id=1, source_target_pairs={{24,16},{25,17},{26,18},{27,19},{28,20},{29,21},{30,22},{31,23}} | collective-permute-start | bytes 1572872 | tf_op jit(solution)/shard_map/ppermute | solution.py:510
  18.3 5.4 %collective-permute-start = (bf16[256,1024]{1,0:T(8,128)(2,1)}, bf16[256,1024]{1,0:T(8,128)(2,1)S(1)}, u32[]{:S(2)}, u32[]{:S(2)}) collective-permute-start(bf16[256,1024]{1,0:T(8,128)(2,1)} %get-tuple-element.55), channel_id=1, source_target_pairs={{24,16},{25,17},{26,18},{27,19},{28,20},{29,21},{30,22},{31,23}} | collective-permute-start | bytes 1572872 | tf_op jit(solution)/shard_map/ppermute | solution.py:510
  19.1 1.6 copy-start.2
  20.7 8.4 %collective-permute-start.6 = (bf16[256,1024]{1,0:T(8,128)(2,1)}, bf16[256,1024]{1,0:T(8,128)(2,1)S(1)}, u32[]{:S(2)}, u32[]{:S(2)}) collective-permute-start(bf16[256,1024]{1,0:T(8,128)(2,1)} %get-tuple-element.67), channel_id=1, source_target_pairs={{16,8},{17,9},{18,10},{19,11},{20,12},{21,13},{22,14},{23,15}} | collective-permute-start | bytes 1572872 | tf_op jit(solution)/shard_map/ppermute | solution.py:510
  21.5 8.9 %collective-permute-start.5 = (bf16[256,1024]{1,0:T(8,128)(2,1)}, bf16[256,1024]{1,0:T(8,128)(2,1)S(1)}, u32[]{:S(2)}, u32[]{:S(2)}) collective-permute-start(bf16[256,1024]{1,0:T(8,128)(2,1)} %get-tuple-element.66), channel_id=1, source_target_pairs={{16,8},{17,9},{18,10},{19,11},{20,12},{21,13},{22,14},{23,15}} | collective-permute-start | bytes 1572872 | tf_op jit(solution)/shard_map/ppermute | solution.py:510
  22.2 9.5 %collective-permute-start.4 = (bf16[256,1024]{1,0:T(8,128)(2,1)}, bf16[256,1024]{1,0:T(8,128)(2,1)}, u32[]{:S(2)}, u32[]{:S(2)}) collective-permute-start(bf16[256,1024]{1,0:T(8,128)(2,1)} %get-tuple-element.65), channel_id=1, source_target_pairs={{16,8},{17,9},{18,10},{19,11},{20,12},{21,13},{22,14},{23,15}} | collective-permute-start | bytes 1572872 | tf_op jit(solution)/shard_map/ppermute | solution.py:510
  23.8 5.3 %copy-start.3 = (bf16[1,1024,1024]{2,1,0:T(8,128)(2,1)S(1)}, bf16[1,1024,1024]{2,1,0:T(8,128)(2,1)}, u32[]{:S(2)}) copy-start(bf16[1,1024,1024]{2,1,0:T(8,128)(2,1)} %param.7) | copy-start | bytes 6291460
  23.8 9.4 %collective-permute-start.10 = (bf16[256,1024]{1,0:T(8,128)(2,1)}, bf16[256,1024]{1,0:T(8,128)(2,1)}, u32[]{:S(2)}, u32[]{:S(2)}) collective-permute-start(bf16[256,1024]{1,0:T(8,128)(2,1)} %get-tuple-element.63.after_hbm), channel_id=1, source_target_pairs={{16,8},{17,9},{18,10},{19,11},{20,12},{21,13},{22,14},{23,15}} | collective-permute-start | bytes 1572872 | tf_op jit(solution)/shard_map/ppermute | solution.py:510
  27.7 1.4 copy-start.4
  29.1 12.8 %collective-permute-start.9 = (bf16[256,1024]{1,0:T(8,128)(2,1)}, bf16[256,1024]{1,0:T(8,128)(2,1)S(1)}, u32[]{:S(2)}, u32[]{:S(2)}) collective-permute-start(bf16[256,1024]{1,0:T(8,128)(2,1)} %get-tuple-element.74), channel_id=1, source_target_pairs={{8,0},{9,1},{10,2},{11,3},{12,4},{13,5},{14,6},{15,7}} | collective-permute-start | bytes 1572872 | tf_op jit(solution)/shard_map/ppermute | solution.py:510
  30.5 17.2 %collective-permute-start.8 = (bf16[256,1024]{1,0:T(8,128)(2,1)}, bf16[256,1024]{1,0:T(8,128)(2,1)}, u32[]{:S(2)}, u32[]{:S(2)}) collective-permute-start(bf16[256,1024]{1,0:T(8,128)(2,1)} %get-tuple-element.73), channel_id=1, source_target_pairs={{8,0},{9,1},{10,2},{11,3},{12,4},{13,5},{14,6},{15,7}} | collective-permute-start | bytes 1572872 | tf_op jit(solution)/shard_map/ppermute | solution.py:510
  31.8 21.7 %collective-permute-start.7 = (bf16[256,1024]{1,0:T(8,128)(2,1)}, bf16[256,1024]{1,0:T(8,128)(2,1)}, u32[]{:S(2)}, u32[]{:S(2)}) collective-permute-start(bf16[256,1024]{1,0:T(8,128)(2,1)} %get-tuple-element.72), channel_id=1, source_target_pairs={{8,0},{9,1},{10,2},{11,3},{12,4},{13,5},{14,6},{15,7}} | collective-permute-start | bytes 1572872 | tf_op jit(solution)/shard_map/ppermute | solution.py:510
  33.4 26.5 %collective-permute-start.11 = (bf16[256,1024]{1,0:T(8,128)(2,1)}, bf16[256,1024]{1,0:T(8,128)(2,1)S(1)}, u32[]{:S(2)}, u32[]{:S(2)}) collective-permute-start(bf16[256,1024]{1,0:T(8,128)(2,1)} %get-tuple-element.77), channel_id=1, source_target_pairs={{8,0},{9,1},{10,2},{11,3},{12,4},{13,5},{14,6},{15,7}} | collective-permute-start | bytes 1572872 | tf_op jit(solution)/shard_map/ppermute | solution.py:510
  49.8 5.9 %copy-start.5 = (bf16[1024,1024]{1,0:T(8,128)(2,1)S(1)}, bf16[1024,1024]{1,0:T(8,128)(2,1)}, u32[]{:S(2)}) copy-start(bf16[1024,1024]{1,0:T(8,128)(2,1)} %copy-done.4) | copy-start | bytes 6291460
  58.9 1.0 copy-start.11
  59.9 2.9 %copy-start.9 = (f32[512,512]{1,0:T(8,128)}, f32[512,512]{1,0:T(8,128)S(1)}, u32[]{:S(2)}) copy-start(f32[512,512]{1,0:T(8,128)S(1)} %get-tuple-element.78.early_first) | copy-start | bytes 3145732
  59.9 6.0 %copy-start.13 = (bf16[4,1,1024]{2,0,1:T(4,128)(2,1)S(1)}, bf16[4,1,1024]{2,0,1:T(4,128)(2,1)}, u32[]{:S(2)}) copy-start(bf16[4,1,1024]{2,0,1:T(4,128)(2,1)} %param.11) | copy-start | bytes 24580
  59.9 6.0 %copy-start.14 = (s32[4,1,64]{2,1,0:T(1,128)S(1)}, s32[4,1,64]{2,1,0:T(1,128)}, u32[]{:S(2)}) copy-start(s32[4,1,64]{2,1,0:T(1,128)} %index_ref.1) | copy-start | bytes 3076
  62.8 12.7 %collective-permute-start.12 = (bf16[512,512]{1,0:T(8,128)(2,1)}, bf16[512,512]{1,0:T(8,128)(2,1)}, u32[]{:S(2)}, u32[]{:S(2)}) collective-permute-start(bf16[512,512]{1,0:T(8,128)(2,1)} %get-tuple-element.83), channel_id=1, source_target_pairs={{0,1},{1,0},{2,3},{3,2},{4,5},{5,4},{6,7},{7,6},{8,9},{9,8},{10,11... | collective-permute-start | bytes 1572872 | tf_op jit(solution)/shard_map/ppermute | solution.py:469
  64.3 15.8 %collective-permute-start.15 = (bf16[512,512]{1,0:T(8,128)(2,1)}, bf16[512,512]{1,0:T(8,128)(2,1)S(1)}, u32[]{:S(2)}, u32[]{:S(2)}) collective-permute-start(bf16[512,512]{1,0:T(8,128)(2,1)} %get-tuple-element.85), channel_id=1, source_target_pairs={{0,2},{1,3},{2,0},{3,1},{4,6},{5,7},{6,4},{7,5},{8,10},{9,11},{10,... | collective-permute-start | bytes 1572872 | tf_op jit(solution)/shard_map/ppermute | solution.py:469
  66.1 12.3 %collective-permute-start.18 = (bf16[128,512]{1,0:T(8,128)(2,1)}, bf16[128,512]{1,0:T(8,128)(2,1)S(1)}, u32[]{:S(2)}, u32[]{:S(2)}) collective-permute-start(bf16[128,512]{1,0:T(8,128)(2,1)} %get-tuple-element.99), channel_id=1, source_target_pairs={{24,0},{25,1},{26,2},{27,3},{28,4},{29,5},{30,6},{31,7}} | collective-permute-start | bytes 393224 | tf_op jit(solution)/shard_map/ppermute | solution.py:524
  67.4 11.0 %collective-permute-start.19 = (bf16[128,512]{1,0:T(8,128)(2,1)}, bf16[128,512]{1,0:T(8,128)(2,1)}, u32[]{:S(2)}, u32[]{:S(2)}) collective-permute-start(bf16[128,512]{1,0:T(8,128)(2,1)} %get-tuple-element.100), channel_id=1, source_target_pairs={{24,8},{25,9},{26,10},{27,11},{28,12},{29,13},{30,14},{31,15}} | collective-permute-start | bytes 393224 | tf_op jit(solution)/shard_map/ppermute | solution.py:524
  68.7 9.7 %collective-permute-start.20 = (bf16[128,512]{1,0:T(8,128)(2,1)}, bf16[128,512]{1,0:T(8,128)(2,1)}, u32[]{:S(2)}, u32[]{:S(2)}) collective-permute-start(bf16[128,512]{1,0:T(8,128)(2,1)} %get-tuple-element.101), channel_id=1, source_target_pairs={{24,16},{25,17},{26,18},{27,19},{28,20},{29,21},{30,22},{31,23}} | collective-permute-start | bytes 393224 | tf_op jit(solution)/shard_map/ppermute | solution.py:524
  70.0 1.2 copy-start.10
  71.2 1.2 copy-start.12
  74.1 1.0 copy-start.7
  75.1 3.3 %copy-start.15 = (bf16[128,512]{1,0:T(8,128)(2,1)S(1)}, bf16[128,512]{1,0:T(8,128)(2,1)}, u32[]{:S(2)}) copy-start(bf16[128,512]{1,0:T(8,128)(2,1)} %get-tuple-element.98) | copy-start | bytes 393220
  75.5 4.6 %copy-start.8 = (f32[512,512]{1,0:T(8,128)S(1)}, f32[512,512]{1,0:T(8,128)}, u32[]{:S(2)}) copy-start(f32[512,512]{1,0:T(8,128)} %copy-done.7) | copy-start | bytes 3145732
  76.8 7.9 %collective-permute-start.13 = (bf16[256,512]{1,0:T(8,128)(2,1)S(1)}, bf16[256,512]{1,0:T(8,128)(2,1)S(1)}, u32[]{:S(2)}, u32[]{:S(2)}) collective-permute-start(bf16[256,512]{1,0:T(8,128)(2,1)S(1)} %get-tuple-element.102), channel_id=1, source_target_pairs={{0,2},{1,3},{2,0},{3,1},{4,6},{5,7},{6,4},{7,5},{8,10},{9,11},{10,... | collective-permute-start | bytes 786440 | tf_op jit(solution)/shard_map/ppermute | solution.py:469
  80.3 64.6 %collective-permute-start.16 = (bf16[256,512]{1,0:T(8,128)(2,1)S(1)}, bf16[256,512]{1,0:T(8,128)(2,1)S(1)}, u32[]{:S(2)}, u32[]{:S(2)}) collective-permute-start(bf16[256,512]{1,0:T(8,128)(2,1)S(1)} %get-tuple-element.104), channel_id=1, source_target_pairs={{0,1},{1,0},{2,3},{3,2},{4,5},{5,4},{6,7},{7,6},{8,9},{9,8},{10,11... | collective-permute-start | bytes 786440 | tf_op jit(solution)/shard_map/ppermute | solution.py:469
  84.7 61.7 %collective-permute-start.14 = (bf16[128,512]{1,0:T(8,128)(2,1)S(1)}, bf16[128,512]{1,0:T(8,128)(2,1)S(1)}, u32[]{:S(2)}, u32[]{:S(2)}) collective-permute-start(bf16[128,512]{1,0:T(8,128)(2,1)S(1)} %fusion.2), channel_id=1, source_target_pairs={{0,4},{1,5},{2,6},{3,7},{4,0},{5,1},{6,2},{7,3},{8,12},{9,13},{10,... | collective-permute-start | bytes 393224 | tf_op jit(solution)/shard_map/ppermute | solution.py:469
  144.9 7.3 %collective-permute-start.17 = (bf16[128,512]{1,0:T(8,128)(2,1)S(1)}, bf16[128,512]{1,0:T(8,128)(2,1)S(1)}, u32[]{:S(2)}, u32[]{:S(2)}) collective-permute-start(bf16[128,512]{1,0:T(8,128)(2,1)S(1)} %fusion.3), channel_id=1, source_target_pairs={{0,4},{1,5},{2,6},{3,7},{4,0},{5,1},{6,2},{7,3},{8,12},{9,13},{10,... | collective-permute-start | bytes 393224 | tf_op jit(solution)/shard_map/ppermute | solution.py:469
Sparse Core Ops, SparseCore 0:
  80.2 63.2 reduce-scatter.1

commit v5 on v4

--- a/solution.py
+++ b/solution.py
@@ -464,13 +464,37 @@
     return pick(1 - mine).astype(BF16), pick(mine)
 
 
-def finish_scatter(send, keep, bits, axes, pairs_of):
-    for n, bit in enumerate(bits):
-        got = lax.ppermute(send, axes, pairs_of(bit))
-        if n + 1 < len(bits):
-            lead = (2, keep.shape[0] // 2, keep.shape[1])
-            send, keep = own_half(keep.reshape(lead), got.reshape(lead), bits[n + 1])
-    return keep + got.astype(F32)
+def join_kernel(first, first_got, second, second_got, out):
+    half = first.shape[1]
+    out[:, :half] = first[...] + first_got[...].astype(F32)
+    out[:, half:] = second[...] + second_got[...].astype(F32)
+
+
+def join_call(keeps, gots):
+    rows, half = keeps[0].shape
+    return pl.pallas_call(
+        join_kernel,
+        out_shape=jax.ShapeDtypeStruct((rows, 2 * half), F32),
+        in_specs=[VMEM] * 4,
+        out_specs=VMEM,
+        cost_estimate=LIGHT,
+        name="join",
+    )(keeps[0], gots[0], keeps[1], gots[1])
+
+
+def scatter_sums(sends, keeps, table, orders, pairs_of):
+    steps = len(orders[0])
+    sends, keeps = list(sends), list(keeps)
+    for n in range(steps):
+        gots = [lax.ppermute(send, "dp", pairs_of(bits[n])) for send, bits in zip(sends, orders)]
+        for c, bits in enumerate(orders):
+            if n + 1 < steps:
+                lead = (2, keeps[c].shape[0] // 2, keeps[c].shape[1])
+                sends[c], keeps[c] = own_half(keeps[c].reshape(lead), gots[c].reshape(lead), bits[n + 1])
+        if n + 2 == steps:
+            table, _ = lax.optimization_barrier((table, tuple(sends)))
+    blocks = lax.all_to_all(table.reshape(1 << steps, -1, table.shape[1]), "dp", 0, 0)
+    return join_call(keeps, gots), jnp.sum(blocks.astype(F32), axis=0)
 
 
 def body(activations, section_weights, cand_table, cand_index, cand_count, pooled_cotangent):
@@ -523,14 +547,13 @@
 
     spread = [lax.ppermute(parts[s], "section", [(last, s)]) for s in range(last)]
     table_part = jnp.where(final_flag, parts[last], sum(spread))
-    table_sum = lax.psum_scatter(table_part, "dp", scatter_dimension=0, tiled=True).astype(F32)
 
     orders = bit_orders(replicas)
     early = early_call(number, turned, delta, replicas)
     sends = weight_call(0, active, number, turned, delta, received[-1], early[::2], replicas)
     keeps = weight_call(1, active, number, turned, delta, received[-1], early[1::2], replicas)
-    sums = [finish_scatter(sends[c], keeps[c], orders[c], "dp", pairs) for c in range(2)]
-    return jnp.concatenate(sums, axis=1)[None], table_sum
+    sums, table_sum = scatter_sums(sends, keeps, table_part, orders, pairs)
+    return sums[None], table_sum
 
 
 def solution(mesh):

time: 161 us -> 108 us (0.67)
  waiting for transfers between devices: 79.8 us -> 40 us
  between operations: 14.5 us -> 1.13 us
  local copies, waits for them, and re-layouts: 7.42 us -> 4.63 us
  starting transfers between devices: 27.7 us -> 30.2 us
  Pallas kernels: 25.1 us -> 27 us
    reduce_scatter x1 -> x0, waiting for transfers between devices: 56.1 us -> none  [body(): lax.psum_scatter(table_part, 'dp', scatter_dimension=0, tiled=True)]
    ppermute x6, waiting for transfers between devices: 9 us -> 25.4 us  [scatter_sums(): lax.ppermute(send, 'dp', pairs_of(bits[n]))]
    all_to_all x0 -> x1, starting transfers between devices: none -> 4.88 us  [scatter_sums(): lax.all_to_all(table.reshape(1 << steps, -1, table.shape[1]), 'dp', 0, 0)]
    unnamed x32, local copies, waits for them, and re-layouts: 7.42 us -> 4.63 us
    pallas_call x0 -> x1, Pallas kernels: none -> 1.97 us  [join_call(): pl.pallas_call(join_kernel, out_shape=jax.ShapeDtypeStruct((rows, 2 * hal...]
  transfers between devices with their start and end apart: 22 -> 22, of which waited for: 7 -> 8; matrix products, arithmetic and copies ran while one was open for 3% -> 3% of each run, Pallas kernels for 9% -> 15%
where the time goes in v5:
time: 108 us; the launch traced here: 107 us
  waiting for transfers between devices  40 us (37%)
  starting transfers between devices  30.2 us (28%)
  Pallas kernels  27 us (25%)
  local copies, waits for them, and re-layouts  4.63 us (4%)
  other arithmetic  4.24 us (4%)
  between operations  1.13 us (1%)
    ppermute x6, waiting for transfers between devices, scatter_sums(): lax.ppermute(send, 'dp', pairs_of(bits[n]))  25.4 us
    ppermute x12, waiting for transfers between devices, body(): lax.ppermute(g, 'section', [(source, source - 1)])  14.6 us
    ppermute x12, starting transfers between devices, body(): lax.ppermute(g, 'section', [(source, source - 1)])  13.2 us
    ppermute x6, starting transfers between devices, scatter_sums(): lax.ppermute(send, 'dp', pairs_of(bits[n]))  9.35 us
    pallas_call x4, Pallas kernels, first_call(): pl.pallas_call(functools.partial(first_kernel, m), out_shape=(block, pltp...  8.11 us
    pallas_call x11, Pallas kernels, hop_call(): pl.pallas_call(functools.partial(hop_kernel, m, with_grad), out_shape=out...  6.86 us
    all_to_all x1, starting transfers between devices, scatter_sums(): lax.all_to_all(table.reshape(1 << steps, -1, table.shape[1]), 'dp', 0, 0)  4.88 us
    unnamed x32, local copies, waits for them, and re-layouts  4.63 us
  transfers between devices with their start and end apart: 22, of which 8 were waited for; matrix products, arithmetic and copies ran while one was open for 3% of the time, Pallas kernels for 15%

profile of v5, /device:TPU:0, one launch (start us, length us, event | category | flops | bytes accessed | tf_op | source)
XLA Modules:
  0.0 107.3 jit_solution(5447349507804479621)
XLA Ops:
  0.7 7.6 %first.4 = (bf16[256,1024]{1,0:T(8,128)(2,1)}, bf16[4,256,1024]{2,1,0:T(8,128)(2,1)}, bf16[1024,256]{1,0:T(8,128)(2,1)}, bf16[1024,256]{1,0:T(8,128)(2,1)}, bf16[256,1024]{1,0:T(8,128)(2,1)}) custom-call(s32[1]{0:T(128)} %bitcast.4.flag_ref, s32[1,4]{1,0:T(1,128)} %bitcast.75, bf16[4,256,1024]{2,1,0:T(8,128)(2,1)} %bitcast.31, bf16[1024,1024]{1,0:T(8,128)(2,1)} %bitcast.47, ...), custom_call_target="tpu_custom_call" | custom-call | flops 1024 | bytes 1024 | tf_op jit(solution)/shard_map/first/pallas_call | solution.py:179
  8.3 0.7 collective-permute-start.3
  9.1 0.7 collective-permute-start.2
  9.8 0.3 first.6
  10.1 1.5 %collective-permute-start.1 = (bf16[256,1024]{1,0:T(8,128)(2,1)}, bf16[256,1024]{1,0:T(8,128)(2,1)}, u32[]{:S(2)}, u32[]{:S(2)}) collective-permute-start(bf16[256,1024]{1,0:T(8,128)(2,1)} %get-tuple-element.57), channel_id=1, source_target_pairs={{24,16},{25,17},{26,18},{27,19},{28,20},{29,21},{30,22},{31,23}} | collective-permute-start | bytes 1572872 | tf_op jit(solution)/shard_map/ppermute | solution.py:534
  11.7 0.7 collective-permute-start
  12.4 1.6 %copy-done.2 = bf16[1,1024,1024]{2,1,0:T(8,128)(2,1)S(1)} copy-done((bf16[1,1024,1024]{2,1,0:T(8,128)(2,1)S(1)}, bf16[1,1024,1024]{2,1,0:T(8,128)(2,1)}, u32[]{:S(2)}) %copy-start.2) | copy-done | bytes 2097176
  14.1 0.7 collective-permute-start.6
  14.8 0.7 collective-permute-start.5
  15.6 1.5 %collective-permute-start.4 = (bf16[256,1024]{1,0:T(8,128)(2,1)}, bf16[256,1024]{1,0:T(8,128)(2,1)}, u32[]{:S(2)}, u32[]{:S(2)}) collective-permute-start(bf16[256,1024]{1,0:T(8,128)(2,1)} %get-tuple-element.66), channel_id=1, source_target_pairs={{16,8},{17,9},{18,10},{19,11},{20,12},{21,13},{22,14},{23,15}} | collective-permute-start | bytes 1572872 | tf_op jit(solution)/shard_map/ppermute | solution.py:534
  17.1 1.7 %collective-permute-start.10 = (bf16[256,1024]{1,0:T(8,128)(2,1)}, bf16[256,1024]{1,0:T(8,128)(2,1)}, u32[]{:S(2)}, u32[]{:S(2)}) collective-permute-start(bf16[256,1024]{1,0:T(8,128)(2,1)} %get-tuple-element.64.after_hbm), channel_id=1, source_target_pairs={{16,8},{17,9},{18,10},{19,11},{20,12},{21,13},{22,14},{23,15}} | collective-permute-start | bytes 1572872 | tf_op jit(solution)/shard_map/ppermute | solution.py:534
  18.8 2.3 %turn.1 = (bf16[1024,1024]{1,0:T(8,128)(2,1)S(1)}, bf16[16,128]{1,0:T(8,128)(2,1)}) custom-call(bf16[4,256,1024]{2,1,0:T(8,128)(2,1)} %bitcast.37, bf16[256,1024]{1,0:T(8,128)(2,1)} %get-tuple-element.64.after_hbm), custom_call_target="tpu_custom_call" | custom-call | flops 1024 | bytes 1024 | tf_op jit(solution)/shard_map/turn/pallas_call | solution.py:360
  21.1 1.3 %copy-done.4 = bf16[1024,1024]{1,0:T(8,128)(2,1)} copy-done((bf16[1024,1024]{1,0:T(8,128)(2,1)}, bf16[1024,1024]{1,0:T(8,128)(2,1)S(1)}, u32[]{:S(2)}) %copy-start.4) | copy-done | bytes 2097176
  22.5 1.3 %collective-permute-start.9 = (bf16[256,1024]{1,0:T(8,128)(2,1)}, bf16[256,1024]{1,0:T(8,128)(2,1)S(1)}, u32[]{:S(2)}, u32[]{:S(2)}) collective-permute-start(bf16[256,1024]{1,0:T(8,128)(2,1)} %get-tuple-element.75), channel_id=1, source_target_pairs={{8,0},{9,1},{10,2},{11,3},{12,4},{13,5},{14,6},{15,7}} | collective-permute-start | bytes 1572872 | tf_op jit(solution)/shard_map/ppermute | solution.py:534
  23.9 1.3 %collective-permute-start.8 = (bf16[256,1024]{1,0:T(8,128)(2,1)}, bf16[256,1024]{1,0:T(8,128)(2,1)}, u32[]{:S(2)}, u32[]{:S(2)}) collective-permute-start(bf16[256,1024]{1,0:T(8,128)(2,1)} %get-tuple-element.74), channel_id=1, source_target_pairs={{8,0},{9,1},{10,2},{11,3},{12,4},{13,5},{14,6},{15,7}} | collective-permute-start | bytes 1572872 | tf_op jit(solution)/shard_map/ppermute | solution.py:534
  25.2 1.3 %collective-permute-start.7 = (bf16[256,1024]{1,0:T(8,128)(2,1)}, bf16[256,1024]{1,0:T(8,128)(2,1)}, u32[]{:S(2)}, u32[]{:S(2)}) collective-permute-start(bf16[256,1024]{1,0:T(8,128)(2,1)} %get-tuple-element.73), channel_id=1, source_target_pairs={{8,0},{9,1},{10,2},{11,3},{12,4},{13,5},{14,6},{15,7}} | collective-permute-start | bytes 1572872 | tf_op jit(solution)/shard_map/ppermute | solution.py:534
  26.8 1.3 %collective-permute-start.11 = (bf16[256,1024]{1,0:T(8,128)(2,1)}, bf16[256,1024]{1,0:T(8,128)(2,1)S(1)}, u32[]{:S(2)}, u32[]{:S(2)}) collective-permute-start(bf16[256,1024]{1,0:T(8,128)(2,1)} %get-tuple-element.78), channel_id=1, source_target_pairs={{8,0},{9,1},{10,2},{11,3},{12,4},{13,5},{14,6},{15,7}} | collective-permute-start | bytes 1572872 | tf_op jit(solution)/shard_map/ppermute | solution.py:534
  28.1 7.2 %collective-permute-done.9.came_hbm = bf16[256,1024]{1,0:T(8,128)(2,1)S(1)} collective-permute-done((bf16[256,1024]{1,0:T(8,128)(2,1)}, bf16[256,1024]{1,0:T(8,128)(2,1)S(1)}, u32[]{:S(2)}, u32[]{:S(2)}) %collective-permute-start.9) | collective-permute-done | bytes 524320 | tf_op jit(solution)/shard_map/ppermute | solution.py:534
  35.3 2.0 %end.3.delta_in = bf16[4,256,1024]{2,1,0:T(8,128)(2,1)} custom-call(s32[1]{0:T(128)} %bitcast.flag_ref, bf16[256,1024]{1,0:T(8,128)(2,1)S(1)} %collective-permute-done.9.came_hbm, bf16[4,256,1024]{2,1,0:T(8,128)(2,1)} %get-tuple-element.77.delta_in, bf16[1024,1024]{1,0:T(8,128)(2,1)} %bitcast.48, ...), custom_call_target="tpu_custom_call", output_to_operand_aliasing={{}: (2, {})} | custom-call | flops 1024 | bytes 1024 | tf_op jit(solution)/shard_map/end/pallas_call | solution.py:321
  37.3 3.7 %collective-permute-done.8.came_hbm = bf16[256,1024]{1,0:T(8,128)(2,1)} collective-permute-done((bf16[256,1024]{1,0:T(8,128)(2,1)}, bf16[256,1024]{1,0:T(8,128)(2,1)}, u32[]{:S(2)}, u32[]{:S(2)}) %collective-permute-start.8) | collective-permute-done | bytes 524320 | tf_op jit(solution)/shard_map/ppermute | solution.py:534
  41.0 2.1 %end.4.delta_in = bf16[4,256,1024]{2,1,0:T(8,128)(2,1)} custom-call(s32[1]{0:T(128)} %bitcast.flag_ref, bf16[256,1024]{1,0:T(8,128)(2,1)} %collective-permute-done.8.came_hbm, bf16[4,256,1024]{2,1,0:T(8,128)(2,1)} %end.3.delta_in, bf16[1024,1024]{1,0:T(8,128)(2,1)} %bitcast.49, bf16[4,256,1024]{2,1,0:T(8,128)(2,1)} %bitcast.42), custom_call_target="tpu_custom_call", output_to_operand_aliasing={{}: (2, {})} | custom-call | flops 1024 | bytes 1024 | tf_op jit(solution)/shard_map/end/pallas_call | solution.py:321
  43.2 3.7 %collective-permute-done.7.came_hbm = bf16[256,1024]{1,0:T(8,128)(2,1)} collective-permute-done((bf16[256,1024]{1,0:T(8,128)(2,1)}, bf16[256,1024]{1,0:T(8,128)(2,1)}, u32[]{:S(2)}, u32[]{:S(2)}) %collective-permute-start.7) | collective-permute-done | bytes 524320 | tf_op jit(solution)/shard_map/ppermute | solution.py:534
  46.9 2.1 %end.5.delta_hbm = bf16[4,256,1024]{2,1,0:T(8,128)(2,1)} custom-call(s32[1]{0:T(128)} %bitcast.flag_ref, bf16[256,1024]{1,0:T(8,128)(2,1)} %collective-permute-done.7.came_hbm, bf16[4,256,1024]{2,1,0:T(8,128)(2,1)} %end.4.delta_in, bf16[1024,1024]{1,0:T(8,128)(2,1)} %bitcast.50, bf16[4,256,1024]{2,1,0:T(8,128)(2,1)} %bitcast.43), custom_call_target="tpu_custom_call", output_to_operand_aliasing={{}: (2, {})} | custom-call | flops 1024 | bytes 1024 | tf_op jit(solution)/shard_map/end/pallas_call | solution.py:321
  49.1 3.2 %early.1 = (f32[512,512]{1,0:T(8,128)S(1)}, f32[512,512]{1,0:T(8,128)S(1)}, f32[512,512]{1,0:T(8,128)S(1)}, f32[512,512]{1,0:T(8,128)S(1)}) custom-call(s32[1]{0:T(128)} %bitcast.1.number_ref, bf16[1024,1024]{1,0:T(8,128)(2,1)S(1)} %copy-done.5, bf16[4,256,1024]{2,1,0:T(8,128)(2,1)} %end.5.delta_hbm), custom_call_target="tpu_custom_call" | custom-call | flops 1024 | bytes 1024 | tf_op jit(solution)/shard_map/early/pallas_call | solution.py:403
  52.3 1.0 copy-done.9
  53.3 2.8 %weight.3 = (bf16[512,512]{1,0:T(8,128)(2,1)}, bf16[512,512]{1,0:T(8,128)(2,1)}) custom-call(s32[1]{0:T(128)} %bitcast.flag_ref, s32[1]{0:T(128)} %bitcast.1.number_ref, bf16[1024,1024]{1,0:T(8,128)(2,1)S(1)} %copy-done.5, bf16[4,256,1024]{2,1,0:T(8,128)(2,1)} %end.5.delta_hbm, bf16[256,1024]{1,0:T(8,128)(2,1)S(1)} %collective-permute-done.11.came, ...), custom_call_target="tpu_custom_call" | custom-call | flops 1024 | bytes 1024 | tf_op jit(solution)/shard_map/weight/pallas_call | solution.py:444
  56.1 1.6 %collective-permute-start.15 = (bf16[512,512]{1,0:T(8,128)(2,1)}, bf16[512,512]{1,0:T(8,128)(2,1)}, u32[]{:S(2)}, u32[]{:S(2)}) collective-permute-start(bf16[512,512]{1,0:T(8,128)(2,1)} %get-tuple-element.86), channel_id=1, source_target_pairs={{0,2},{1,3},{2,0},{3,1},{4,6},{5,7},{6,4},{7,5},{8,10},{9,11},{10,... | collective-permute-start | bytes 1572872 | tf_op jit(solution)/shard_map/ppermute | solution.py:489
  57.8 1.5 %collective-permute-start.12 = (bf16[512,512]{1,0:T(8,128)(2,1)}, bf16[512,512]{1,0:T(8,128)(2,1)S(1)}, u32[]{:S(2)}, u32[]{:S(2)}) collective-permute-start(bf16[512,512]{1,0:T(8,128)(2,1)} %get-tuple-element.84), channel_id=1, source_target_pairs={{0,1},{1,0},{2,3},{3,2},{4,5},{5,4},{6,7},{7,6},{8,9},{9,8},{10,11... | collective-permute-start | bytes 1572872 | tf_op jit(solution)/shard_map/ppermute | solution.py:489
  59.5 1.4 %collective-permute-start.18 = (bf16[128,512]{1,0:T(8,128)(2,1)}, bf16[128,512]{1,0:T(8,128)(2,1)S(1)}, u32[]{:S(2)}, u32[]{:S(2)}) collective-permute-start(bf16[128,512]{1,0:T(8,128)(2,1)} %get-tuple-element.100), channel_id=1, source_target_pairs={{24,0},{25,1},{26,2},{27,3},{28,4},{29,5},{30,6},{31,7}} | collective-permute-start | bytes 393224 | tf_op jit(solution)/shard_map/ppermute | solution.py:548
  60.9 0.7 collective-permute-start.19
  61.6 0.7 collective-permute-start.20
  62.3 1.6 %weight.2 = (f32[512,512]{1,0:T(8,128)S(1)}, f32[512,512]{1,0:T(8,128)S(1)}) custom-call(s32[1]{0:T(128)} %bitcast.flag_ref, s32[1]{0:T(128)} %bitcast.1.number_ref, bf16[1024,1024]{1,0:T(8,128)(2,1)S(1)} %copy-done.5, bf16[4,256,1024]{2,1,0:T(8,128)(2,1)} %end.5.delta_hbm, bf16[256,1024]{1,0:T(8,128)(2,1)S(1)} %collective-permute-done.11.came, ...), custom_call_target="tpu_custom_call" | custom-call | flops 1024 | bytes 1024 | tf_op jit(solution)/shard_map/weight/pallas_call | solution.py:444
  63.9 5.0 %collective-permute-done.15 = bf16[512,512]{1,0:T(8,128)(2,1)} collective-permute-done((bf16[512,512]{1,0:T(8,128)(2,1)}, bf16[512,512]{1,0:T(8,128)(2,1)}, u32[]{:S(2)}, u32[]{:S(2)}) %collective-permute-start.15) | collective-permute-done | bytes 524320 | tf_op jit(solution)/shard_map/ppermute | solution.py:489
  68.9 1.2 %fusion.1 = (bf16[256,512]{1,0:T(8,128)(2,1)S(1)}, f32[1,256,512]{2,1,0:T(8,128)S(1)}) fusion(f32[2,256,512]{2,1,0:T(8,128)S(1)} %bitcast.63, s32[]{:T(128)S(6)} %select_n.45, bf16[2,256,512]{2,1,0:T(8,128)(2,1)} %bitcast.17, s32[]{:T(128)S(6)} %select_n.44), kind=kLoop, calls=%fused_computation.5 | loop fusion | flops 655360 | bytes 2359304 | tf_op jit(solution)/shard_map/convert_element_type | solution.py:464
  70.1 1.6 %collective-permute-start.16 = (bf16[256,512]{1,0:T(8,128)(2,1)S(1)}, bf16[256,512]{1,0:T(8,128)(2,1)S(1)}, u32[]{:S(2)}, u32[]{:S(2)}) collective-permute-start(bf16[256,512]{1,0:T(8,128)(2,1)S(1)} %get-tuple-element.104), channel_id=1, source_target_pairs={{0,1},{1,0},{2,3},{3,2},{4,5},{5,4},{6,7},{7,6},{8,9},{9,8},{10,11... | collective-permute-start | bytes 786440 | tf_op jit(solution)/shard_map/ppermute | solution.py:489
  71.9 1.6 %collective-permute-start.13 = (bf16[256,512]{1,0:T(8,128)(2,1)S(1)}, bf16[256,512]{1,0:T(8,128)(2,1)S(1)}, u32[]{:S(2)}, u32[]{:S(2)}) collective-permute-start(bf16[256,512]{1,0:T(8,128)(2,1)S(1)} %get-tuple-element.106), channel_id=1, source_target_pairs={{0,2},{1,3},{2,0},{3,1},{4,6},{5,7},{6,4},{7,5},{8,10},{9,11},{10,... | collective-permute-start | bytes 786440 | tf_op jit(solution)/shard_map/ppermute | solution.py:489
  73.5 0.7 add_select_fusion
  74.2 3.8 %collective-permute-done.16 = bf16[256,512]{1,0:T(8,128)(2,1)S(1)} collective-permute-done((bf16[256,512]{1,0:T(8,128)(2,1)S(1)}, bf16[256,512]{1,0:T(8,128)(2,1)S(1)}, u32[]{:S(2)}, u32[]{:S(2)}) %collective-permute-start.16) | collective-permute-done | bytes 262176 | tf_op jit(solution)/shard_map/ppermute | solution.py:489
  78.0 0.8 fusion.3
  78.8 1.3 %collective-permute-done.13 = bf16[256,512]{1,0:T(8,128)(2,1)S(1)} collective-permute-done((bf16[256,512]{1,0:T(8,128)(2,1)S(1)}, bf16[256,512]{1,0:T(8,128)(2,1)S(1)}, u32[]{:S(2)}, u32[]{:S(2)}) %collective-permute-start.13) | collective-permute-done | bytes 262176 | tf_op jit(solution)/shard_map/ppermute | solution.py:489
  80.1 0.8 fusion.2
  80.8 4.9 %all-to-all-start = ((bf16[8,16,512]{2,1,0:T(8,128)(2,1)}), bf16[8,16,512]{2,1,0:T(8,128)(2,1)S(1)}, u32[]{:S(2)}, u32[]{:S(2)}) async-start(bf16[8,16,512]{2,1,0:T(8,128)(2,1)} %bitcast.24), calls=%async_computation | async-start | bytes 262144 | tf_op jit(solution)/shard_map/all_to_all | solution.py:496
  85.7 2.9 %collective-permute-start.17 = (bf16[128,512]{1,0:T(8,128)(2,1)S(1)}, bf16[128,512]{1,0:T(8,128)(2,1)S(1)}, u32[]{:S(2)}, u32[]{:S(2)}) collective-permute-start(bf16[128,512]{1,0:T(8,128)(2,1)S(1)} %get-tuple-element.108), channel_id=1, source_target_pairs={{0,4},{1,5},{2,6},{3,7},{4,0},{5,1},{6,2},{7,3},{8,12},{9,13},{10,... | collective-permute-start | bytes 393224 | tf_op jit(solution)/shard_map/ppermute | solution.py:489
  88.7 12.8 %collective-permute-done.17.second_got = bf16[128,512]{1,0:T(8,128)(2,1)S(1)} collective-permute-done((bf16[128,512]{1,0:T(8,128)(2,1)S(1)}, bf16[128,512]{1,0:T(8,128)(2,1)S(1)}, u32[]{:S(2)}, u32[]{:S(2)}) %collective-permute-start.17) | collective-permute-done | bytes 131104 | tf_op jit(solution)/shard_map/ppermute | solution.py:489
  101.5 2.5 %collective-permute-done.14.first_got = bf16[128,512]{1,0:T(8,128)(2,1)S(1)} collective-permute-done((bf16[128,512]{1,0:T(8,128)(2,1)S(1)}, bf16[128,512]{1,0:T(8,128)(2,1)S(1)}, u32[]{:S(2)}, u32[]{:S(2)}) %collective-permute-start.14) | collective-permute-done | bytes 131104 | tf_op jit(solution)/shard_map/ppermute | solution.py:489
  104.0 0.6 copy-done.14
  104.7 2.0 %join.1 = f32[128,1024]{1,0:T(8,128)} custom-call(f32[128,512]{1,0:T(8,128)} %get-tuple-element.111.first, bf16[128,512]{1,0:T(8,128)(2,1)} %copy-done.14, f32[128,512]{1,0:T(8,128)} %get-tuple-element.109.second, bf16[128,512]{1,0:T(8,128)(2,1)} %copy-done.13), custom_call_target="tpu_custom_call" | custom-call | flops 1024 | bytes 1024 | tf_op jit(solution)/shard_map/join/pallas_call | solution.py:475
  106.6 0.6 convert_reduce_fusion
  (55 shorter events, 1.3 us)
Async XLA Ops:
  0.6 8.4 %copy-start = (bf16[1,4,256,1024]{3,2,1,0:T(8,128)(2,1)S(1)}, bf16[1,4,256,1024]{3,2,1,0:T(8,128)(2,1)}, u32[]{:S(2)}) copy-start(bf16[1,4,256,1024]{3,2,1,0:T(8,128)(2,1)} %param.6) | copy-start | bytes 6291460
  0.7 8.4 %copy-start.1 = (bf16[1,1024,1024]{2,1,0:T(8,128)(2,1)S(1)}, bf16[1,1024,1024]{2,1,0:T(8,128)(2,1)}, u32[]{:S(2)}) copy-start(bf16[1,1024,1024]{2,1,0:T(8,128)(2,1)} %param.7) | copy-start | bytes 6291460
  0.7 8.4 %copy-start.6 = (bf16[128,2048]{1,0:T(8,128)(2,1)S(1)}, bf16[128,2048]{1,0:T(8,128)(2,1)}, u32[]{:S(2)}) copy-start(bf16[128,2048]{1,0:T(8,128)(2,1)} %table_in.7) | copy-start | bytes 1572868
  8.3 4.1 %collective-permute-start.3 = (bf16[256,1024]{1,0:T(8,128)(2,1)}, bf16[256,1024]{1,0:T(8,128)(2,1)S(1)}, u32[]{:S(2)}, u32[]{:S(2)}) collective-permute-start(bf16[256,1024]{1,0:T(8,128)(2,1)} %get-tuple-element.59), channel_id=1, source_target_pairs={{24,16},{25,17},{26,18},{27,19},{28,20},{29,21},{30,22},{31,23}} | collective-permute-start | bytes 1572872 | tf_op jit(solution)/shard_map/ppermute | solution.py:534
  9.1 5.6 %collective-permute-start.2 = (bf16[256,1024]{1,0:T(8,128)(2,1)}, bf16[256,1024]{1,0:T(8,128)(2,1)S(1)}, u32[]{:S(2)}, u32[]{:S(2)}) collective-permute-start(bf16[256,1024]{1,0:T(8,128)(2,1)} %get-tuple-element.58), channel_id=1, source_target_pairs={{24,16},{25,17},{26,18},{27,19},{28,20},{29,21},{30,22},{31,23}} | collective-permute-start | bytes 1572872 | tf_op jit(solution)/shard_map/ppermute | solution.py:534
  10.1 5.4 %collective-permute-start.1 = (bf16[256,1024]{1,0:T(8,128)(2,1)}, bf16[256,1024]{1,0:T(8,128)(2,1)}, u32[]{:S(2)}, u32[]{:S(2)}) collective-permute-start(bf16[256,1024]{1,0:T(8,128)(2,1)} %get-tuple-element.57), channel_id=1, source_target_pairs={{24,16},{25,17},{26,18},{27,19},{28,20},{29,21},{30,22},{31,23}} | collective-permute-start | bytes 1572872 | tf_op jit(solution)/shard_map/ppermute | solution.py:534
  11.7 5.4 %collective-permute-start = (bf16[256,1024]{1,0:T(8,128)(2,1)}, bf16[256,1024]{1,0:T(8,128)(2,1)S(1)}, u32[]{:S(2)}, u32[]{:S(2)}) collective-permute-start(bf16[256,1024]{1,0:T(8,128)(2,1)} %get-tuple-element.56), channel_id=1, source_target_pairs={{24,16},{25,17},{26,18},{27,19},{28,20},{29,21},{30,22},{31,23}} | collective-permute-start | bytes 1572872 | tf_op jit(solution)/shard_map/ppermute | solution.py:534
  12.4 1.6 %copy-start.2 = (bf16[1,1024,1024]{2,1,0:T(8,128)(2,1)S(1)}, bf16[1,1024,1024]{2,1,0:T(8,128)(2,1)}, u32[]{:S(2)}) copy-start(bf16[1,1024,1024]{2,1,0:T(8,128)(2,1)} %param.7) | copy-start | bytes 6291460
  14.1 8.4 %collective-permute-start.6 = (bf16[256,1024]{1,0:T(8,128)(2,1)}, bf16[256,1024]{1,0:T(8,128)(2,1)S(1)}, u32[]{:S(2)}, u32[]{:S(2)}) collective-permute-start(bf16[256,1024]{1,0:T(8,128)(2,1)} %get-tuple-element.68), channel_id=1, source_target_pairs={{16,8},{17,9},{18,10},{19,11},{20,12},{21,13},{22,14},{23,15}} | collective-permute-start | bytes 1572872 | tf_op jit(solution)/shard_map/ppermute | solution.py:534
  14.8 9.0 %collective-permute-start.5 = (bf16[256,1024]{1,0:T(8,128)(2,1)}, bf16[256,1024]{1,0:T(8,128)(2,1)S(1)}, u32[]{:S(2)}, u32[]{:S(2)}) collective-permute-start(bf16[256,1024]{1,0:T(8,128)(2,1)} %get-tuple-element.67), channel_id=1, source_target_pairs={{16,8},{17,9},{18,10},{19,11},{20,12},{21,13},{22,14},{23,15}} | collective-permute-start | bytes 1572872 | tf_op jit(solution)/shard_map/ppermute | solution.py:534
  15.6 9.6 %collective-permute-start.4 = (bf16[256,1024]{1,0:T(8,128)(2,1)}, bf16[256,1024]{1,0:T(8,128)(2,1)}, u32[]{:S(2)}, u32[]{:S(2)}) collective-permute-start(bf16[256,1024]{1,0:T(8,128)(2,1)} %get-tuple-element.66), channel_id=1, source_target_pairs={{16,8},{17,9},{18,10},{19,11},{20,12},{21,13},{22,14},{23,15}} | collective-permute-start | bytes 1572872 | tf_op jit(solution)/shard_map/ppermute | solution.py:534
  17.1 5.3 %copy-start.3 = (bf16[1,1024,1024]{2,1,0:T(8,128)(2,1)S(1)}, bf16[1,1024,1024]{2,1,0:T(8,128)(2,1)}, u32[]{:S(2)}) copy-start(bf16[1,1024,1024]{2,1,0:T(8,128)(2,1)} %param.7) | copy-start | bytes 6291460
  17.1 9.4 %collective-permute-start.10 = (bf16[256,1024]{1,0:T(8,128)(2,1)}, bf16[256,1024]{1,0:T(8,128)(2,1)}, u32[]{:S(2)}, u32[]{:S(2)}) collective-permute-start(bf16[256,1024]{1,0:T(8,128)(2,1)} %get-tuple-element.64.after_hbm), channel_id=1, source_target_pairs={{16,8},{17,9},{18,10},{19,11},{20,12},{21,13},{22,14},{23,15}} | collective-permute-start | bytes 1572872 | tf_op jit(solution)/shard_map/ppermute | solution.py:534
  21.1 1.3 %copy-start.4 = (bf16[1024,1024]{1,0:T(8,128)(2,1)}, bf16[1024,1024]{1,0:T(8,128)(2,1)S(1)}, u32[]{:S(2)}) copy-start(bf16[1024,1024]{1,0:T(8,128)(2,1)S(1)} %get-tuple-element.65.turned) | copy-start | bytes 6291460
  22.5 12.8 %collective-permute-start.9 = (bf16[256,1024]{1,0:T(8,128)(2,1)}, bf16[256,1024]{1,0:T(8,128)(2,1)S(1)}, u32[]{:S(2)}, u32[]{:S(2)}) collective-permute-start(bf16[256,1024]{1,0:T(8,128)(2,1)} %get-tuple-element.75), channel_id=1, source_target_pairs={{8,0},{9,1},{10,2},{11,3},{12,4},{13,5},{14,6},{15,7}} | collective-permute-start | bytes 1572872 | tf_op jit(solution)/shard_map/ppermute | solution.py:534
  23.9 17.2 %collective-permute-start.8 = (bf16[256,1024]{1,0:T(8,128)(2,1)}, bf16[256,1024]{1,0:T(8,128)(2,1)}, u32[]{:S(2)}, u32[]{:S(2)}) collective-permute-start(bf16[256,1024]{1,0:T(8,128)(2,1)} %get-tuple-element.74), channel_id=1, source_target_pairs={{8,0},{9,1},{10,2},{11,3},{12,4},{13,5},{14,6},{15,7}} | collective-permute-start | bytes 1572872 | tf_op jit(solution)/shard_map/ppermute | solution.py:534
  25.2 21.7 %collective-permute-start.7 = (bf16[256,1024]{1,0:T(8,128)(2,1)}, bf16[256,1024]{1,0:T(8,128)(2,1)}, u32[]{:S(2)}, u32[]{:S(2)}) collective-permute-start(bf16[256,1024]{1,0:T(8,128)(2,1)} %get-tuple-element.73), channel_id=1, source_target_pairs={{8,0},{9,1},{10,2},{11,3},{12,4},{13,5},{14,6},{15,7}} | collective-permute-start | bytes 1572872 | tf_op jit(solution)/shard_map/ppermute | solution.py:534
  26.8 26.5 %collective-permute-start.11 = (bf16[256,1024]{1,0:T(8,128)(2,1)}, bf16[256,1024]{1,0:T(8,128)(2,1)S(1)}, u32[]{:S(2)}, u32[]{:S(2)}) collective-permute-start(bf16[256,1024]{1,0:T(8,128)(2,1)} %get-tuple-element.78), channel_id=1, source_target_pairs={{8,0},{9,1},{10,2},{11,3},{12,4},{13,5},{14,6},{15,7}} | collective-permute-start | bytes 1572872 | tf_op jit(solution)/shard_map/ppermute | solution.py:534
  43.2 5.9 %copy-start.5 = (bf16[1024,1024]{1,0:T(8,128)(2,1)S(1)}, bf16[1024,1024]{1,0:T(8,128)(2,1)}, u32[]{:S(2)}) copy-start(bf16[1024,1024]{1,0:T(8,128)(2,1)} %copy-done.4) | copy-start | bytes 6291460
  52.3 1.0 copy-start.9
  53.3 2.9 %copy-start.7 = (f32[512,512]{1,0:T(8,128)}, f32[512,512]{1,0:T(8,128)S(1)}, u32[]{:S(2)}) copy-start(f32[512,512]{1,0:T(8,128)S(1)} %get-tuple-element.79.early_first) | copy-start | bytes 3145732
  53.3 6.0 %copy-start.11 = (bf16[4,1,1024]{2,0,1:T(4,128)(2,1)S(1)}, bf16[4,1,1024]{2,0,1:T(4,128)(2,1)}, u32[]{:S(2)}) copy-start(bf16[4,1,1024]{2,0,1:T(4,128)(2,1)} %param.11) | copy-start | bytes 24580
  53.3 6.0 %copy-start.12 = (s32[4,1,64]{2,1,0:T(1,128)S(1)}, s32[4,1,64]{2,1,0:T(1,128)}, u32[]{:S(2)}) copy-start(s32[4,1,64]{2,1,0:T(1,128)} %index_ref.1) | copy-start | bytes 3076
  56.1 12.7 %collective-permute-start.15 = (bf16[512,512]{1,0:T(8,128)(2,1)}, bf16[512,512]{1,0:T(8,128)(2,1)}, u32[]{:S(2)}, u32[]{:S(2)}) collective-permute-start(bf16[512,512]{1,0:T(8,128)(2,1)} %get-tuple-element.86), channel_id=1, source_target_pairs={{0,2},{1,3},{2,0},{3,1},{4,6},{5,7},{6,4},{7,5},{8,10},{9,11},{10,... | collective-permute-start | bytes 1572872 | tf_op jit(solution)/shard_map/ppermute | solution.py:489
  57.8 13.9 %collective-permute-start.12 = (bf16[512,512]{1,0:T(8,128)(2,1)}, bf16[512,512]{1,0:T(8,128)(2,1)S(1)}, u32[]{:S(2)}, u32[]{:S(2)}) collective-permute-start(bf16[512,512]{1,0:T(8,128)(2,1)} %get-tuple-element.84), channel_id=1, source_target_pairs={{0,1},{1,0},{2,3},{3,2},{4,5},{5,4},{6,7},{7,6},{8,9},{9,8},{10,11... | collective-permute-start | bytes 1572872 | tf_op jit(solution)/shard_map/ppermute | solution.py:489
  59.3 3.0 %copy-start.8 = (f32[512,512]{1,0:T(8,128)S(1)}, f32[512,512]{1,0:T(8,128)}, u32[]{:S(2)}) copy-start(f32[512,512]{1,0:T(8,128)} %copy-done.7) | copy-start | bytes 3145732
  59.3 3.0 %copy-start.10 = (f32[512,512]{1,0:T(8,128)S(1)}, f32[512,512]{1,0:T(8,128)}, u32[]{:S(2)}) copy-start(f32[512,512]{1,0:T(8,128)} %copy-done.9) | copy-start | bytes 3145732
  59.5 14.0 %collective-permute-start.18 = (bf16[128,512]{1,0:T(8,128)(2,1)}, bf16[128,512]{1,0:T(8,128)(2,1)S(1)}, u32[]{:S(2)}, u32[]{:S(2)}) collective-permute-start(bf16[128,512]{1,0:T(8,128)(2,1)} %get-tuple-element.100), channel_id=1, source_target_pairs={{24,0},{25,1},{26,2},{27,3},{28,4},{29,5},{30,6},{31,7}} | collective-permute-start | bytes 393224 | tf_op jit(solution)/shard_map/ppermute | solution.py:548
  60.9 12.6 %collective-permute-start.19 = (bf16[128,512]{1,0:T(8,128)(2,1)}, bf16[128,512]{1,0:T(8,128)(2,1)S(1)}, u32[]{:S(2)}, u32[]{:S(2)}) collective-permute-start(bf16[128,512]{1,0:T(8,128)(2,1)} %get-tuple-element.101), channel_id=1, source_target_pairs={{24,8},{25,9},{26,10},{27,11},{28,12},{29,13},{30,14},{31,15}} | collective-permute-start | bytes 393224 | tf_op jit(solution)/shard_map/ppermute | solution.py:548
  61.6 11.9 %collective-permute-start.20 = (bf16[128,512]{1,0:T(8,128)(2,1)}, bf16[128,512]{1,0:T(8,128)(2,1)S(1)}, u32[]{:S(2)}, u32[]{:S(2)}) collective-permute-start(bf16[128,512]{1,0:T(8,128)(2,1)} %get-tuple-element.102), channel_id=1, source_target_pairs={{24,16},{25,17},{26,18},{27,19},{28,20},{29,21},{30,22},{31,23}} | collective-permute-start | bytes 393224 | tf_op jit(solution)/shard_map/ppermute | solution.py:548
  68.9 4.7 %copy-start.15 = (bf16[128,512]{1,0:T(8,128)(2,1)S(1)}, bf16[128,512]{1,0:T(8,128)(2,1)}, u32[]{:S(2)}) copy-start(bf16[128,512]{1,0:T(8,128)(2,1)} %get-tuple-element.99) | copy-start | bytes 393220
  70.1 7.9 %collective-permute-start.16 = (bf16[256,512]{1,0:T(8,128)(2,1)S(1)}, bf16[256,512]{1,0:T(8,128)(2,1)S(1)}, u32[]{:S(2)}, u32[]{:S(2)}) collective-permute-start(bf16[256,512]{1,0:T(8,128)(2,1)S(1)} %get-tuple-element.104), channel_id=1, source_target_pairs={{0,1},{1,0},{2,3},{3,2},{4,5},{5,4},{6,7},{7,6},{8,9},{9,8},{10,11... | collective-permute-start | bytes 786440 | tf_op jit(solution)/shard_map/ppermute | solution.py:489
  71.9 8.2 %collective-permute-start.13 = (bf16[256,512]{1,0:T(8,128)(2,1)S(1)}, bf16[256,512]{1,0:T(8,128)(2,1)S(1)}, u32[]{:S(2)}, u32[]{:S(2)}) collective-permute-start(bf16[256,512]{1,0:T(8,128)(2,1)S(1)} %get-tuple-element.106), channel_id=1, source_target_pairs={{0,2},{1,3},{2,0},{3,1},{4,6},{5,7},{6,4},{7,5},{8,10},{9,11},{10,... | collective-permute-start | bytes 786440 | tf_op jit(solution)/shard_map/ppermute | solution.py:489
  80.8 25.8 %all-to-all-start = ((bf16[8,16,512]{2,1,0:T(8,128)(2,1)}), bf16[8,16,512]{2,1,0:T(8,128)(2,1)S(1)}, u32[]{:S(2)}, u32[]{:S(2)}) async-start(bf16[8,16,512]{2,1,0:T(8,128)(2,1)} %bitcast.24), calls=%async_computation | async-start | bytes 262144 | tf_op jit(solution)/shard_map/all_to_all | solution.py:496
  85.7 15.8 %collective-permute-start.17 = (bf16[128,512]{1,0:T(8,128)(2,1)S(1)}, bf16[128,512]{1,0:T(8,128)(2,1)S(1)}, u32[]{:S(2)}, u32[]{:S(2)}) collective-permute-start(bf16[128,512]{1,0:T(8,128)(2,1)S(1)} %get-tuple-element.108), channel_id=1, source_target_pairs={{0,4},{1,5},{2,6},{3,7},{4,0},{5,1},{6,2},{7,3},{8,12},{9,13},{10,... | collective-permute-start | bytes 393224 | tf_op jit(solution)/shard_map/ppermute | solution.py:489
  88.6 15.4 %collective-permute-start.14 = (bf16[128,512]{1,0:T(8,128)(2,1)S(1)}, bf16[128,512]{1,0:T(8,128)(2,1)S(1)}, u32[]{:S(2)}, u32[]{:S(2)}) collective-permute-start(bf16[128,512]{1,0:T(8,128)(2,1)S(1)} %get-tuple-element.110), channel_id=1, source_target_pairs={{0,4},{1,5},{2,6},{3,7},{4,0},{5,1},{6,2},{7,3},{8,12},{9,13},{10,... | collective-permute-start | bytes 393224 | tf_op jit(solution)/shard_map/ppermute | solution.py:489
  101.5 2.5 %copy-start.13 = (bf16[128,512]{1,0:T(8,128)(2,1)}, bf16[128,512]{1,0:T(8,128)(2,1)S(1)}, u32[]{:S(2)}) copy-start(bf16[128,512]{1,0:T(8,128)(2,1)S(1)} %collective-permute-done.17.second_got) | copy-start | bytes 393220
  104.0 0.7 copy-start.14

commit v6 on v5

--- a/solution.py
+++ b/solution.py
@@ -464,24 +464,6 @@
     return pick(1 - mine).astype(BF16), pick(mine)
 
 
-def join_kernel(first, first_got, second, second_got, out):
-    half = first.shape[1]
-    out[:, :half] = first[...] + first_got[...].astype(F32)
-    out[:, half:] = second[...] + second_got[...].astype(F32)
-
-
-def join_call(keeps, gots):
-    rows, half = keeps[0].shape
-    return pl.pallas_call(
-        join_kernel,
-        out_shape=jax.ShapeDtypeStruct((rows, 2 * half), F32),
-        in_specs=[VMEM] * 4,
-        out_specs=VMEM,
-        cost_estimate=LIGHT,
-        name="join",
-    )(keeps[0], gots[0], keeps[1], gots[1])
-
-
 def scatter_sums(sends, keeps, table, orders, pairs_of):
     steps = len(orders[0])
     sends, keeps = list(sends), list(keeps)
@@ -491,10 +473,11 @@
             if n + 1 < steps:
                 lead = (2, keeps[c].shape[0] // 2, keeps[c].shape[1])
                 sends[c], keeps[c] = own_half(keeps[c].reshape(lead), gots[c].reshape(lead), bits[n + 1])
-        if n + 2 == steps:
+        if n == 0:
             table, _ = lax.optimization_barrier((table, tuple(sends)))
     blocks = lax.all_to_all(table.reshape(1 << steps, -1, table.shape[1]), "dp", 0, 0)
-    return join_call(keeps, gots), jnp.sum(blocks.astype(F32), axis=0)
+    sums = [keep + got.astype(F32) for keep, got in zip(keeps, gots)]
+    return jnp.concatenate(sums, axis=1), jnp.sum(blocks.astype(F32), axis=0)
 
 
 def body(activations, section_weights, cand_table, cand_index, cand_count, pooled_cotangent):

time: 108 us -> 99.2 us (0.919)
  waiting for transfers between devices: 40 us -> 29.6 us
  starting transfers between devices: 30.2 us -> 32.6 us
  Pallas kernels: 27 us -> 25 us
  local copies, waits for them, and re-layouts: 4.63 us -> 6.38 us
    ppermute x6, waiting for transfers between devices: 25.4 us -> 11.9 us  [scatter_sums(): lax.ppermute(send, 'dp', pairs_of(bits[n]))]
    all_to_all x1, waiting for transfers between devices: 0.01 us -> 3.05 us  [scatter_sums(): lax.all_to_all(table.reshape(1 << steps, -1, table.shape[1]), 'dp', 0, 0)]
    ppermute x6, starting transfers between devices: 9.35 us -> 11.9 us  [scatter_sums(): lax.ppermute(send, 'dp', pairs_of(bits[n]))]
    pallas_call x1 -> x0, Pallas kernels: 1.97 us -> none  [join_call(): pl.pallas_call(join_kernel, out_shape=jax.ShapeDtypeStruct((rows, 2 * hal...]
    unnamed x32 -> x28, local copies, waits for them, and re-layouts: 4.63 us -> 6.38 us
    convert_element_type x4, other arithmetic: 2.92 us -> 1.38 us  [own_half(): return (pick(1 - mine).astype(BF16), pick(mine))]
where the time goes in v6:
time: 99.2 us; the launch traced here: 98.4 us
  starting transfers between devices  32.6 us (33%)
  waiting for transfers between devices  29.6 us (30%)
  Pallas kernels  25 us (25%)
  local copies, waits for them, and re-layouts  6.38 us (6%)
  other arithmetic  3.61 us (4%)
  between operations  1.15 us (1%)
    ppermute x12, waiting for transfers between devices, body(): lax.ppermute(g, 'section', [(source, source - 1)])  14.6 us
    ppermute x12, starting transfers between devices, body(): lax.ppermute(g, 'section', [(source, source - 1)])  13.3 us
    ppermute x6, starting transfers between devices, scatter_sums(): lax.ppermute(send, 'dp', pairs_of(bits[n]))  11.9 us
    ppermute x6, waiting for transfers between devices, scatter_sums(): lax.ppermute(send, 'dp', pairs_of(bits[n]))  11.9 us
    pallas_call x4, Pallas kernels, first_call(): pl.pallas_call(functools.partial(first_kernel, m), out_shape=(block, pltp...  8.11 us
    pallas_call x11, Pallas kernels, hop_call(): pl.pallas_call(functools.partial(hop_kernel, m, with_grad), out_shape=out...  6.86 us
    unnamed x28, local copies, waits for them, and re-layouts  6.38 us
    all_to_all x1, starting transfers between devices, scatter_sums(): lax.all_to_all(table.reshape(1 << steps, -1, table.shape[1]), 'dp', 0, 0)  4.83 us
  transfers between devices with their start and end apart: 22, of which 8 were waited for; matrix products, arithmetic and copies ran while one was open for 3% of the time, Pallas kernels for 15%

profile of v6, /device:TPU:0, one launch (start us, length us, event | category | flops | bytes accessed | tf_op | source)
XLA Modules:
  0.0 98.4 jit_solution(7781379825306065207)
XLA Ops:
  0.7 7.6 %first.4 = (bf16[256,1024]{1,0:T(8,128)(2,1)}, bf16[4,256,1024]{2,1,0:T(8,128)(2,1)}, bf16[1024,256]{1,0:T(8,128)(2,1)}, bf16[1024,256]{1,0:T(8,128)(2,1)}, bf16[256,1024]{1,0:T(8,128)(2,1)}) custom-call(s32[1]{0:T(128)} %bitcast.4.flag_ref, s32[1,4]{1,0:T(1,128)} %bitcast.79, bf16[4,256,1024]{2,1,0:T(8,128)(2,1)} %bitcast.32, bf16[1024,1024]{1,0:T(8,128)(2,1)} %bitcast.48, ...), custom_call_target="tpu_custom_call" | custom-call | flops 1024 | bytes 1024 | tf_op jit(solution)/shard_map/first/pallas_call | solution.py:179
  8.3 0.7 collective-permute-start.3
  9.1 0.7 collective-permute-start.2
  9.8 0.3 first.6
  10.1 1.5 %collective-permute-start.1 = (bf16[256,1024]{1,0:T(8,128)(2,1)}, bf16[256,1024]{1,0:T(8,128)(2,1)}, u32[]{:S(2)}, u32[]{:S(2)}) collective-permute-start(bf16[256,1024]{1,0:T(8,128)(2,1)} %get-tuple-element.57), channel_id=1, source_target_pairs={{24,16},{25,17},{26,18},{27,19},{28,20},{29,21},{30,22},{31,23}} | collective-permute-start | bytes 1572872 | tf_op jit(solution)/shard_map/ppermute | solution.py:517
  11.7 0.7 collective-permute-start
  12.5 1.6 %copy-done.2 = bf16[1,1024,1024]{2,1,0:T(8,128)(2,1)S(1)} copy-done((bf16[1,1024,1024]{2,1,0:T(8,128)(2,1)S(1)}, bf16[1,1024,1024]{2,1,0:T(8,128)(2,1)}, u32[]{:S(2)}) %copy-start.2) | copy-done | bytes 2097176
  14.1 0.7 collective-permute-start.6
  14.9 0.7 collective-permute-start.5
  15.6 1.5 %collective-permute-start.4 = (bf16[256,1024]{1,0:T(8,128)(2,1)}, bf16[256,1024]{1,0:T(8,128)(2,1)}, u32[]{:S(2)}, u32[]{:S(2)}) collective-permute-start(bf16[256,1024]{1,0:T(8,128)(2,1)} %get-tuple-element.66), channel_id=1, source_target_pairs={{16,8},{17,9},{18,10},{19,11},{20,12},{21,13},{22,14},{23,15}} | collective-permute-start | bytes 1572872 | tf_op jit(solution)/shard_map/ppermute | solution.py:517
  17.2 1.6 %collective-permute-start.10 = (bf16[256,1024]{1,0:T(8,128)(2,1)}, bf16[256,1024]{1,0:T(8,128)(2,1)}, u32[]{:S(2)}, u32[]{:S(2)}) collective-permute-start(bf16[256,1024]{1,0:T(8,128)(2,1)} %get-tuple-element.64.after_hbm), channel_id=1, source_target_pairs={{16,8},{17,9},{18,10},{19,11},{20,12},{21,13},{22,14},{23,15}} | collective-permute-start | bytes 1572872 | tf_op jit(solution)/shard_map/ppermute | solution.py:517
  18.8 2.3 %turn.1 = (bf16[1024,1024]{1,0:T(8,128)(2,1)S(1)}, bf16[16,128]{1,0:T(8,128)(2,1)}) custom-call(bf16[4,256,1024]{2,1,0:T(8,128)(2,1)} %bitcast.38, bf16[256,1024]{1,0:T(8,128)(2,1)} %get-tuple-element.64.after_hbm), custom_call_target="tpu_custom_call" | custom-call | flops 1024 | bytes 1024 | tf_op jit(solution)/shard_map/turn/pallas_call | solution.py:360
  21.1 1.3 %copy-done.4 = bf16[1024,1024]{1,0:T(8,128)(2,1)} copy-done((bf16[1024,1024]{1,0:T(8,128)(2,1)}, bf16[1024,1024]{1,0:T(8,128)(2,1)S(1)}, u32[]{:S(2)}) %copy-start.4) | copy-done | bytes 2097176
  22.5 1.3 %collective-permute-start.9 = (bf16[256,1024]{1,0:T(8,128)(2,1)}, bf16[256,1024]{1,0:T(8,128)(2,1)S(1)}, u32[]{:S(2)}, u32[]{:S(2)}) collective-permute-start(bf16[256,1024]{1,0:T(8,128)(2,1)} %get-tuple-element.75), channel_id=1, source_target_pairs={{8,0},{9,1},{10,2},{11,3},{12,4},{13,5},{14,6},{15,7}} | collective-permute-start | bytes 1572872 | tf_op jit(solution)/shard_map/ppermute | solution.py:517
  23.9 1.3 %collective-permute-start.8 = (bf16[256,1024]{1,0:T(8,128)(2,1)}, bf16[256,1024]{1,0:T(8,128)(2,1)}, u32[]{:S(2)}, u32[]{:S(2)}) collective-permute-start(bf16[256,1024]{1,0:T(8,128)(2,1)} %get-tuple-element.74), channel_id=1, source_target_pairs={{8,0},{9,1},{10,2},{11,3},{12,4},{13,5},{14,6},{15,7}} | collective-permute-start | bytes 1572872 | tf_op jit(solution)/shard_map/ppermute | solution.py:517
  25.2 1.3 %collective-permute-start.7 = (bf16[256,1024]{1,0:T(8,128)(2,1)}, bf16[256,1024]{1,0:T(8,128)(2,1)}, u32[]{:S(2)}, u32[]{:S(2)}) collective-permute-start(bf16[256,1024]{1,0:T(8,128)(2,1)} %get-tuple-element.73), channel_id=1, source_target_pairs={{8,0},{9,1},{10,2},{11,3},{12,4},{13,5},{14,6},{15,7}} | collective-permute-start | bytes 1572872 | tf_op jit(solution)/shard_map/ppermute | solution.py:517
  26.8 1.3 %collective-permute-start.11 = (bf16[256,1024]{1,0:T(8,128)(2,1)}, bf16[256,1024]{1,0:T(8,128)(2,1)S(1)}, u32[]{:S(2)}, u32[]{:S(2)}) collective-permute-start(bf16[256,1024]{1,0:T(8,128)(2,1)} %get-tuple-element.78), channel_id=1, source_target_pairs={{8,0},{9,1},{10,2},{11,3},{12,4},{13,5},{14,6},{15,7}} | collective-permute-start | bytes 1572872 | tf_op jit(solution)/shard_map/ppermute | solution.py:517
  28.1 7.2 %collective-permute-done.9.came_hbm = bf16[256,1024]{1,0:T(8,128)(2,1)S(1)} collective-permute-done((bf16[256,1024]{1,0:T(8,128)(2,1)}, bf16[256,1024]{1,0:T(8,128)(2,1)S(1)}, u32[]{:S(2)}, u32[]{:S(2)}) %collective-permute-start.9) | collective-permute-done | bytes 524320 | tf_op jit(solution)/shard_map/ppermute | solution.py:517
  35.3 2.0 %end.3.delta_in = bf16[4,256,1024]{2,1,0:T(8,128)(2,1)} custom-call(s32[1]{0:T(128)} %bitcast.flag_ref, bf16[256,1024]{1,0:T(8,128)(2,1)S(1)} %collective-permute-done.9.came_hbm, bf16[4,256,1024]{2,1,0:T(8,128)(2,1)} %get-tuple-element.77.delta_in, bf16[1024,1024]{1,0:T(8,128)(2,1)} %bitcast.49, ...), custom_call_target="tpu_custom_call", output_to_operand_aliasing={{}: (2, {})} | custom-call | flops 1024 | bytes 1024 | tf_op jit(solution)/shard_map/end/pallas_call | solution.py:321
  37.3 3.7 %collective-permute-done.8.came_hbm = bf16[256,1024]{1,0:T(8,128)(2,1)} collective-permute-done((bf16[256,1024]{1,0:T(8,128)(2,1)}, bf16[256,1024]{1,0:T(8,128)(2,1)}, u32[]{:S(2)}, u32[]{:S(2)}) %collective-permute-start.8) | collective-permute-done | bytes 524320 | tf_op jit(solution)/shard_map/ppermute | solution.py:517
  41.0 2.1 %end.4.delta_in = bf16[4,256,1024]{2,1,0:T(8,128)(2,1)} custom-call(s32[1]{0:T(128)} %bitcast.flag_ref, bf16[256,1024]{1,0:T(8,128)(2,1)} %collective-permute-done.8.came_hbm, bf16[4,256,1024]{2,1,0:T(8,128)(2,1)} %end.3.delta_in, bf16[1024,1024]{1,0:T(8,128)(2,1)} %bitcast.50, bf16[4,256,1024]{2,1,0:T(8,128)(2,1)} %bitcast.43), custom_call_target="tpu_custom_call", output_to_operand_aliasing={{}: (2, {})} | custom-call | flops 1024 | bytes 1024 | tf_op jit(solution)/shard_map/end/pallas_call | solution.py:321
  43.2 3.7 %collective-permute-done.7.came_hbm = bf16[256,1024]{1,0:T(8,128)(2,1)} collective-permute-done((bf16[256,1024]{1,0:T(8,128)(2,1)}, bf16[256,1024]{1,0:T(8,128)(2,1)}, u32[]{:S(2)}, u32[]{:S(2)}) %collective-permute-start.7) | collective-permute-done | bytes 524320 | tf_op jit(solution)/shard_map/ppermute | solution.py:517
  46.9 2.1 %end.5.delta_hbm = bf16[4,256,1024]{2,1,0:T(8,128)(2,1)} custom-call(s32[1]{0:T(128)} %bitcast.flag_ref, bf16[256,1024]{1,0:T(8,128)(2,1)} %collective-permute-done.7.came_hbm, bf16[4,256,1024]{2,1,0:T(8,128)(2,1)} %end.4.delta_in, bf16[1024,1024]{1,0:T(8,128)(2,1)} %bitcast.51, bf16[4,256,1024]{2,1,0:T(8,128)(2,1)} %bitcast.44), custom_call_target="tpu_custom_call", output_to_operand_aliasing={{}: (2, {})} | custom-call | flops 1024 | bytes 1024 | tf_op jit(solution)/shard_map/end/pallas_call | solution.py:321
  49.1 3.2 %early.1 = (f32[512,512]{1,0:T(8,128)S(1)}, f32[512,512]{1,0:T(8,128)S(1)}, f32[512,512]{1,0:T(8,128)S(1)}, f32[512,512]{1,0:T(8,128)S(1)}) custom-call(s32[1]{0:T(128)} %bitcast.1.number_ref, bf16[1024,1024]{1,0:T(8,128)(2,1)S(1)} %copy-done.5, bf16[4,256,1024]{2,1,0:T(8,128)(2,1)} %end.5.delta_hbm), custom_call_target="tpu_custom_call" | custom-call | flops 1024 | bytes 1024 | tf_op jit(solution)/shard_map/early/pallas_call | solution.py:403
  52.3 1.0 %copy-done.9 = f32[512,512]{1,0:T(8,128)} copy-done((f32[512,512]{1,0:T(8,128)}, f32[512,512]{1,0:T(8,128)S(1)}, u32[]{:S(2)}) %copy-start.9) | copy-done | bytes 1048600
  53.3 2.8 %weight.3 = (bf16[512,512]{1,0:T(8,128)(2,1)}, bf16[512,512]{1,0:T(8,128)(2,1)}) custom-call(s32[1]{0:T(128)} %bitcast.flag_ref, s32[1]{0:T(128)} %bitcast.1.number_ref, bf16[1024,1024]{1,0:T(8,128)(2,1)S(1)} %copy-done.5, bf16[4,256,1024]{2,1,0:T(8,128)(2,1)} %end.5.delta_hbm, bf16[256,1024]{1,0:T(8,128)(2,1)S(1)} %collective-permute-done.11.came, ...), custom_call_target="tpu_custom_call" | custom-call | flops 1024 | bytes 1024 | tf_op jit(solution)/shard_map/weight/pallas_call | solution.py:444
  56.1 1.6 %collective-permute-start.12 = (bf16[512,512]{1,0:T(8,128)(2,1)}, bf16[512,512]{1,0:T(8,128)(2,1)}, u32[]{:S(2)}, u32[]{:S(2)}) collective-permute-start(bf16[512,512]{1,0:T(8,128)(2,1)} %get-tuple-element.84), channel_id=1, source_target_pairs={{0,1},{1,0},{2,3},{3,2},{4,5},{5,4},{6,7},{7,6},{8,9},{9,8},{10,11... | collective-permute-start | bytes 1572872 | tf_op jit(solution)/shard_map/ppermute | solution.py:471
  57.7 1.6 %collective-permute-start.15 = (bf16[512,512]{1,0:T(8,128)(2,1)}, bf16[512,512]{1,0:T(8,128)(2,1)S(1)}, u32[]{:S(2)}, u32[]{:S(2)}) collective-permute-start(bf16[512,512]{1,0:T(8,128)(2,1)} %get-tuple-element.86), channel_id=1, source_target_pairs={{0,2},{1,3},{2,0},{3,1},{4,6},{5,7},{6,4},{7,5},{8,10},{9,11},{10,... | collective-permute-start | bytes 1572872 | tf_op jit(solution)/shard_map/ppermute | solution.py:471
  59.4 1.3 %collective-permute-start.18 = (bf16[128,512]{1,0:T(8,128)(2,1)}, bf16[128,512]{1,0:T(8,128)(2,1)S(1)}, u32[]{:S(2)}, u32[]{:S(2)}) collective-permute-start(bf16[128,512]{1,0:T(8,128)(2,1)} %get-tuple-element.100), channel_id=1, source_target_pairs={{24,0},{25,1},{26,2},{27,3},{28,4},{29,5},{30,6},{31,7}} | collective-permute-start | bytes 393224 | tf_op jit(solution)/shard_map/ppermute | solution.py:531
  60.7 0.7 collective-permute-start.19
  61.4 0.7 collective-permute-start.20
  62.1 1.2 %copy-done.8 = f32[512,512]{1,0:T(8,128)S(1)} copy-done((f32[512,512]{1,0:T(8,128)S(1)}, f32[512,512]{1,0:T(8,128)}, u32[]{:S(2)}) %copy-start.8) | copy-done | bytes 1048600
  63.3 1.2 %copy-done.10 = f32[512,512]{1,0:T(8,128)S(1)} copy-done((f32[512,512]{1,0:T(8,128)S(1)}, f32[512,512]{1,0:T(8,128)}, u32[]{:S(2)}) %copy-start.10) | copy-done | bytes 1048600
  64.6 1.6 %weight.2 = (f32[512,512]{1,0:T(8,128)S(1)}, f32[512,512]{1,0:T(8,128)S(1)}) custom-call(s32[1]{0:T(128)} %bitcast.flag_ref, s32[1]{0:T(128)} %bitcast.1.number_ref, bf16[1024,1024]{1,0:T(8,128)(2,1)S(1)} %copy-done.5, bf16[4,256,1024]{2,1,0:T(8,128)(2,1)} %end.5.delta_hbm, bf16[256,1024]{1,0:T(8,128)(2,1)S(1)} %collective-permute-done.11.came, ...), custom_call_target="tpu_custom_call" | custom-call | flops 1024 | bytes 1024 | tf_op jit(solution)/shard_map/weight/pallas_call | solution.py:444
  66.2 2.7 %collective-permute-done.12 = bf16[512,512]{1,0:T(8,128)(2,1)} collective-permute-done((bf16[512,512]{1,0:T(8,128)(2,1)}, bf16[512,512]{1,0:T(8,128)(2,1)}, u32[]{:S(2)}, u32[]{:S(2)}) %collective-permute-start.12) | collective-permute-done | bytes 524320 | tf_op jit(solution)/shard_map/ppermute | solution.py:471
  68.9 1.2 %fusion = (bf16[256,512]{1,0:T(8,128)(2,1)S(1)}, f32[1,256,512]{2,1,0:T(8,128)S(1)}) fusion(f32[2,256,512]{2,1,0:T(8,128)S(1)} %bitcast.64, s32[]{:T(128)S(6)} %select_n.42, bf16[2,256,512]{2,1,0:T(8,128)(2,1)} %bitcast.10, s32[]{:T(128)S(6)} %select_n.40), kind=kLoop, calls=%fused_computation.5 | loop fusion | flops 655360 | bytes 2359304 | tf_op jit(solution)/shard_map/convert_element_type | solution.py:464
  70.0 1.6 %collective-permute-start.13 = (bf16[256,512]{1,0:T(8,128)(2,1)S(1)}, bf16[256,512]{1,0:T(8,128)(2,1)S(1)}, u32[]{:S(2)}, u32[]{:S(2)}) collective-permute-start(bf16[256,512]{1,0:T(8,128)(2,1)S(1)} %get-tuple-element.104), channel_id=1, source_target_pairs={{0,2},{1,3},{2,0},{3,1},{4,6},{5,7},{6,4},{7,5},{8,10},{9,11},{10,... | collective-permute-start | bytes 786440 | tf_op jit(solution)/shard_map/ppermute | solution.py:471
  71.7 0.7 add_select_fusion
  72.6 4.8 %all-to-all-start = ((bf16[8,16,512]{2,1,0:T(8,128)(2,1)}), bf16[8,16,512]{2,1,0:T(8,128)(2,1)S(1)}, u32[]{:S(2)}, u32[]{:S(2)}) async-start(bf16[8,16,512]{2,1,0:T(8,128)(2,1)} %bitcast.24), calls=%async_computation | async-start | bytes 262144 | tf_op jit(solution)/shard_map/all_to_all | solution.py:478
  77.4 2.0 %collective-permute-start.16 = (bf16[256,512]{1,0:T(8,128)(2,1)S(1)}, bf16[256,512]{1,0:T(8,128)(2,1)S(1)}, u32[]{:S(2)}, u32[]{:S(2)}) collective-permute-start(bf16[256,512]{1,0:T(8,128)(2,1)S(1)} %get-tuple-element.106), channel_id=1, source_target_pairs={{0,1},{1,0},{2,3},{3,2},{4,5},{5,4},{6,7},{7,6},{8,9},{9,8},{10,11... | collective-permute-start | bytes 786440 | tf_op jit(solution)/shard_map/ppermute | solution.py:471
  79.4 2.4 %collective-permute-start.14 = (bf16[128,512]{1,0:T(8,128)(2,1)S(1)}, bf16[128,512]{1,0:T(8,128)(2,1)S(1)}, u32[]{:S(2)}, u32[]{:S(2)}) collective-permute-start(bf16[128,512]{1,0:T(8,128)(2,1)S(1)} %fusion.2), channel_id=1, source_target_pairs={{0,4},{1,5},{2,6},{3,7},{4,0},{5,1},{6,2},{7,3},{8,12},{9,13},{10,... | collective-permute-start | bytes 393224 | tf_op jit(solution)/shard_map/ppermute | solution.py:471
  81.9 3.0 %all-to-all-done = bf16[8,16,512]{2,1,0:T(8,128)(2,1)S(1)} async-done(((bf16[8,16,512]{2,1,0:T(8,128)(2,1)}), bf16[8,16,512]{2,1,0:T(8,128)(2,1)S(1)}, u32[]{:S(2)}, u32[]{:S(2)}) %all-to-all-start) | async-done | bytes 131104 | tf_op jit(solution)/shard_map/all_to_all | solution.py:478
  84.9 0.6 convert_reduce_fusion
  85.6 1.9 %collective-permute-done.16 = bf16[256,512]{1,0:T(8,128)(2,1)S(1)} collective-permute-done((bf16[256,512]{1,0:T(8,128)(2,1)S(1)}, bf16[256,512]{1,0:T(8,128)(2,1)S(1)}, u32[]{:S(2)}, u32[]{:S(2)}) %collective-permute-start.16) | collective-permute-done | bytes 262176 | tf_op jit(solution)/shard_map/ppermute | solution.py:471
  87.5 2.7 %collective-permute-start.17 = (bf16[128,512]{1,0:T(8,128)(2,1)S(1)}, bf16[128,512]{1,0:T(8,128)(2,1)S(1)}, u32[]{:S(2)}, u32[]{:S(2)}) collective-permute-start(bf16[128,512]{1,0:T(8,128)(2,1)S(1)} %fusion.3), channel_id=1, source_target_pairs={{0,4},{1,5},{2,6},{3,7},{4,0},{5,1},{6,2},{7,3},{8,12},{9,13},{10,... | collective-permute-start | bytes 393224 | tf_op jit(solution)/shard_map/ppermute | solution.py:471
  90.2 0.3 collective-permute-done.14
  90.6 6.9 %collective-permute-done.17 = bf16[128,512]{1,0:T(8,128)(2,1)S(1)} collective-permute-done((bf16[128,512]{1,0:T(8,128)(2,1)S(1)}, bf16[128,512]{1,0:T(8,128)(2,1)S(1)}, u32[]{:S(2)}, u32[]{:S(2)}) %collective-permute-start.17) | collective-permute-done | bytes 131104 | tf_op jit(solution)/shard_map/ppermute | solution.py:471
  97.5 0.8 maximum_bitcast_fusion
  (53 shorter events, 1.3 us)
Async XLA Ops:
  0.6 8.4 %copy-start = (bf16[1,4,256,1024]{3,2,1,0:T(8,128)(2,1)S(1)}, bf16[1,4,256,1024]{3,2,1,0:T(8,128)(2,1)}, u32[]{:S(2)}) copy-start(bf16[1,4,256,1024]{3,2,1,0:T(8,128)(2,1)} %param.6) | copy-start | bytes 6291460
  0.7 8.4 %copy-start.1 = (bf16[1,1024,1024]{2,1,0:T(8,128)(2,1)S(1)}, bf16[1,1024,1024]{2,1,0:T(8,128)(2,1)}, u32[]{:S(2)}) copy-start(bf16[1,1024,1024]{2,1,0:T(8,128)(2,1)} %param.7) | copy-start | bytes 6291460
  0.7 8.3 %copy-start.6 = (bf16[128,2048]{1,0:T(8,128)(2,1)S(1)}, bf16[128,2048]{1,0:T(8,128)(2,1)}, u32[]{:S(2)}) copy-start(bf16[128,2048]{1,0:T(8,128)(2,1)} %table_in.7) | copy-start | bytes 1572868
  8.3 4.2 %collective-permute-start.3 = (bf16[256,1024]{1,0:T(8,128)(2,1)}, bf16[256,1024]{1,0:T(8,128)(2,1)S(1)}, u32[]{:S(2)}, u32[]{:S(2)}) collective-permute-start(bf16[256,1024]{1,0:T(8,128)(2,1)} %get-tuple-element.59), channel_id=1, source_target_pairs={{24,16},{25,17},{26,18},{27,19},{28,20},{29,21},{30,22},{31,23}} | collective-permute-start | bytes 1572872 | tf_op jit(solution)/shard_map/ppermute | solution.py:517
  9.1 5.7 %collective-permute-start.2 = (bf16[256,1024]{1,0:T(8,128)(2,1)}, bf16[256,1024]{1,0:T(8,128)(2,1)S(1)}, u32[]{:S(2)}, u32[]{:S(2)}) collective-permute-start(bf16[256,1024]{1,0:T(8,128)(2,1)} %get-tuple-element.58), channel_id=1, source_target_pairs={{24,16},{25,17},{26,18},{27,19},{28,20},{29,21},{30,22},{31,23}} | collective-permute-start | bytes 1572872 | tf_op jit(solution)/shard_map/ppermute | solution.py:517
  10.1 5.4 %collective-permute-start.1 = (bf16[256,1024]{1,0:T(8,128)(2,1)}, bf16[256,1024]{1,0:T(8,128)(2,1)}, u32[]{:S(2)}, u32[]{:S(2)}) collective-permute-start(bf16[256,1024]{1,0:T(8,128)(2,1)} %get-tuple-element.57), channel_id=1, source_target_pairs={{24,16},{25,17},{26,18},{27,19},{28,20},{29,21},{30,22},{31,23}} | collective-permute-start | bytes 1572872 | tf_op jit(solution)/shard_map/ppermute | solution.py:517
  11.7 5.4 %collective-permute-start = (bf16[256,1024]{1,0:T(8,128)(2,1)}, bf16[256,1024]{1,0:T(8,128)(2,1)S(1)}, u32[]{:S(2)}, u32[]{:S(2)}) collective-permute-start(bf16[256,1024]{1,0:T(8,128)(2,1)} %get-tuple-element.56), channel_id=1, source_target_pairs={{24,16},{25,17},{26,18},{27,19},{28,20},{29,21},{30,22},{31,23}} | collective-permute-start | bytes 1572872 | tf_op jit(solution)/shard_map/ppermute | solution.py:517
  12.5 1.6 %copy-start.2 = (bf16[1,1024,1024]{2,1,0:T(8,128)(2,1)S(1)}, bf16[1,1024,1024]{2,1,0:T(8,128)(2,1)}, u32[]{:S(2)}) copy-start(bf16[1,1024,1024]{2,1,0:T(8,128)(2,1)} %param.7) | copy-start | bytes 6291460
  14.1 8.3 %collective-permute-start.6 = (bf16[256,1024]{1,0:T(8,128)(2,1)}, bf16[256,1024]{1,0:T(8,128)(2,1)S(1)}, u32[]{:S(2)}, u32[]{:S(2)}) collective-permute-start(bf16[256,1024]{1,0:T(8,128)(2,1)} %get-tuple-element.68), channel_id=1, source_target_pairs={{16,8},{17,9},{18,10},{19,11},{20,12},{21,13},{22,14},{23,15}} | collective-permute-start | bytes 1572872 | tf_op jit(solution)/shard_map/ppermute | solution.py:517
  14.9 8.9 %collective-permute-start.5 = (bf16[256,1024]{1,0:T(8,128)(2,1)}, bf16[256,1024]{1,0:T(8,128)(2,1)S(1)}, u32[]{:S(2)}, u32[]{:S(2)}) collective-permute-start(bf16[256,1024]{1,0:T(8,128)(2,1)} %get-tuple-element.67), channel_id=1, source_target_pairs={{16,8},{17,9},{18,10},{19,11},{20,12},{21,13},{22,14},{23,15}} | collective-permute-start | bytes 1572872 | tf_op jit(solution)/shard_map/ppermute | solution.py:517
  15.6 9.5 %collective-permute-start.4 = (bf16[256,1024]{1,0:T(8,128)(2,1)}, bf16[256,1024]{1,0:T(8,128)(2,1)}, u32[]{:S(2)}, u32[]{:S(2)}) collective-permute-start(bf16[256,1024]{1,0:T(8,128)(2,1)} %get-tuple-element.66), channel_id=1, source_target_pairs={{16,8},{17,9},{18,10},{19,11},{20,12},{21,13},{22,14},{23,15}} | collective-permute-start | bytes 1572872 | tf_op jit(solution)/shard_map/ppermute | solution.py:517
  17.2 5.3 %copy-start.3 = (bf16[1,1024,1024]{2,1,0:T(8,128)(2,1)S(1)}, bf16[1,1024,1024]{2,1,0:T(8,128)(2,1)}, u32[]{:S(2)}) copy-start(bf16[1,1024,1024]{2,1,0:T(8,128)(2,1)} %param.7) | copy-start | bytes 6291460
  17.2 9.4 %collective-permute-start.10 = (bf16[256,1024]{1,0:T(8,128)(2,1)}, bf16[256,1024]{1,0:T(8,128)(2,1)}, u32[]{:S(2)}, u32[]{:S(2)}) collective-permute-start(bf16[256,1024]{1,0:T(8,128)(2,1)} %get-tuple-element.64.after_hbm), channel_id=1, source_target_pairs={{16,8},{17,9},{18,10},{19,11},{20,12},{21,13},{22,14},{23,15}} | collective-permute-start | bytes 1572872 | tf_op jit(solution)/shard_map/ppermute | solution.py:517
  21.1 1.3 %copy-start.4 = (bf16[1024,1024]{1,0:T(8,128)(2,1)}, bf16[1024,1024]{1,0:T(8,128)(2,1)S(1)}, u32[]{:S(2)}) copy-start(bf16[1024,1024]{1,0:T(8,128)(2,1)S(1)} %get-tuple-element.65.turned) | copy-start | bytes 6291460
  22.5 12.8 %collective-permute-start.9 = (bf16[256,1024]{1,0:T(8,128)(2,1)}, bf16[256,1024]{1,0:T(8,128)(2,1)S(1)}, u32[]{:S(2)}, u32[]{:S(2)}) collective-permute-start(bf16[256,1024]{1,0:T(8,128)(2,1)} %get-tuple-element.75), channel_id=1, source_target_pairs={{8,0},{9,1},{10,2},{11,3},{12,4},{13,5},{14,6},{15,7}} | collective-permute-start | bytes 1572872 | tf_op jit(solution)/shard_map/ppermute | solution.py:517
  23.9 17.2 %collective-permute-start.8 = (bf16[256,1024]{1,0:T(8,128)(2,1)}, bf16[256,1024]{1,0:T(8,128)(2,1)}, u32[]{:S(2)}, u32[]{:S(2)}) collective-permute-start(bf16[256,1024]{1,0:T(8,128)(2,1)} %get-tuple-element.74), channel_id=1, source_target_pairs={{8,0},{9,1},{10,2},{11,3},{12,4},{13,5},{14,6},{15,7}} | collective-permute-start | bytes 1572872 | tf_op jit(solution)/shard_map/ppermute | solution.py:517
  25.2 21.7 %collective-permute-start.7 = (bf16[256,1024]{1,0:T(8,128)(2,1)}, bf16[256,1024]{1,0:T(8,128)(2,1)}, u32[]{:S(2)}, u32[]{:S(2)}) collective-permute-start(bf16[256,1024]{1,0:T(8,128)(2,1)} %get-tuple-element.73), channel_id=1, source_target_pairs={{8,0},{9,1},{10,2},{11,3},{12,4},{13,5},{14,6},{15,7}} | collective-permute-start | bytes 1572872 | tf_op jit(solution)/shard_map/ppermute | solution.py:517
  26.8 26.5 %collective-permute-start.11 = (bf16[256,1024]{1,0:T(8,128)(2,1)}, bf16[256,1024]{1,0:T(8,128)(2,1)S(1)}, u32[]{:S(2)}, u32[]{:S(2)}) collective-permute-start(bf16[256,1024]{1,0:T(8,128)(2,1)} %get-tuple-element.78), channel_id=1, source_target_pairs={{8,0},{9,1},{10,2},{11,3},{12,4},{13,5},{14,6},{15,7}} | collective-permute-start | bytes 1572872 | tf_op jit(solution)/shard_map/ppermute | solution.py:517
  43.2 5.9 %copy-start.5 = (bf16[1024,1024]{1,0:T(8,128)(2,1)S(1)}, bf16[1024,1024]{1,0:T(8,128)(2,1)}, u32[]{:S(2)}) copy-start(bf16[1024,1024]{1,0:T(8,128)(2,1)} %copy-done.4) | copy-start | bytes 6291460
  52.2 1.0 %copy-start.9 = (f32[512,512]{1,0:T(8,128)}, f32[512,512]{1,0:T(8,128)S(1)}, u32[]{:S(2)}) copy-start(f32[512,512]{1,0:T(8,128)S(1)} %get-tuple-element.80.early_second) | copy-start | bytes 3145732
  53.2 2.9 %copy-start.7 = (f32[512,512]{1,0:T(8,128)}, f32[512,512]{1,0:T(8,128)S(1)}, u32[]{:S(2)}) copy-start(f32[512,512]{1,0:T(8,128)S(1)} %get-tuple-element.79.early_first) | copy-start | bytes 3145732
  53.3 6.0 %copy-start.11 = (bf16[4,1,1024]{2,0,1:T(4,128)(2,1)S(1)}, bf16[4,1,1024]{2,0,1:T(4,128)(2,1)}, u32[]{:S(2)}) copy-start(bf16[4,1,1024]{2,0,1:T(4,128)(2,1)} %param.11) | copy-start | bytes 24580
  53.3 6.0 %copy-start.12 = (s32[4,1,64]{2,1,0:T(1,128)S(1)}, s32[4,1,64]{2,1,0:T(1,128)}, u32[]{:S(2)}) copy-start(s32[4,1,64]{2,1,0:T(1,128)} %index_ref.1) | copy-start | bytes 3076
  56.1 12.7 %collective-permute-start.12 = (bf16[512,512]{1,0:T(8,128)(2,1)}, bf16[512,512]{1,0:T(8,128)(2,1)}, u32[]{:S(2)}, u32[]{:S(2)}) collective-permute-start(bf16[512,512]{1,0:T(8,128)(2,1)} %get-tuple-element.84), channel_id=1, source_target_pairs={{0,1},{1,0},{2,3},{3,2},{4,5},{5,4},{6,7},{7,6},{8,9},{9,8},{10,11... | collective-permute-start | bytes 1572872 | tf_op jit(solution)/shard_map/ppermute | solution.py:471
  57.7 14.7 %collective-permute-start.15 = (bf16[512,512]{1,0:T(8,128)(2,1)}, bf16[512,512]{1,0:T(8,128)(2,1)S(1)}, u32[]{:S(2)}, u32[]{:S(2)}) collective-permute-start(bf16[512,512]{1,0:T(8,128)(2,1)} %get-tuple-element.86), channel_id=1, source_target_pairs={{0,2},{1,3},{2,0},{3,1},{4,6},{5,7},{6,4},{7,5},{8,10},{9,11},{10,... | collective-permute-start | bytes 1572872 | tf_op jit(solution)/shard_map/ppermute | solution.py:471
  59.4 12.3 %collective-permute-start.18 = (bf16[128,512]{1,0:T(8,128)(2,1)}, bf16[128,512]{1,0:T(8,128)(2,1)S(1)}, u32[]{:S(2)}, u32[]{:S(2)}) collective-permute-start(bf16[128,512]{1,0:T(8,128)(2,1)} %get-tuple-element.100), channel_id=1, source_target_pairs={{24,0},{25,1},{26,2},{27,3},{28,4},{29,5},{30,6},{31,7}} | collective-permute-start | bytes 393224 | tf_op jit(solution)/shard_map/ppermute | solution.py:531
  60.7 11.0 %collective-permute-start.19 = (bf16[128,512]{1,0:T(8,128)(2,1)}, bf16[128,512]{1,0:T(8,128)(2,1)S(1)}, u32[]{:S(2)}, u32[]{:S(2)}) collective-permute-start(bf16[128,512]{1,0:T(8,128)(2,1)} %get-tuple-element.101), channel_id=1, source_target_pairs={{24,8},{25,9},{26,10},{27,11},{28,12},{29,13},{30,14},{31,15}} | collective-permute-start | bytes 393224 | tf_op jit(solution)/shard_map/ppermute | solution.py:531
  61.4 10.3 %collective-permute-start.20 = (bf16[128,512]{1,0:T(8,128)(2,1)}, bf16[128,512]{1,0:T(8,128)(2,1)S(1)}, u32[]{:S(2)}, u32[]{:S(2)}) collective-permute-start(bf16[128,512]{1,0:T(8,128)(2,1)} %get-tuple-element.102), channel_id=1, source_target_pairs={{24,16},{25,17},{26,18},{27,19},{28,20},{29,21},{30,22},{31,23}} | collective-permute-start | bytes 393224 | tf_op jit(solution)/shard_map/ppermute | solution.py:531
  62.1 1.2 %copy-start.8 = (f32[512,512]{1,0:T(8,128)S(1)}, f32[512,512]{1,0:T(8,128)}, u32[]{:S(2)}) copy-start(f32[512,512]{1,0:T(8,128)} %copy-done.7) | copy-start | bytes 3145732
  63.3 1.2 %copy-start.10 = (f32[512,512]{1,0:T(8,128)S(1)}, f32[512,512]{1,0:T(8,128)}, u32[]{:S(2)}) copy-start(f32[512,512]{1,0:T(8,128)} %copy-done.9) | copy-start | bytes 3145732
  66.2 5.5 %copy-start.13 = (bf16[128,512]{1,0:T(8,128)(2,1)S(1)}, bf16[128,512]{1,0:T(8,128)(2,1)}, u32[]{:S(2)}) copy-start(bf16[128,512]{1,0:T(8,128)(2,1)} %get-tuple-element.99) | copy-start | bytes 393220
  70.0 9.4 %collective-permute-start.13 = (bf16[256,512]{1,0:T(8,128)(2,1)S(1)}, bf16[256,512]{1,0:T(8,128)(2,1)S(1)}, u32[]{:S(2)}, u32[]{:S(2)}) collective-permute-start(bf16[256,512]{1,0:T(8,128)(2,1)S(1)} %get-tuple-element.104), channel_id=1, source_target_pairs={{0,2},{1,3},{2,0},{3,1},{4,6},{5,7},{6,4},{7,5},{8,10},{9,11},{10,... | collective-permute-start | bytes 786440 | tf_op jit(solution)/shard_map/ppermute | solution.py:471
  72.6 12.4 %all-to-all-start = ((bf16[8,16,512]{2,1,0:T(8,128)(2,1)}), bf16[8,16,512]{2,1,0:T(8,128)(2,1)S(1)}, u32[]{:S(2)}, u32[]{:S(2)}) async-start(bf16[8,16,512]{2,1,0:T(8,128)(2,1)} %bitcast.24), calls=%async_computation | async-start | bytes 262144 | tf_op jit(solution)/shard_map/all_to_all | solution.py:478
  77.4 10.1 %collective-permute-start.16 = (bf16[256,512]{1,0:T(8,128)(2,1)S(1)}, bf16[256,512]{1,0:T(8,128)(2,1)S(1)}, u32[]{:S(2)}, u32[]{:S(2)}) collective-permute-start(bf16[256,512]{1,0:T(8,128)(2,1)S(1)} %get-tuple-element.106), channel_id=1, source_target_pairs={{0,1},{1,0},{2,3},{3,2},{4,5},{5,4},{6,7},{7,6},{8,9},{9,8},{10,11... | collective-permute-start | bytes 786440 | tf_op jit(solution)/shard_map/ppermute | solution.py:471
  79.4 11.1 %collective-permute-start.14 = (bf16[128,512]{1,0:T(8,128)(2,1)S(1)}, bf16[128,512]{1,0:T(8,128)(2,1)S(1)}, u32[]{:S(2)}, u32[]{:S(2)}) collective-permute-start(bf16[128,512]{1,0:T(8,128)(2,1)S(1)} %fusion.2), channel_id=1, source_target_pairs={{0,4},{1,5},{2,6},{3,7},{4,0},{5,1},{6,2},{7,3},{8,12},{9,13},{10,... | collective-permute-start | bytes 393224 | tf_op jit(solution)/shard_map/ppermute | solution.py:471
  87.5 10.0 %collective-permute-start.17 = (bf16[128,512]{1,0:T(8,128)(2,1)S(1)}, bf16[128,512]{1,0:T(8,128)(2,1)S(1)}, u32[]{:S(2)}, u32[]{:S(2)}) collective-permute-start(bf16[128,512]{1,0:T(8,128)(2,1)S(1)} %fusion.3), channel_id=1, source_target_pairs={{0,4},{1,5},{2,6},{3,7},{4,0},{5,1},{6,2},{7,3},{8,12},{9,13},{10,... | collective-permute-start | bytes 393224 | tf_op jit(solution)/shard_map/ppermute | solution.py:471

commit v7 on v6

--- a/solution.py
+++ b/solution.py
@@ -379,7 +379,7 @@
 
 
 def early_kernel(replicas, number_ref, turned, delta_hbm, *refs):
-    outs, (delta, sems) = refs[:4], refs[4:]
+    outs, (delta, sems) = refs[:2], refs[2:]
     micros, rows, width = delta.shape
     half = width // 2
     loads = [pltpu.make_async_copy(delta_hbm.at[m], delta.at[m], sems.at[m]) for m in range(micros)]
@@ -389,12 +389,9 @@
         load.wait()
     flat = delta.reshape(micros * rows, width)
     for c, bits in enumerate(bit_orders(replicas)):
-        for which in range(2):
-            left = picked_rows(turned, number_ref[0], bits, which, width // replicas, slice(0, micros * rows))
-            for at in range(0, half, TILE):
-                outs[2 * c + which][:, at : at + TILE] = dot(
-                    left, flat[:, c * half + at : c * half + at + TILE], NN
-                )
+        left = picked_rows(turned, number_ref[0], bits, 0, width // replicas, slice(0, micros * rows))
+        for at in range(0, half, TILE):
+            outs[c][:, at : at + TILE] = dot(left, flat[:, c * half + at : c * half + at + TILE], NN)
 
 
 def early_call(number, turned, delta, replicas):
@@ -402,9 +399,9 @@
     half = jax.ShapeDtypeStruct((width // 2, width // 2), F32)
     return pl.pallas_call(
         functools.partial(early_kernel, replicas),
-        out_shape=(half,) * 4,
+        out_shape=(half,) * 2,
         in_specs=[SMEM, VMEM, HBM],
-        out_specs=(VMEM,) * 4,
+        out_specs=(VMEM,) * 2,
         scratch_shapes=[
             pltpu.VMEM((micros - 1, rows, width), BF16),
             pltpu.SemaphoreType.DMA((micros - 1,)),
@@ -415,39 +412,46 @@
     )(number, turned, stay(delta))
 
 
-def weight_kernel(
-    replicas, which, flag_ref, number_ref, turned, delta_hbm, came, early_first, early_second, *refs
-):
-    outs, (delta, sem) = refs[:2], refs[2:]
-    rows, width = delta.shape
+def weight_kernel(replicas, which, flag_ref, number_ref, turned, delta_hbm, came, *refs):
+    early, outs, (delta, sems) = refs[:-4], refs[-4:-2], refs[-2:]
+    micros, rows, width = delta_hbm.shape
     half = width // 2
-    last = delta_hbm.shape[0] - 1
-    load = pltpu.make_async_copy(delta_hbm.at[last], delta, sem.at[0])
-    load.start()
-    load.wait()
+    begin = micros - 1 if early else 0
+    loads = [
+        pltpu.make_async_copy(delta_hbm.at[m], delta.at[pl.ds((m - begin) * rows, rows)], sems.at[m - begin])
+        for m in range(begin, micros)
+    ]
+    for load in loads:
+        load.start()
+    for load in loads:
+        load.wait()
 
     @pl.when(flag_ref[0] == 1)
     def _():
-        delta[...] = (came[...].astype(F32) * delta[...].astype(F32)).astype(BF16)
-
-    for c, (bits, early) in enumerate(zip(bit_orders(replicas), (early_first, early_second))):
-        columns = slice(last * rows, (last + 1) * rows)
+        tail = pl.ds((micros - 1 - begin) * rows, rows)
+        delta[tail] = (came[...].astype(F32) * delta[tail].astype(F32)).astype(BF16)
+
+    for c, bits in enumerate(bit_orders(replicas)):
+        columns = slice(begin * rows, micros * rows)
         left = picked_rows(turned, number_ref[0], bits, which, width // replicas, columns)
         for at in range(0, half, TILE):
             product = dot(left, delta[:, c * half + at : c * half + at + TILE], NN)
-            outs[c][:, at : at + TILE] = (early[:, at : at + TILE] + product).astype(outs[c].dtype)
+            if early:
+                product = early[c][:, at : at + TILE] + product
+            outs[c][:, at : at + TILE] = product.astype(outs[c].dtype)
 
 
 def weight_call(which, flag, number, turned, delta, came, early, replicas):
     micros, rows, width = delta.shape
     half = (width // 2, width // 2)
+    taken = 1 if early else micros
     return pl.pallas_call(
         functools.partial(weight_kernel, replicas, which),
         out_shape=(jax.ShapeDtypeStruct(half, F32) if which else pltpu.HBM(half, BF16),) * 2,
-        in_specs=[SMEM, SMEM, VMEM, HBM, VMEM, VMEM, VMEM],
+        in_specs=[SMEM, SMEM, VMEM, HBM] + [VMEM] * (1 + len(early)),
         out_specs=(VMEM,) * 2,
-        scratch_shapes=[pltpu.VMEM((rows, width), BF16), pltpu.SemaphoreType.DMA((1,))],
-        compiler_params=pltpu.CompilerParams(vmem_limit_bytes=14 * MIB),
+        scratch_shapes=[pltpu.VMEM((taken * rows, width), BF16), pltpu.SemaphoreType.DMA((taken,))],
+        compiler_params=pltpu.CompilerParams(vmem_limit_bytes=18 * MIB),
         cost_estimate=LIGHT,
         name="weight",
     )(flag, number, turned, stay(delta), came, *early)
@@ -533,8 +537,8 @@
 
     orders = bit_orders(replicas)
     early = early_call(number, turned, delta, replicas)
-    sends = weight_call(0, active, number, turned, delta, received[-1], early[::2], replicas)
-    keeps = weight_call(1, active, number, turned, delta, received[-1], early[1::2], replicas)
+    sends = weight_call(0, active, number, turned, delta, received[-1], early, replicas)
+    keeps = weight_call(1, active, number, turned, delta, received[-1], (), replicas)
     sums, table_sum = scatter_sums(sends, keeps, table_part, orders, pairs)
     return sums[None], table_sum
 

time: 99.2 us -> 98.4 us (level)
  local copies, waits for them, and re-layouts: 6.38 us -> 2.95 us
  waiting for transfers between devices: 29.6 us -> 32.4 us
    unnamed x28 -> x20, local copies, waits for them, and re-layouts: 6.38 us -> 2.95 us
    ppermute x6, waiting for transfers between devices: 11.9 us -> 13.1 us  [scatter_sums(): lax.ppermute(send, 'dp', pairs_of(bits[n]))]
where the time goes in v7:
time: 98.4 us; the launch traced here: 97.7 us
  starting transfers between devices  32.4 us (33%)
  waiting for transfers between devices  32.4 us (33%)
  Pallas kernels  25.2 us (26%)
  other arithmetic  3.61 us (4%)
  local copies, waits for them, and re-layouts  2.95 us (3%)
  between operations  1.12 us (1%)
    ppermute x12, waiting for transfers between devices, body(): lax.ppermute(g, 'section', [(source, source - 1)])  15.5 us
    ppermute x12, starting transfers between devices, body(): lax.ppermute(g, 'section', [(source, source - 1)])  13.2 us
    ppermute x6, waiting for transfers between devices, scatter_sums(): lax.ppermute(send, 'dp', pairs_of(bits[n]))  13.1 us
    ppermute x6, starting transfers between devices, scatter_sums(): lax.ppermute(send, 'dp', pairs_of(bits[n]))  11.7 us
    pallas_call x4, Pallas kernels, first_call(): pl.pallas_call(functools.partial(first_kernel, m), out_shape=(block, pltp...  8.1 us
    pallas_call x11, Pallas kernels, hop_call(): pl.pallas_call(functools.partial(hop_kernel, m, with_grad), out_shape=out...  6.9 us
    pallas_call x2, Pallas kernels, weight_call(): pl.pallas_call(functools.partial(weight_kernel, replicas, which), out_sha...  5.42 us
    all_to_all x1, starting transfers between devices, scatter_sums(): lax.all_to_all(table.reshape(1 << steps, -1, table.shape[1]), 'dp', 0, 0)  4.83 us
  transfers between devices with their start and end apart: 22, of which 8 were waited for; matrix products, arithmetic and copies ran while one was open for 3% of the time, Pallas kernels for 15%

profile of v7, /device:TPU:0, one launch (start us, length us, event | category | flops | bytes accessed | tf_op | source)
XLA Modules:
  0.0 97.7 jit_solution(18147251341380871365)
XLA Ops:
  0.7 7.6 %first.4 = (bf16[256,1024]{1,0:T(8,128)(2,1)}, bf16[4,256,1024]{2,1,0:T(8,128)(2,1)}, bf16[1024,256]{1,0:T(8,128)(2,1)}, bf16[1024,256]{1,0:T(8,128)(2,1)}, bf16[256,1024]{1,0:T(8,128)(2,1)}) custom-call(s32[1]{0:T(128)} %bitcast.4.flag_ref, s32[1,4]{1,0:T(1,128)} %bitcast.79, bf16[4,256,1024]{2,1,0:T(8,128)(2,1)} %bitcast.32, bf16[1024,1024]{1,0:T(8,128)(2,1)} %bitcast.48, ...), custom_call_target="tpu_custom_call" | custom-call | flops 1024 | bytes 1024 | tf_op jit(solution)/shard_map/first/pallas_call | solution.py:179
  8.3 0.7 collective-permute-start.3
  9.1 0.7 collective-permute-start.2
  9.8 0.3 first.6
  10.1 1.5 %collective-permute-start.1 = (bf16[256,1024]{1,0:T(8,128)(2,1)}, bf16[256,1024]{1,0:T(8,128)(2,1)}, u32[]{:S(2)}, u32[]{:S(2)}) collective-permute-start(bf16[256,1024]{1,0:T(8,128)(2,1)} %get-tuple-element.55), channel_id=1, source_target_pairs={{24,16},{25,17},{26,18},{27,19},{28,20},{29,21},{30,22},{31,23}} | collective-permute-start | bytes 1572872 | tf_op jit(solution)/shard_map/ppermute | solution.py:521
  11.7 0.7 collective-permute-start
  12.5 1.6 %copy-done.2 = bf16[1,1024,1024]{2,1,0:T(8,128)(2,1)S(1)} copy-done((bf16[1,1024,1024]{2,1,0:T(8,128)(2,1)S(1)}, bf16[1,1024,1024]{2,1,0:T(8,128)(2,1)}, u32[]{:S(2)}) %copy-start.2) | copy-done | bytes 2097176
  14.1 0.7 collective-permute-start.6
  14.9 0.7 collective-permute-start.5
  15.6 1.5 %collective-permute-start.4 = (bf16[256,1024]{1,0:T(8,128)(2,1)}, bf16[256,1024]{1,0:T(8,128)(2,1)}, u32[]{:S(2)}, u32[]{:S(2)}) collective-permute-start(bf16[256,1024]{1,0:T(8,128)(2,1)} %get-tuple-element.64), channel_id=1, source_target_pairs={{16,8},{17,9},{18,10},{19,11},{20,12},{21,13},{22,14},{23,15}} | collective-permute-start | bytes 1572872 | tf_op jit(solution)/shard_map/ppermute | solution.py:521
  17.1 1.6 %collective-permute-start.10 = (bf16[256,1024]{1,0:T(8,128)(2,1)}, bf16[256,1024]{1,0:T(8,128)(2,1)}, u32[]{:S(2)}, u32[]{:S(2)}) collective-permute-start(bf16[256,1024]{1,0:T(8,128)(2,1)} %get-tuple-element.62.after_hbm), channel_id=1, source_target_pairs={{16,8},{17,9},{18,10},{19,11},{20,12},{21,13},{22,14},{23,15}} | collective-permute-start | bytes 1572872 | tf_op jit(solution)/shard_map/ppermute | solution.py:521
  18.8 2.3 %turn.1 = (bf16[1024,1024]{1,0:T(8,128)(2,1)S(1)}, bf16[16,128]{1,0:T(8,128)(2,1)}) custom-call(bf16[4,256,1024]{2,1,0:T(8,128)(2,1)} %bitcast.38, bf16[256,1024]{1,0:T(8,128)(2,1)} %get-tuple-element.62.after_hbm), custom_call_target="tpu_custom_call" | custom-call | flops 1024 | bytes 1024 | tf_op jit(solution)/shard_map/turn/pallas_call | solution.py:360
  21.1 1.3 %copy-done.4 = bf16[1024,1024]{1,0:T(8,128)(2,1)} copy-done((bf16[1024,1024]{1,0:T(8,128)(2,1)}, bf16[1024,1024]{1,0:T(8,128)(2,1)S(1)}, u32[]{:S(2)}) %copy-start.4) | copy-done | bytes 2097176
  22.5 1.3 %collective-permute-start.9 = (bf16[256,1024]{1,0:T(8,128)(2,1)}, bf16[256,1024]{1,0:T(8,128)(2,1)S(1)}, u32[]{:S(2)}, u32[]{:S(2)}) collective-permute-start(bf16[256,1024]{1,0:T(8,128)(2,1)} %get-tuple-element.73), channel_id=1, source_target_pairs={{8,0},{9,1},{10,2},{11,3},{12,4},{13,5},{14,6},{15,7}} | collective-permute-start | bytes 1572872 | tf_op jit(solution)/shard_map/ppermute | solution.py:521
  23.8 1.3 %collective-permute-start.8 = (bf16[256,1024]{1,0:T(8,128)(2,1)}, bf16[256,1024]{1,0:T(8,128)(2,1)}, u32[]{:S(2)}, u32[]{:S(2)}) collective-permute-start(bf16[256,1024]{1,0:T(8,128)(2,1)} %get-tuple-element.72), channel_id=1, source_target_pairs={{8,0},{9,1},{10,2},{11,3},{12,4},{13,5},{14,6},{15,7}} | collective-permute-start | bytes 1572872 | tf_op jit(solution)/shard_map/ppermute | solution.py:521
  25.2 1.3 %collective-permute-start.7 = (bf16[256,1024]{1,0:T(8,128)(2,1)}, bf16[256,1024]{1,0:T(8,128)(2,1)}, u32[]{:S(2)}, u32[]{:S(2)}) collective-permute-start(bf16[256,1024]{1,0:T(8,128)(2,1)} %get-tuple-element.71), channel_id=1, source_target_pairs={{8,0},{9,1},{10,2},{11,3},{12,4},{13,5},{14,6},{15,7}} | collective-permute-start | bytes 1572872 | tf_op jit(solution)/shard_map/ppermute | solution.py:521
  26.5 0.3 hop.15
  26.8 1.3 %collective-permute-start.11 = (bf16[256,1024]{1,0:T(8,128)(2,1)}, bf16[256,1024]{1,0:T(8,128)(2,1)S(1)}, u32[]{:S(2)}, u32[]{:S(2)}) collective-permute-start(bf16[256,1024]{1,0:T(8,128)(2,1)} %get-tuple-element.76), channel_id=1, source_target_pairs={{8,0},{9,1},{10,2},{11,3},{12,4},{13,5},{14,6},{15,7}} | collective-permute-start | bytes 1572872 | tf_op jit(solution)/shard_map/ppermute | solution.py:521
  28.1 7.2 %collective-permute-done.9.came_hbm = bf16[256,1024]{1,0:T(8,128)(2,1)S(1)} collective-permute-done((bf16[256,1024]{1,0:T(8,128)(2,1)}, bf16[256,1024]{1,0:T(8,128)(2,1)S(1)}, u32[]{:S(2)}, u32[]{:S(2)}) %collective-permute-start.9) | collective-permute-done | bytes 524320 | tf_op jit(solution)/shard_map/ppermute | solution.py:521
  35.3 2.0 %end.3.delta_in = bf16[4,256,1024]{2,1,0:T(8,128)(2,1)} custom-call(s32[1]{0:T(128)} %bitcast.flag_ref, bf16[256,1024]{1,0:T(8,128)(2,1)S(1)} %collective-permute-done.9.came_hbm, bf16[4,256,1024]{2,1,0:T(8,128)(2,1)} %get-tuple-element.75.delta_in, bf16[1024,1024]{1,0:T(8,128)(2,1)} %bitcast.49, ...), custom_call_target="tpu_custom_call", output_to_operand_aliasing={{}: (2, {})} | custom-call | flops 1024 | bytes 1024 | tf_op jit(solution)/shard_map/end/pallas_call | solution.py:321
  37.3 3.7 %collective-permute-done.8.came_hbm = bf16[256,1024]{1,0:T(8,128)(2,1)} collective-permute-done((bf16[256,1024]{1,0:T(8,128)(2,1)}, bf16[256,1024]{1,0:T(8,128)(2,1)}, u32[]{:S(2)}, u32[]{:S(2)}) %collective-permute-start.8) | collective-permute-done | bytes 524320 | tf_op jit(solution)/shard_map/ppermute | solution.py:521
  41.0 2.1 %end.4.delta_in = bf16[4,256,1024]{2,1,0:T(8,128)(2,1)} custom-call(s32[1]{0:T(128)} %bitcast.flag_ref, bf16[256,1024]{1,0:T(8,128)(2,1)} %collective-permute-done.8.came_hbm, bf16[4,256,1024]{2,1,0:T(8,128)(2,1)} %end.3.delta_in, bf16[1024,1024]{1,0:T(8,128)(2,1)} %bitcast.50, bf16[4,256,1024]{2,1,0:T(8,128)(2,1)} %bitcast.43), custom_call_target="tpu_custom_call", output_to_operand_aliasing={{}: (2, {})} | custom-call | flops 1024 | bytes 1024 | tf_op jit(solution)/shard_map/end/pallas_call | solution.py:321
  43.2 3.7 %collective-permute-done.7.came_hbm = bf16[256,1024]{1,0:T(8,128)(2,1)} collective-permute-done((bf16[256,1024]{1,0:T(8,128)(2,1)}, bf16[256,1024]{1,0:T(8,128)(2,1)}, u32[]{:S(2)}, u32[]{:S(2)}) %collective-permute-start.7) | collective-permute-done | bytes 524320 | tf_op jit(solution)/shard_map/ppermute | solution.py:521
  46.9 2.2 %end.5.delta_hbm = bf16[4,256,1024]{2,1,0:T(8,128)(2,1)} custom-call(s32[1]{0:T(128)} %bitcast.flag_ref, bf16[256,1024]{1,0:T(8,128)(2,1)} %collective-permute-done.7.came_hbm, bf16[4,256,1024]{2,1,0:T(8,128)(2,1)} %end.4.delta_in, bf16[1024,1024]{1,0:T(8,128)(2,1)} %bitcast.51, bf16[4,256,1024]{2,1,0:T(8,128)(2,1)} %bitcast.44), custom_call_target="tpu_custom_call", output_to_operand_aliasing={{}: (2, {})} | custom-call | flops 1024 | bytes 1024 | tf_op jit(solution)/shard_map/end/pallas_call | solution.py:321
  49.1 2.4 %early.1 = (f32[512,512]{1,0:T(8,128)S(1)}, f32[512,512]{1,0:T(8,128)S(1)}) custom-call(s32[1]{0:T(128)} %bitcast.1.number_ref, bf16[1024,1024]{1,0:T(8,128)(2,1)S(1)} %copy-done.5, bf16[4,256,1024]{2,1,0:T(8,128)(2,1)} %end.5.delta_hbm), custom_call_target="tpu_custom_call" | custom-call | flops 1024 | bytes 1024 | tf_op jit(solution)/shard_map/early/pallas_call | solution.py:400
  51.4 0.9 collective-permute-done.11.came
  52.4 2.5 %weight.3 = (bf16[512,512]{1,0:T(8,128)(2,1)}, bf16[512,512]{1,0:T(8,128)(2,1)}) custom-call(s32[1]{0:T(128)} %bitcast.flag_ref, s32[1]{0:T(128)} %bitcast.1.number_ref, bf16[1024,1024]{1,0:T(8,128)(2,1)S(1)} %copy-done.5, bf16[4,256,1024]{2,1,0:T(8,128)(2,1)} %end.5.delta_hbm, bf16[256,1024]{1,0:T(8,128)(2,1)S(1)} %collective-permute-done.11.came, ...), custom_call_target="tpu_custom_call" | custom-call | flops 1024 | bytes 1024 | tf_op jit(solution)/shard_map/weight/pallas_call | solution.py:448
  54.9 1.6 %collective-permute-start.12 = (bf16[512,512]{1,0:T(8,128)(2,1)}, bf16[512,512]{1,0:T(8,128)(2,1)}, u32[]{:S(2)}, u32[]{:S(2)}) collective-permute-start(bf16[512,512]{1,0:T(8,128)(2,1)} %get-tuple-element.80), channel_id=1, source_target_pairs={{0,1},{1,0},{2,3},{3,2},{4,5},{5,4},{6,7},{7,6},{8,9},{9,8},{10,11... | collective-permute-start | bytes 1572872 | tf_op jit(solution)/shard_map/ppermute | solution.py:475
  56.4 1.6 %collective-permute-start.15 = (bf16[512,512]{1,0:T(8,128)(2,1)}, bf16[512,512]{1,0:T(8,128)(2,1)S(1)}, u32[]{:S(2)}, u32[]{:S(2)}) collective-permute-start(bf16[512,512]{1,0:T(8,128)(2,1)} %get-tuple-element.82), channel_id=1, source_target_pairs={{0,2},{1,3},{2,0},{3,1},{4,6},{5,7},{6,4},{7,5},{8,10},{9,11},{10,... | collective-permute-start | bytes 1572872 | tf_op jit(solution)/shard_map/ppermute | solution.py:475
  58.0 0.1 table.1
  58.2 1.3 %collective-permute-start.18 = (bf16[128,512]{1,0:T(8,128)(2,1)}, bf16[128,512]{1,0:T(8,128)(2,1)S(1)}, u32[]{:S(2)}, u32[]{:S(2)}) collective-permute-start(bf16[128,512]{1,0:T(8,128)(2,1)} %get-tuple-element.96), channel_id=1, source_target_pairs={{24,0},{25,1},{26,2},{27,3},{28,4},{29,5},{30,6},{31,7}} | collective-permute-start | bytes 393224 | tf_op jit(solution)/shard_map/ppermute | solution.py:535
  59.5 0.7 collective-permute-start.19
  60.2 0.7 collective-permute-start.20
  60.8 2.9 %weight.2 = (f32[512,512]{1,0:T(8,128)S(1)}, f32[512,512]{1,0:T(8,128)S(1)}) custom-call(s32[1]{0:T(128)} %bitcast.flag_ref, s32[1]{0:T(128)} %bitcast.1.number_ref, bf16[1024,1024]{1,0:T(8,128)(2,1)S(1)} %copy-done.5, bf16[4,256,1024]{2,1,0:T(8,128)(2,1)} %end.5.delta_hbm, bf16[256,1024]{1,0:T(8,128)(2,1)S(1)} %collective-permute-done.11.came), custom_call_target="tpu_custom_call" | custom-call | flops 1024 | bytes 1024 | tf_op jit(solution)/shard_map/weight/pallas_call | solution.py:448
  63.8 4.7 %collective-permute-done.12 = bf16[512,512]{1,0:T(8,128)(2,1)} collective-permute-done((bf16[512,512]{1,0:T(8,128)(2,1)}, bf16[512,512]{1,0:T(8,128)(2,1)}, u32[]{:S(2)}, u32[]{:S(2)}) %collective-permute-start.12) | collective-permute-done | bytes 524320 | tf_op jit(solution)/shard_map/ppermute | solution.py:475
  68.5 1.2 %fusion = (bf16[256,512]{1,0:T(8,128)(2,1)S(1)}, f32[1,256,512]{2,1,0:T(8,128)S(1)}) fusion(f32[2,256,512]{2,1,0:T(8,128)S(1)} %bitcast.64, s32[]{:T(128)S(6)} %select_n.42, bf16[2,256,512]{2,1,0:T(8,128)(2,1)} %bitcast.10, s32[]{:T(128)S(6)} %select_n.40), kind=kLoop, calls=%fused_computation.5 | loop fusion | flops 655360 | bytes 2359304 | tf_op jit(solution)/shard_map/convert_element_type | solution.py:468
  69.7 1.7 %collective-permute-start.13 = (bf16[256,512]{1,0:T(8,128)(2,1)S(1)}, bf16[256,512]{1,0:T(8,128)(2,1)S(1)}, u32[]{:S(2)}, u32[]{:S(2)}) collective-permute-start(bf16[256,512]{1,0:T(8,128)(2,1)S(1)} %get-tuple-element.100), channel_id=1, source_target_pairs={{0,2},{1,3},{2,0},{3,1},{4,6},{5,7},{6,4},{7,5},{8,10},{9,11},{10,... | collective-permute-start | bytes 786440 | tf_op jit(solution)/shard_map/ppermute | solution.py:475
  71.4 0.7 add_select_fusion
  72.1 0.1 fusion.1
  72.2 4.8 %all-to-all-start = ((bf16[8,16,512]{2,1,0:T(8,128)(2,1)}), bf16[8,16,512]{2,1,0:T(8,128)(2,1)S(1)}, u32[]{:S(2)}, u32[]{:S(2)}) async-start(bf16[8,16,512]{2,1,0:T(8,128)(2,1)} %bitcast.24), calls=%async_computation | async-start | bytes 262144 | tf_op jit(solution)/shard_map/all_to_all | solution.py:482
  77.0 2.0 %collective-permute-start.16 = (bf16[256,512]{1,0:T(8,128)(2,1)S(1)}, bf16[256,512]{1,0:T(8,128)(2,1)S(1)}, u32[]{:S(2)}, u32[]{:S(2)}) collective-permute-start(bf16[256,512]{1,0:T(8,128)(2,1)S(1)} %get-tuple-element.102), channel_id=1, source_target_pairs={{0,1},{1,0},{2,3},{3,2},{4,5},{5,4},{6,7},{7,6},{8,9},{9,8},{10,11... | collective-permute-start | bytes 786440 | tf_op jit(solution)/shard_map/ppermute | solution.py:475
  79.1 2.4 %collective-permute-start.14 = (bf16[128,512]{1,0:T(8,128)(2,1)S(1)}, bf16[128,512]{1,0:T(8,128)(2,1)S(1)}, u32[]{:S(2)}, u32[]{:S(2)}) collective-permute-start(bf16[128,512]{1,0:T(8,128)(2,1)S(1)} %fusion.2), channel_id=1, source_target_pairs={{0,4},{1,5},{2,6},{3,7},{4,0},{5,1},{6,2},{7,3},{8,12},{9,13},{10,... | collective-permute-start | bytes 393224 | tf_op jit(solution)/shard_map/ppermute | solution.py:475
  81.5 3.7 %all-to-all-done = bf16[8,16,512]{2,1,0:T(8,128)(2,1)S(1)} async-done(((bf16[8,16,512]{2,1,0:T(8,128)(2,1)}), bf16[8,16,512]{2,1,0:T(8,128)(2,1)S(1)}, u32[]{:S(2)}, u32[]{:S(2)}) %all-to-all-start) | async-done | bytes 131104 | tf_op jit(solution)/shard_map/all_to_all | solution.py:482
  85.3 0.6 convert_reduce_fusion
  85.9 1.7 %collective-permute-done.16 = bf16[256,512]{1,0:T(8,128)(2,1)S(1)} collective-permute-done((bf16[256,512]{1,0:T(8,128)(2,1)S(1)}, bf16[256,512]{1,0:T(8,128)(2,1)S(1)}, u32[]{:S(2)}, u32[]{:S(2)}) %collective-permute-start.16) | collective-permute-done | bytes 262176 | tf_op jit(solution)/shard_map/ppermute | solution.py:475
  87.7 2.4 %collective-permute-start.17 = (bf16[128,512]{1,0:T(8,128)(2,1)S(1)}, bf16[128,512]{1,0:T(8,128)(2,1)S(1)}, u32[]{:S(2)}, u32[]{:S(2)}) collective-permute-start(bf16[128,512]{1,0:T(8,128)(2,1)S(1)} %fusion.3), channel_id=1, source_target_pairs={{0,4},{1,5},{2,6},{3,7},{4,0},{5,1},{6,2},{7,3},{8,12},{9,13},{10,... | collective-permute-start | bytes 393224 | tf_op jit(solution)/shard_map/ppermute | solution.py:475
  90.2 6.6 %collective-permute-done.17 = bf16[128,512]{1,0:T(8,128)(2,1)S(1)} collective-permute-done((bf16[128,512]{1,0:T(8,128)(2,1)S(1)}, bf16[128,512]{1,0:T(8,128)(2,1)S(1)}, u32[]{:S(2)}, u32[]{:S(2)}) %collective-permute-start.17) | collective-permute-done | bytes 131104 | tf_op jit(solution)/shard_map/ppermute | solution.py:475
  96.8 0.8 maximum_bitcast_fusion
  (45 shorter events, 0.7 us)
Async XLA Ops:
  0.6 8.4 %copy-start = (bf16[1,4,256,1024]{3,2,1,0:T(8,128)(2,1)S(1)}, bf16[1,4,256,1024]{3,2,1,0:T(8,128)(2,1)}, u32[]{:S(2)}) copy-start(bf16[1,4,256,1024]{3,2,1,0:T(8,128)(2,1)} %param.6) | copy-start | bytes 6291460
  0.7 8.3 %copy-start.1 = (bf16[1,1024,1024]{2,1,0:T(8,128)(2,1)S(1)}, bf16[1,1024,1024]{2,1,0:T(8,128)(2,1)}, u32[]{:S(2)}) copy-start(bf16[1,1024,1024]{2,1,0:T(8,128)(2,1)} %param.7) | copy-start | bytes 6291460
  0.7 8.3 %copy-start.6 = (bf16[128,2048]{1,0:T(8,128)(2,1)S(1)}, bf16[128,2048]{1,0:T(8,128)(2,1)}, u32[]{:S(2)}) copy-start(bf16[128,2048]{1,0:T(8,128)(2,1)} %table_in.7) | copy-start | bytes 1572868
  8.3 4.2 %collective-permute-start.3 = (bf16[256,1024]{1,0:T(8,128)(2,1)}, bf16[256,1024]{1,0:T(8,128)(2,1)S(1)}, u32[]{:S(2)}, u32[]{:S(2)}) collective-permute-start(bf16[256,1024]{1,0:T(8,128)(2,1)} %get-tuple-element.57), channel_id=1, source_target_pairs={{24,16},{25,17},{26,18},{27,19},{28,20},{29,21},{30,22},{31,23}} | collective-permute-start | bytes 1572872 | tf_op jit(solution)/shard_map/ppermute | solution.py:521
  9.1 5.7 %collective-permute-start.2 = (bf16[256,1024]{1,0:T(8,128)(2,1)}, bf16[256,1024]{1,0:T(8,128)(2,1)S(1)}, u32[]{:S(2)}, u32[]{:S(2)}) collective-permute-start(bf16[256,1024]{1,0:T(8,128)(2,1)} %get-tuple-element.56), channel_id=1, source_target_pairs={{24,16},{25,17},{26,18},{27,19},{28,20},{29,21},{30,22},{31,23}} | collective-permute-start | bytes 1572872 | tf_op jit(solution)/shard_map/ppermute | solution.py:521
  10.1 5.4 %collective-permute-start.1 = (bf16[256,1024]{1,0:T(8,128)(2,1)}, bf16[256,1024]{1,0:T(8,128)(2,1)}, u32[]{:S(2)}, u32[]{:S(2)}) collective-permute-start(bf16[256,1024]{1,0:T(8,128)(2,1)} %get-tuple-element.55), channel_id=1, source_target_pairs={{24,16},{25,17},{26,18},{27,19},{28,20},{29,21},{30,22},{31,23}} | collective-permute-start | bytes 1572872 | tf_op jit(solution)/shard_map/ppermute | solution.py:521
  11.7 5.4 %collective-permute-start = (bf16[256,1024]{1,0:T(8,128)(2,1)}, bf16[256,1024]{1,0:T(8,128)(2,1)S(1)}, u32[]{:S(2)}, u32[]{:S(2)}) collective-permute-start(bf16[256,1024]{1,0:T(8,128)(2,1)} %get-tuple-element.54), channel_id=1, source_target_pairs={{24,16},{25,17},{26,18},{27,19},{28,20},{29,21},{30,22},{31,23}} | collective-permute-start | bytes 1572872 | tf_op jit(solution)/shard_map/ppermute | solution.py:521
  12.5 1.6 %copy-start.2 = (bf16[1,1024,1024]{2,1,0:T(8,128)(2,1)S(1)}, bf16[1,1024,1024]{2,1,0:T(8,128)(2,1)}, u32[]{:S(2)}) copy-start(bf16[1,1024,1024]{2,1,0:T(8,128)(2,1)} %param.7) | copy-start | bytes 6291460
  14.1 8.3 %collective-permute-start.6 = (bf16[256,1024]{1,0:T(8,128)(2,1)}, bf16[256,1024]{1,0:T(8,128)(2,1)S(1)}, u32[]{:S(2)}, u32[]{:S(2)}) collective-permute-start(bf16[256,1024]{1,0:T(8,128)(2,1)} %get-tuple-element.66), channel_id=1, source_target_pairs={{16,8},{17,9},{18,10},{19,11},{20,12},{21,13},{22,14},{23,15}} | collective-permute-start | bytes 1572872 | tf_op jit(solution)/shard_map/ppermute | solution.py:521
  14.9 8.9 %collective-permute-start.5 = (bf16[256,1024]{1,0:T(8,128)(2,1)}, bf16[256,1024]{1,0:T(8,128)(2,1)S(1)}, u32[]{:S(2)}, u32[]{:S(2)}) collective-permute-start(bf16[256,1024]{1,0:T(8,128)(2,1)} %get-tuple-element.65), channel_id=1, source_target_pairs={{16,8},{17,9},{18,10},{19,11},{20,12},{21,13},{22,14},{23,15}} | collective-permute-start | bytes 1572872 | tf_op jit(solution)/shard_map/ppermute | solution.py:521
  15.6 9.5 %collective-permute-start.4 = (bf16[256,1024]{1,0:T(8,128)(2,1)}, bf16[256,1024]{1,0:T(8,128)(2,1)}, u32[]{:S(2)}, u32[]{:S(2)}) collective-permute-start(bf16[256,1024]{1,0:T(8,128)(2,1)} %get-tuple-element.64), channel_id=1, source_target_pairs={{16,8},{17,9},{18,10},{19,11},{20,12},{21,13},{22,14},{23,15}} | collective-permute-start | bytes 1572872 | tf_op jit(solution)/shard_map/ppermute | solution.py:521
  17.1 5.3 %copy-start.3 = (bf16[1,1024,1024]{2,1,0:T(8,128)(2,1)S(1)}, bf16[1,1024,1024]{2,1,0:T(8,128)(2,1)}, u32[]{:S(2)}) copy-start(bf16[1,1024,1024]{2,1,0:T(8,128)(2,1)} %param.7) | copy-start | bytes 6291460
  17.1 9.3 %collective-permute-start.10 = (bf16[256,1024]{1,0:T(8,128)(2,1)}, bf16[256,1024]{1,0:T(8,128)(2,1)}, u32[]{:S(2)}, u32[]{:S(2)}) collective-permute-start(bf16[256,1024]{1,0:T(8,128)(2,1)} %get-tuple-element.62.after_hbm), channel_id=1, source_target_pairs={{16,8},{17,9},{18,10},{19,11},{20,12},{21,13},{22,14},{23,15}} | collective-permute-start | bytes 1572872 | tf_op jit(solution)/shard_map/ppermute | solution.py:521
  21.1 1.3 %copy-start.4 = (bf16[1024,1024]{1,0:T(8,128)(2,1)}, bf16[1024,1024]{1,0:T(8,128)(2,1)S(1)}, u32[]{:S(2)}) copy-start(bf16[1024,1024]{1,0:T(8,128)(2,1)S(1)} %get-tuple-element.63.turned) | copy-start | bytes 6291460
  22.5 12.8 %collective-permute-start.9 = (bf16[256,1024]{1,0:T(8,128)(2,1)}, bf16[256,1024]{1,0:T(8,128)(2,1)S(1)}, u32[]{:S(2)}, u32[]{:S(2)}) collective-permute-start(bf16[256,1024]{1,0:T(8,128)(2,1)} %get-tuple-element.73), channel_id=1, source_target_pairs={{8,0},{9,1},{10,2},{11,3},{12,4},{13,5},{14,6},{15,7}} | collective-permute-start | bytes 1572872 | tf_op jit(solution)/shard_map/ppermute | solution.py:521
  23.8 17.2 %collective-permute-start.8 = (bf16[256,1024]{1,0:T(8,128)(2,1)}, bf16[256,1024]{1,0:T(8,128)(2,1)}, u32[]{:S(2)}, u32[]{:S(2)}) collective-permute-start(bf16[256,1024]{1,0:T(8,128)(2,1)} %get-tuple-element.72), channel_id=1, source_target_pairs={{8,0},{9,1},{10,2},{11,3},{12,4},{13,5},{14,6},{15,7}} | collective-permute-start | bytes 1572872 | tf_op jit(solution)/shard_map/ppermute | solution.py:521
  25.2 21.7 %collective-permute-start.7 = (bf16[256,1024]{1,0:T(8,128)(2,1)}, bf16[256,1024]{1,0:T(8,128)(2,1)}, u32[]{:S(2)}, u32[]{:S(2)}) collective-permute-start(bf16[256,1024]{1,0:T(8,128)(2,1)} %get-tuple-element.71), channel_id=1, source_target_pairs={{8,0},{9,1},{10,2},{11,3},{12,4},{13,5},{14,6},{15,7}} | collective-permute-start | bytes 1572872 | tf_op jit(solution)/shard_map/ppermute | solution.py:521
  26.8 25.6 %collective-permute-start.11 = (bf16[256,1024]{1,0:T(8,128)(2,1)}, bf16[256,1024]{1,0:T(8,128)(2,1)S(1)}, u32[]{:S(2)}, u32[]{:S(2)}) collective-permute-start(bf16[256,1024]{1,0:T(8,128)(2,1)} %get-tuple-element.76), channel_id=1, source_target_pairs={{8,0},{9,1},{10,2},{11,3},{12,4},{13,5},{14,6},{15,7}} | collective-permute-start | bytes 1572872 | tf_op jit(solution)/shard_map/ppermute | solution.py:521
  43.2 5.9 %copy-start.5 = (bf16[1024,1024]{1,0:T(8,128)(2,1)S(1)}, bf16[1024,1024]{1,0:T(8,128)(2,1)}, u32[]{:S(2)}) copy-start(bf16[1024,1024]{1,0:T(8,128)(2,1)} %copy-done.4) | copy-start | bytes 6291460
  52.4 5.7 %copy-start.7 = (bf16[4,1,1024]{2,0,1:T(4,128)(2,1)S(1)}, bf16[4,1,1024]{2,0,1:T(4,128)(2,1)}, u32[]{:S(2)}) copy-start(bf16[4,1,1024]{2,0,1:T(4,128)(2,1)} %param.11) | copy-start | bytes 24580
  52.4 5.7 %copy-start.8 = (s32[4,1,64]{2,1,0:T(1,128)S(1)}, s32[4,1,64]{2,1,0:T(1,128)}, u32[]{:S(2)}) copy-start(s32[4,1,64]{2,1,0:T(1,128)} %index_ref.1) | copy-start | bytes 3076
  54.9 13.6 %collective-permute-start.12 = (bf16[512,512]{1,0:T(8,128)(2,1)}, bf16[512,512]{1,0:T(8,128)(2,1)}, u32[]{:S(2)}, u32[]{:S(2)}) collective-permute-start(bf16[512,512]{1,0:T(8,128)(2,1)} %get-tuple-element.80), channel_id=1, source_target_pairs={{0,1},{1,0},{2,3},{3,2},{4,5},{5,4},{6,7},{7,6},{8,9},{9,8},{10,11... | collective-permute-start | bytes 1572872 | tf_op jit(solution)/shard_map/ppermute | solution.py:475
  56.4 15.6 %collective-permute-start.15 = (bf16[512,512]{1,0:T(8,128)(2,1)}, bf16[512,512]{1,0:T(8,128)(2,1)S(1)}, u32[]{:S(2)}, u32[]{:S(2)}) collective-permute-start(bf16[512,512]{1,0:T(8,128)(2,1)} %get-tuple-element.82), channel_id=1, source_target_pairs={{0,2},{1,3},{2,0},{3,1},{4,6},{5,7},{6,4},{7,5},{8,10},{9,11},{10,... | collective-permute-start | bytes 1572872 | tf_op jit(solution)/shard_map/ppermute | solution.py:475
  58.2 13.2 %collective-permute-start.18 = (bf16[128,512]{1,0:T(8,128)(2,1)}, bf16[128,512]{1,0:T(8,128)(2,1)S(1)}, u32[]{:S(2)}, u32[]{:S(2)}) collective-permute-start(bf16[128,512]{1,0:T(8,128)(2,1)} %get-tuple-element.96), channel_id=1, source_target_pairs={{24,0},{25,1},{26,2},{27,3},{28,4},{29,5},{30,6},{31,7}} | collective-permute-start | bytes 393224 | tf_op jit(solution)/shard_map/ppermute | solution.py:535
  59.5 11.9 %collective-permute-start.19 = (bf16[128,512]{1,0:T(8,128)(2,1)}, bf16[128,512]{1,0:T(8,128)(2,1)S(1)}, u32[]{:S(2)}, u32[]{:S(2)}) collective-permute-start(bf16[128,512]{1,0:T(8,128)(2,1)} %get-tuple-element.97), channel_id=1, source_target_pairs={{24,8},{25,9},{26,10},{27,11},{28,12},{29,13},{30,14},{31,15}} | collective-permute-start | bytes 393224 | tf_op jit(solution)/shard_map/ppermute | solution.py:535
  60.2 11.2 %collective-permute-start.20 = (bf16[128,512]{1,0:T(8,128)(2,1)}, bf16[128,512]{1,0:T(8,128)(2,1)S(1)}, u32[]{:S(2)}, u32[]{:S(2)}) collective-permute-start(bf16[128,512]{1,0:T(8,128)(2,1)} %get-tuple-element.98), channel_id=1, source_target_pairs={{24,16},{25,17},{26,18},{27,19},{28,20},{29,21},{30,22},{31,23}} | collective-permute-start | bytes 393224 | tf_op jit(solution)/shard_map/ppermute | solution.py:535
  63.8 7.6 %copy-start.9 = (bf16[128,512]{1,0:T(8,128)(2,1)S(1)}, bf16[128,512]{1,0:T(8,128)(2,1)}, u32[]{:S(2)}) copy-start(bf16[128,512]{1,0:T(8,128)(2,1)} %get-tuple-element.95) | copy-start | bytes 393220
  69.7 9.4 %collective-permute-start.13 = (bf16[256,512]{1,0:T(8,128)(2,1)S(1)}, bf16[256,512]{1,0:T(8,128)(2,1)S(1)}, u32[]{:S(2)}, u32[]{:S(2)}) collective-permute-start(bf16[256,512]{1,0:T(8,128)(2,1)S(1)} %get-tuple-element.100), channel_id=1, source_target_pairs={{0,2},{1,3},{2,0},{3,1},{4,6},{5,7},{6,4},{7,5},{8,10},{9,11},{10,... | collective-permute-start | bytes 786440 | tf_op jit(solution)/shard_map/ppermute | solution.py:475
  72.2 13.1 %all-to-all-start = ((bf16[8,16,512]{2,1,0:T(8,128)(2,1)}), bf16[8,16,512]{2,1,0:T(8,128)(2,1)S(1)}, u32[]{:S(2)}, u32[]{:S(2)}) async-start(bf16[8,16,512]{2,1,0:T(8,128)(2,1)} %bitcast.24), calls=%async_computation | async-start | bytes 262144 | tf_op jit(solution)/shard_map/all_to_all | solution.py:482
  77.0 10.6 %collective-permute-start.16 = (bf16[256,512]{1,0:T(8,128)(2,1)S(1)}, bf16[256,512]{1,0:T(8,128)(2,1)S(1)}, u32[]{:S(2)}, u32[]{:S(2)}) collective-permute-start(bf16[256,512]{1,0:T(8,128)(2,1)S(1)} %get-tuple-element.102), channel_id=1, source_target_pairs={{0,1},{1,0},{2,3},{3,2},{4,5},{5,4},{6,7},{7,6},{8,9},{9,8},{10,11... | collective-permute-start | bytes 786440 | tf_op jit(solution)/shard_map/ppermute | solution.py:475
  79.1 11.0 %collective-permute-start.14 = (bf16[128,512]{1,0:T(8,128)(2,1)S(1)}, bf16[128,512]{1,0:T(8,128)(2,1)S(1)}, u32[]{:S(2)}, u32[]{:S(2)}) collective-permute-start(bf16[128,512]{1,0:T(8,128)(2,1)S(1)} %fusion.2), channel_id=1, source_target_pairs={{0,4},{1,5},{2,6},{3,7},{4,0},{5,1},{6,2},{7,3},{8,12},{9,13},{10,... | collective-permute-start | bytes 393224 | tf_op jit(solution)/shard_map/ppermute | solution.py:475
  87.7 9.1 %collective-permute-start.17 = (bf16[128,512]{1,0:T(8,128)(2,1)S(1)}, bf16[128,512]{1,0:T(8,128)(2,1)S(1)}, u32[]{:S(2)}, u32[]{:S(2)}) collective-permute-start(bf16[128,512]{1,0:T(8,128)(2,1)S(1)} %fusion.3), channel_id=1, source_target_pairs={{0,4},{1,5},{2,6},{3,7},{4,0},{5,1},{6,2},{7,3},{8,12},{9,13},{10,... | collective-permute-start | bytes 393224 | tf_op jit(solution)/shard_map/ppermute | solution.py:475

commit v8 on v7

--- a/solution.py
+++ b/solution.py
@@ -359,7 +359,7 @@
     count, rows, width = acts.shape
     return pl.pallas_call(
         turn_kernel,
-        out_shape=(jax.ShapeDtypeStruct((width, count * rows), BF16), pltpu.HBM((16, 128), BF16)),
+        out_shape=(pltpu.HBM((width, count * rows), BF16), pltpu.HBM((16, 128), BF16)),
         in_specs=[HBM, HBM],
         out_specs=(VMEM,) * 2,
         scratch_shapes=[pltpu.VMEM(acts.shape, BF16), pltpu.SemaphoreType.DMA((count,))],
@@ -378,11 +378,12 @@
     )
 
 
-def early_kernel(replicas, number_ref, turned, delta_hbm, *refs):
-    outs, (delta, sems) = refs[:2], refs[2:]
+def early_kernel(replicas, number_ref, turned_hbm, delta_hbm, *refs):
+    outs, (turned, delta, sems) = refs[:2], refs[2:]
     micros, rows, width = delta.shape
     half = width // 2
     loads = [pltpu.make_async_copy(delta_hbm.at[m], delta.at[m], sems.at[m]) for m in range(micros)]
+    loads.append(pltpu.make_async_copy(turned_hbm.at[:, pl.ds(0, micros * rows)], turned, sems.at[micros]))
     for load in loads:
         load.start()
     for load in loads:
@@ -400,20 +401,21 @@
     return pl.pallas_call(
         functools.partial(early_kernel, replicas),
         out_shape=(half,) * 2,
-        in_specs=[SMEM, VMEM, HBM],
+        in_specs=[SMEM, HBM, HBM],
         out_specs=(VMEM,) * 2,
         scratch_shapes=[
+            pltpu.VMEM((width, (micros - 1) * rows), BF16),
             pltpu.VMEM((micros - 1, rows, width), BF16),
-            pltpu.SemaphoreType.DMA((micros - 1,)),
+            pltpu.SemaphoreType.DMA((micros,)),
         ],
         compiler_params=pltpu.CompilerParams(vmem_limit_bytes=18 * MIB),
         cost_estimate=LIGHT,
         name="early",
-    )(number, turned, stay(delta))
-
-
-def weight_kernel(replicas, which, flag_ref, number_ref, turned, delta_hbm, came, *refs):
-    early, outs, (delta, sems) = refs[:-4], refs[-4:-2], refs[-2:]
+    )(number, stay(turned), stay(delta))
+
+
+def weight_kernel(replicas, which, flag_ref, number_ref, turned_hbm, delta_hbm, came, *refs):
+    early, outs, (turned, delta, sems) = refs[:-5], refs[-5:-3], refs[-3:]
     micros, rows, width = delta_hbm.shape
     half = width // 2
     begin = micros - 1 if early else 0
@@ -421,6 +423,8 @@
         pltpu.make_async_copy(delta_hbm.at[m], delta.at[pl.ds((m - begin) * rows, rows)], sems.at[m - begin])
         for m in range(begin, micros)
     ]
+    columns = pl.ds(begin * rows, (micros - begin) * rows)
+    loads.append(pltpu.make_async_copy(turned_hbm.at[:, columns], turned, sems.at[micros - begin]))
     for load in loads:
         load.start()
     for load in loads:
@@ -432,8 +436,7 @@
         delta[tail] = (came[...].astype(F32) * delta[tail].astype(F32)).astype(BF16)
 
     for c, bits in enumerate(bit_orders(replicas)):
-        columns = slice(begin * rows, micros * rows)
-        left = picked_rows(turned, number_ref[0], bits, which, width // replicas, columns)
+        left = picked_rows(turned, number_ref[0], bits, which, width // replicas, slice(None))
         for at in range(0, half, TILE):
             product = dot(left, delta[:, c * half + at : c * half + at + TILE], NN)
             if early:
@@ -448,13 +451,17 @@
     return pl.pallas_call(
         functools.partial(weight_kernel, replicas, which),
         out_shape=(jax.ShapeDtypeStruct(half, F32) if which else pltpu.HBM(half, BF16),) * 2,
-        in_specs=[SMEM, SMEM, VMEM, HBM] + [VMEM] * (1 + len(early)),
+        in_specs=[SMEM, SMEM, HBM, HBM] + [VMEM] * (1 + len(early)),
         out_specs=(VMEM,) * 2,
-        scratch_shapes=[pltpu.VMEM((taken * rows, width), BF16), pltpu.SemaphoreType.DMA((taken,))],
+        scratch_shapes=[
+            pltpu.VMEM((width, taken * rows), BF16),
+            pltpu.VMEM((taken * rows, width), BF16),
+            pltpu.SemaphoreType.DMA((taken + 1,)),
+        ],
         compiler_params=pltpu.CompilerParams(vmem_limit_bytes=18 * MIB),
         cost_estimate=LIGHT,
         name="weight",
-    )(flag, number, turned, stay(delta), came, *early)
+    )(flag, number, stay(turned), stay(delta), came, *early)
 
 
 def own_half(keep, got, bit):

time: 98.4 us -> 96.8 us (0.984)
  Pallas kernels: 25.2 us -> 27.5 us
  local copies, waits for them, and re-layouts: 2.95 us -> 1.62 us
  other arithmetic: 3.61 us -> 2.59 us
  starting transfers between devices: 32.4 us -> 31.4 us
    ppermute x6, waiting for transfers between devices: 13.1 us -> 10.8 us  [scatter_sums(): lax.ppermute(send, 'dp', pairs_of(bits[n]))]
    all_to_all x1, waiting for transfers between devices: 3.74 us -> 5.62 us  [scatter_sums(): lax.all_to_all(table.reshape(1 << steps, -1, table.shape[1]), 'dp', 0, 0)]
    unnamed x20 -> x16, local copies, waits for them, and re-layouts: 2.95 us -> 1.62 us
    convert_element_type x4, other arithmetic: 1.38 us -> 0.35 us  [own_half(): return (pick(1 - mine).astype(BF16), pick(mine))]
  transfers between devices with their start and end apart: 22 -> 22, of which waited for: 8 -> 8; matrix products, arithmetic and copies ran while one was open for 3% -> 2% of each run, Pallas kernels for 15% -> 18%
where the time goes in v8:
time: 96.8 us; the launch traced here: 96.2 us
  waiting for transfers between devices  32 us (33%)
  starting transfers between devices  31.4 us (32%)
  Pallas kernels  27.5 us (28%)
  other arithmetic  2.59 us (3%)
  local copies, waits for them, and re-layouts  1.62 us (2%)
  between operations  1.11 us (1%)
    ppermute x12, waiting for transfers between devices, body(): lax.ppermute(g, 'section', [(source, source - 1)])  15.5 us
    ppermute x12, starting transfers between devices, body(): lax.ppermute(g, 'section', [(source, source - 1)])  13.2 us
    ppermute x6, waiting for transfers between devices, scatter_sums(): lax.ppermute(send, 'dp', pairs_of(bits[n]))  10.8 us
    ppermute x6, starting transfers between devices, scatter_sums(): lax.ppermute(send, 'dp', pairs_of(bits[n]))  10.7 us
    pallas_call x4, Pallas kernels, first_call(): pl.pallas_call(functools.partial(first_kernel, m), out_shape=(block, pltp...  8.1 us
    pallas_call x11, Pallas kernels, hop_call(): pl.pallas_call(functools.partial(hop_kernel, m, with_grad), out_shape=out...  6.79 us
    pallas_call x2, Pallas kernels, weight_call(): pl.pallas_call(functools.partial(weight_kernel, replicas, which), out_sha...  6.31 us
    all_to_all x1, waiting for transfers between devices, scatter_sums(): lax.all_to_all(table.reshape(1 << steps, -1, table.shape[1]), 'dp', 0, 0)  5.62 us
  transfers between devices with their start and end apart: 22, of which 8 were waited for; matrix products, arithmetic and copies ran while one was open for 2% of the time, Pallas kernels for 18%

profile of v8, /device:TPU:0, one launch (start us, length us, event | category | flops | bytes accessed | tf_op | source)
XLA Modules:
  0.0 96.2 jit_solution(14793781521031062635)
XLA Ops:
  0.7 7.6 %first.4 = (bf16[256,1024]{1,0:T(8,128)(2,1)}, bf16[4,256,1024]{2,1,0:T(8,128)(2,1)}, bf16[1024,256]{1,0:T(8,128)(2,1)}, bf16[1024,256]{1,0:T(8,128)(2,1)}, bf16[256,1024]{1,0:T(8,128)(2,1)}) custom-call(s32[1]{0:T(128)} %bitcast.4.flag_ref, s32[1,4]{1,0:T(1,128)} %bitcast.80, bf16[4,256,1024]{2,1,0:T(8,128)(2,1)} %bitcast.32, bf16[1024,1024]{1,0:T(8,128)(2,1)} %bitcast.48, ...), custom_call_target="tpu_custom_call" | custom-call | flops 1024 | bytes 1024 | tf_op jit(solution)/shard_map/first/pallas_call | solution.py:179
  8.3 0.7 collective-permute-start.3
  9.0 0.1 first.5
  9.1 0.7 collective-permute-start.2
  9.8 0.3 first.6
  10.1 1.5 %collective-permute-start.1 = (bf16[256,1024]{1,0:T(8,128)(2,1)}, bf16[256,1024]{1,0:T(8,128)(2,1)}, u32[]{:S(2)}, u32[]{:S(2)}) collective-permute-start(bf16[256,1024]{1,0:T(8,128)(2,1)} %get-tuple-element.55), channel_id=1, source_target_pairs={{24,16},{25,17},{26,18},{27,19},{28,20},{29,21},{30,22},{31,23}} | collective-permute-start | bytes 1572872 | tf_op jit(solution)/shard_map/ppermute | solution.py:528
  11.7 0.7 collective-permute-start
  12.4 1.6 %copy-done.2 = bf16[1,1024,1024]{2,1,0:T(8,128)(2,1)S(1)} copy-done((bf16[1,1024,1024]{2,1,0:T(8,128)(2,1)S(1)}, bf16[1,1024,1024]{2,1,0:T(8,128)(2,1)}, u32[]{:S(2)}) %copy-start.2) | copy-done | bytes 2097176
  14.1 0.7 collective-permute-start.6
  14.8 0.7 collective-permute-start.5
  15.6 1.5 %collective-permute-start.4 = (bf16[256,1024]{1,0:T(8,128)(2,1)}, bf16[256,1024]{1,0:T(8,128)(2,1)}, u32[]{:S(2)}, u32[]{:S(2)}) collective-permute-start(bf16[256,1024]{1,0:T(8,128)(2,1)} %get-tuple-element.64), channel_id=1, source_target_pairs={{16,8},{17,9},{18,10},{19,11},{20,12},{21,13},{22,14},{23,15}} | collective-permute-start | bytes 1572872 | tf_op jit(solution)/shard_map/ppermute | solution.py:528
  17.2 1.6 %collective-permute-start.10 = (bf16[256,1024]{1,0:T(8,128)(2,1)}, bf16[256,1024]{1,0:T(8,128)(2,1)}, u32[]{:S(2)}, u32[]{:S(2)}) collective-permute-start(bf16[256,1024]{1,0:T(8,128)(2,1)} %get-tuple-element.62.after_hbm), channel_id=1, source_target_pairs={{16,8},{17,9},{18,10},{19,11},{20,12},{21,13},{22,14},{23,15}} | collective-permute-start | bytes 1572872 | tf_op jit(solution)/shard_map/ppermute | solution.py:528
  18.8 3.2 %turn.1 = (bf16[1024,1024]{1,0:T(8,128)(2,1)}, bf16[16,128]{1,0:T(8,128)(2,1)}) custom-call(bf16[4,256,1024]{2,1,0:T(8,128)(2,1)} %bitcast.38, bf16[256,1024]{1,0:T(8,128)(2,1)} %get-tuple-element.62.after_hbm), custom_call_target="tpu_custom_call" | custom-call | flops 1024 | bytes 1024 | tf_op jit(solution)/shard_map/turn/pallas_call | solution.py:360
  22.1 1.3 %collective-permute-start.9 = (bf16[256,1024]{1,0:T(8,128)(2,1)}, bf16[256,1024]{1,0:T(8,128)(2,1)S(1)}, u32[]{:S(2)}, u32[]{:S(2)}) collective-permute-start(bf16[256,1024]{1,0:T(8,128)(2,1)} %get-tuple-element.73), channel_id=1, source_target_pairs={{8,0},{9,1},{10,2},{11,3},{12,4},{13,5},{14,6},{15,7}} | collective-permute-start | bytes 1572872 | tf_op jit(solution)/shard_map/ppermute | solution.py:528
  23.5 1.3 %collective-permute-start.8 = (bf16[256,1024]{1,0:T(8,128)(2,1)}, bf16[256,1024]{1,0:T(8,128)(2,1)S(1)}, u32[]{:S(2)}, u32[]{:S(2)}) collective-permute-start(bf16[256,1024]{1,0:T(8,128)(2,1)} %get-tuple-element.72), channel_id=1, source_target_pairs={{8,0},{9,1},{10,2},{11,3},{12,4},{13,5},{14,6},{15,7}} | collective-permute-start | bytes 1572872 | tf_op jit(solution)/shard_map/ppermute | solution.py:528
  24.8 1.3 %collective-permute-start.7 = (bf16[256,1024]{1,0:T(8,128)(2,1)}, bf16[256,1024]{1,0:T(8,128)(2,1)}, u32[]{:S(2)}, u32[]{:S(2)}) collective-permute-start(bf16[256,1024]{1,0:T(8,128)(2,1)} %get-tuple-element.71), channel_id=1, source_target_pairs={{8,0},{9,1},{10,2},{11,3},{12,4},{13,5},{14,6},{15,7}} | collective-permute-start | bytes 1572872 | tf_op jit(solution)/shard_map/ppermute | solution.py:528
  26.1 0.3 hop.15
  26.4 1.3 %collective-permute-start.11 = (bf16[256,1024]{1,0:T(8,128)(2,1)}, bf16[256,1024]{1,0:T(8,128)(2,1)S(1)}, u32[]{:S(2)}, u32[]{:S(2)}) collective-permute-start(bf16[256,1024]{1,0:T(8,128)(2,1)} %get-tuple-element.76), channel_id=1, source_target_pairs={{8,0},{9,1},{10,2},{11,3},{12,4},{13,5},{14,6},{15,7}} | collective-permute-start | bytes 1572872 | tf_op jit(solution)/shard_map/ppermute | solution.py:528
  27.7 7.6 %collective-permute-done.9.came_hbm = bf16[256,1024]{1,0:T(8,128)(2,1)S(1)} collective-permute-done((bf16[256,1024]{1,0:T(8,128)(2,1)}, bf16[256,1024]{1,0:T(8,128)(2,1)S(1)}, u32[]{:S(2)}, u32[]{:S(2)}) %collective-permute-start.9) | collective-permute-done | bytes 524320 | tf_op jit(solution)/shard_map/ppermute | solution.py:528
  35.3 2.0 %end.3.delta_in = bf16[4,256,1024]{2,1,0:T(8,128)(2,1)} custom-call(s32[1]{0:T(128)} %bitcast.flag_ref, bf16[256,1024]{1,0:T(8,128)(2,1)S(1)} %collective-permute-done.9.came_hbm, bf16[4,256,1024]{2,1,0:T(8,128)(2,1)} %get-tuple-element.75.delta_in, bf16[1024,1024]{1,0:T(8,128)(2,1)} %bitcast.49, ...), custom_call_target="tpu_custom_call", output_to_operand_aliasing={{}: (2, {})} | custom-call | flops 1024 | bytes 1024 | tf_op jit(solution)/shard_map/end/pallas_call | solution.py:321
  37.3 3.6 %collective-permute-done.8.came_hbm = bf16[256,1024]{1,0:T(8,128)(2,1)S(1)} collective-permute-done((bf16[256,1024]{1,0:T(8,128)(2,1)}, bf16[256,1024]{1,0:T(8,128)(2,1)S(1)}, u32[]{:S(2)}, u32[]{:S(2)}) %collective-permute-start.8) | collective-permute-done | bytes 524320 | tf_op jit(solution)/shard_map/ppermute | solution.py:528
  40.9 2.0 %end.4.delta_in = bf16[4,256,1024]{2,1,0:T(8,128)(2,1)} custom-call(s32[1]{0:T(128)} %bitcast.flag_ref, bf16[256,1024]{1,0:T(8,128)(2,1)S(1)} %collective-permute-done.8.came_hbm, bf16[4,256,1024]{2,1,0:T(8,128)(2,1)} %end.3.delta_in, bf16[1024,1024]{1,0:T(8,128)(2,1)} %bitcast.50, bf16[4,256,1024]{2,1,0:T(8,128)(2,1)} %bitcast.43), custom_call_target="tpu_custom_call", output_to_operand_aliasing={{}: (2, {})} | custom-call | flops 1024 | bytes 1024 | tf_op jit(solution)/shard_map/end/pallas_call | solution.py:321
  42.9 3.9 %collective-permute-done.7.came_hbm = bf16[256,1024]{1,0:T(8,128)(2,1)} collective-permute-done((bf16[256,1024]{1,0:T(8,128)(2,1)}, bf16[256,1024]{1,0:T(8,128)(2,1)}, u32[]{:S(2)}, u32[]{:S(2)}) %collective-permute-start.7) | collective-permute-done | bytes 524320 | tf_op jit(solution)/shard_map/ppermute | solution.py:528
  46.9 2.1 %end.5.delta_hbm = bf16[4,256,1024]{2,1,0:T(8,128)(2,1)} custom-call(s32[1]{0:T(128)} %bitcast.flag_ref, bf16[256,1024]{1,0:T(8,128)(2,1)} %collective-permute-done.7.came_hbm, bf16[4,256,1024]{2,1,0:T(8,128)(2,1)} %end.4.delta_in, bf16[1024,1024]{1,0:T(8,128)(2,1)} %bitcast.51, bf16[4,256,1024]{2,1,0:T(8,128)(2,1)} %bitcast.44), custom_call_target="tpu_custom_call", output_to_operand_aliasing={{}: (2, {})} | custom-call | flops 1024 | bytes 1024 | tf_op jit(solution)/shard_map/end/pallas_call | solution.py:321
  49.0 2.9 %early.1 = (f32[512,512]{1,0:T(8,128)S(1)}, f32[512,512]{1,0:T(8,128)S(1)}) custom-call(s32[1]{0:T(128)} %bitcast.1.number_ref, bf16[1024,1024]{1,0:T(8,128)(2,1)} %get-tuple-element.63.turned_hbm, bf16[4,256,1024]{2,1,0:T(8,128)(2,1)} %end.5.delta_hbm), custom_call_target="tpu_custom_call" | custom-call | flops 1024 | bytes 1024 | tf_op jit(solution)/shard_map/early/pallas_call | solution.py:401
  52.0 0.4 collective-permute-done.11.came
  52.4 2.6 %weight.3 = (bf16[512,512]{1,0:T(8,128)(2,1)}, bf16[512,512]{1,0:T(8,128)(2,1)}) custom-call(s32[1]{0:T(128)} %bitcast.flag_ref, s32[1]{0:T(128)} %bitcast.1.number_ref, bf16[1024,1024]{1,0:T(8,128)(2,1)} %get-tuple-element.63.turned_hbm, bf16[4,256,1024]{2,1,0:T(8,128)(2,1)} %end.5.delta_hbm, bf16[256,1024]{1,0:T(8,128)(2,1)S(1)} %collective-permute-done.11.came, ...), custom_call_target="tpu_custom_call" | custom-call | flops 1024 | bytes 1024 | tf_op jit(solution)/shard_map/weight/pallas_call | solution.py:451
  55.0 1.6 %collective-permute-start.12 = (bf16[512,512]{1,0:T(8,128)(2,1)}, bf16[512,512]{1,0:T(8,128)(2,1)S(1)}, u32[]{:S(2)}, u32[]{:S(2)}) collective-permute-start(bf16[512,512]{1,0:T(8,128)(2,1)} %get-tuple-element.80), channel_id=1, source_target_pairs={{0,1},{1,0},{2,3},{3,2},{4,5},{5,4},{6,7},{7,6},{8,9},{9,8},{10,11... | collective-permute-start | bytes 1572872 | tf_op jit(solution)/shard_map/ppermute | solution.py:482
  56.6 1.6 %collective-permute-start.15 = (bf16[512,512]{1,0:T(8,128)(2,1)}, bf16[512,512]{1,0:T(8,128)(2,1)S(1)}, u32[]{:S(2)}, u32[]{:S(2)}) collective-permute-start(bf16[512,512]{1,0:T(8,128)(2,1)} %get-tuple-element.82), channel_id=1, source_target_pairs={{0,2},{1,3},{2,0},{3,1},{4,6},{5,7},{6,4},{7,5},{8,10},{9,11},{10,... | collective-permute-start | bytes 1572872 | tf_op jit(solution)/shard_map/ppermute | solution.py:482
  58.2 0.1 table.1
  58.4 1.3 %collective-permute-start.18 = (bf16[128,512]{1,0:T(8,128)(2,1)}, bf16[128,512]{1,0:T(8,128)(2,1)S(1)}, u32[]{:S(2)}, u32[]{:S(2)}) collective-permute-start(bf16[128,512]{1,0:T(8,128)(2,1)} %get-tuple-element.96), channel_id=1, source_target_pairs={{24,0},{25,1},{26,2},{27,3},{28,4},{29,5},{30,6},{31,7}} | collective-permute-start | bytes 393224 | tf_op jit(solution)/shard_map/ppermute | solution.py:542
  59.7 0.7 collective-permute-start.19
  60.3 0.7 collective-permute-start.20
  61.0 3.7 %weight.2 = (f32[512,512]{1,0:T(8,128)S(1)}, f32[512,512]{1,0:T(8,128)S(1)}) custom-call(s32[1]{0:T(128)} %bitcast.flag_ref, s32[1]{0:T(128)} %bitcast.1.number_ref, bf16[1024,1024]{1,0:T(8,128)(2,1)} %get-tuple-element.63.turned_hbm, bf16[4,256,1024]{2,1,0:T(8,128)(2,1)} %end.5.delta_hbm, bf16[256,1024]{1,0:T(8,128)(2,1)S(1)} %collective-permute-done.11.came), custom_call_target="tpu_custom_call" | custom-call | flops 1024 | bytes 1024 | tf_op jit(solution)/shard_map/weight/pallas_call | solution.py:451
  64.7 5.0 %collective-permute-done.12 = bf16[512,512]{1,0:T(8,128)(2,1)S(1)} collective-permute-done((bf16[512,512]{1,0:T(8,128)(2,1)}, bf16[512,512]{1,0:T(8,128)(2,1)S(1)}, u32[]{:S(2)}, u32[]{:S(2)}) %collective-permute-start.12) | collective-permute-done | bytes 524320 | tf_op jit(solution)/shard_map/ppermute | solution.py:482
  69.7 0.1 fusion
  69.8 1.6 %collective-permute-start.13 = (bf16[256,512]{1,0:T(8,128)(2,1)S(1)}, bf16[256,512]{1,0:T(8,128)(2,1)S(1)}, u32[]{:S(2)}, u32[]{:S(2)}) collective-permute-start(bf16[256,512]{1,0:T(8,128)(2,1)S(1)} %get-tuple-element.100), channel_id=1, source_target_pairs={{0,2},{1,3},{2,0},{3,1},{4,6},{5,7},{6,4},{7,5},{8,10},{9,11},{10,... | collective-permute-start | bytes 786440 | tf_op jit(solution)/shard_map/ppermute | solution.py:482
  71.5 0.7 add_select_fusion
  72.2 0.1 fusion.1
  72.4 4.8 %all-to-all-start = ((bf16[8,16,512]{2,1,0:T(8,128)(2,1)}), bf16[8,16,512]{2,1,0:T(8,128)(2,1)S(1)}, u32[]{:S(2)}, u32[]{:S(2)}) async-start(bf16[8,16,512]{2,1,0:T(8,128)(2,1)} %bitcast.24), calls=%async_computation | async-start | bytes 262144 | tf_op jit(solution)/shard_map/all_to_all | solution.py:489
  77.2 2.0 %collective-permute-start.16 = (bf16[256,512]{1,0:T(8,128)(2,1)S(1)}, bf16[256,512]{1,0:T(8,128)(2,1)S(1)}, u32[]{:S(2)}, u32[]{:S(2)}) collective-permute-start(bf16[256,512]{1,0:T(8,128)(2,1)S(1)} %get-tuple-element.102), channel_id=1, source_target_pairs={{0,1},{1,0},{2,3},{3,2},{4,5},{5,4},{6,7},{7,6},{8,9},{9,8},{10,11... | collective-permute-start | bytes 786440 | tf_op jit(solution)/shard_map/ppermute | solution.py:482
  79.2 2.4 %collective-permute-start.14 = (bf16[128,512]{1,0:T(8,128)(2,1)S(1)}, bf16[128,512]{1,0:T(8,128)(2,1)S(1)}, u32[]{:S(2)}, u32[]{:S(2)}) collective-permute-start(bf16[128,512]{1,0:T(8,128)(2,1)S(1)} %fusion.2), channel_id=1, source_target_pairs={{0,4},{1,5},{2,6},{3,7},{4,0},{5,1},{6,2},{7,3},{8,12},{9,13},{10,... | collective-permute-start | bytes 393224 | tf_op jit(solution)/shard_map/ppermute | solution.py:482
  81.7 5.6 %all-to-all-done = bf16[8,16,512]{2,1,0:T(8,128)(2,1)S(1)} async-done(((bf16[8,16,512]{2,1,0:T(8,128)(2,1)}), bf16[8,16,512]{2,1,0:T(8,128)(2,1)S(1)}, u32[]{:S(2)}, u32[]{:S(2)}) %all-to-all-start) | async-done | bytes 131104 | tf_op jit(solution)/shard_map/all_to_all | solution.py:489
  87.3 0.6 convert_reduce_fusion
  88.0 1.5 %collective-permute-start.17 = (bf16[128,512]{1,0:T(8,128)(2,1)S(1)}, bf16[128,512]{1,0:T(8,128)(2,1)S(1)}, u32[]{:S(2)}, u32[]{:S(2)}) collective-permute-start(bf16[128,512]{1,0:T(8,128)(2,1)S(1)} %fusion.3), channel_id=1, source_target_pairs={{0,4},{1,5},{2,6},{3,7},{4,0},{5,1},{6,2},{7,3},{8,12},{9,13},{10,... | collective-permute-start | bytes 393224 | tf_op jit(solution)/shard_map/ppermute | solution.py:482
  89.4 0.1 collective-permute-done.14
  89.6 5.7 %collective-permute-done.17 = bf16[128,512]{1,0:T(8,128)(2,1)S(1)} collective-permute-done((bf16[128,512]{1,0:T(8,128)(2,1)S(1)}, bf16[128,512]{1,0:T(8,128)(2,1)S(1)}, u32[]{:S(2)}, u32[]{:S(2)}) %collective-permute-start.17) | collective-permute-done | bytes 131104 | tf_op jit(solution)/shard_map/ppermute | solution.py:482
  95.3 0.8 maximum_bitcast_fusion
  (41 shorter events, 0.6 us)
Async XLA Ops:
  0.6 8.4 %copy-start = (bf16[1,4,256,1024]{3,2,1,0:T(8,128)(2,1)S(1)}, bf16[1,4,256,1024]{3,2,1,0:T(8,128)(2,1)}, u32[]{:S(2)}) copy-start(bf16[1,4,256,1024]{3,2,1,0:T(8,128)(2,1)} %param.6) | copy-start | bytes 6291460
  0.7 8.3 %copy-start.1 = (bf16[1,1024,1024]{2,1,0:T(8,128)(2,1)S(1)}, bf16[1,1024,1024]{2,1,0:T(8,128)(2,1)}, u32[]{:S(2)}) copy-start(bf16[1,1024,1024]{2,1,0:T(8,128)(2,1)} %param.7) | copy-start | bytes 6291460
  0.7 8.3 %copy-start.4 = (bf16[128,2048]{1,0:T(8,128)(2,1)S(1)}, bf16[128,2048]{1,0:T(8,128)(2,1)}, u32[]{:S(2)}) copy-start(bf16[128,2048]{1,0:T(8,128)(2,1)} %table_in.7) | copy-start | bytes 1572868
  8.3 4.1 %collective-permute-start.3 = (bf16[256,1024]{1,0:T(8,128)(2,1)}, bf16[256,1024]{1,0:T(8,128)(2,1)S(1)}, u32[]{:S(2)}, u32[]{:S(2)}) collective-permute-start(bf16[256,1024]{1,0:T(8,128)(2,1)} %get-tuple-element.57), channel_id=1, source_target_pairs={{24,16},{25,17},{26,18},{27,19},{28,20},{29,21},{30,22},{31,23}} | collective-permute-start | bytes 1572872 | tf_op jit(solution)/shard_map/ppermute | solution.py:528
  9.1 5.6 %collective-permute-start.2 = (bf16[256,1024]{1,0:T(8,128)(2,1)}, bf16[256,1024]{1,0:T(8,128)(2,1)S(1)}, u32[]{:S(2)}, u32[]{:S(2)}) collective-permute-start(bf16[256,1024]{1,0:T(8,128)(2,1)} %get-tuple-element.56), channel_id=1, source_target_pairs={{24,16},{25,17},{26,18},{27,19},{28,20},{29,21},{30,22},{31,23}} | collective-permute-start | bytes 1572872 | tf_op jit(solution)/shard_map/ppermute | solution.py:528
  10.1 5.4 %collective-permute-start.1 = (bf16[256,1024]{1,0:T(8,128)(2,1)}, bf16[256,1024]{1,0:T(8,128)(2,1)}, u32[]{:S(2)}, u32[]{:S(2)}) collective-permute-start(bf16[256,1024]{1,0:T(8,128)(2,1)} %get-tuple-element.55), channel_id=1, source_target_pairs={{24,16},{25,17},{26,18},{27,19},{28,20},{29,21},{30,22},{31,23}} | collective-permute-start | bytes 1572872 | tf_op jit(solution)/shard_map/ppermute | solution.py:528
  11.7 5.4 %collective-permute-start = (bf16[256,1024]{1,0:T(8,128)(2,1)}, bf16[256,1024]{1,0:T(8,128)(2,1)S(1)}, u32[]{:S(2)}, u32[]{:S(2)}) collective-permute-start(bf16[256,1024]{1,0:T(8,128)(2,1)} %get-tuple-element.54), channel_id=1, source_target_pairs={{24,16},{25,17},{26,18},{27,19},{28,20},{29,21},{30,22},{31,23}} | collective-permute-start | bytes 1572872 | tf_op jit(solution)/shard_map/ppermute | solution.py:528
  12.4 1.6 %copy-start.2 = (bf16[1,1024,1024]{2,1,0:T(8,128)(2,1)S(1)}, bf16[1,1024,1024]{2,1,0:T(8,128)(2,1)}, u32[]{:S(2)}) copy-start(bf16[1,1024,1024]{2,1,0:T(8,128)(2,1)} %param.7) | copy-start | bytes 6291460
  14.1 7.9 %collective-permute-start.6 = (bf16[256,1024]{1,0:T(8,128)(2,1)}, bf16[256,1024]{1,0:T(8,128)(2,1)S(1)}, u32[]{:S(2)}, u32[]{:S(2)}) collective-permute-start(bf16[256,1024]{1,0:T(8,128)(2,1)} %get-tuple-element.66), channel_id=1, source_target_pairs={{16,8},{17,9},{18,10},{19,11},{20,12},{21,13},{22,14},{23,15}} | collective-permute-start | bytes 1572872 | tf_op jit(solution)/shard_map/ppermute | solution.py:528
  14.8 8.5 %collective-permute-start.5 = (bf16[256,1024]{1,0:T(8,128)(2,1)}, bf16[256,1024]{1,0:T(8,128)(2,1)S(1)}, u32[]{:S(2)}, u32[]{:S(2)}) collective-permute-start(bf16[256,1024]{1,0:T(8,128)(2,1)} %get-tuple-element.65), channel_id=1, source_target_pairs={{16,8},{17,9},{18,10},{19,11},{20,12},{21,13},{22,14},{23,15}} | collective-permute-start | bytes 1572872 | tf_op jit(solution)/shard_map/ppermute | solution.py:528
  15.6 9.1 %collective-permute-start.4 = (bf16[256,1024]{1,0:T(8,128)(2,1)}, bf16[256,1024]{1,0:T(8,128)(2,1)}, u32[]{:S(2)}, u32[]{:S(2)}) collective-permute-start(bf16[256,1024]{1,0:T(8,128)(2,1)} %get-tuple-element.64), channel_id=1, source_target_pairs={{16,8},{17,9},{18,10},{19,11},{20,12},{21,13},{22,14},{23,15}} | collective-permute-start | bytes 1572872 | tf_op jit(solution)/shard_map/ppermute | solution.py:528
  17.2 4.9 %copy-start.3 = (bf16[1,1024,1024]{2,1,0:T(8,128)(2,1)S(1)}, bf16[1,1024,1024]{2,1,0:T(8,128)(2,1)}, u32[]{:S(2)}) copy-start(bf16[1,1024,1024]{2,1,0:T(8,128)(2,1)} %param.7) | copy-start | bytes 6291460
  17.2 9.0 %collective-permute-start.10 = (bf16[256,1024]{1,0:T(8,128)(2,1)}, bf16[256,1024]{1,0:T(8,128)(2,1)}, u32[]{:S(2)}, u32[]{:S(2)}) collective-permute-start(bf16[256,1024]{1,0:T(8,128)(2,1)} %get-tuple-element.62.after_hbm), channel_id=1, source_target_pairs={{16,8},{17,9},{18,10},{19,11},{20,12},{21,13},{22,14},{23,15}} | collective-permute-start | bytes 1572872 | tf_op jit(solution)/shard_map/ppermute | solution.py:528
  22.1 13.2 %collective-permute-start.9 = (bf16[256,1024]{1,0:T(8,128)(2,1)}, bf16[256,1024]{1,0:T(8,128)(2,1)S(1)}, u32[]{:S(2)}, u32[]{:S(2)}) collective-permute-start(bf16[256,1024]{1,0:T(8,128)(2,1)} %get-tuple-element.73), channel_id=1, source_target_pairs={{8,0},{9,1},{10,2},{11,3},{12,4},{13,5},{14,6},{15,7}} | collective-permute-start | bytes 1572872 | tf_op jit(solution)/shard_map/ppermute | solution.py:528
  23.5 17.5 %collective-permute-start.8 = (bf16[256,1024]{1,0:T(8,128)(2,1)}, bf16[256,1024]{1,0:T(8,128)(2,1)S(1)}, u32[]{:S(2)}, u32[]{:S(2)}) collective-permute-start(bf16[256,1024]{1,0:T(8,128)(2,1)} %get-tuple-element.72), channel_id=1, source_target_pairs={{8,0},{9,1},{10,2},{11,3},{12,4},{13,5},{14,6},{15,7}} | collective-permute-start | bytes 1572872 | tf_op jit(solution)/shard_map/ppermute | solution.py:528
  24.8 22.1 %collective-permute-start.7 = (bf16[256,1024]{1,0:T(8,128)(2,1)}, bf16[256,1024]{1,0:T(8,128)(2,1)}, u32[]{:S(2)}, u32[]{:S(2)}) collective-permute-start(bf16[256,1024]{1,0:T(8,128)(2,1)} %get-tuple-element.71), channel_id=1, source_target_pairs={{8,0},{9,1},{10,2},{11,3},{12,4},{13,5},{14,6},{15,7}} | collective-permute-start | bytes 1572872 | tf_op jit(solution)/shard_map/ppermute | solution.py:528
  26.4 26.0 %collective-permute-start.11 = (bf16[256,1024]{1,0:T(8,128)(2,1)}, bf16[256,1024]{1,0:T(8,128)(2,1)S(1)}, u32[]{:S(2)}, u32[]{:S(2)}) collective-permute-start(bf16[256,1024]{1,0:T(8,128)(2,1)} %get-tuple-element.76), channel_id=1, source_target_pairs={{8,0},{9,1},{10,2},{11,3},{12,4},{13,5},{14,6},{15,7}} | collective-permute-start | bytes 1572872 | tf_op jit(solution)/shard_map/ppermute | solution.py:528
  52.4 5.8 %copy-start.5 = (bf16[4,1,1024]{2,0,1:T(4,128)(2,1)S(1)}, bf16[4,1,1024]{2,0,1:T(4,128)(2,1)}, u32[]{:S(2)}) copy-start(bf16[4,1,1024]{2,0,1:T(4,128)(2,1)} %param.11) | copy-start | bytes 24580
  52.4 5.8 %copy-start.6 = (s32[4,1,64]{2,1,0:T(1,128)S(1)}, s32[4,1,64]{2,1,0:T(1,128)}, u32[]{:S(2)}) copy-start(s32[4,1,64]{2,1,0:T(1,128)} %index_ref.1) | copy-start | bytes 3076
  55.0 14.7 %collective-permute-start.12 = (bf16[512,512]{1,0:T(8,128)(2,1)}, bf16[512,512]{1,0:T(8,128)(2,1)S(1)}, u32[]{:S(2)}, u32[]{:S(2)}) collective-permute-start(bf16[512,512]{1,0:T(8,128)(2,1)} %get-tuple-element.80), channel_id=1, source_target_pairs={{0,1},{1,0},{2,3},{3,2},{4,5},{5,4},{6,7},{7,6},{8,9},{9,8},{10,11... | collective-permute-start | bytes 1572872 | tf_op jit(solution)/shard_map/ppermute | solution.py:482
  56.6 15.6 %collective-permute-start.15 = (bf16[512,512]{1,0:T(8,128)(2,1)}, bf16[512,512]{1,0:T(8,128)(2,1)S(1)}, u32[]{:S(2)}, u32[]{:S(2)}) collective-permute-start(bf16[512,512]{1,0:T(8,128)(2,1)} %get-tuple-element.82), channel_id=1, source_target_pairs={{0,2},{1,3},{2,0},{3,1},{4,6},{5,7},{6,4},{7,5},{8,10},{9,11},{10,... | collective-permute-start | bytes 1572872 | tf_op jit(solution)/shard_map/ppermute | solution.py:482
  58.4 13.1 %collective-permute-start.18 = (bf16[128,512]{1,0:T(8,128)(2,1)}, bf16[128,512]{1,0:T(8,128)(2,1)S(1)}, u32[]{:S(2)}, u32[]{:S(2)}) collective-permute-start(bf16[128,512]{1,0:T(8,128)(2,1)} %get-tuple-element.96), channel_id=1, source_target_pairs={{24,0},{25,1},{26,2},{27,3},{28,4},{29,5},{30,6},{31,7}} | collective-permute-start | bytes 393224 | tf_op jit(solution)/shard_map/ppermute | solution.py:542
  59.7 11.8 %collective-permute-start.19 = (bf16[128,512]{1,0:T(8,128)(2,1)}, bf16[128,512]{1,0:T(8,128)(2,1)S(1)}, u32[]{:S(2)}, u32[]{:S(2)}) collective-permute-start(bf16[128,512]{1,0:T(8,128)(2,1)} %get-tuple-element.97), channel_id=1, source_target_pairs={{24,8},{25,9},{26,10},{27,11},{28,12},{29,13},{30,14},{31,15}} | collective-permute-start | bytes 393224 | tf_op jit(solution)/shard_map/ppermute | solution.py:542
  60.3 11.2 %collective-permute-start.20 = (bf16[128,512]{1,0:T(8,128)(2,1)}, bf16[128,512]{1,0:T(8,128)(2,1)S(1)}, u32[]{:S(2)}, u32[]{:S(2)}) collective-permute-start(bf16[128,512]{1,0:T(8,128)(2,1)} %get-tuple-element.98), channel_id=1, source_target_pairs={{24,16},{25,17},{26,18},{27,19},{28,20},{29,21},{30,22},{31,23}} | collective-permute-start | bytes 393224 | tf_op jit(solution)/shard_map/ppermute | solution.py:542
  64.7 6.8 %copy-start.7 = (bf16[128,512]{1,0:T(8,128)(2,1)S(1)}, bf16[128,512]{1,0:T(8,128)(2,1)}, u32[]{:S(2)}) copy-start(bf16[128,512]{1,0:T(8,128)(2,1)} %get-tuple-element.95) | copy-start | bytes 393220
  69.8 9.4 %collective-permute-start.13 = (bf16[256,512]{1,0:T(8,128)(2,1)S(1)}, bf16[256,512]{1,0:T(8,128)(2,1)S(1)}, u32[]{:S(2)}, u32[]{:S(2)}) collective-permute-start(bf16[256,512]{1,0:T(8,128)(2,1)S(1)} %get-tuple-element.100), channel_id=1, source_target_pairs={{0,2},{1,3},{2,0},{3,1},{4,6},{5,7},{6,4},{7,5},{8,10},{9,11},{10,... | collective-permute-start | bytes 786440 | tf_op jit(solution)/shard_map/ppermute | solution.py:482
  72.4 14.9 %all-to-all-start = ((bf16[8,16,512]{2,1,0:T(8,128)(2,1)}), bf16[8,16,512]{2,1,0:T(8,128)(2,1)S(1)}, u32[]{:S(2)}, u32[]{:S(2)}) async-start(bf16[8,16,512]{2,1,0:T(8,128)(2,1)} %bitcast.24), calls=%async_computation | async-start | bytes 262144 | tf_op jit(solution)/shard_map/all_to_all | solution.py:489
  77.2 10.7 %collective-permute-start.16 = (bf16[256,512]{1,0:T(8,128)(2,1)S(1)}, bf16[256,512]{1,0:T(8,128)(2,1)S(1)}, u32[]{:S(2)}, u32[]{:S(2)}) collective-permute-start(bf16[256,512]{1,0:T(8,128)(2,1)S(1)} %get-tuple-element.102), channel_id=1, source_target_pairs={{0,1},{1,0},{2,3},{3,2},{4,5},{5,4},{6,7},{7,6},{8,9},{9,8},{10,11... | collective-permute-start | bytes 786440 | tf_op jit(solution)/shard_map/ppermute | solution.py:482
  79.2 10.3 %collective-permute-start.14 = (bf16[128,512]{1,0:T(8,128)(2,1)S(1)}, bf16[128,512]{1,0:T(8,128)(2,1)S(1)}, u32[]{:S(2)}, u32[]{:S(2)}) collective-permute-start(bf16[128,512]{1,0:T(8,128)(2,1)S(1)} %fusion.2), channel_id=1, source_target_pairs={{0,4},{1,5},{2,6},{3,7},{4,0},{5,1},{6,2},{7,3},{8,12},{9,13},{10,... | collective-permute-start | bytes 393224 | tf_op jit(solution)/shard_map/ppermute | solution.py:482
  88.0 7.3 %collective-permute-start.17 = (bf16[128,512]{1,0:T(8,128)(2,1)S(1)}, bf16[128,512]{1,0:T(8,128)(2,1)S(1)}, u32[]{:S(2)}, u32[]{:S(2)}) collective-permute-start(bf16[128,512]{1,0:T(8,128)(2,1)S(1)} %fusion.3), channel_id=1, source_target_pairs={{0,4},{1,5},{2,6},{3,7},{4,0},{5,1},{6,2},{7,3},{8,12},{9,13},{10,... | collective-permute-start | bytes 393224 | tf_op jit(solution)/shard_map/ppermute | solution.py:482

commit v9 on v8

--- a/solution.py
+++ b/solution.py
@@ -283,7 +283,10 @@
     )(flag, index, pooled, stay(after), *map(stay, shares), *map(stay, slants), *map(stay, highs))
 
 
-def hop_kernel(m, with_grad, flag_ref, came_hbm, delta_in, weight, after_hbm, *rest):
+def hop_kernel(m, with_grad, fetch, flag_ref, came_hbm, delta_in, weight_in, after_hbm, *rest):
+    weight = weight_in
+    if fetch:
+        rest, weight = rest[:-1], rest[-1]
     if with_grad:
         grad_hbm, delta_hbm, came, aux, grad, sems = rest
     else:
@@ -293,14 +296,19 @@
     @pl.when(flag_ref[0] == 1)
     def _():
         first = pltpu.make_async_copy(came_hbm, came, sems.at[0])
+        third = pltpu.make_async_copy(weight_in, weight, sems.at[4]) if fetch else None
         second = pltpu.make_async_copy(delta_in.at[m], aux, sems.at[1])
         first.start()
         second.start()
+        if fetch:
+            third.start()
         first.wait()
         second.wait()
         aux[...] = (came[...].astype(F32) * aux[...].astype(F32)).astype(BF16)
         stores = [pltpu.make_async_copy(aux, delta_hbm.at[m], sems.at[2])]
         stores[0].start()
+        if fetch:
+            third.wait()
         if with_grad:
             for n in range(width // TILE):
                 part = slice(n * TILE, (n + 1) * TILE)
@@ -311,24 +319,27 @@
             store.wait()
 
 
-def hop_call(m, flag, came, delta, weight, after, with_grad):
+def hop_call(m, flag, came, delta, weight, after, with_grad, fetch=False):
     rows, width = came.shape
     scratch = [pltpu.VMEM((rows, width), BF16)] * (3 if with_grad else 2)
-    scratch.append(pltpu.SemaphoreType.DMA((4,)))
+    scratch.append(pltpu.SemaphoreType.DMA((5,)))
+    if fetch:
+        scratch.append(pltpu.VMEM(weight.shape, BF16))
+    held = with_grad and not fetch
     outs = (pltpu.HBM(delta.shape, BF16),)
     if with_grad:
         outs = (pltpu.HBM((rows, width), BF16),) + outs
     return pl.pallas_call(
-        functools.partial(hop_kernel, m, with_grad),
+        functools.partial(hop_kernel, m, with_grad, fetch),
         out_shape=outs,
-        in_specs=[SMEM, HBM, HBM, VMEM if with_grad else HBM, HBM],
+        in_specs=[SMEM, HBM, HBM, VMEM if held else HBM, HBM],
         out_specs=(HBM,) * len(outs),
         scratch_shapes=scratch,
         input_output_aliases={2: len(outs) - 1},
         compiler_params=pltpu.CompilerParams(vmem_limit_bytes=12 * MIB),
         cost_estimate=LIGHT,
         name="hop" if with_grad else "end",
-    )(flag, came, stay(delta), weight if with_grad else stay(weight), stay(after))
+    )(flag, came, stay(delta), weight if held else stay(weight), stay(after))
 
 
 def bit_orders(replicas):
@@ -530,7 +541,7 @@
         for m in range(micro_count):
             if hop + 1 < last:
                 after = token if hop == 1 and m == 0 else acts
-                grads[m], delta = hop_call(m, active, received[m], delta, weight, after, True)
+                grads[m], delta = hop_call(m, active, received[m], delta, weight, after, True, hop == 0 and m == 0)
             elif m + 1 < micro_count:
                 (delta,) = hop_call(m, active, received[m], delta, weight, acts, False)
         if hop == 0:

time: 96.8 us -> 96.1 us (level)
  no operation moved by 1% of the time
where the time goes in v9:
time: 96.1 us; the launch traced here: 95.5 us
  starting transfers between devices  32.3 us (34%)
  waiting for transfers between devices  31.3 us (33%)
  Pallas kernels  27.6 us (29%)
  other arithmetic  2.59 us (3%)
  between operations  1.06 us (1%)
    ppermute x12, waiting for transfers between devices, body(): lax.ppermute(g, 'section', [(source, source - 1)])  14.9 us
    ppermute x12, starting transfers between devices, body(): lax.ppermute(g, 'section', [(source, source - 1)])  14 us
    ppermute x6, waiting for transfers between devices, scatter_sums(): lax.ppermute(send, 'dp', pairs_of(bits[n]))  10.8 us
    ppermute x6, starting transfers between devices, scatter_sums(): lax.ppermute(send, 'dp', pairs_of(bits[n]))  10.8 us
    pallas_call x4, Pallas kernels, first_call(): pl.pallas_call(functools.partial(first_kernel, m), out_shape=(block, pltp...  8.11 us
    pallas_call x11, Pallas kernels, hop_call(): pl.pallas_call(functools.partial(hop_kernel, m, with_grad, fetch), out_sh...  6.87 us
    pallas_call x2, Pallas kernels, weight_call(): pl.pallas_call(functools.partial(weight_kernel, replicas, which), out_sha...  6.3 us
    all_to_all x1, waiting for transfers between devices, scatter_sums(): lax.all_to_all(table.reshape(1 << steps, -1, table.shape[1]), 'dp', 0, 0)  5.59 us
  transfers between devices with their start and end apart: 22, of which 8 were waited for; matrix products, arithmetic and copies ran while one was open for 2% of the time, Pallas kernels for 18%

profile of v9, /device:TPU:0, one launch (start us, length us, event | category | flops | bytes accessed | tf_op | source)
XLA Modules:
  0.0 95.5 jit_solution(15777292218012403670)
XLA Ops:
  0.7 7.6 %first.4 = (bf16[256,1024]{1,0:T(8,128)(2,1)}, bf16[4,256,1024]{2,1,0:T(8,128)(2,1)}, bf16[1024,256]{1,0:T(8,128)(2,1)}, bf16[1024,256]{1,0:T(8,128)(2,1)}, bf16[256,1024]{1,0:T(8,128)(2,1)}) custom-call(s32[1]{0:T(128)} %bitcast.4.flag_ref, s32[1,4]{1,0:T(1,128)} %bitcast.80, bf16[4,256,1024]{2,1,0:T(8,128)(2,1)} %bitcast.32, bf16[1024,1024]{1,0:T(8,128)(2,1)} %bitcast.48, ...), custom_call_target="tpu_custom_call" | custom-call | flops 1024 | bytes 1024 | tf_op jit(solution)/shard_map/first/pallas_call | solution.py:179
  8.3 0.7 collective-permute-start.3
  9.0 0.1 first.5
  9.1 0.7 collective-permute-start.2
  9.8 0.3 first.6
  10.1 1.5 %collective-permute-start.1 = (bf16[256,1024]{1,0:T(8,128)(2,1)}, bf16[256,1024]{1,0:T(8,128)(2,1)}, u32[]{:S(2)}, u32[]{:S(2)}) collective-permute-start(bf16[256,1024]{1,0:T(8,128)(2,1)} %get-tuple-element.55), channel_id=1, source_target_pairs={{24,16},{25,17},{26,18},{27,19},{28,20},{29,21},{30,22},{31,23}} | collective-permute-start | bytes 1572872 | tf_op jit(solution)/shard_map/ppermute | solution.py:539
  11.7 1.5 %collective-permute-start = (bf16[256,1024]{1,0:T(8,128)(2,1)}, bf16[256,1024]{1,0:T(8,128)(2,1)}, u32[]{:S(2)}, u32[]{:S(2)}) collective-permute-start(bf16[256,1024]{1,0:T(8,128)(2,1)} %get-tuple-element.54), channel_id=1, source_target_pairs={{24,16},{25,17},{26,18},{27,19},{28,20},{29,21},{30,22},{31,23}} | collective-permute-start | bytes 1572872 | tf_op jit(solution)/shard_map/ppermute | solution.py:539
  13.3 0.8 collective-permute-start.6
  14.1 0.7 copy-done.2
  14.8 0.7 collective-permute-start.5
  15.6 1.5 %collective-permute-start.4 = (bf16[256,1024]{1,0:T(8,128)(2,1)}, bf16[256,1024]{1,0:T(8,128)(2,1)}, u32[]{:S(2)}, u32[]{:S(2)}) collective-permute-start(bf16[256,1024]{1,0:T(8,128)(2,1)} %get-tuple-element.64), channel_id=1, source_target_pairs={{16,8},{17,9},{18,10},{19,11},{20,12},{21,13},{22,14},{23,15}} | collective-permute-start | bytes 1572872 | tf_op jit(solution)/shard_map/ppermute | solution.py:539
  17.2 1.5 %collective-permute-start.10 = (bf16[256,1024]{1,0:T(8,128)(2,1)}, bf16[256,1024]{1,0:T(8,128)(2,1)}, u32[]{:S(2)}, u32[]{:S(2)}) collective-permute-start(bf16[256,1024]{1,0:T(8,128)(2,1)} %get-tuple-element.62.after_hbm), channel_id=1, source_target_pairs={{16,8},{17,9},{18,10},{19,11},{20,12},{21,13},{22,14},{23,15}} | collective-permute-start | bytes 1572872 | tf_op jit(solution)/shard_map/ppermute | solution.py:539
  18.6 3.2 %turn.1 = (bf16[1024,1024]{1,0:T(8,128)(2,1)}, bf16[16,128]{1,0:T(8,128)(2,1)}) custom-call(bf16[4,256,1024]{2,1,0:T(8,128)(2,1)} %bitcast.38, bf16[256,1024]{1,0:T(8,128)(2,1)} %get-tuple-element.62.after_hbm), custom_call_target="tpu_custom_call" | custom-call | flops 1024 | bytes 1024 | tf_op jit(solution)/shard_map/turn/pallas_call | solution.py:371
  22.0 1.3 %collective-permute-start.9 = (bf16[256,1024]{1,0:T(8,128)(2,1)}, bf16[256,1024]{1,0:T(8,128)(2,1)S(1)}, u32[]{:S(2)}, u32[]{:S(2)}) collective-permute-start(bf16[256,1024]{1,0:T(8,128)(2,1)} %get-tuple-element.73), channel_id=1, source_target_pairs={{8,0},{9,1},{10,2},{11,3},{12,4},{13,5},{14,6},{15,7}} | collective-permute-start | bytes 1572872 | tf_op jit(solution)/shard_map/ppermute | solution.py:539
  23.3 1.3 %collective-permute-start.8 = (bf16[256,1024]{1,0:T(8,128)(2,1)}, bf16[256,1024]{1,0:T(8,128)(2,1)S(1)}, u32[]{:S(2)}, u32[]{:S(2)}) collective-permute-start(bf16[256,1024]{1,0:T(8,128)(2,1)} %get-tuple-element.72), channel_id=1, source_target_pairs={{8,0},{9,1},{10,2},{11,3},{12,4},{13,5},{14,6},{15,7}} | collective-permute-start | bytes 1572872 | tf_op jit(solution)/shard_map/ppermute | solution.py:539
  24.7 1.3 %collective-permute-start.7 = (bf16[256,1024]{1,0:T(8,128)(2,1)}, bf16[256,1024]{1,0:T(8,128)(2,1)}, u32[]{:S(2)}, u32[]{:S(2)}) collective-permute-start(bf16[256,1024]{1,0:T(8,128)(2,1)} %get-tuple-element.71), channel_id=1, source_target_pairs={{8,0},{9,1},{10,2},{11,3},{12,4},{13,5},{14,6},{15,7}} | collective-permute-start | bytes 1572872 | tf_op jit(solution)/shard_map/ppermute | solution.py:539
  26.0 0.3 hop.15
  26.3 1.3 %collective-permute-start.11 = (bf16[256,1024]{1,0:T(8,128)(2,1)}, bf16[256,1024]{1,0:T(8,128)(2,1)S(1)}, u32[]{:S(2)}, u32[]{:S(2)}) collective-permute-start(bf16[256,1024]{1,0:T(8,128)(2,1)} %get-tuple-element.76), channel_id=1, source_target_pairs={{8,0},{9,1},{10,2},{11,3},{12,4},{13,5},{14,6},{15,7}} | collective-permute-start | bytes 1572872 | tf_op jit(solution)/shard_map/ppermute | solution.py:539
  27.6 7.0 %collective-permute-done.9.came_hbm = bf16[256,1024]{1,0:T(8,128)(2,1)S(1)} collective-permute-done((bf16[256,1024]{1,0:T(8,128)(2,1)}, bf16[256,1024]{1,0:T(8,128)(2,1)S(1)}, u32[]{:S(2)}, u32[]{:S(2)}) %collective-permute-start.9) | collective-permute-done | bytes 524320 | tf_op jit(solution)/shard_map/ppermute | solution.py:539
  34.6 2.0 %end.3.delta_in = bf16[4,256,1024]{2,1,0:T(8,128)(2,1)} custom-call(s32[1]{0:T(128)} %bitcast.flag_ref, bf16[256,1024]{1,0:T(8,128)(2,1)S(1)} %collective-permute-done.9.came_hbm, bf16[4,256,1024]{2,1,0:T(8,128)(2,1)} %get-tuple-element.75.delta_in, bf16[1024,1024]{1,0:T(8,128)(2,1)} %bitcast.50, ...), custom_call_target="tpu_custom_call", output_to_operand_aliasing={{}: (2, {})} | custom-call | flops 1024 | bytes 1024 | tf_op jit(solution)/shard_map/end/pallas_call | solution.py:332
  36.6 3.6 %collective-permute-done.8.came_hbm = bf16[256,1024]{1,0:T(8,128)(2,1)S(1)} collective-permute-done((bf16[256,1024]{1,0:T(8,128)(2,1)}, bf16[256,1024]{1,0:T(8,128)(2,1)S(1)}, u32[]{:S(2)}, u32[]{:S(2)}) %collective-permute-start.8) | collective-permute-done | bytes 524320 | tf_op jit(solution)/shard_map/ppermute | solution.py:539
  40.2 2.0 %end.4.delta_in = bf16[4,256,1024]{2,1,0:T(8,128)(2,1)} custom-call(s32[1]{0:T(128)} %bitcast.flag_ref, bf16[256,1024]{1,0:T(8,128)(2,1)S(1)} %collective-permute-done.8.came_hbm, bf16[4,256,1024]{2,1,0:T(8,128)(2,1)} %end.3.delta_in, bf16[1024,1024]{1,0:T(8,128)(2,1)} %bitcast.51, bf16[4,256,1024]{2,1,0:T(8,128)(2,1)} %bitcast.43), custom_call_target="tpu_custom_call", output_to_operand_aliasing={{}: (2, {})} | custom-call | flops 1024 | bytes 1024 | tf_op jit(solution)/shard_map/end/pallas_call | solution.py:332
  42.2 3.9 %collective-permute-done.7.came_hbm = bf16[256,1024]{1,0:T(8,128)(2,1)} collective-permute-done((bf16[256,1024]{1,0:T(8,128)(2,1)}, bf16[256,1024]{1,0:T(8,128)(2,1)}, u32[]{:S(2)}, u32[]{:S(2)}) %collective-permute-start.7) | collective-permute-done | bytes 524320 | tf_op jit(solution)/shard_map/ppermute | solution.py:539
  46.2 2.1 %end.5.delta_hbm = bf16[4,256,1024]{2,1,0:T(8,128)(2,1)} custom-call(s32[1]{0:T(128)} %bitcast.flag_ref, bf16[256,1024]{1,0:T(8,128)(2,1)} %collective-permute-done.7.came_hbm, bf16[4,256,1024]{2,1,0:T(8,128)(2,1)} %end.4.delta_in, bf16[1024,1024]{1,0:T(8,128)(2,1)} %bitcast.52, bf16[4,256,1024]{2,1,0:T(8,128)(2,1)} %bitcast.44), custom_call_target="tpu_custom_call", output_to_operand_aliasing={{}: (2, {})} | custom-call | flops 1024 | bytes 1024 | tf_op jit(solution)/shard_map/end/pallas_call | solution.py:332
  48.3 2.9 %early.1 = (f32[512,512]{1,0:T(8,128)S(1)}, f32[512,512]{1,0:T(8,128)S(1)}) custom-call(s32[1]{0:T(128)} %bitcast.1.number_ref, bf16[1024,1024]{1,0:T(8,128)(2,1)} %get-tuple-element.63.turned_hbm, bf16[4,256,1024]{2,1,0:T(8,128)(2,1)} %end.5.delta_hbm), custom_call_target="tpu_custom_call" | custom-call | flops 1024 | bytes 1024 | tf_op jit(solution)/shard_map/early/pallas_call | solution.py:412
  51.2 0.4 collective-permute-done.11.came
  51.7 2.6 %weight.3 = (bf16[512,512]{1,0:T(8,128)(2,1)}, bf16[512,512]{1,0:T(8,128)(2,1)}) custom-call(s32[1]{0:T(128)} %bitcast.flag_ref, s32[1]{0:T(128)} %bitcast.1.number_ref, bf16[1024,1024]{1,0:T(8,128)(2,1)} %get-tuple-element.63.turned_hbm, bf16[4,256,1024]{2,1,0:T(8,128)(2,1)} %end.5.delta_hbm, bf16[256,1024]{1,0:T(8,128)(2,1)S(1)} %collective-permute-done.11.came, ...), custom_call_target="tpu_custom_call" | custom-call | flops 1024 | bytes 1024 | tf_op jit(solution)/shard_map/weight/pallas_call | solution.py:462
  54.3 1.6 %collective-permute-start.12 = (bf16[512,512]{1,0:T(8,128)(2,1)}, bf16[512,512]{1,0:T(8,128)(2,1)S(1)}, u32[]{:S(2)}, u32[]{:S(2)}) collective-permute-start(bf16[512,512]{1,0:T(8,128)(2,1)} %get-tuple-element.80), channel_id=1, source_target_pairs={{0,1},{1,0},{2,3},{3,2},{4,5},{5,4},{6,7},{7,6},{8,9},{9,8},{10,11... | collective-permute-start | bytes 1572872 | tf_op jit(solution)/shard_map/ppermute | solution.py:493
  55.9 1.6 %collective-permute-start.15 = (bf16[512,512]{1,0:T(8,128)(2,1)}, bf16[512,512]{1,0:T(8,128)(2,1)S(1)}, u32[]{:S(2)}, u32[]{:S(2)}) collective-permute-start(bf16[512,512]{1,0:T(8,128)(2,1)} %get-tuple-element.82), channel_id=1, source_target_pairs={{0,2},{1,3},{2,0},{3,1},{4,6},{5,7},{6,4},{7,5},{8,10},{9,11},{10,... | collective-permute-start | bytes 1572872 | tf_op jit(solution)/shard_map/ppermute | solution.py:493
  57.5 0.1 table.1
  57.6 1.3 %collective-permute-start.18 = (bf16[128,512]{1,0:T(8,128)(2,1)}, bf16[128,512]{1,0:T(8,128)(2,1)S(1)}, u32[]{:S(2)}, u32[]{:S(2)}) collective-permute-start(bf16[128,512]{1,0:T(8,128)(2,1)} %get-tuple-element.96), channel_id=1, source_target_pairs={{24,0},{25,1},{26,2},{27,3},{28,4},{29,5},{30,6},{31,7}} | collective-permute-start | bytes 393224 | tf_op jit(solution)/shard_map/ppermute | solution.py:553
  58.9 0.7 collective-permute-start.19
  59.6 0.7 collective-permute-start.20
  60.3 3.7 %weight.2 = (f32[512,512]{1,0:T(8,128)S(1)}, f32[512,512]{1,0:T(8,128)S(1)}) custom-call(s32[1]{0:T(128)} %bitcast.flag_ref, s32[1]{0:T(128)} %bitcast.1.number_ref, bf16[1024,1024]{1,0:T(8,128)(2,1)} %get-tuple-element.63.turned_hbm, bf16[4,256,1024]{2,1,0:T(8,128)(2,1)} %end.5.delta_hbm, bf16[256,1024]{1,0:T(8,128)(2,1)S(1)} %collective-permute-done.11.came), custom_call_target="tpu_custom_call" | custom-call | flops 1024 | bytes 1024 | tf_op jit(solution)/shard_map/weight/pallas_call | solution.py:462
  64.0 5.0 %collective-permute-done.12 = bf16[512,512]{1,0:T(8,128)(2,1)S(1)} collective-permute-done((bf16[512,512]{1,0:T(8,128)(2,1)}, bf16[512,512]{1,0:T(8,128)(2,1)S(1)}, u32[]{:S(2)}, u32[]{:S(2)}) %collective-permute-start.12) | collective-permute-done | bytes 524320 | tf_op jit(solution)/shard_map/ppermute | solution.py:493
  68.9 0.1 fusion
  69.1 1.6 %collective-permute-start.13 = (bf16[256,512]{1,0:T(8,128)(2,1)S(1)}, bf16[256,512]{1,0:T(8,128)(2,1)S(1)}, u32[]{:S(2)}, u32[]{:S(2)}) collective-permute-start(bf16[256,512]{1,0:T(8,128)(2,1)S(1)} %get-tuple-element.100), channel_id=1, source_target_pairs={{0,2},{1,3},{2,0},{3,1},{4,6},{5,7},{6,4},{7,5},{8,10},{9,11},{10,... | collective-permute-start | bytes 786440 | tf_op jit(solution)/shard_map/ppermute | solution.py:493
  70.8 0.7 add_select_fusion
  71.4 0.1 fusion.1
  71.6 4.9 %all-to-all-start = ((bf16[8,16,512]{2,1,0:T(8,128)(2,1)}), bf16[8,16,512]{2,1,0:T(8,128)(2,1)S(1)}, u32[]{:S(2)}, u32[]{:S(2)}) async-start(bf16[8,16,512]{2,1,0:T(8,128)(2,1)} %bitcast.24), calls=%async_computation | async-start | bytes 262144 | tf_op jit(solution)/shard_map/all_to_all | solution.py:500
  76.5 2.0 %collective-permute-start.16 = (bf16[256,512]{1,0:T(8,128)(2,1)S(1)}, bf16[256,512]{1,0:T(8,128)(2,1)S(1)}, u32[]{:S(2)}, u32[]{:S(2)}) collective-permute-start(bf16[256,512]{1,0:T(8,128)(2,1)S(1)} %get-tuple-element.102), channel_id=1, source_target_pairs={{0,1},{1,0},{2,3},{3,2},{4,5},{5,4},{6,7},{7,6},{8,9},{9,8},{10,11... | collective-permute-start | bytes 786440 | tf_op jit(solution)/shard_map/ppermute | solution.py:493
  78.5 2.4 %collective-permute-start.14 = (bf16[128,512]{1,0:T(8,128)(2,1)S(1)}, bf16[128,512]{1,0:T(8,128)(2,1)S(1)}, u32[]{:S(2)}, u32[]{:S(2)}) collective-permute-start(bf16[128,512]{1,0:T(8,128)(2,1)S(1)} %fusion.2), channel_id=1, source_target_pairs={{0,4},{1,5},{2,6},{3,7},{4,0},{5,1},{6,2},{7,3},{8,12},{9,13},{10,... | collective-permute-start | bytes 393224 | tf_op jit(solution)/shard_map/ppermute | solution.py:493
  80.9 5.6 %all-to-all-done = bf16[8,16,512]{2,1,0:T(8,128)(2,1)S(1)} async-done(((bf16[8,16,512]{2,1,0:T(8,128)(2,1)}), bf16[8,16,512]{2,1,0:T(8,128)(2,1)S(1)}, u32[]{:S(2)}, u32[]{:S(2)}) %all-to-all-start) | async-done | bytes 131104 | tf_op jit(solution)/shard_map/all_to_all | solution.py:500
  86.5 0.6 convert_reduce_fusion
  87.2 1.5 %collective-permute-start.17 = (bf16[128,512]{1,0:T(8,128)(2,1)S(1)}, bf16[128,512]{1,0:T(8,128)(2,1)S(1)}, u32[]{:S(2)}, u32[]{:S(2)}) collective-permute-start(bf16[128,512]{1,0:T(8,128)(2,1)S(1)} %fusion.3), channel_id=1, source_target_pairs={{0,4},{1,5},{2,6},{3,7},{4,0},{5,1},{6,2},{7,3},{8,12},{9,13},{10,... | collective-permute-start | bytes 393224 | tf_op jit(solution)/shard_map/ppermute | solution.py:493
  88.7 0.1 collective-permute-done.14
  88.9 5.7 %collective-permute-done.17 = bf16[128,512]{1,0:T(8,128)(2,1)S(1)} collective-permute-done((bf16[128,512]{1,0:T(8,128)(2,1)S(1)}, bf16[128,512]{1,0:T(8,128)(2,1)S(1)}, u32[]{:S(2)}, u32[]{:S(2)}) %collective-permute-start.17) | collective-permute-done | bytes 131104 | tf_op jit(solution)/shard_map/ppermute | solution.py:493
  94.7 0.8 maximum_bitcast_fusion
  (39 shorter events, 0.7 us)
Async XLA Ops:
  0.6 8.4 %copy-start = (bf16[1,4,256,1024]{3,2,1,0:T(8,128)(2,1)S(1)}, bf16[1,4,256,1024]{3,2,1,0:T(8,128)(2,1)}, u32[]{:S(2)}) copy-start(bf16[1,4,256,1024]{3,2,1,0:T(8,128)(2,1)} %param.6) | copy-start | bytes 6291460
  0.7 8.4 %copy-start.1 = (bf16[1,1024,1024]{2,1,0:T(8,128)(2,1)S(1)}, bf16[1,1024,1024]{2,1,0:T(8,128)(2,1)}, u32[]{:S(2)}) copy-start(bf16[1,1024,1024]{2,1,0:T(8,128)(2,1)} %param.7) | copy-start | bytes 6291460
  0.7 8.4 %copy-start.3 = (bf16[128,2048]{1,0:T(8,128)(2,1)S(1)}, bf16[128,2048]{1,0:T(8,128)(2,1)}, u32[]{:S(2)}) copy-start(bf16[128,2048]{1,0:T(8,128)(2,1)} %table_in.7) | copy-start | bytes 1572868
  8.3 4.9 %collective-permute-start.3 = (bf16[256,1024]{1,0:T(8,128)(2,1)}, bf16[256,1024]{1,0:T(8,128)(2,1)S(1)}, u32[]{:S(2)}, u32[]{:S(2)}) collective-permute-start(bf16[256,1024]{1,0:T(8,128)(2,1)} %get-tuple-element.57), channel_id=1, source_target_pairs={{24,16},{25,17},{26,18},{27,19},{28,20},{29,21},{30,22},{31,23}} | collective-permute-start | bytes 1572872 | tf_op jit(solution)/shard_map/ppermute | solution.py:539
  9.1 5.0 %collective-permute-start.2 = (bf16[256,1024]{1,0:T(8,128)(2,1)}, bf16[256,1024]{1,0:T(8,128)(2,1)S(1)}, u32[]{:S(2)}, u32[]{:S(2)}) collective-permute-start(bf16[256,1024]{1,0:T(8,128)(2,1)} %get-tuple-element.56), channel_id=1, source_target_pairs={{24,16},{25,17},{26,18},{27,19},{28,20},{29,21},{30,22},{31,23}} | collective-permute-start | bytes 1572872 | tf_op jit(solution)/shard_map/ppermute | solution.py:539
  10.1 5.4 %collective-permute-start.1 = (bf16[256,1024]{1,0:T(8,128)(2,1)}, bf16[256,1024]{1,0:T(8,128)(2,1)}, u32[]{:S(2)}, u32[]{:S(2)}) collective-permute-start(bf16[256,1024]{1,0:T(8,128)(2,1)} %get-tuple-element.55), channel_id=1, source_target_pairs={{24,16},{25,17},{26,18},{27,19},{28,20},{29,21},{30,22},{31,23}} | collective-permute-start | bytes 1572872 | tf_op jit(solution)/shard_map/ppermute | solution.py:539
  11.7 5.4 %collective-permute-start = (bf16[256,1024]{1,0:T(8,128)(2,1)}, bf16[256,1024]{1,0:T(8,128)(2,1)}, u32[]{:S(2)}, u32[]{:S(2)}) collective-permute-start(bf16[256,1024]{1,0:T(8,128)(2,1)} %get-tuple-element.54), channel_id=1, source_target_pairs={{24,16},{25,17},{26,18},{27,19},{28,20},{29,21},{30,22},{31,23}} | collective-permute-start | bytes 1572872 | tf_op jit(solution)/shard_map/ppermute | solution.py:539
  13.2 1.6 %copy-start.2 = (bf16[1,1024,1024]{2,1,0:T(8,128)(2,1)S(1)}, bf16[1,1024,1024]{2,1,0:T(8,128)(2,1)}, u32[]{:S(2)}) copy-start(bf16[1,1024,1024]{2,1,0:T(8,128)(2,1)} %param.7) | copy-start | bytes 6291460
  13.3 8.6 %collective-permute-start.6 = (bf16[256,1024]{1,0:T(8,128)(2,1)}, bf16[256,1024]{1,0:T(8,128)(2,1)S(1)}, u32[]{:S(2)}, u32[]{:S(2)}) collective-permute-start(bf16[256,1024]{1,0:T(8,128)(2,1)} %get-tuple-element.66), channel_id=1, source_target_pairs={{16,8},{17,9},{18,10},{19,11},{20,12},{21,13},{22,14},{23,15}} | collective-permute-start | bytes 1572872 | tf_op jit(solution)/shard_map/ppermute | solution.py:539
  14.8 8.4 %collective-permute-start.5 = (bf16[256,1024]{1,0:T(8,128)(2,1)}, bf16[256,1024]{1,0:T(8,128)(2,1)S(1)}, u32[]{:S(2)}, u32[]{:S(2)}) collective-permute-start(bf16[256,1024]{1,0:T(8,128)(2,1)} %get-tuple-element.65), channel_id=1, source_target_pairs={{16,8},{17,9},{18,10},{19,11},{20,12},{21,13},{22,14},{23,15}} | collective-permute-start | bytes 1572872 | tf_op jit(solution)/shard_map/ppermute | solution.py:539
  15.6 9.0 %collective-permute-start.4 = (bf16[256,1024]{1,0:T(8,128)(2,1)}, bf16[256,1024]{1,0:T(8,128)(2,1)}, u32[]{:S(2)}, u32[]{:S(2)}) collective-permute-start(bf16[256,1024]{1,0:T(8,128)(2,1)} %get-tuple-element.64), channel_id=1, source_target_pairs={{16,8},{17,9},{18,10},{19,11},{20,12},{21,13},{22,14},{23,15}} | collective-permute-start | bytes 1572872 | tf_op jit(solution)/shard_map/ppermute | solution.py:539
  17.2 8.8 %collective-permute-start.10 = (bf16[256,1024]{1,0:T(8,128)(2,1)}, bf16[256,1024]{1,0:T(8,128)(2,1)}, u32[]{:S(2)}, u32[]{:S(2)}) collective-permute-start(bf16[256,1024]{1,0:T(8,128)(2,1)} %get-tuple-element.62.after_hbm), channel_id=1, source_target_pairs={{16,8},{17,9},{18,10},{19,11},{20,12},{21,13},{22,14},{23,15}} | collective-permute-start | bytes 1572872 | tf_op jit(solution)/shard_map/ppermute | solution.py:539
  22.0 12.6 %collective-permute-start.9 = (bf16[256,1024]{1,0:T(8,128)(2,1)}, bf16[256,1024]{1,0:T(8,128)(2,1)S(1)}, u32[]{:S(2)}, u32[]{:S(2)}) collective-permute-start(bf16[256,1024]{1,0:T(8,128)(2,1)} %get-tuple-element.73), channel_id=1, source_target_pairs={{8,0},{9,1},{10,2},{11,3},{12,4},{13,5},{14,6},{15,7}} | collective-permute-start | bytes 1572872 | tf_op jit(solution)/shard_map/ppermute | solution.py:539
  23.3 16.9 %collective-permute-start.8 = (bf16[256,1024]{1,0:T(8,128)(2,1)}, bf16[256,1024]{1,0:T(8,128)(2,1)S(1)}, u32[]{:S(2)}, u32[]{:S(2)}) collective-permute-start(bf16[256,1024]{1,0:T(8,128)(2,1)} %get-tuple-element.72), channel_id=1, source_target_pairs={{8,0},{9,1},{10,2},{11,3},{12,4},{13,5},{14,6},{15,7}} | collective-permute-start | bytes 1572872 | tf_op jit(solution)/shard_map/ppermute | solution.py:539
  24.7 21.5 %collective-permute-start.7 = (bf16[256,1024]{1,0:T(8,128)(2,1)}, bf16[256,1024]{1,0:T(8,128)(2,1)}, u32[]{:S(2)}, u32[]{:S(2)}) collective-permute-start(bf16[256,1024]{1,0:T(8,128)(2,1)} %get-tuple-element.71), channel_id=1, source_target_pairs={{8,0},{9,1},{10,2},{11,3},{12,4},{13,5},{14,6},{15,7}} | collective-permute-start | bytes 1572872 | tf_op jit(solution)/shard_map/ppermute | solution.py:539
  26.3 25.4 %collective-permute-start.11 = (bf16[256,1024]{1,0:T(8,128)(2,1)}, bf16[256,1024]{1,0:T(8,128)(2,1)S(1)}, u32[]{:S(2)}, u32[]{:S(2)}) collective-permute-start(bf16[256,1024]{1,0:T(8,128)(2,1)} %get-tuple-element.76), channel_id=1, source_target_pairs={{8,0},{9,1},{10,2},{11,3},{12,4},{13,5},{14,6},{15,7}} | collective-permute-start | bytes 1572872 | tf_op jit(solution)/shard_map/ppermute | solution.py:539
  51.7 5.8 %copy-start.4 = (bf16[4,1,1024]{2,0,1:T(4,128)(2,1)S(1)}, bf16[4,1,1024]{2,0,1:T(4,128)(2,1)}, u32[]{:S(2)}) copy-start(bf16[4,1,1024]{2,0,1:T(4,128)(2,1)} %param.11) | copy-start | bytes 24580
  51.7 5.8 %copy-start.5 = (s32[4,1,64]{2,1,0:T(1,128)S(1)}, s32[4,1,64]{2,1,0:T(1,128)}, u32[]{:S(2)}) copy-start(s32[4,1,64]{2,1,0:T(1,128)} %index_ref.1) | copy-start | bytes 3076
  54.3 14.6 %collective-permute-start.12 = (bf16[512,512]{1,0:T(8,128)(2,1)}, bf16[512,512]{1,0:T(8,128)(2,1)S(1)}, u32[]{:S(2)}, u32[]{:S(2)}) collective-permute-start(bf16[512,512]{1,0:T(8,128)(2,1)} %get-tuple-element.80), channel_id=1, source_target_pairs={{0,1},{1,0},{2,3},{3,2},{4,5},{5,4},{6,7},{7,6},{8,9},{9,8},{10,11... | collective-permute-start | bytes 1572872 | tf_op jit(solution)/shard_map/ppermute | solution.py:493
  55.9 15.5 %collective-permute-start.15 = (bf16[512,512]{1,0:T(8,128)(2,1)}, bf16[512,512]{1,0:T(8,128)(2,1)S(1)}, u32[]{:S(2)}, u32[]{:S(2)}) collective-permute-start(bf16[512,512]{1,0:T(8,128)(2,1)} %get-tuple-element.82), channel_id=1, source_target_pairs={{0,2},{1,3},{2,0},{3,1},{4,6},{5,7},{6,4},{7,5},{8,10},{9,11},{10,... | collective-permute-start | bytes 1572872 | tf_op jit(solution)/shard_map/ppermute | solution.py:493
  57.6 13.1 %collective-permute-start.18 = (bf16[128,512]{1,0:T(8,128)(2,1)}, bf16[128,512]{1,0:T(8,128)(2,1)S(1)}, u32[]{:S(2)}, u32[]{:S(2)}) collective-permute-start(bf16[128,512]{1,0:T(8,128)(2,1)} %get-tuple-element.96), channel_id=1, source_target_pairs={{24,0},{25,1},{26,2},{27,3},{28,4},{29,5},{30,6},{31,7}} | collective-permute-start | bytes 393224 | tf_op jit(solution)/shard_map/ppermute | solution.py:553
  58.9 11.8 %collective-permute-start.19 = (bf16[128,512]{1,0:T(8,128)(2,1)}, bf16[128,512]{1,0:T(8,128)(2,1)S(1)}, u32[]{:S(2)}, u32[]{:S(2)}) collective-permute-start(bf16[128,512]{1,0:T(8,128)(2,1)} %get-tuple-element.97), channel_id=1, source_target_pairs={{24,8},{25,9},{26,10},{27,11},{28,12},{29,13},{30,14},{31,15}} | collective-permute-start | bytes 393224 | tf_op jit(solution)/shard_map/ppermute | solution.py:553
  59.6 11.1 %collective-permute-start.20 = (bf16[128,512]{1,0:T(8,128)(2,1)}, bf16[128,512]{1,0:T(8,128)(2,1)S(1)}, u32[]{:S(2)}, u32[]{:S(2)}) collective-permute-start(bf16[128,512]{1,0:T(8,128)(2,1)} %get-tuple-element.98), channel_id=1, source_target_pairs={{24,16},{25,17},{26,18},{27,19},{28,20},{29,21},{30,22},{31,23}} | collective-permute-start | bytes 393224 | tf_op jit(solution)/shard_map/ppermute | solution.py:553
  64.0 6.8 %copy-start.6 = (bf16[128,512]{1,0:T(8,128)(2,1)S(1)}, bf16[128,512]{1,0:T(8,128)(2,1)}, u32[]{:S(2)}) copy-start(bf16[128,512]{1,0:T(8,128)(2,1)} %get-tuple-element.95) | copy-start | bytes 393220
  69.1 9.4 %collective-permute-start.13 = (bf16[256,512]{1,0:T(8,128)(2,1)S(1)}, bf16[256,512]{1,0:T(8,128)(2,1)S(1)}, u32[]{:S(2)}, u32[]{:S(2)}) collective-permute-start(bf16[256,512]{1,0:T(8,128)(2,1)S(1)} %get-tuple-element.100), channel_id=1, source_target_pairs={{0,2},{1,3},{2,0},{3,1},{4,6},{5,7},{6,4},{7,5},{8,10},{9,11},{10,... | collective-permute-start | bytes 786440 | tf_op jit(solution)/shard_map/ppermute | solution.py:493
  71.6 14.9 %all-to-all-start = ((bf16[8,16,512]{2,1,0:T(8,128)(2,1)}), bf16[8,16,512]{2,1,0:T(8,128)(2,1)S(1)}, u32[]{:S(2)}, u32[]{:S(2)}) async-start(bf16[8,16,512]{2,1,0:T(8,128)(2,1)} %bitcast.24), calls=%async_computation | async-start | bytes 262144 | tf_op jit(solution)/shard_map/all_to_all | solution.py:500
  76.5 10.7 %collective-permute-start.16 = (bf16[256,512]{1,0:T(8,128)(2,1)S(1)}, bf16[256,512]{1,0:T(8,128)(2,1)S(1)}, u32[]{:S(2)}, u32[]{:S(2)}) collective-permute-start(bf16[256,512]{1,0:T(8,128)(2,1)S(1)} %get-tuple-element.102), channel_id=1, source_target_pairs={{0,1},{1,0},{2,3},{3,2},{4,5},{5,4},{6,7},{7,6},{8,9},{9,8},{10,11... | collective-permute-start | bytes 786440 | tf_op jit(solution)/shard_map/ppermute | solution.py:493
  78.5 10.3 %collective-permute-start.14 = (bf16[128,512]{1,0:T(8,128)(2,1)S(1)}, bf16[128,512]{1,0:T(8,128)(2,1)S(1)}, u32[]{:S(2)}, u32[]{:S(2)}) collective-permute-start(bf16[128,512]{1,0:T(8,128)(2,1)S(1)} %fusion.2), channel_id=1, source_target_pairs={{0,4},{1,5},{2,6},{3,7},{4,0},{5,1},{6,2},{7,3},{8,12},{9,13},{10,... | collective-permute-start | bytes 393224 | tf_op jit(solution)/shard_map/ppermute | solution.py:493
  87.2 7.4 %collective-permute-start.17 = (bf16[128,512]{1,0:T(8,128)(2,1)S(1)}, bf16[128,512]{1,0:T(8,128)(2,1)S(1)}, u32[]{:S(2)}, u32[]{:S(2)}) collective-permute-start(bf16[128,512]{1,0:T(8,128)(2,1)S(1)} %fusion.3), channel_id=1, source_target_pairs={{0,4},{1,5},{2,6},{3,7},{4,0},{5,1},{6,2},{7,3},{8,12},{9,13},{10,... | collective-permute-start | bytes 393224 | tf_op jit(solution)/shard_map/ppermute | solution.py:493
